TPU v7x, 256 devices: a whole 4x4x8 slice. The times are simulated.
256 devices in a mesh: dom: 64 (over x, z, y_hi), head: 4 (over y_lo, core).
Axes of the slice: x: 4, y: 4 (y_hi: 2, y_lo: 2; y = y_hi * 2 + y_lo), z: 8, core: 2. Of those that a mesh axis runs over, the one named last changes fastest.
Arguments:
- vertex_embeddings: bfloat16 [32768, 512], P(('dom', 'head')), may hold values from -6 to 6
- adjacent_group_bank_ids: int32 [64, 4, 12], P('dom', 'head'), may hold values from -1 to 15, as said below
- coupling_strength_panels: bfloat16 [16, 128, 128], replicated, may hold values from -0.3125 to 0.3125
- asking_projector: bfloat16 [512, 512], replicated, may hold values from -0.25 to 0.25
- lookup_projector: bfloat16 [512, 512], replicated, may hold values from -0.25 to 0.25
- content_projector: bfloat16 [512, 512], replicated, may hold values from -0.25 to 0.25
- final_projector: bfloat16 [512, 512], replicated, may hold values from -0.25 to 0.25
- passing_inner_coefficients: bfloat16 [512, 1024], replicated, may hold values from -0.25 to 0.25
- passing_outer_coefficients: bfloat16 [1024, 512], replicated, may hold values from -0.1875 to 0.1875
- softness_per_subspace: float32 [8], replicated, may hold values from 0.5 to 2
- mixing_layer_gain: float32 [512], replicated, may hold values from 0.5 to 1.5
Outputs:
- result: bfloat16 [32768, 512], P(('dom', 'head'))
Inputs may be any that keep to these rules, and one draw needn't show every extreme that they name: `adjacent_group_bank_ids`: -1 marks a block without edges. The entry of a block for itself is never -1, nor is at least one entry for each neighbouring partition.
All inputs are finite; a program needn't handle non-finite values.
Results may differ from a plain program's by a relative error of at most 0.0054.
Values may be sent and summed in bfloat16 or wider, within the bound.
A program may use at most 64 MiB of HBM per device.

v0:
```python
import math

import jax
import jax.numpy as jnp
from jax import lax
from jax.sharding import PartitionSpec as P

NUM_SUBSPACES = 8
SUBSPACE_WIDTH = 64


norm_eps = 1e-06


def extended(shard, sides, width):
    for axis, dim in sides:
        devices, length = (lax.axis_size(axis), shard.shape[dim])
        up = [(i, (i + 1) % devices) for i in range(devices - 1)]
        down = [(j, i) for i, j in up]
        last = lax.slice_in_dim(shard, length - width, length, axis=dim)
        first = lax.slice_in_dim(shard, 0, width, axis=dim)
        before = lax.ppermute(last, axis, up)
        after = lax.ppermute(first, axis, down)
        shard = jnp.concatenate([before, shard, after], axis=dim)
    return shard


def head_norm(projected, scales):
    rows = projected.shape[0]
    grouped = projected.reshape(rows, -1, SUBSPACE_WIDTH)
    mean_square = jnp.mean(grouped * grouped, axis=-1, keepdims=True)
    scaled = grouped * lax.rsqrt(mean_square + norm_eps)
    if scales is not None:
        scaled = scaled * scales[None, :, None]
    return scaled.reshape(rows, -1).astype(jnp.bfloat16)


def shards(
    vertex_embeddings,
    adjacent_group_bank_ids,
    coupling_strength_panels,
    asking_projector,
    lookup_projector,
    content_projector,
    final_projector,
    passing_inner_coefficients,
    passing_outer_coefficients,
    softness_per_subspace,
    mixing_layer_gain,
):
    block_len = vertex_embeddings.shape[0]
    group_size = lax.axis_size("head")
    heads_here = NUM_SUBSPACES // group_size
    head_cols = heads_here * SUBSPACE_WIDTH
    slot_ids = adjacent_group_bank_ids.reshape(-1)
    halo_rows = extended(vertex_embeddings, (("dom", 0),), block_len)
    nearby = lax.all_gather(halo_rows, "head", axis=0, tiled=True)
    slot_order = slot_ids.reshape(3, group_size).T.reshape(-1)
    asking_vector_multiplier = softness_per_subspace / math.sqrt(SUBSPACE_WIDTH)
    queries = head_norm(
        jnp.dot(vertex_embeddings, asking_projector, preferred_element_type=jnp.float32),
        asking_vector_multiplier,
    )
    keys_all = head_norm(
        jnp.dot(vertex_embeddings, lookup_projector, preferred_element_type=jnp.float32), None
    )
    values_all = jnp.dot(
        vertex_embeddings, content_projector, preferred_element_type=jnp.float32
    ).astype(jnp.bfloat16)
    queries, keys_all, values_all = (
        lax.all_to_all(queries, "head", split_axis=1, concat_axis=0, tiled=True),
        lax.all_to_all(keys_all, "head", split_axis=1, concat_axis=0, tiled=True),
        lax.all_to_all(values_all, "head", split_axis=1, concat_axis=0, tiled=True),
    )
    selected = jnp.take(coupling_strength_panels, jnp.maximum(slot_order, 0), axis=0)
    selected = jnp.where((slot_order >= 0)[:, None, None], selected, jnp.zeros_like(selected))
    wide_tiles = jnp.transpose(selected, (1, 0, 2)).reshape(block_len, -1)
    aggregate = jnp.dot(wide_tiles, nearby, preferred_element_type=jnp.float32).astype(jnp.bfloat16)
    hidden = jax.nn.gelu(
        jnp.dot(aggregate, passing_inner_coefficients, preferred_element_type=jnp.float32)
    ).astype(jnp.bfloat16)
    local_term = jnp.dot(hidden, passing_outer_coefficients, preferred_element_type=jnp.float32)
    query_rows = queries.shape[0]
    start_totals = (
        jnp.zeros((query_rows, head_cols), jnp.float32),
        jnp.zeros((query_rows, heads_here), jnp.float32),
    )
    keys_in = lax.all_gather(keys_all, "dom", axis=0, tiled=True)
    values_in = lax.all_gather(values_all, "dom", axis=0, tiled=True)
    key_count = keys_in.shape[0]
    block_step = key_count
    while block_step > 2048 and block_step % 2 == 0:
        block_step = block_step // 2

    def accumulate(turn_index, totals):
        numerator, denominator = totals
        key_block = lax.dynamic_slice_in_dim(keys_in, turn_index * block_step, block_step, 0)
        value_block = lax.dynamic_slice_in_dim(values_in, turn_index * block_step, block_step, 0)
        new_numer = []
        new_denom = []
        for head_id in range(heads_here):
            cols = slice(head_id * SUBSPACE_WIDTH, (head_id + 1) * SUBSPACE_WIDTH)
            scores = jnp.einsum(
                "qd,kd->qk",
                queries[:, cols],
                key_block[:, cols],
                preferred_element_type=jnp.float32,
            )
            weights = jnp.exp(scores).astype(jnp.bfloat16)
            new_denom.append(jnp.sum(weights, axis=1, dtype=jnp.float32))
            new_numer.append(
                jnp.dot(weights, value_block[:, cols], preferred_element_type=jnp.float32)
            )
        return (
            numerator + jnp.concatenate(new_numer, axis=1),
            denominator + jnp.stack(new_denom, axis=1),
        )

    numerator, denominator = lax.fori_loop(0, key_count // block_step, accumulate, start_totals)
    merged = (
        (numerator.reshape(query_rows, heads_here, SUBSPACE_WIDTH) / denominator[:, :, None])
        .reshape(query_rows, head_cols)
        .astype(jnp.bfloat16)
    )
    node_heads = lax.all_to_all(merged, "head", split_axis=0, concat_axis=1, tiled=True)
    attended = jnp.dot(node_heads, final_projector, preferred_element_type=jnp.float32)
    normed = (
        attended
        * lax.rsqrt(jnp.mean(attended * attended, axis=-1, keepdims=True) + norm_eps)
        * mixing_layer_gain
    )
    return (vertex_embeddings.astype(jnp.float32) + local_term + normed).astype(jnp.bfloat16)


def solution(mesh):
    in_specs = (
        P(("dom", "head"), None),
        P("dom", "head", None),
        P(),
        P(),
        P(),
        P(),
        P(),
        P(),
        P(),
        P(),
        P(),
    )
    out_specs = P(("dom", "head"), None)
    return jax.shard_map(shards, mesh=mesh, in_specs=in_specs, out_specs=out_specs, check_vma=False)
```

profile of v0, /device:TPU:4, one launch (start us, length us, event | category | flops | bytes accessed | tf_op | source)
XLA Modules:
  0.0 445.6 jit_solution(16894264735324568818)
XLA Ops:
  8.4 7.7 %all_to_all.76 = bf16[128,4,128]{2,0,1:T(8,128)(2,1)} all-to-all(bf16[128,4,128]{2,0,1:T(8,128)(2,1)S(1)} %copy_bitcast_fusion.2), channel_id=1, replica_groups=mesh['dom'=64,'head'=4] {'head'}, dimensions={1} | all-to-all | bytes 262144 | tf_op jit(solution)/shard_map/all_to_all | solution.py:72
  17.6 7.7 %all_to_all.77 = bf16[128,4,128]{2,0,1:T(8,128)(2,1)} all-to-all(bf16[128,4,128]{2,0,1:T(8,128)(2,1)S(1)} %bitcast.74), channel_id=1, replica_groups=mesh['dom'=64,'head'=4] {'head'}, dimensions={1} | all-to-all | bytes 262144 | tf_op jit(solution)/shard_map/all_to_all | solution.py:73
  25.3 5.1 %collective-permute-start = (bf16[128,512]{1,0:T(8,128)(2,1)S(1)}, bf16[128,512]{1,0:T(8,128)(2,1)S(1)}, u32[]{:S(2)}, u32[]{:S(2)}) collective-permute-start(bf16[128,512]{1,0:T(8,128)(2,1)S(1)} %copy-done.1), channel_id=1, source_target_pairs={{0,4},{4,8},{8,12},{12,16},{16,20},{20,24},{24,28},{28,32},{32,36}... | collective-permute-start | bytes 393224 | tf_op jit(solution)/shard_map/ppermute | solution.py:22
  30.4 7.2 %collective-permute-start.1 = (bf16[128,512]{1,0:T(8,128)(2,1)S(1)}, bf16[128,512]{1,0:T(8,128)(2,1)S(1)}, u32[]{:S(2)}, u32[]{:S(2)}) collective-permute-start(bf16[128,512]{1,0:T(8,128)(2,1)S(1)} %copy-done.1), channel_id=1, source_target_pairs={{4,0},{8,4},{12,8},{16,12},{20,16},{24,20},{28,24},{32,28},{36,32}... | collective-permute-start | bytes 393224 | tf_op jit(solution)/shard_map/ppermute | solution.py:23
  39.0 3.3 all-to-all-start.1
  45.2 1.8 all-to-all-done.1
  47.0 119.3 %all-gather.6.cloned.1.call-done = bf16[32768,128]{1,0:T(8,128)(2,1)} async-done(((bf16[512,128]{1,0:T(8,128)(2,1)}), bf16[32768,128]{1,0:T(8,128)(2,1)}) %all-gather.6.cloned.1.call-update) | async-done | bytes 8388624 | tf_op jit(solution)/shard_map/all_gather | solution.py:88
  166.3 147.5 %all-gather.8.cloned.1.call-done = bf16[32768,128]{1,0:T(8,128)(2,1)} async-done(((bf16[512,128]{1,0:T(8,128)(2,1)}), bf16[32768,128]{1,0:T(8,128)(2,1)}) %all-gather.8.cloned.1.call-update) | async-done | bytes 8388624 | tf_op jit(solution)/shard_map/all_gather | solution.py:89
  313.7 114.2 %while.16 = (s32[]{:T(128)}, f32[512,128]{0,1:T(8,128)S(1)}, f32[512,2]{0,1:T(2,128)S(1)}, bf16[32768,128]{1,0:T(8,128)(2,1)}, bf16[512,128]{1,0:T(8,128)(2,1)S(...) while((s32[]{:T(128)}, f32[512,128]{0,1:T(8,128)S(1)}, ...), condition=%wide.region_5.6_spmd.clone, body=%wide.region_2.5_spmd.clone.sunk | while | flops 543361024 | bytes 11813066 | solution.py:119
  313.7 1.9 convert_reduce_fusion.4
  315.6 1.7 fusion.54
  317.4 1.8 convert_reduce_fusion.5
  320.9 1.9 convert_reduce_fusion.4
  322.8 1.7 fusion.54
  324.5 1.8 convert_reduce_fusion.5
  328.0 1.9 convert_reduce_fusion.4
  331.7 1.8 convert_reduce_fusion.5
  335.2 1.9 convert_reduce_fusion.4
  337.1 1.7 fusion.54
  338.8 1.8 convert_reduce_fusion.5
  342.3 1.9 convert_reduce_fusion.4
  346.0 1.8 convert_reduce_fusion.5
  349.4 1.9 convert_reduce_fusion.4
  353.1 1.8 convert_reduce_fusion.5
  356.6 1.9 convert_reduce_fusion.4
  360.2 1.8 convert_reduce_fusion.5
  363.7 1.9 convert_reduce_fusion.4
  367.4 1.8 convert_reduce_fusion.5
  370.8 1.9 convert_reduce_fusion.4
  374.5 1.8 convert_reduce_fusion.5
  378.0 1.9 convert_reduce_fusion.4
  381.6 1.8 convert_reduce_fusion.5
  385.1 1.9 convert_reduce_fusion.4
  388.8 1.8 convert_reduce_fusion.5
  392.2 1.9 convert_reduce_fusion.4
  395.9 1.8 convert_reduce_fusion.5
  399.4 1.9 convert_reduce_fusion.4
  403.0 1.8 convert_reduce_fusion.5
  406.5 1.9 convert_reduce_fusion.4
  410.2 1.8 convert_reduce_fusion.5
  413.6 1.9 convert_reduce_fusion.4
  417.3 1.8 convert_reduce_fusion.5
  420.8 1.9 convert_reduce_fusion.4
  424.4 1.8 convert_reduce_fusion.5
  428.7 3.3 all-to-all-start.3
  432.1 2.8 fusion.21
  434.9 1.7 all-to-all-done.3
  437.2 1.9 fusion.11
  (130 shorter events, 57.7 us)
Async XLA Ops:
  6.5 425.6 %copy-start = (bf16[512,1024]{1,0:T(8,128)(2,1)S(1)}, bf16[512,1024]{1,0:T(8,128)(2,1)}, u32[]{:S(2)}) copy-start(bf16[512,1024]{1,0:T(8,128)(2,1)} %param.20) | copy-start | bytes 3145732
  6.5 18.7 %copy-start.1 = (bf16[128,512]{1,0:T(8,128)(2,1)S(1)}, bf16[128,512]{1,0:T(8,128)(2,1)}, u32[]{:S(2)}) copy-start(bf16[128,512]{1,0:T(8,128)(2,1)} %param.13) | copy-start | bytes 393220
  6.5 31.1 %copy-start.3 = (bf16[512,512]{1,0:T(8,128)(2,1)S(1)}, bf16[512,512]{1,0:T(8,128)(2,1)}, u32[]{:S(2)}) copy-start(bf16[512,512]{1,0:T(8,128)(2,1)} %param.16) | copy-start | bytes 1572868
  6.5 31.6 %copy-start.7 = (f32[8]{0:T(128)S(1)}, f32[8]{0:T(128)}, u32[]{:S(2)}) copy-start(f32[8]{0:T(128)} %param.22) | copy-start | bytes 100
  6.5 159.7 %all-gather.6.cloned.1.call-start = ((), (), s32[]{:S(2)}) async-start(), calls=%async_computation.5 | async-start | bytes 8519680 | tf_op jit(solution)/shard_map/all_gather | solution.py:88
  8.0 34.4 %copy-start.8 = (s32[1,1,12]{2,1,0:T(1,128)S(1)}, s32[1,1,12]{2,1,0:T(1,128)}, u32[]{:S(2)}) copy-start(s32[1,1,12]{2,1,0:T(1,128)} %param.14) | copy-start | bytes 148
  8.1 35.3 %copy-start.5 = (bf16[16,128,128]{2,1,0:T(8,128)(2,1)S(1)}, bf16[16,128,128]{2,1,0:T(8,128)(2,1)}, u32[]{:S(2)}) copy-start(bf16[16,128,128]{2,1,0:T(8,128)(2,1)} %param.15) | copy-start | bytes 1572868
  16.1 297.6 %all-gather.8.cloned.1.call-start = ((), (), s32[]{:S(2)}) async-start(), calls=%async_computation.6 | async-start | bytes 8519680 | tf_op jit(solution)/shard_map/all_gather | solution.py:89
  25.3 19.1 %collective-permute-start = (bf16[128,512]{1,0:T(8,128)(2,1)S(1)}, bf16[128,512]{1,0:T(8,128)(2,1)S(1)}, u32[]{:S(2)}, u32[]{:S(2)}) collective-permute-start(bf16[128,512]{1,0:T(8,128)(2,1)S(1)} %copy-done.1), channel_id=1, source_target_pairs={{0,4},{4,8},{8,12},{12,16},{16,20},{20,24},{24,28},{28,32},{32,36}... | collective-permute-start | bytes 393224 | tf_op jit(solution)/shard_map/ppermute | solution.py:22
  30.4 14.0 %collective-permute-start.1 = (bf16[128,512]{1,0:T(8,128)(2,1)S(1)}, bf16[128,512]{1,0:T(8,128)(2,1)S(1)}, u32[]{:S(2)}, u32[]{:S(2)}) collective-permute-start(bf16[128,512]{1,0:T(8,128)(2,1)S(1)} %copy-done.1), channel_id=1, source_target_pairs={{4,0},{8,4},{12,8},{16,12},{20,16},{24,20},{28,24},{32,28},{36,32}... | collective-permute-start | bytes 393224 | tf_op jit(solution)/shard_map/ppermute | solution.py:23
  39.0 7.9 %all-to-all-start.1 = ((bf16[128,4,128]{2,0,1:T(8,128)(2,1)}), bf16[128,4,128]{2,0,1:T(8,128)(2,1)S(1)}, u32[]{:S(2)}, u32[]{:S(2)}) async-start(bf16[128,4,128]{2,0,1:T(8,128)(2,1)} %copy_bitcast_fusion.1), calls=%async_computation.1 | async-start | bytes 262144 | tf_op jit(solution)/shard_map/all_to_all | solution.py:71
  42.4 389.7 %all-gather.4.cloned.1.call-start = ((), (), s32[]{:S(2)}) async-start(), calls=%async_computation.4 | async-start | bytes 1966080 | tf_op jit(solution)/shard_map/all_gather | solution.py:57
  427.9 8.9 %copy-start.4 = (bf16[512,512]{1,0:T(8,128)(2,1)S(1)}, bf16[512,512]{1,0:T(8,128)(2,1)}, u32[]{:S(2)}) copy-start(bf16[512,512]{1,0:T(8,128)(2,1)} %param.19) | copy-start | bytes 1572868
  427.9 9.2 %copy-start.2 = (bf16[1024,512]{1,0:T(8,128)(2,1)S(1)}, bf16[1024,512]{1,0:T(8,128)(2,1)}, u32[]{:S(2)}) copy-start(bf16[1024,512]{1,0:T(8,128)(2,1)} %param.21) | copy-start | bytes 3145732
  427.9 9.2 %copy-start.6 = (f32[512]{0:T(512)S(1)}, f32[512]{0:T(512)}, u32[]{:S(2)}) copy-start(f32[512]{0:T(512)} %param.23) | copy-start | bytes 6148
  428.7 7.9 %all-to-all-start.3 = ((bf16[4,128,128]{2,1,0:T(8,128)(2,1)}), bf16[4,128,128]{2,1,0:T(8,128)(2,1)S(1)}, u32[]{:S(2)}, u32[]{:S(2)}) async-start(bf16[4,128,128]{2,1,0:T(8,128)(2,1)} %bitcast.16), calls=%async_computation.3 | async-start | bytes 262144 | tf_op jit(solution)/shard_map/all_to_all | solution.py:125
Sparse Core Ops, SparseCore 0:
  16.3 149.9 all-gather.5
  169.9 143.8 all-gather.7
  315.5 24.1 all-gather.3
where the time goes:
time: 450 us; the launch traced here: 446 us
  waiting for transfers between devices  270 us (60%)
  matrix products  120 us (27%)
  starting transfers between devices  19.1 us (4%)
  blocking collectives  15.3 us (3%)
  between operations  13.5 us (3%)
    all_gather x1, waiting for transfers between devices, shards(): values_in = lax.all_gather(values_all, 'dom', axis=0, tiled=True)  147 us
    all_gather x1, waiting for transfers between devices, shards(): keys_in = lax.all_gather(keys_all, 'dom', axis=0, tiled=True)  119 us
    dot_general x32, matrix products, accumulate(): jnp.einsum('qd,kd->qk', queries[:, cols], key_block[:, cols], preferred_e...  59.1 us
    dot_general x32, matrix products, accumulate(): jnp.dot(weights, value_block[:, cols], preferred_element_type=jnp.float32)  52.5 us
  transfers between devices with their start and end apart: 7, of which 4 were waited for; matrix products, arithmetic and copies ran while one was open for 27% of the time, Pallas kernels for 0%

commit v1 on v0

v1 whole, which is shorter than its diff:
```python
import math

import jax
import jax.numpy as jnp
from jax import lax
from jax.sharding import Mesh
from jax.sharding import PartitionSpec as P

NUM_SUBSPACES = 8
SUBSPACE_WIDTH = 64
KEY_BLOCK = 2048

norm_eps = 1e-06

PLANE = "xz"
PAIR = "yhi"
DOM = (PLANE, PAIR)
GROUP = (PAIR, "head")


def extended(shard, width):
    devices = lax.axis_size(PLANE) * lax.axis_size(PAIR)
    length = shard.shape[0]
    up = [(i, (i + 1) % devices) for i in range(devices - 1)]
    down = [(j, i) for i, j in up]
    last = lax.slice_in_dim(shard, length - width, length, axis=0)
    first = lax.slice_in_dim(shard, 0, width, axis=0)
    before = lax.ppermute(last, DOM, up)
    after = lax.ppermute(first, DOM, down)
    return jnp.concatenate([before, shard, after], axis=0)


def head_norm(projected, scales):
    rows = projected.shape[0]
    grouped = projected.reshape(rows, -1, SUBSPACE_WIDTH)
    mean_square = jnp.mean(grouped * grouped, axis=-1, keepdims=True)
    scaled = grouped * lax.rsqrt(mean_square + norm_eps)
    if scales is not None:
        scaled = scaled * scales[None, :, None]
    return scaled.reshape(rows, -1).astype(jnp.bfloat16)


def shards(
    vertex_embeddings,
    adjacent_group_bank_ids,
    coupling_strength_panels,
    asking_projector,
    lookup_projector,
    content_projector,
    final_projector,
    passing_inner_coefficients,
    passing_outer_coefficients,
    softness_per_subspace,
    mixing_layer_gain,
):
    block_len = vertex_embeddings.shape[0]
    group_size = lax.axis_size("head")
    pair_size = lax.axis_size(PAIR)
    members = group_size * pair_size
    slot_ids = adjacent_group_bank_ids.reshape(-1)
    halo_rows = extended(vertex_embeddings, block_len)
    nearby = lax.all_gather(halo_rows, "head", axis=0, tiled=True)
    slot_order = slot_ids.reshape(3, group_size).T.reshape(-1)
    asking_vector_multiplier = softness_per_subspace / math.sqrt(SUBSPACE_WIDTH)
    queries = head_norm(
        jnp.dot(vertex_embeddings, asking_projector, preferred_element_type=jnp.float32),
        asking_vector_multiplier,
    )
    keys_all = head_norm(
        jnp.dot(vertex_embeddings, lookup_projector, preferred_element_type=jnp.float32), None
    )
    values_all = jnp.dot(
        vertex_embeddings, content_projector, preferred_element_type=jnp.float32
    ).astype(jnp.bfloat16)

    head_of = [(j % group_size) * pair_size + j // group_size for j in range(members)]
    member_of = [head_of.index(h) for h in range(NUM_SUBSPACES)]
    packed = jnp.stack(
        [t.reshape(block_len, NUM_SUBSPACES, SUBSPACE_WIDTH) for t in (queries, keys_all, values_all)],
        axis=2,
    )[:, jnp.array(head_of)]
    packed = packed.reshape(block_len, -1)
    mine = lax.all_to_all(packed, GROUP, split_axis=1, concat_axis=0, tiled=True)
    query_rows = mine.shape[0]
    head_queries = mine[:, :SUBSPACE_WIDTH]
    key_values = mine[:, SUBSPACE_WIDTH:]

    selected = jnp.take(coupling_strength_panels, jnp.maximum(slot_order, 0), axis=0)
    selected = jnp.where((slot_order >= 0)[:, None, None], selected, jnp.zeros_like(selected))
    wide_tiles = jnp.transpose(selected, (1, 0, 2)).reshape(block_len, -1)
    aggregate = jnp.dot(wide_tiles, nearby, preferred_element_type=jnp.float32).astype(jnp.bfloat16)
    hidden = jax.nn.gelu(
        jnp.dot(aggregate, passing_inner_coefficients, preferred_element_type=jnp.float32)
    ).astype(jnp.bfloat16)
    local_term = jnp.dot(hidden, passing_outer_coefficients, preferred_element_type=jnp.float32)

    kv_in = lax.all_gather(key_values, PLANE, axis=0, tiled=True)
    key_count = kv_in.shape[0]
    block_step = min(KEY_BLOCK, key_count)
    ones = jnp.ones((block_step, SUBSPACE_WIDTH), jnp.bfloat16)

    def accumulate(turn_index, totals):
        block = lax.dynamic_slice_in_dim(kv_in, turn_index * block_step, block_step, 0)
        scores = jnp.einsum(
            "qd,kd->qk",
            head_queries,
            block[:, :SUBSPACE_WIDTH],
            preferred_element_type=jnp.float32,
        )
        weights = jnp.exp(scores).astype(jnp.bfloat16)
        widened = jnp.concatenate([block[:, SUBSPACE_WIDTH:], ones], axis=1)
        return totals + jnp.dot(weights, widened, preferred_element_type=jnp.float32)

    totals = lax.fori_loop(
        0,
        key_count // block_step,
        accumulate,
        jnp.zeros((query_rows, 2 * SUBSPACE_WIDTH), jnp.float32),
    )
    merged = (totals[:, :SUBSPACE_WIDTH] / totals[:, SUBSPACE_WIDTH : SUBSPACE_WIDTH + 1]).astype(
        jnp.bfloat16
    )
    back = lax.all_to_all(merged, GROUP, split_axis=0, concat_axis=1, tiled=True)
    node_heads = back.reshape(block_len, members, SUBSPACE_WIDTH)[:, jnp.array(member_of)]
    node_heads = node_heads.reshape(block_len, -1)
    attended = jnp.dot(node_heads, final_projector, preferred_element_type=jnp.float32)
    normed = (
        attended
        * lax.rsqrt(jnp.mean(attended * attended, axis=-1, keepdims=True) + norm_eps)
        * mixing_layer_gain
    )
    return (vertex_embeddings.astype(jnp.float32) + local_term + normed).astype(jnp.bfloat16)


def solution(mesh):
    n_dom, n_head = mesh.shape["dom"], mesh.shape["head"]
    fine = Mesh(mesh.devices.reshape(n_dom // 2, 2, n_head), (PLANE, PAIR, "head"))
    in_specs = (
        P((PLANE, PAIR, "head"), None),
        P(DOM, "head", None),
        P(),
        P(),
        P(),
        P(),
        P(),
        P(),
        P(),
        P(),
        P(),
    )
    out_specs = P((PLANE, PAIR, "head"), None)
    return jax.shard_map(shards, mesh=fine, in_specs=in_specs, out_specs=out_specs, check_vma=False)
```

time: 450 us -> 229 us (0.51)
  waiting for transfers between devices: 270 us -> 87.6 us
  matrix products: 120 us -> 66.6 us
  local copies, waits for them, and re-layouts: 3.35 us -> 26.4 us
    all_gather x2 -> x1, waiting for transfers between devices: 267 us -> 82.5 us  [shards(): kv_in = lax.all_gather(key_values, PLANE, axis=0, tiled=True)]
    dot_general x64 -> x16, matrix products: 112 us -> 60 us  [accumulate(): jnp.dot(weights, widened, preferred_element_type=jnp.float32)]
    slice x0 -> x19, local copies, waits for them, and re-layouts: none -> 16.7 us  [the longest x16 15.6 us: accumulate(): widened = jnp.concatenate([block[:, SUBSPACE_WIDTH:], ones], axis=1)]
    while x0 -> x17, local copies, waits for them, and re-layouts: none -> 4.8 us
    all_to_all x2 -> x1, blocking collectives: 15.3 us -> 13.2 us  [shards(): lax.all_to_all(packed, GROUP, split_axis=1, concat_axis=0, tiled=True)]
  transfers between devices with their start and end apart: 7 -> 5, of which waited for: 4 -> 3; matrix products, arithmetic and copies ran while one was open for 27% -> 39% of each run, Pallas kernels for 0% -> 0%
where the time goes in v1:
time: 229 us; the launch traced here: 226 us
  waiting for transfers between devices  87.6 us (38%)
  matrix products  66.6 us (29%)
  local copies, waits for them, and re-layouts  26.4 us (12%)
  starting transfers between devices  14.7 us (6%)
  between operations  13.8 us (6%)
  blocking collectives  13.2 us (6%)
  other arithmetic  2.54 us (1%)
    all_gather x1, waiting for transfers between devices, shards(): kv_in = lax.all_gather(key_values, PLANE, axis=0, tiled=True)  82.5 us
    dot_general x16, matrix products, accumulate(): jnp.dot(weights, widened, preferred_element_type=jnp.float32)  60 us
    slice x16, local copies, waits for them, and re-layouts, accumulate(): widened = jnp.concatenate([block[:, SUBSPACE_WIDTH:], ones], axis=1)  15.6 us
    all_to_all x1, blocking collectives, shards(): lax.all_to_all(packed, GROUP, split_axis=1, concat_axis=0, tiled=True)  13.2 us
    ppermute x1, starting transfers between devices, extended(): after = lax.ppermute(first, DOM, down)  7.63 us
    while x16, local copies, waits for them, and re-layouts  4.61 us
  transfers between devices with their start and end apart: 5, of which 3 were waited for; matrix products, arithmetic and copies ran while one was open for 39% of the time, Pallas kernels for 0%

profile of v1, /device:TPU:4, one launch (start us, length us, event | category | flops | bytes accessed | tf_op | source)
XLA Modules:
  0.0 225.6 jit_solution(16693271092361854173)
XLA Ops:
  6.6 1.5 fusion.22
  9.4 1.4 fusion.21
  12.4 13.2 %all_to_all.35 = bf16[128,8,192]{0,2,1:T(8,128)(2,1)S(1)} all-to-all(bf16[128,8,192]{0,2,1:T(8,128)(2,1)S(1)} %bitcast.55), channel_id=1, replica_groups=mesh['xz'=32,'yhi'=2,'head'=4] {'yhi','head'}, dimensions={1} | all-to-all | bytes 786432 | tf_op jit(solution)/shard_map/all_to_all | solution.py:83
  25.6 0.7 slice.38
  26.4 2.7 %collective-permute-start = (bf16[128,512]{1,0:T(8,128)(2,1)S(1)}, bf16[128,512]{1,0:T(8,128)(2,1)S(1)}, u32[]{:S(2)}, u32[]{:S(2)}) collective-permute-start(bf16[128,512]{1,0:T(8,128)(2,1)S(1)} %copy-done.1), channel_id=1, source_target_pairs={{0,4},{4,8},{8,12},{12,16},{16,20},{20,24},{24,28},{28,32},{32,36}... | collective-permute-start | bytes 393224 | tf_op jit(solution)/shard_map/ppermute | solution.py:28
  29.2 7.6 %collective-permute-start.1 = (bf16[128,512]{1,0:T(8,128)(2,1)S(1)}, bf16[128,512]{1,0:T(8,128)(2,1)S(1)}, u32[]{:S(2)}, u32[]{:S(2)}) collective-permute-start(bf16[128,512]{1,0:T(8,128)(2,1)S(1)} %copy-done.1), channel_id=1, source_target_pairs={{4,0},{8,4},{12,8},{16,12},{20,16},{24,20},{28,24},{32,28},{36,32}... | collective-permute-start | bytes 393224 | tf_op jit(solution)/shard_map/ppermute | solution.py:29
  38.5 0.9 copy.69
  39.4 1.3 collective-permute-done.1
  40.7 0.8 pad_maximum_fusion
  41.7 82.5 %all-gather.5.cloned.1.call-done = bf16[32768,128]{0,1:T(8,128)(2,1)} async-done(((bf16[1024,128]{0,1:T(8,128)(2,1)}), bf16[32768,128]{0,1:T(8,128)(2,1)}) %all-gather.5.cloned.1.call-update) | async-done | bytes 8388624 | tf_op jit(solution)/shard_map/all_gather | solution.py:97
  124.2 80.8 %while.14 = (s32[]{:T(128)}, f32[1024,128]{1,0:T(8,128)S(1)}, bf16[32768,128]{0,1:T(8,128)(2,1)}, bf16[1024,64]{1,0:T(8,128)(2,1)S(1)}, s32[]{:T(128)}, /*index=5*/s32[]{:T(128)}, s32[]{:T(128)}, s32[]{:T(128)}, s32[]{}) while((s32[]{:T(128)}, f32[1024,128]{1,0:T(8,128)S(1)}, bf16[32768,128]{0,1:T(8,128)(2,1)}, ...), condition=%wide.region_3.4_spmd.clone, body=%wide.region_2.3_spmd.clone.sunk | while | flops 807665664 | bytes 2752681 | solution.py:114
  124.2 1.0 dynamic-slice.8
  125.5 3.7 %fusion.46 = f32[1024,128]{1,0:T(8,128)S(1)} fusion(bf16[1024,64]{1,0:T(8,128)(2,1)S(1)} %get-tuple-element.174, f32[1024,128]{1,0:T(8,128)S(1)} %get-tuple-element.163, bf16[2048,64]{1,0:T(8,128)(2,1)S(1)} %copy.93, bf16[32768,128]{0,1:T(8,128)(2,1)} %get-tuple-element.173, s32[]{:T(128)S(6)} %select_n.39, pred[]{:T(512)S(6)} %compare.4), kind=kOutput, calls=%fused_computation.5.clone.1 | convolution fusion | flops 807665664 | bytes 1703941 | tf_op jit(solution)/shard_map/while/body/eval_jaxpr/dot_general | solution.py:112
  129.3 1.0 dynamic-slice.8
  130.5 3.7 %fusion.46 = f32[1024,128]{1,0:T(8,128)S(1)} fusion(bf16[1024,64]{1,0:T(8,128)(2,1)S(1)} %get-tuple-element.174, f32[1024,128]{1,0:T(8,128)S(1)} %get-tuple-element.163, bf16[2048,64]{1,0:T(8,128)(2,1)S(1)} %copy.93, bf16[32768,128]{0,1:T(8,128)(2,1)} %get-tuple-element.173, s32[]{:T(128)S(6)} %select_n.39, pred[]{:T(512)S(6)} %compare.4), kind=kOutput, calls=%fused_computation.5.clone.1 | convolution fusion | flops 807665664 | bytes 1703941 | tf_op jit(solution)/shard_map/while/body/eval_jaxpr/dot_general | solution.py:112
  134.3 1.0 dynamic-slice.8
  135.6 3.8 %fusion.46 = f32[1024,128]{1,0:T(8,128)S(1)} fusion(bf16[1024,64]{1,0:T(8,128)(2,1)S(1)} %get-tuple-element.174, f32[1024,128]{1,0:T(8,128)S(1)} %get-tuple-element.163, bf16[2048,64]{1,0:T(8,128)(2,1)S(1)} %copy.93, bf16[32768,128]{0,1:T(8,128)(2,1)} %get-tuple-element.173, s32[]{:T(128)S(6)} %select_n.39, pred[]{:T(512)S(6)} %compare.4), kind=kOutput, calls=%fused_computation.5.clone.1 | convolution fusion | flops 807665664 | bytes 1703941 | tf_op jit(solution)/shard_map/while/body/eval_jaxpr/dot_general | solution.py:112
  139.4 1.0 dynamic-slice.8
  140.6 3.8 %fusion.46 = f32[1024,128]{1,0:T(8,128)S(1)} fusion(bf16[1024,64]{1,0:T(8,128)(2,1)S(1)} %get-tuple-element.174, f32[1024,128]{1,0:T(8,128)S(1)} %get-tuple-element.163, bf16[2048,64]{1,0:T(8,128)(2,1)S(1)} %copy.93, bf16[32768,128]{0,1:T(8,128)(2,1)} %get-tuple-element.173, s32[]{:T(128)S(6)} %select_n.39, pred[]{:T(512)S(6)} %compare.4), kind=kOutput, calls=%fused_computation.5.clone.1 | convolution fusion | flops 807665664 | bytes 1703941 | tf_op jit(solution)/shard_map/while/body/eval_jaxpr/dot_general | solution.py:112
  144.4 1.0 dynamic-slice.8
  145.7 3.8 %fusion.46 = f32[1024,128]{1,0:T(8,128)S(1)} fusion(bf16[1024,64]{1,0:T(8,128)(2,1)S(1)} %get-tuple-element.174, f32[1024,128]{1,0:T(8,128)S(1)} %get-tuple-element.163, bf16[2048,64]{1,0:T(8,128)(2,1)S(1)} %copy.93, bf16[32768,128]{0,1:T(8,128)(2,1)} %get-tuple-element.173, s32[]{:T(128)S(6)} %select_n.39, pred[]{:T(512)S(6)} %compare.4), kind=kOutput, calls=%fused_computation.5.clone.1 | convolution fusion | flops 807665664 | bytes 1703941 | tf_op jit(solution)/shard_map/while/body/eval_jaxpr/dot_general | solution.py:112
  149.5 1.0 dynamic-slice.8
  150.8 3.7 %fusion.46 = f32[1024,128]{1,0:T(8,128)S(1)} fusion(bf16[1024,64]{1,0:T(8,128)(2,1)S(1)} %get-tuple-element.174, f32[1024,128]{1,0:T(8,128)S(1)} %get-tuple-element.163, bf16[2048,64]{1,0:T(8,128)(2,1)S(1)} %copy.93, bf16[32768,128]{0,1:T(8,128)(2,1)} %get-tuple-element.173, s32[]{:T(128)S(6)} %select_n.39, pred[]{:T(512)S(6)} %compare.4), kind=kOutput, calls=%fused_computation.5.clone.1 | convolution fusion | flops 807665664 | bytes 1703941 | tf_op jit(solution)/shard_map/while/body/eval_jaxpr/dot_general | solution.py:112
  154.5 1.0 dynamic-slice.8
  155.8 3.7 %fusion.46 = f32[1024,128]{1,0:T(8,128)S(1)} fusion(bf16[1024,64]{1,0:T(8,128)(2,1)S(1)} %get-tuple-element.174, f32[1024,128]{1,0:T(8,128)S(1)} %get-tuple-element.163, bf16[2048,64]{1,0:T(8,128)(2,1)S(1)} %copy.93, bf16[32768,128]{0,1:T(8,128)(2,1)} %get-tuple-element.173, s32[]{:T(128)S(6)} %select_n.39, pred[]{:T(512)S(6)} %compare.4), kind=kOutput, calls=%fused_computation.5.clone.1 | convolution fusion | flops 807665664 | bytes 1703941 | tf_op jit(solution)/shard_map/while/body/eval_jaxpr/dot_general | solution.py:112
  159.6 1.0 dynamic-slice.8
  160.9 3.7 %fusion.46 = f32[1024,128]{1,0:T(8,128)S(1)} fusion(bf16[1024,64]{1,0:T(8,128)(2,1)S(1)} %get-tuple-element.174, f32[1024,128]{1,0:T(8,128)S(1)} %get-tuple-element.163, bf16[2048,64]{1,0:T(8,128)(2,1)S(1)} %copy.93, bf16[32768,128]{0,1:T(8,128)(2,1)} %get-tuple-element.173, s32[]{:T(128)S(6)} %select_n.39, pred[]{:T(512)S(6)} %compare.4), kind=kOutput, calls=%fused_computation.5.clone.1 | convolution fusion | flops 807665664 | bytes 1703941 | tf_op jit(solution)/shard_map/while/body/eval_jaxpr/dot_general | solution.py:112
  164.6 1.0 dynamic-slice.8
  165.9 3.7 %fusion.46 = f32[1024,128]{1,0:T(8,128)S(1)} fusion(bf16[1024,64]{1,0:T(8,128)(2,1)S(1)} %get-tuple-element.174, f32[1024,128]{1,0:T(8,128)S(1)} %get-tuple-element.163, bf16[2048,64]{1,0:T(8,128)(2,1)S(1)} %copy.93, bf16[32768,128]{0,1:T(8,128)(2,1)} %get-tuple-element.173, s32[]{:T(128)S(6)} %select_n.39, pred[]{:T(512)S(6)} %compare.4), kind=kOutput, calls=%fused_computation.5.clone.1 | convolution fusion | flops 807665664 | bytes 1703941 | tf_op jit(solution)/shard_map/while/body/eval_jaxpr/dot_general | solution.py:112
  169.7 1.0 dynamic-slice.8
  171.0 3.7 %fusion.46 = f32[1024,128]{1,0:T(8,128)S(1)} fusion(bf16[1024,64]{1,0:T(8,128)(2,1)S(1)} %get-tuple-element.174, f32[1024,128]{1,0:T(8,128)S(1)} %get-tuple-element.163, bf16[2048,64]{1,0:T(8,128)(2,1)S(1)} %copy.93, bf16[32768,128]{0,1:T(8,128)(2,1)} %get-tuple-element.173, s32[]{:T(128)S(6)} %select_n.39, pred[]{:T(512)S(6)} %compare.4), kind=kOutput, calls=%fused_computation.5.clone.1 | convolution fusion | flops 807665664 | bytes 1703941 | tf_op jit(solution)/shard_map/while/body/eval_jaxpr/dot_general | solution.py:112
  174.8 1.0 dynamic-slice.8
  176.0 3.7 %fusion.46 = f32[1024,128]{1,0:T(8,128)S(1)} fusion(bf16[1024,64]{1,0:T(8,128)(2,1)S(1)} %get-tuple-element.174, f32[1024,128]{1,0:T(8,128)S(1)} %get-tuple-element.163, bf16[2048,64]{1,0:T(8,128)(2,1)S(1)} %copy.93, bf16[32768,128]{0,1:T(8,128)(2,1)} %get-tuple-element.173, s32[]{:T(128)S(6)} %select_n.39, pred[]{:T(512)S(6)} %compare.4), kind=kOutput, calls=%fused_computation.5.clone.1 | convolution fusion | flops 807665664 | bytes 1703941 | tf_op jit(solution)/shard_map/while/body/eval_jaxpr/dot_general | solution.py:112
  179.8 1.0 dynamic-slice.8
  181.1 3.7 %fusion.46 = f32[1024,128]{1,0:T(8,128)S(1)} fusion(bf16[1024,64]{1,0:T(8,128)(2,1)S(1)} %get-tuple-element.174, f32[1024,128]{1,0:T(8,128)S(1)} %get-tuple-element.163, bf16[2048,64]{1,0:T(8,128)(2,1)S(1)} %copy.93, bf16[32768,128]{0,1:T(8,128)(2,1)} %get-tuple-element.173, s32[]{:T(128)S(6)} %select_n.39, pred[]{:T(512)S(6)} %compare.4), kind=kOutput, calls=%fused_computation.5.clone.1 | convolution fusion | flops 807665664 | bytes 1703941 | tf_op jit(solution)/shard_map/while/body/eval_jaxpr/dot_general | solution.py:112
  184.9 1.0 dynamic-slice.8
  186.1 3.7 %fusion.46 = f32[1024,128]{1,0:T(8,128)S(1)} fusion(bf16[1024,64]{1,0:T(8,128)(2,1)S(1)} %get-tuple-element.174, f32[1024,128]{1,0:T(8,128)S(1)} %get-tuple-element.163, bf16[2048,64]{1,0:T(8,128)(2,1)S(1)} %copy.93, bf16[32768,128]{0,1:T(8,128)(2,1)} %get-tuple-element.173, s32[]{:T(128)S(6)} %select_n.39, pred[]{:T(512)S(6)} %compare.4), kind=kOutput, calls=%fused_computation.5.clone.1 | convolution fusion | flops 807665664 | bytes 1703941 | tf_op jit(solution)/shard_map/while/body/eval_jaxpr/dot_general | solution.py:112
  189.9 1.0 dynamic-slice.8
  191.2 3.7 %fusion.46 = f32[1024,128]{1,0:T(8,128)S(1)} fusion(bf16[1024,64]{1,0:T(8,128)(2,1)S(1)} %get-tuple-element.174, f32[1024,128]{1,0:T(8,128)S(1)} %get-tuple-element.163, bf16[2048,64]{1,0:T(8,128)(2,1)S(1)} %copy.93, bf16[32768,128]{0,1:T(8,128)(2,1)} %get-tuple-element.173, s32[]{:T(128)S(6)} %select_n.39, pred[]{:T(512)S(6)} %compare.4), kind=kOutput, calls=%fused_computation.5.clone.1 | convolution fusion | flops 807665664 | bytes 1703941 | tf_op jit(solution)/shard_map/while/body/eval_jaxpr/dot_general | solution.py:112
  195.0 1.0 dynamic-slice.8
  196.2 3.7 %fusion.46 = f32[1024,128]{1,0:T(8,128)S(1)} fusion(bf16[1024,64]{1,0:T(8,128)(2,1)S(1)} %get-tuple-element.174, f32[1024,128]{1,0:T(8,128)S(1)} %get-tuple-element.163, bf16[2048,64]{1,0:T(8,128)(2,1)S(1)} %copy.93, bf16[32768,128]{0,1:T(8,128)(2,1)} %get-tuple-element.173, s32[]{:T(128)S(6)} %select_n.39, pred[]{:T(512)S(6)} %compare.4), kind=kOutput, calls=%fused_computation.5.clone.1 | convolution fusion | flops 807665664 | bytes 1703941 | tf_op jit(solution)/shard_map/while/body/eval_jaxpr/dot_general | solution.py:112
  200.0 1.0 dynamic-slice.8
  201.3 3.7 %fusion.46 = f32[1024,128]{1,0:T(8,128)S(1)} fusion(bf16[1024,64]{1,0:T(8,128)(2,1)S(1)} %get-tuple-element.174, f32[1024,128]{1,0:T(8,128)S(1)} %get-tuple-element.163, bf16[2048,64]{1,0:T(8,128)(2,1)S(1)} %copy.93, bf16[32768,128]{0,1:T(8,128)(2,1)} %get-tuple-element.173, s32[]{:T(128)S(6)} %select_n.39, pred[]{:T(512)S(6)} %compare.4), kind=kOutput, calls=%fused_computation.5.clone.1 | convolution fusion | flops 807665664 | bytes 1703941 | tf_op jit(solution)/shard_map/while/body/eval_jaxpr/dot_general | solution.py:112
  205.7 0.7 copy_bitcast_fusion.1
  206.4 4.3 %all-to-all-start.1 = ((bf16[8,128,64]{1,2,0:T(8,128)(2,1)}), bf16[8,128,64]{1,2,0:T(8,128)(2,1)S(1)}, u32[]{:S(2)}, u32[]{:S(2)}) async-start(bf16[8,128,64]{1,2,0:T(8,128)(2,1)} %copy_bitcast_fusion.1), calls=%async_computation.1 | async-start | bytes 262144 | tf_op jit(solution)/shard_map/all_to_all | solution.py:123
  210.7 2.3 %fusion.18 = bf16[128,1024]{1,0:T(8,128)(2,1)S(1)} fusion(bf16[512,1024]{1,0:T(8,128)(2,1)S(1)} %copy-done, bf16[128,1536]{0,1:T(8,128)(2,1)} %bitcast.63, bf16[1536,512]{1,0:T(8,128)(2,1)} %all-gather.3.cloned.1.call-done), kind=kOutput, calls=%fused_computation.24 | convolution fusion | flops 336789504 | bytes 3276800 | tf_op jit(solution)/shard_map/dot_general | solution.py:93
  212.9 3.8 %all-to-all-done.1 = bf16[8,128,64]{1,2,0:T(8,128)(2,1)S(1)} async-done(((bf16[8,128,64]{1,2,0:T(8,128)(2,1)}), bf16[8,128,64]{1,2,0:T(8,128)(2,1)S(1)}, u32[]{:S(2)}, u32[]{:S(2)}) %all-to-all-start.1) | async-done | bytes 131104 | tf_op jit(solution)/shard_map/all_to_all | solution.py:123
  217.7 1.0 fusion.9
  (88 shorter events, 10.9 us)
Async XLA Ops:
  6.5 204.1 %copy-start = (bf16[512,1024]{1,0:T(8,128)(2,1)S(1)}, bf16[512,1024]{1,0:T(8,128)(2,1)}, u32[]{:S(2)}) copy-start(bf16[512,1024]{1,0:T(8,128)(2,1)} %param.22) | copy-start | bytes 3145732
  6.5 5.1 %copy-start.8 = (s32[8]{0:T(128)S(1)}, s32[8]{0:T(128)}, u32[]{:S(2)}) copy-start(s32[8]{0:T(128)} %constant.100) | copy-start | bytes 100
  6.5 4.7 %copy-start.1 = (bf16[128,512]{1,0:T(8,128)(2,1)S(1)}, bf16[128,512]{1,0:T(8,128)(2,1)}, u32[]{:S(2)}) copy-start(bf16[128,512]{1,0:T(8,128)(2,1)} %param.15) | copy-start | bytes 393220
  6.5 4.7 %copy-start.3 = (bf16[512,512]{1,0:T(8,128)(2,1)S(1)}, bf16[512,512]{1,0:T(8,128)(2,1)}, u32[]{:S(2)}) copy-start(bf16[512,512]{1,0:T(8,128)(2,1)} %param.20) | copy-start | bytes 1572868
  6.5 117.7 %all-gather.5.cloned.1.call-start = ((), (), s32[]{:S(2)}) async-start(), calls=%async_computation.3 | async-start | bytes 8650752 | tf_op jit(solution)/shard_map/all_gather | solution.py:97
  10.9 25.9 %copy-start.9 = (s32[1,1,12]{2,1,0:T(1,128)S(1)}, s32[1,1,12]{2,1,0:T(1,128)}, u32[]{:S(2)}) copy-start(s32[1,1,12]{2,1,0:T(1,128)} %param.16) | copy-start | bytes 148
  10.9 26.8 %copy-start.5 = (bf16[16,128,128]{2,1,0:T(8,128)(2,1)S(1)}, bf16[16,128,128]{2,1,0:T(8,128)(2,1)}, u32[]{:S(2)}) copy-start(bf16[16,128,128]{2,1,0:T(8,128)(2,1)} %param.17) | copy-start | bytes 1572868
  11.3 28.1 %copy-start.7 = (s32[8]{0:T(128)S(1)}, s32[8]{0:T(128)}, u32[]{:S(2)}) copy-start(s32[8]{0:T(128)} %constant.101) | copy-start | bytes 100
  26.4 184.3 %all-gather.3.cloned.1.call-start = ((), (), s32[]{:S(2)}) async-start(), calls=%async_computation.2 | async-start | bytes 1966080 | tf_op jit(solution)/shard_map/all_gather | solution.py:62
  26.4 13.0 %collective-permute-start = (bf16[128,512]{1,0:T(8,128)(2,1)S(1)}, bf16[128,512]{1,0:T(8,128)(2,1)S(1)}, u32[]{:S(2)}, u32[]{:S(2)}) collective-permute-start(bf16[128,512]{1,0:T(8,128)(2,1)S(1)} %copy-done.1), channel_id=1, source_target_pairs={{0,4},{4,8},{8,12},{12,16},{16,20},{20,24},{24,28},{28,32},{32,36}... | collective-permute-start | bytes 393224 | tf_op jit(solution)/shard_map/ppermute | solution.py:28
  29.2 11.5 %collective-permute-start.1 = (bf16[128,512]{1,0:T(8,128)(2,1)S(1)}, bf16[128,512]{1,0:T(8,128)(2,1)S(1)}, u32[]{:S(2)}, u32[]{:S(2)}) collective-permute-start(bf16[128,512]{1,0:T(8,128)(2,1)S(1)} %copy-done.1), channel_id=1, source_target_pairs={{4,0},{8,4},{12,8},{16,12},{20,16},{24,20},{28,24},{32,28},{36,32}... | collective-permute-start | bytes 393224 | tf_op jit(solution)/shard_map/ppermute | solution.py:29
  205.1 12.7 %copy-start.2 = (bf16[1024,512]{1,0:T(8,128)(2,1)S(1)}, bf16[1024,512]{1,0:T(8,128)(2,1)}, u32[]{:S(2)}) copy-start(bf16[1024,512]{1,0:T(8,128)(2,1)} %param.23) | copy-start | bytes 3145732
  205.1 12.7 %copy-start.6 = (f32[512]{0:T(512)S(1)}, f32[512]{0:T(512)}, u32[]{:S(2)}) copy-start(f32[512]{0:T(512)} %param.25) | copy-start | bytes 6148
  205.7 11.7 %copy-start.4 = (bf16[512,512]{1,0:T(8,128)(2,1)S(1)}, bf16[512,512]{1,0:T(8,128)(2,1)}, u32[]{:S(2)}) copy-start(bf16[512,512]{1,0:T(8,128)(2,1)} %param.21) | copy-start | bytes 1572868
  206.4 10.4 %all-to-all-start.1 = ((bf16[8,128,64]{1,2,0:T(8,128)(2,1)}), bf16[8,128,64]{1,2,0:T(8,128)(2,1)S(1)}, u32[]{:S(2)}, u32[]{:S(2)}) async-start(bf16[8,128,64]{1,2,0:T(8,128)(2,1)} %copy_bitcast_fusion.1), calls=%async_computation.1 | async-start | bytes 262144 | tf_op jit(solution)/shard_map/all_to_all | solution.py:123
Sparse Core Ops, SparseCore 0:
  26.5 97.6 all-gather.4
  126.0 25.9 all-gather.2

commit v2 on v1

--- a/solution.py
+++ b/solution.py
@@ -9,6 +9,7 @@
 NUM_SUBSPACES = 8
 SUBSPACE_WIDTH = 64
 KEY_BLOCK = 2048
+KV_PIECES = 4
 
 norm_eps = 1e-06
 
@@ -59,7 +60,14 @@
     members = group_size * pair_size
     slot_ids = adjacent_group_bank_ids.reshape(-1)
     halo_rows = extended(vertex_embeddings, block_len)
-    nearby = lax.all_gather(halo_rows, "head", axis=0, tiled=True)
+    me = lax.axis_index("head")
+    gathered = [halo_rows]
+    for shift in range(1, group_size):
+        pairs = [(i, (i + shift) % group_size) for i in range(group_size)]
+        gathered.append(lax.ppermute(halo_rows, "head", pairs))
+    stacked = jnp.stack(gathered)
+    order = (me - jnp.arange(group_size)) % group_size
+    nearby = jnp.zeros_like(stacked).at[order].set(stacked).reshape(-1, halo_rows.shape[1])
     slot_order = slot_ids.reshape(3, group_size).T.reshape(-1)
     asking_vector_multiplier = softness_per_subspace / math.sqrt(SUBSPACE_WIDTH)
     queries = head_norm(
@@ -94,29 +102,30 @@
     ).astype(jnp.bfloat16)
     local_term = jnp.dot(hidden, passing_outer_coefficients, preferred_element_type=jnp.float32)
 
-    kv_in = lax.all_gather(key_values, PLANE, axis=0, tiled=True)
-    key_count = kv_in.shape[0]
-    block_step = min(KEY_BLOCK, key_count)
-    ones = jnp.ones((block_step, SUBSPACE_WIDTH), jnp.bfloat16)
+    local_term, head_queries = lax.optimization_barrier((local_term, head_queries))
+    piece_rows = query_rows // KV_PIECES
+    totals = jnp.zeros((query_rows, 2 * SUBSPACE_WIDTH), jnp.float32)
+    for piece in range(KV_PIECES):
+        kv_in = lax.all_gather(
+            key_values[piece * piece_rows : (piece + 1) * piece_rows], PLANE, axis=0, tiled=True
+        )
+        key_count = kv_in.shape[0]
+        block_step = min(KEY_BLOCK, key_count)
+        ones = jnp.ones((block_step, SUBSPACE_WIDTH), jnp.bfloat16)
 
-    def accumulate(turn_index, totals):
-        block = lax.dynamic_slice_in_dim(kv_in, turn_index * block_step, block_step, 0)
-        scores = jnp.einsum(
-            "qd,kd->qk",
-            head_queries,
-            block[:, :SUBSPACE_WIDTH],
-            preferred_element_type=jnp.float32,
-        )
-        weights = jnp.exp(scores).astype(jnp.bfloat16)
-        widened = jnp.concatenate([block[:, SUBSPACE_WIDTH:], ones], axis=1)
-        return totals + jnp.dot(weights, widened, preferred_element_type=jnp.float32)
+        def accumulate(turn_index, totals, kv_in=kv_in, block_step=block_step, ones=ones):
+            block = lax.dynamic_slice_in_dim(kv_in, turn_index * block_step, block_step, 0)
+            scores = jnp.einsum(
+                "qd,kd->qk",
+                head_queries,
+                block[:, :SUBSPACE_WIDTH],
+                preferred_element_type=jnp.float32,
+            )
+            weights = jnp.exp(scores).astype(jnp.bfloat16)
+            widened = jnp.concatenate([block[:, SUBSPACE_WIDTH:], ones], axis=1)
+            return totals + jnp.dot(weights, widened, preferred_element_type=jnp.float32)
 
-    totals = lax.fori_loop(
-        0,
-        key_count // block_step,
-        accumulate,
-        jnp.zeros((query_rows, 2 * SUBSPACE_WIDTH), jnp.float32),
-    )
+        totals = lax.fori_loop(0, key_count // block_step, accumulate, totals)
     merged = (totals[:, :SUBSPACE_WIDTH] / totals[:, SUBSPACE_WIDTH : SUBSPACE_WIDTH + 1]).astype(
         jnp.bfloat16
     )

time: 229 us -> 373 us (1.63)
  waiting for transfers between devices: 87.6 us -> 227 us
  local copies, waits for them, and re-layouts: 26.4 us -> 32.4 us
    all_gather x2 -> x4, waiting for transfers between devices: 82.5 us -> 202 us  [shards(): lax.all_gather(key_values[piece * piece_rows:(piece + 1) * piece_rows], P...]
    ppermute x0 -> x3, waiting for transfers between devices: none -> 13.5 us  [shards(): gathered.append(lax.ppermute(halo_rows, 'head', pairs))]
    scatter x0 -> x1, local copies, waits for them, and re-layouts: none -> 4.71 us  [shards(): jnp.zeros_like(stacked).at[order].set(stacked)]
  transfers between devices with their start and end apart: 5 -> 10, of which waited for: 3 -> 10; matrix products, arithmetic and copies ran while one was open for 39% -> 19% of each run, Pallas kernels for 0% -> 0%
where the time goes in v2:
time: 373 us; the launch traced here: 371 us
  waiting for transfers between devices  227 us (61%)
  matrix products  63.2 us (17%)
  local copies, waits for them, and re-layouts  32.4 us (9%)
  starting transfers between devices  17.2 us (5%)
  between operations  13.6 us (4%)
  blocking collectives  13.2 us (4%)
  other arithmetic  4.16 us (1%)
    all_gather x4, waiting for transfers between devices, shards(): lax.all_gather(key_values[piece * piece_rows:(piece + 1) * piece_rows], P...  202 us
    dot_general x16, matrix products, accumulate(): jnp.dot(weights, widened, preferred_element_type=jnp.float32)  58.4 us
    slice x16, local copies, waits for them, and re-layouts, accumulate(): widened = jnp.concatenate([block[:, SUBSPACE_WIDTH:], ones], axis=1)  15.6 us
    ppermute x3, waiting for transfers between devices, shards(): gathered.append(lax.ppermute(halo_rows, 'head', pairs))  13.5 us
    all_to_all x1, blocking collectives, shards(): lax.all_to_all(packed, GROUP, split_axis=1, concat_axis=0, tiled=True)  13.2 us
    ppermute x1, starting transfers between devices, extended(): after = lax.ppermute(first, DOM, down)  7.63 us
  transfers between devices with their start and end apart: 10, of which 10 were waited for; matrix products, arithmetic and copies ran while one was open for 19% of the time, Pallas kernels for 0%

profile of v2, /device:TPU:4, one launch (start us, length us, event | category | flops | bytes accessed | tf_op | source)
XLA Modules:
  0.0 370.9 jit_solution(10361992699685915470)
XLA Ops:
  7.6 1.3 fusion.47
  11.7 13.2 %all_to_all.35 = bf16[128,8,192]{0,2,1:T(8,128)(2,1)S(1)} all-to-all(bf16[128,8,192]{0,2,1:T(8,128)(2,1)S(1)} %bitcast.72), channel_id=1, replica_groups=mesh['xz'=32,'yhi'=2,'head'=4] {'yhi','head'}, dimensions={1} | all-to-all | bytes 786432 | tf_op jit(solution)/shard_map/all_to_all | solution.py:91
  27.3 2.7 collective-permute-start
  30.0 7.6 %collective-permute-start.1 = (bf16[128,512]{1,0:T(8,128)(2,1)S(1)}, bf16[128,512]{1,0:T(8,128)(2,1)S(1)}, u32[]{:S(2)}, u32[]{:S(2)}) collective-permute-start(bf16[128,512]{1,0:T(8,128)(2,1)S(1)} %copy-done.1), channel_id=1, source_target_pairs={{4,0},{8,4},{12,8},{16,12},{20,16},{24,20},{28,24},{32,28},{36,32}... | collective-permute-start | bytes 393224 | tf_op jit(solution)/shard_map/ppermute | solution.py:30
  37.7 1.2 collective-permute-done
  38.9 2.7 collective-permute-done.1
  42.6 1.4 collective-permute-start.4
  46.3 6.2 %collective-permute-done.2 = bf16[384,512]{1,0:T(8,128)(2,1)} collective-permute-done((bf16[384,512]{1,0:T(8,128)(2,1)S(1)}, bf16[384,512]{1,0:T(8,128)(2,1)}, u32[]{:S(2)}, u32[]{:S(2)}) %collective-permute-start.2) | collective-permute-done | bytes 393248 | tf_op jit(solution)/shard_map/ppermute | solution.py:67
  52.5 1.3 collective-permute-done.3
  53.8 6.0 %collective-permute-done.4 = bf16[384,512]{1,0:T(8,128)(2,1)} collective-permute-done((bf16[384,512]{1,0:T(8,128)(2,1)S(1)}, bf16[384,512]{1,0:T(8,128)(2,1)}, u32[]{:S(2)}, u32[]{:S(2)}) %collective-permute-start.4) | collective-permute-done | bytes 393248 | tf_op jit(solution)/shard_map/ppermute | solution.py:67
  59.8 1.5 pad_maximum_fusion
  61.4 1.3 broadcast_in_dim.44
  62.7 4.7 %scatter_fusion = bf16[4,384,512]{2,1,0:T(8,128)(2,1)} fusion(bf16[4,384,512]{2,1,0:T(8,128)(2,1)} %broadcast_in_dim.44, s32[4]{0:T(128)S(1)} %fusion.44, bf16[4,384,512]{2,1,0:T(8,128)(2,1)S(1)} %pad_maximum_fusion), kind=kCustom, calls=%fused_computation.3 | custom fusion | bytes 4718608 | tf_op jit(solution)/shard_map/scatter | solution.py:70
  67.4 2.3 fusion.40
  70.3 31.5 %all-gather.5.cloned.1.call-done = bf16[8192,128]{0,1:T(8,128)(2,1)} async-done(((bf16[256,128]{0,1:T(8,128)(2,1)}), bf16[8192,128]{0,1:T(8,128)(2,1)}) %all-gather.5.cloned.1.call-update) | async-done | bytes 2097168 | tf_op jit(solution)/shard_map/all_gather | solution.py:109
  101.8 20.0 %while.56 = (s32[]{:T(128)}, f32[1024,128]{1,0:T(8,128)S(1)}, bf16[8192,128]{0,1:T(8,128)(2,1)}, bf16[1024,64]{1,0:T(8,128)(2,1)S(1)}, s32[]{:T(128)}, /*index=5*/s32[]{:T(128)}, s32[]{:T(128)}, s32[]{:T(128)}, s32[]{}) while((s32[]{:T(128)}, f32[1024,128]{1,0:T(8,128)S(1)}, bf16[8192,128]{0,1:T(8,128)(2,1)}, ...), condition=%wide.region_4.5_spmd.clone, body=%wide.region_3.4_spmd.clone.sunk | while | flops 807665664 | bytes 2752681 | solution.py:128
  103.1 3.7 %fusion.99 = f32[1024,128]{1,0:T(8,128)S(1)} fusion(bf16[1024,64]{1,0:T(8,128)(2,1)S(1)} %get-tuple-element.559, f32[1024,128]{1,0:T(8,128)S(1)} %get-tuple-element.548, bf16[2048,64]{1,0:T(8,128)(2,1)S(1)} %copy.126, bf16[8192,128]{0,1:T(8,128)(2,1)} %get-tuple-element.558, s32[]{:T(128)S(6)} %select_n.100, pred[]{:T(512)S(6)} %compare.14), kind=kOutput, calls=%fused_computation.27.clone.1 | convolution fusion | flops 807665664 | bytes 1703941 | tf_op jit(solution)/shard_map/while/body/eval_jaxpr/dot_general | solution.py:126
  106.8 1.0 dynamic-slice.35
  108.1 3.7 %fusion.99 = f32[1024,128]{1,0:T(8,128)S(1)} fusion(bf16[1024,64]{1,0:T(8,128)(2,1)S(1)} %get-tuple-element.559, f32[1024,128]{1,0:T(8,128)S(1)} %get-tuple-element.548, bf16[2048,64]{1,0:T(8,128)(2,1)S(1)} %copy.126, bf16[8192,128]{0,1:T(8,128)(2,1)} %get-tuple-element.558, s32[]{:T(128)S(6)} %select_n.100, pred[]{:T(512)S(6)} %compare.14), kind=kOutput, calls=%fused_computation.27.clone.1 | convolution fusion | flops 807665664 | bytes 1703941 | tf_op jit(solution)/shard_map/while/body/eval_jaxpr/dot_general | solution.py:126
  111.8 1.0 dynamic-slice.35
  113.1 3.7 %fusion.99 = f32[1024,128]{1,0:T(8,128)S(1)} fusion(bf16[1024,64]{1,0:T(8,128)(2,1)S(1)} %get-tuple-element.559, f32[1024,128]{1,0:T(8,128)S(1)} %get-tuple-element.548, bf16[2048,64]{1,0:T(8,128)(2,1)S(1)} %copy.126, bf16[8192,128]{0,1:T(8,128)(2,1)} %get-tuple-element.558, s32[]{:T(128)S(6)} %select_n.100, pred[]{:T(512)S(6)} %compare.14), kind=kOutput, calls=%fused_computation.27.clone.1 | convolution fusion | flops 807665664 | bytes 1703941 | tf_op jit(solution)/shard_map/while/body/eval_jaxpr/dot_general | solution.py:126
  116.9 1.0 dynamic-slice.35
  118.1 3.7 %fusion.99 = f32[1024,128]{1,0:T(8,128)S(1)} fusion(bf16[1024,64]{1,0:T(8,128)(2,1)S(1)} %get-tuple-element.559, f32[1024,128]{1,0:T(8,128)S(1)} %get-tuple-element.548, bf16[2048,64]{1,0:T(8,128)(2,1)S(1)} %copy.126, bf16[8192,128]{0,1:T(8,128)(2,1)} %get-tuple-element.558, s32[]{:T(128)S(6)} %select_n.100, pred[]{:T(512)S(6)} %compare.14), kind=kOutput, calls=%fused_computation.27.clone.1 | convolution fusion | flops 807665664 | bytes 1703941 | tf_op jit(solution)/shard_map/while/body/eval_jaxpr/dot_general | solution.py:126
  121.9 56.5 %all-gather.7.cloned.1.call-done = bf16[8192,128]{0,1:T(8,128)(2,1)} async-done(((bf16[256,128]{0,1:T(8,128)(2,1)}), bf16[8192,128]{0,1:T(8,128)(2,1)}) %all-gather.7.cloned.1.call-update) | async-done | bytes 2097168 | tf_op jit(solution)/shard_map/all_gather | solution.py:109
  178.4 19.6 %while.53 = (s32[]{:T(128)}, f32[1024,128]{1,0:T(8,128)S(1)}, bf16[8192,128]{0,1:T(8,128)(2,1)}, bf16[1024,64]{1,0:T(8,128)(2,1)S(1)}, s32[]{:T(128)}, /*index=5*/s32[]{:T(128)}, s32[]{:T(128)}, s32[]{:T(128)}, s32[]{}) while((s32[]{:T(128)}, f32[1024,128]{1,0:T(8,128)S(1)}, bf16[8192,128]{0,1:T(8,128)(2,1)}, bf16[1024,64]{1,0:T(8,128)(2,1)S(1)}, ...), condition=%wide.region_6.7_spmd, body=%wide.region_5.6_spmd.sunk | while | flops 807534592 | bytes 2752671 | solution.py:128
  179.6 3.6 fusion.87
  183.3 1.0 dynamic-slice.29
  184.5 3.6 fusion.87
  188.2 1.0 dynamic-slice.29
  189.4 3.6 fusion.87
  194.3 3.6 fusion.87
  198.0 56.9 %all-gather.9.cloned.1.call-done = bf16[8192,128]{0,1:T(8,128)(2,1)} async-done(((bf16[256,128]{0,1:T(8,128)(2,1)}), bf16[8192,128]{0,1:T(8,128)(2,1)}) %all-gather.9.cloned.1.call-update) | async-done | bytes 2097168 | tf_op jit(solution)/shard_map/all_gather | solution.py:109
  254.9 19.6 %while.54 = (s32[]{:T(128)}, f32[1024,128]{1,0:T(8,128)S(1)}, bf16[8192,128]{0,1:T(8,128)(2,1)}, bf16[1024,64]{1,0:T(8,128)(2,1)S(1)}, s32[]{:T(128)}, /*index=5*/s32[]{:T(128)}, s32[]{:T(128)}, s32[]{:T(128)}, s32[]{}) while((s32[]{:T(128)}, f32[1024,128]{1,0:T(8,128)S(1)}, bf16[8192,128]{0,1:T(8,128)(2,1)}, bf16[1024,64]{1,0:T(8,128)(2,1)S(1)}, ...), condition=%wide.region_8.9_spmd, body=%wide.region_7.8_spmd.sunk | while | flops 807534592 | bytes 2752671 | solution.py:128
  256.2 3.6 fusion.91
  261.1 3.6 fusion.91
  266.0 3.6 fusion.91
  270.9 3.6 fusion.91
  274.5 56.8 %all-gather.11.cloned.1.call-done = bf16[8192,128]{0,1:T(8,128)(2,1)} async-done(((bf16[256,128]{0,1:T(8,128)(2,1)}), bf16[8192,128]{0,1:T(8,128)(2,1)}) %all-gather.11.cloned.1.call-update) | async-done | bytes 2097168 | tf_op jit(solution)/shard_map/all_gather | solution.py:109
  331.3 19.6 %while.55 = (s32[]{:T(128)}, f32[1024,128]{1,0:T(8,128)S(1)}, bf16[8192,128]{0,1:T(8,128)(2,1)}, bf16[1024,64]{1,0:T(8,128)(2,1)S(1)}, s32[]{:T(128)}, /*index=5*/s32[]{:T(128)}, s32[]{:T(128)}, s32[]{:T(128)}, s32[]{}) while((s32[]{:T(128)}, f32[1024,128]{1,0:T(8,128)S(1)}, bf16[8192,128]{0,1:T(8,128)(2,1)}, ...), condition=%wide.region_10.11_spmd, body=%wide.region_9.10_spmd.sunk | while | flops 807534592 | bytes 2752671 | solution.py:128
  332.6 3.6 fusion.95
  336.2 1.0 dynamic-slice.33
  337.5 3.6 fusion.95
  341.1 1.0 dynamic-slice.33
  342.4 3.6 fusion.95
  346.0 1.0 dynamic-slice.33
  347.3 3.6 fusion.95
  352.2 4.3 %all-to-all-start.1 = ((bf16[8,128,64]{1,2,0:T(8,128)(2,1)}), bf16[8,128,64]{1,2,0:T(8,128)(2,1)S(1)}, u32[]{:S(2)}, u32[]{:S(2)}) async-start(bf16[8,128,64]{1,2,0:T(8,128)(2,1)} %copy_bitcast_fusion.1), calls=%async_computation.1 | async-start | bytes 262144 | tf_op jit(solution)/shard_map/all_to_all | solution.py:132
  356.6 6.1 %all-to-all-done.1 = bf16[8,128,64]{1,2,0:T(8,128)(2,1)S(1)} async-done(((bf16[8,128,64]{1,2,0:T(8,128)(2,1)}), bf16[8,128,64]{1,2,0:T(8,128)(2,1)S(1)}, u32[]{:S(2)}, u32[]{:S(2)}) %all-to-all-start.1) | async-done | bytes 131104 | tf_op jit(solution)/shard_map/all_to_all | solution.py:132
  (118 shorter events, 24.8 us)
Async XLA Ops:
  6.5 60.9 %copy-start = (bf16[512,1024]{1,0:T(8,128)(2,1)S(1)}, bf16[512,1024]{1,0:T(8,128)(2,1)}, u32[]{:S(2)}) copy-start(bf16[512,1024]{1,0:T(8,128)(2,1)} %param.28) | copy-start | bytes 3145732
  6.5 3.2 copy-start.1
  6.5 2.8 copy-start.12
  6.5 3.2 copy-start.6
  6.5 95.3 %all-gather.5.cloned.1.call-start = ((), (), s32[]{:S(2)}) async-start(), calls=%async_computation.2 | async-start | bytes 2162688 | tf_op jit(solution)/shard_map/all_gather | solution.py:109
  9.6 1.0 copy-start.5
  9.7 1.2 copy-start.11
  11.0 32.9 %copy-start.13 = (s32[1,1,12]{2,1,0:T(1,128)S(1)}, s32[1,1,12]{2,1,0:T(1,128)}, u32[]{:S(2)}) copy-start(s32[1,1,12]{2,1,0:T(1,128)} %param.22) | copy-start | bytes 148
  11.0 33.5 %copy-start.8 = (bf16[16,128,128]{2,1,0:T(8,128)(2,1)S(1)}, bf16[16,128,128]{2,1,0:T(8,128)(2,1)}, u32[]{:S(2)}) copy-start(bf16[16,128,128]{2,1,0:T(8,128)(2,1)} %param.23) | copy-start | bytes 1572868
  25.0 21.4 %copy-start.2 = (bf16[1024,192]{0,1:T(8,128)(2,1)}, bf16[1024,192]{0,1:T(8,128)(2,1)S(1)}, u32[]{:S(2)}) copy-start(bf16[1024,192]{0,1:T(8,128)(2,1)S(1)} %copy_bitcast_fusion) | copy-start | bytes 1179652
  25.7 152.6 %all-gather.7.cloned.1.call-start = ((), (), s32[]{:S(2)}) async-start(), calls=%async_computation.3 | async-start | bytes 2162688 | tf_op jit(solution)/shard_map/all_gather | solution.py:109
  26.5 228.4 %all-gather.9.cloned.1.call-start = ((), (), s32[]{:S(2)}) async-start(), calls=%async_computation.4 | async-start | bytes 2162688 | tf_op jit(solution)/shard_map/all_gather | solution.py:109
  27.2 304.1 %all-gather.11.cloned.1.call-start = ((), (), s32[]{:S(2)}) async-start(), calls=%async_computation.5 | async-start | bytes 2162688 | tf_op jit(solution)/shard_map/all_gather | solution.py:109
  27.3 11.6 %collective-permute-start = (bf16[128,512]{1,0:T(8,128)(2,1)S(1)}, bf16[128,512]{1,0:T(8,128)(2,1)S(1)}, u32[]{:S(2)}, u32[]{:S(2)}) collective-permute-start(bf16[128,512]{1,0:T(8,128)(2,1)S(1)} %copy-done.1), channel_id=1, source_target_pairs={{0,4},{4,8},{8,12},{12,16},{16,20},{20,24},{24,28},{28,32},{32,36}... | collective-permute-start | bytes 393224 | tf_op jit(solution)/shard_map/ppermute | solution.py:29
  30.0 11.5 %collective-permute-start.1 = (bf16[128,512]{1,0:T(8,128)(2,1)S(1)}, bf16[128,512]{1,0:T(8,128)(2,1)S(1)}, u32[]{:S(2)}, u32[]{:S(2)}) collective-permute-start(bf16[128,512]{1,0:T(8,128)(2,1)S(1)} %copy-done.1), channel_id=1, source_target_pairs={{4,0},{8,4},{12,8},{16,12},{20,16},{24,20},{28,24},{32,28},{36,32}... | collective-permute-start | bytes 393224 | tf_op jit(solution)/shard_map/ppermute | solution.py:30
  41.6 18.3 %copy-start.4 = (bf16[384,512]{1,0:T(8,128)(2,1)}, bf16[384,512]{1,0:T(8,128)(2,1)S(1)}, u32[]{:S(2)}) copy-start(bf16[384,512]{1,0:T(8,128)(2,1)S(1)} %constant_dynamic-update-slice_fusion) | copy-start | bytes 1179652
  41.6 11.0 %collective-permute-start.2 = (bf16[384,512]{1,0:T(8,128)(2,1)S(1)}, bf16[384,512]{1,0:T(8,128)(2,1)}, u32[]{:S(2)}, u32[]{:S(2)}) collective-permute-start(bf16[384,512]{1,0:T(8,128)(2,1)S(1)} %constant_dynamic-update-slice_fusion), channel_id=1, source_target_pairs={{0,1},{1,2},{2,3},{3,0},{4,5},{5,6},{6,7},{7,4},{8,9},{9,10},{10,1... | collective-permute-start | bytes 1179656 | tf_op jit(solution)/shard_map/ppermute | solution.py:67
  41.7 12.1 %collective-permute-start.3 = (bf16[384,512]{1,0:T(8,128)(2,1)S(1)}, bf16[384,512]{1,0:T(8,128)(2,1)}, u32[]{:S(2)}, u32[]{:S(2)}) collective-permute-start(bf16[384,512]{1,0:T(8,128)(2,1)S(1)} %constant_dynamic-update-slice_fusion), channel_id=1, source_target_pairs={{0,2},{1,3},{2,0},{3,1},{4,6},{5,7},{6,4},{7,5},{8,10},{9,11},{10,... | collective-permute-start | bytes 1179656 | tf_op jit(solution)/shard_map/ppermute | solution.py:67
  42.6 17.3 %collective-permute-start.4 = (bf16[384,512]{1,0:T(8,128)(2,1)S(1)}, bf16[384,512]{1,0:T(8,128)(2,1)}, u32[]{:S(2)}, u32[]{:S(2)}) collective-permute-start(bf16[384,512]{1,0:T(8,128)(2,1)S(1)} %constant_dynamic-update-slice_fusion), channel_id=1, source_target_pairs={{0,3},{1,0},{2,1},{3,2},{4,7},{5,4},{6,5},{7,6},{8,11},{9,8},{10,9... | collective-permute-start | bytes 1179656 | tf_op jit(solution)/shard_map/ppermute | solution.py:67
  67.4 2.4 copy-start.3
  67.4 2.7 slice-start
  350.9 5.6 %copy-start.10 = (s32[8]{0:T(128)S(1)}, s32[8]{0:T(128)}, u32[]{:S(2)}) copy-start(s32[8]{0:T(128)} %constant.230) | copy-start | bytes 100
  351.0 12.3 %copy-start.7 = (bf16[512,512]{1,0:T(8,128)(2,1)S(1)}, bf16[512,512]{1,0:T(8,128)(2,1)}, u32[]{:S(2)}) copy-start(bf16[512,512]{1,0:T(8,128)(2,1)} %param.27) | copy-start | bytes 1572868
  351.0 12.6 %copy-start.9 = (f32[512]{0:T(512)S(1)}, f32[512]{0:T(512)}, u32[]{:S(2)}) copy-start(f32[512]{0:T(512)} %param.31) | copy-start | bytes 6148
  352.2 10.4 %all-to-all-start.1 = ((bf16[8,128,64]{1,2,0:T(8,128)(2,1)}), bf16[8,128,64]{1,2,0:T(8,128)(2,1)S(1)}, u32[]{:S(2)}, u32[]{:S(2)}) async-start(bf16[8,128,64]{1,2,0:T(8,128)(2,1)} %copy_bitcast_fusion.1), calls=%async_computation.1 | async-start | bytes 262144 | tf_op jit(solution)/shard_map/all_to_all | solution.py:132
Sparse Core Ops, SparseCore 0:
  25.9 75.8 all-gather.4
  104.3 74.0 all-gather.6
  180.8 74.0 all-gather.8
  257.2 74.0 all-gather.10

commit v3 on v1

--- a/solution.py
+++ b/solution.py
@@ -12,14 +12,15 @@
 
 norm_eps = 1e-06
 
-PLANE = "xz"
+ROW = "x"
+COLUMN = "z"
 PAIR = "yhi"
-DOM = (PLANE, PAIR)
+DOM = (ROW, COLUMN, PAIR)
 GROUP = (PAIR, "head")
 
 
 def extended(shard, width):
-    devices = lax.axis_size(PLANE) * lax.axis_size(PAIR)
+    devices = lax.axis_size(ROW) * lax.axis_size(COLUMN) * lax.axis_size(PAIR)
     length = shard.shape[0]
     up = [(i, (i + 1) % devices) for i in range(devices - 1)]
     down = [(j, i) for i, j in up]
@@ -59,7 +60,14 @@
     members = group_size * pair_size
     slot_ids = adjacent_group_bank_ids.reshape(-1)
     halo_rows = extended(vertex_embeddings, block_len)
-    nearby = lax.all_gather(halo_rows, "head", axis=0, tiled=True)
+    me = lax.axis_index("head")
+    gathered = [halo_rows]
+    for shift in range(1, group_size):
+        pairs = [(i, (i + shift) % group_size) for i in range(group_size)]
+        gathered.append(lax.ppermute(halo_rows, "head", pairs))
+    stacked = jnp.stack(gathered)
+    order = (me - jnp.arange(group_size)) % group_size
+    nearby = jnp.zeros_like(stacked).at[order].set(stacked).reshape(-1, halo_rows.shape[1])
     slot_order = slot_ids.reshape(3, group_size).T.reshape(-1)
     asking_vector_multiplier = softness_per_subspace / math.sqrt(SUBSPACE_WIDTH)
     queries = head_norm(
@@ -94,7 +102,9 @@
     ).astype(jnp.bfloat16)
     local_term = jnp.dot(hidden, passing_outer_coefficients, preferred_element_type=jnp.float32)
 
-    kv_in = lax.all_gather(key_values, PLANE, axis=0, tiled=True)
+    local_term, head_queries = lax.optimization_barrier((local_term, head_queries))
+    kv_in = lax.all_gather(key_values, COLUMN, axis=0, tiled=True)
+    kv_in = lax.all_gather(kv_in, ROW, axis=0, tiled=True)
     key_count = kv_in.shape[0]
     block_step = min(KEY_BLOCK, key_count)
     ones = jnp.ones((block_step, SUBSPACE_WIDTH), jnp.bfloat16)
@@ -134,9 +144,9 @@
 
 def solution(mesh):
     n_dom, n_head = mesh.shape["dom"], mesh.shape["head"]
-    fine = Mesh(mesh.devices.reshape(n_dom // 2, 2, n_head), (PLANE, PAIR, "head"))
+    fine = Mesh(mesh.devices.reshape(n_dom // 16, 8, 2, n_head), (ROW, COLUMN, PAIR, "head"))
     in_specs = (
-        P((PLANE, PAIR, "head"), None),
+        P((ROW, COLUMN, PAIR, "head"), None),
         P(DOM, "head", None),
         P(),
         P(),
@@ -148,5 +158,5 @@
         P(),
         P(),
     )
-    out_specs = P((PLANE, PAIR, "head"), None)
+    out_specs = P((ROW, COLUMN, PAIR, "head"), None)
     return jax.shard_map(shards, mesh=fine, in_specs=in_specs, out_specs=out_specs, check_vma=False)

time: 229 us -> 257 us (1.12)
  waiting for transfers between devices: 87.6 us -> 107 us
  local copies, waits for them, and re-layouts: 26.4 us -> 34.2 us
  starting transfers between devices: 14.7 us -> 17.3 us
    ppermute x0 -> x3, waiting for transfers between devices: none -> 12.5 us  [shards(): gathered.append(lax.ppermute(halo_rows, 'head', pairs))]
    scatter x0 -> x1, local copies, waits for them, and re-layouts: none -> 4.7 us  [shards(): jnp.zeros_like(stacked).at[order].set(stacked)]
    ppermute x0 -> x3, starting transfers between devices: none -> 2.6 us  [shards(): gathered.append(lax.ppermute(halo_rows, 'head', pairs))]
  transfers between devices with their start and end apart: 5 -> 8, of which waited for: 3 -> 8; matrix products, arithmetic and copies ran while one was open for 39% -> 5% of each run, Pallas kernels for 0% -> 0%
where the time goes in v3:
time: 257 us; the launch traced here: 254 us
  waiting for transfers between devices  107 us (42%)
  matrix products  64.5 us (25%)
  local copies, waits for them, and re-layouts  34.2 us (13%)
  starting transfers between devices  17.3 us (7%)
  between operations  13.8 us (5%)
  blocking collectives  13.2 us (5%)
  other arithmetic  4.15 us (2%)
    dot_general x16, matrix products, accumulate(): jnp.dot(weights, widened, preferred_element_type=jnp.float32)  59.7 us
    all_gather x1, waiting for transfers between devices, shards(): kv_in = lax.all_gather(kv_in, ROW, axis=0, tiled=True)  42.9 us
    all_gather x1, waiting for transfers between devices, shards(): kv_in = lax.all_gather(key_values, COLUMN, axis=0, tiled=True)  42.1 us
    slice x16, local copies, waits for them, and re-layouts, accumulate(): widened = jnp.concatenate([block[:, SUBSPACE_WIDTH:], ones], axis=1)  15.6 us
    all_to_all x1, blocking collectives, shards(): lax.all_to_all(packed, GROUP, split_axis=1, concat_axis=0, tiled=True)  13.2 us
    ppermute x3, waiting for transfers between devices, shards(): gathered.append(lax.ppermute(halo_rows, 'head', pairs))  12.5 us
    all_to_all x1, waiting for transfers between devices, shards(): lax.all_to_all(merged, GROUP, split_axis=0, concat_axis=1, tiled=True)  6.12 us
    ppermute x1, starting transfers between devices, extended(): after = lax.ppermute(first, DOM, down)  5.43 us
  transfers between devices with their start and end apart: 8, of which 8 were waited for; matrix products, arithmetic and copies ran while one was open for 5% of the time, Pallas kernels for 0%

profile of v3, /device:TPU:4, one launch (start us, length us, event | category | flops | bytes accessed | tf_op | source)
XLA Modules:
  0.0 254.4 jit_solution(3346050789966244546)
XLA Ops:
  7.6 1.4 fusion.22
  11.8 13.2 %all_to_all.35 = bf16[128,8,192]{0,2,1:T(8,128)(2,1)S(1)} all-to-all(bf16[128,8,192]{0,2,1:T(8,128)(2,1)S(1)} %bitcast.63), channel_id=1, replica_groups=mesh['x'=4,'z'=8,'yhi'=2,'head'=4] {'yhi','head'}, dimensions={1} | all-to-all | bytes 786432 | tf_op jit(solution)/shard_map/all_to_all | solution.py:91
  26.0 42.1 %all-gather.3.cloned.1.call-done = bf16[8192,128]{0,1:T(8,128)(2,1)} async-done(((bf16[1024,128]{0,1:T(8,128)(2,1)}), bf16[8192,128]{0,1:T(8,128)(2,1)}) %all-gather.3.cloned.1.call-update) | async-done | bytes 2097168 | tf_op jit(solution)/shard_map/all_gather | solution.py:106
  68.1 4.9 %collective-permute-start = (bf16[128,512]{1,0:T(8,128)(2,1)S(1)}, bf16[128,512]{1,0:T(8,128)(2,1)S(1)}, u32[]{:S(2)}, u32[]{:S(2)}) collective-permute-start(bf16[128,512]{1,0:T(8,128)(2,1)S(1)} %copy-done.1), channel_id=1, source_target_pairs={{0,4},{4,8},{8,12},{12,16},{16,20},{20,24},{24,28},{28,32},{32,36}... | collective-permute-start | bytes 393224 | tf_op jit(solution)/shard_map/ppermute | solution.py:29
  73.0 5.4 %collective-permute-start.1 = (bf16[128,512]{1,0:T(8,128)(2,1)S(1)}, bf16[128,512]{1,0:T(8,128)(2,1)S(1)}, u32[]{:S(2)}, u32[]{:S(2)}) collective-permute-start(bf16[128,512]{1,0:T(8,128)(2,1)S(1)} %copy-done.1), channel_id=1, source_target_pairs={{4,0},{8,4},{12,8},{16,12},{20,16},{24,20},{28,24},{32,28},{36,32}... | collective-permute-start | bytes 393224 | tf_op jit(solution)/shard_map/ppermute | solution.py:30
  78.5 1.0 collective-permute-done
  79.5 1.9 collective-permute-done.1
  81.5 1.1 collective-permute-start.3
  82.7 1.4 collective-permute-start.4
  84.6 1.7 gather_fusion
  87.5 4.9 %collective-permute-done.2 = bf16[384,512]{1,0:T(8,128)(2,1)} collective-permute-done((bf16[384,512]{1,0:T(8,128)(2,1)S(1)}, bf16[384,512]{1,0:T(8,128)(2,1)}, u32[]{:S(2)}, u32[]{:S(2)}) %collective-permute-start.2) | collective-permute-done | bytes 393248 | tf_op jit(solution)/shard_map/ppermute | solution.py:67
  92.4 1.3 collective-permute-done.3
  93.7 6.3 %collective-permute-done.4 = bf16[384,512]{1,0:T(8,128)(2,1)} collective-permute-done((bf16[384,512]{1,0:T(8,128)(2,1)S(1)}, bf16[384,512]{1,0:T(8,128)(2,1)}, u32[]{:S(2)}, u32[]{:S(2)}) %collective-permute-start.4) | collective-permute-done | bytes 393248 | tf_op jit(solution)/shard_map/ppermute | solution.py:67
  99.9 1.6 pad_maximum_fusion
  101.5 1.3 broadcast_in_dim.47
  102.8 4.7 %scatter_fusion = bf16[4,384,512]{2,1,0:T(8,128)(2,1)} fusion(bf16[4,384,512]{2,1,0:T(8,128)(2,1)} %broadcast_in_dim.47, s32[4]{0:T(128)S(1)} %fusion.20, bf16[4,384,512]{2,1,0:T(8,128)(2,1)S(1)} %pad_maximum_fusion), kind=kCustom, calls=%fused_computation.3 | custom fusion | bytes 4718608 | tf_op jit(solution)/shard_map/scatter | solution.py:70
  107.5 2.4 fusion.16
  110.9 42.9 %all-gather.5.cloned.1.call-done = bf16[32768,128]{0,1:T(8,128)(2,1)} async-done(((bf16[8192,128]{0,1:T(8,128)(2,1)}), bf16[32768,128]{0,1:T(8,128)(2,1)}) %all-gather.5.cloned.1.call-update) | async-done | bytes 8388624 | tf_op jit(solution)/shard_map/all_gather | solution.py:107
  153.9 80.3 %while.14 = (s32[]{:T(128)}, f32[1024,128]{1,0:T(8,128)S(1)}, bf16[32768,128]{0,1:T(8,128)(2,1)}, bf16[1024,64]{1,0:T(8,128)(2,1)S(1)}, s32[]{:T(128)}, /*index=5*/s32[]{:T(128)}, s32[]{:T(128)}, s32[]{:T(128)}, s32[]{}) while((s32[]{:T(128)}, f32[1024,128]{1,0:T(8,128)S(1)}, bf16[32768,128]{0,1:T(8,128)(2,1)}, ...), condition=%wide.region_4.5_spmd.clone, body=%wide.region_3.4_spmd.clone.sunk | while | flops 807665664 | bytes 2752681 | solution.py:124
  155.1 3.7 %fusion.47 = f32[1024,128]{1,0:T(8,128)S(1)} fusion(bf16[1024,64]{1,0:T(8,128)(2,1)S(1)} %get-tuple-element.180, f32[1024,128]{1,0:T(8,128)S(1)} %get-tuple-element.169, bf16[2048,64]{1,0:T(8,128)(2,1)S(1)} %copy.93, bf16[32768,128]{0,1:T(8,128)(2,1)} %get-tuple-element.179, s32[]{:T(128)S(6)} %select_n.73, pred[]{:T(512)S(6)} %compare.11), kind=kOutput, calls=%fused_computation.6.clone.1 | convolution fusion | flops 807665664 | bytes 1703941 | tf_op jit(solution)/shard_map/while/body/eval_jaxpr/dot_general | solution.py:122
  158.9 1.0 dynamic-slice.8
  160.1 3.7 %fusion.47 = f32[1024,128]{1,0:T(8,128)S(1)} fusion(bf16[1024,64]{1,0:T(8,128)(2,1)S(1)} %get-tuple-element.180, f32[1024,128]{1,0:T(8,128)S(1)} %get-tuple-element.169, bf16[2048,64]{1,0:T(8,128)(2,1)S(1)} %copy.93, bf16[32768,128]{0,1:T(8,128)(2,1)} %get-tuple-element.179, s32[]{:T(128)S(6)} %select_n.73, pred[]{:T(512)S(6)} %compare.11), kind=kOutput, calls=%fused_computation.6.clone.1 | convolution fusion | flops 807665664 | bytes 1703941 | tf_op jit(solution)/shard_map/while/body/eval_jaxpr/dot_general | solution.py:122
  163.9 1.0 dynamic-slice.8
  165.1 3.7 %fusion.47 = f32[1024,128]{1,0:T(8,128)S(1)} fusion(bf16[1024,64]{1,0:T(8,128)(2,1)S(1)} %get-tuple-element.180, f32[1024,128]{1,0:T(8,128)S(1)} %get-tuple-element.169, bf16[2048,64]{1,0:T(8,128)(2,1)S(1)} %copy.93, bf16[32768,128]{0,1:T(8,128)(2,1)} %get-tuple-element.179, s32[]{:T(128)S(6)} %select_n.73, pred[]{:T(512)S(6)} %compare.11), kind=kOutput, calls=%fused_computation.6.clone.1 | convolution fusion | flops 807665664 | bytes 1703941 | tf_op jit(solution)/shard_map/while/body/eval_jaxpr/dot_general | solution.py:122
  168.9 1.0 dynamic-slice.8
  170.2 3.7 %fusion.47 = f32[1024,128]{1,0:T(8,128)S(1)} fusion(bf16[1024,64]{1,0:T(8,128)(2,1)S(1)} %get-tuple-element.180, f32[1024,128]{1,0:T(8,128)S(1)} %get-tuple-element.169, bf16[2048,64]{1,0:T(8,128)(2,1)S(1)} %copy.93, bf16[32768,128]{0,1:T(8,128)(2,1)} %get-tuple-element.179, s32[]{:T(128)S(6)} %select_n.73, pred[]{:T(512)S(6)} %compare.11), kind=kOutput, calls=%fused_computation.6.clone.1 | convolution fusion | flops 807665664 | bytes 1703941 | tf_op jit(solution)/shard_map/while/body/eval_jaxpr/dot_general | solution.py:122
  173.9 1.0 dynamic-slice.8
  175.2 3.7 %fusion.47 = f32[1024,128]{1,0:T(8,128)S(1)} fusion(bf16[1024,64]{1,0:T(8,128)(2,1)S(1)} %get-tuple-element.180, f32[1024,128]{1,0:T(8,128)S(1)} %get-tuple-element.169, bf16[2048,64]{1,0:T(8,128)(2,1)S(1)} %copy.93, bf16[32768,128]{0,1:T(8,128)(2,1)} %get-tuple-element.179, s32[]{:T(128)S(6)} %select_n.73, pred[]{:T(512)S(6)} %compare.11), kind=kOutput, calls=%fused_computation.6.clone.1 | convolution fusion | flops 807665664 | bytes 1703941 | tf_op jit(solution)/shard_map/while/body/eval_jaxpr/dot_general | solution.py:122
  178.9 1.0 dynamic-slice.8
  180.2 3.7 %fusion.47 = f32[1024,128]{1,0:T(8,128)S(1)} fusion(bf16[1024,64]{1,0:T(8,128)(2,1)S(1)} %get-tuple-element.180, f32[1024,128]{1,0:T(8,128)S(1)} %get-tuple-element.169, bf16[2048,64]{1,0:T(8,128)(2,1)S(1)} %copy.93, bf16[32768,128]{0,1:T(8,128)(2,1)} %get-tuple-element.179, s32[]{:T(128)S(6)} %select_n.73, pred[]{:T(512)S(6)} %compare.11), kind=kOutput, calls=%fused_computation.6.clone.1 | convolution fusion | flops 807665664 | bytes 1703941 | tf_op jit(solution)/shard_map/while/body/eval_jaxpr/dot_general | solution.py:122
  184.0 1.0 dynamic-slice.8
  185.2 3.7 %fusion.47 = f32[1024,128]{1,0:T(8,128)S(1)} fusion(bf16[1024,64]{1,0:T(8,128)(2,1)S(1)} %get-tuple-element.180, f32[1024,128]{1,0:T(8,128)S(1)} %get-tuple-element.169, bf16[2048,64]{1,0:T(8,128)(2,1)S(1)} %copy.93, bf16[32768,128]{0,1:T(8,128)(2,1)} %get-tuple-element.179, s32[]{:T(128)S(6)} %select_n.73, pred[]{:T(512)S(6)} %compare.11), kind=kOutput, calls=%fused_computation.6.clone.1 | convolution fusion | flops 807665664 | bytes 1703941 | tf_op jit(solution)/shard_map/while/body/eval_jaxpr/dot_general | solution.py:122
  189.0 1.0 dynamic-slice.8
  190.2 3.7 %fusion.47 = f32[1024,128]{1,0:T(8,128)S(1)} fusion(bf16[1024,64]{1,0:T(8,128)(2,1)S(1)} %get-tuple-element.180, f32[1024,128]{1,0:T(8,128)S(1)} %get-tuple-element.169, bf16[2048,64]{1,0:T(8,128)(2,1)S(1)} %copy.93, bf16[32768,128]{0,1:T(8,128)(2,1)} %get-tuple-element.179, s32[]{:T(128)S(6)} %select_n.73, pred[]{:T(512)S(6)} %compare.11), kind=kOutput, calls=%fused_computation.6.clone.1 | convolution fusion | flops 807665664 | bytes 1703941 | tf_op jit(solution)/shard_map/while/body/eval_jaxpr/dot_general | solution.py:122
  195.3 3.7 %fusion.47 = f32[1024,128]{1,0:T(8,128)S(1)} fusion(bf16[1024,64]{1,0:T(8,128)(2,1)S(1)} %get-tuple-element.180, f32[1024,128]{1,0:T(8,128)S(1)} %get-tuple-element.169, bf16[2048,64]{1,0:T(8,128)(2,1)S(1)} %copy.93, bf16[32768,128]{0,1:T(8,128)(2,1)} %get-tuple-element.179, s32[]{:T(128)S(6)} %select_n.73, pred[]{:T(512)S(6)} %compare.11), kind=kOutput, calls=%fused_computation.6.clone.1 | convolution fusion | flops 807665664 | bytes 1703941 | tf_op jit(solution)/shard_map/while/body/eval_jaxpr/dot_general | solution.py:122
  200.3 3.7 %fusion.47 = f32[1024,128]{1,0:T(8,128)S(1)} fusion(bf16[1024,64]{1,0:T(8,128)(2,1)S(1)} %get-tuple-element.180, f32[1024,128]{1,0:T(8,128)S(1)} %get-tuple-element.169, bf16[2048,64]{1,0:T(8,128)(2,1)S(1)} %copy.93, bf16[32768,128]{0,1:T(8,128)(2,1)} %get-tuple-element.179, s32[]{:T(128)S(6)} %select_n.73, pred[]{:T(512)S(6)} %compare.11), kind=kOutput, calls=%fused_computation.6.clone.1 | convolution fusion | flops 807665664 | bytes 1703941 | tf_op jit(solution)/shard_map/while/body/eval_jaxpr/dot_general | solution.py:122
  204.0 1.0 dynamic-slice.8
  205.3 3.7 %fusion.47 = f32[1024,128]{1,0:T(8,128)S(1)} fusion(bf16[1024,64]{1,0:T(8,128)(2,1)S(1)} %get-tuple-element.180, f32[1024,128]{1,0:T(8,128)S(1)} %get-tuple-element.169, bf16[2048,64]{1,0:T(8,128)(2,1)S(1)} %copy.93, bf16[32768,128]{0,1:T(8,128)(2,1)} %get-tuple-element.179, s32[]{:T(128)S(6)} %select_n.73, pred[]{:T(512)S(6)} %compare.11), kind=kOutput, calls=%fused_computation.6.clone.1 | convolution fusion | flops 807665664 | bytes 1703941 | tf_op jit(solution)/shard_map/while/body/eval_jaxpr/dot_general | solution.py:122
  210.3 3.7 %fusion.47 = f32[1024,128]{1,0:T(8,128)S(1)} fusion(bf16[1024,64]{1,0:T(8,128)(2,1)S(1)} %get-tuple-element.180, f32[1024,128]{1,0:T(8,128)S(1)} %get-tuple-element.169, bf16[2048,64]{1,0:T(8,128)(2,1)S(1)} %copy.93, bf16[32768,128]{0,1:T(8,128)(2,1)} %get-tuple-element.179, s32[]{:T(128)S(6)} %select_n.73, pred[]{:T(512)S(6)} %compare.11), kind=kOutput, calls=%fused_computation.6.clone.1 | convolution fusion | flops 807665664 | bytes 1703941 | tf_op jit(solution)/shard_map/while/body/eval_jaxpr/dot_general | solution.py:122
  214.1 1.0 dynamic-slice.8
  215.3 3.7 %fusion.47 = f32[1024,128]{1,0:T(8,128)S(1)} fusion(bf16[1024,64]{1,0:T(8,128)(2,1)S(1)} %get-tuple-element.180, f32[1024,128]{1,0:T(8,128)S(1)} %get-tuple-element.169, bf16[2048,64]{1,0:T(8,128)(2,1)S(1)} %copy.93, bf16[32768,128]{0,1:T(8,128)(2,1)} %get-tuple-element.179, s32[]{:T(128)S(6)} %select_n.73, pred[]{:T(512)S(6)} %compare.11), kind=kOutput, calls=%fused_computation.6.clone.1 | convolution fusion | flops 807665664 | bytes 1703941 | tf_op jit(solution)/shard_map/while/body/eval_jaxpr/dot_general | solution.py:122
  219.1 1.0 dynamic-slice.8
  220.4 3.7 %fusion.47 = f32[1024,128]{1,0:T(8,128)S(1)} fusion(bf16[1024,64]{1,0:T(8,128)(2,1)S(1)} %get-tuple-element.180, f32[1024,128]{1,0:T(8,128)S(1)} %get-tuple-element.169, bf16[2048,64]{1,0:T(8,128)(2,1)S(1)} %copy.93, bf16[32768,128]{0,1:T(8,128)(2,1)} %get-tuple-element.179, s32[]{:T(128)S(6)} %select_n.73, pred[]{:T(512)S(6)} %compare.11), kind=kOutput, calls=%fused_computation.6.clone.1 | convolution fusion | flops 807665664 | bytes 1703941 | tf_op jit(solution)/shard_map/while/body/eval_jaxpr/dot_general | solution.py:122
  225.4 3.7 %fusion.47 = f32[1024,128]{1,0:T(8,128)S(1)} fusion(bf16[1024,64]{1,0:T(8,128)(2,1)S(1)} %get-tuple-element.180, f32[1024,128]{1,0:T(8,128)S(1)} %get-tuple-element.169, bf16[2048,64]{1,0:T(8,128)(2,1)S(1)} %copy.93, bf16[32768,128]{0,1:T(8,128)(2,1)} %get-tuple-element.179, s32[]{:T(128)S(6)} %select_n.73, pred[]{:T(512)S(6)} %compare.11), kind=kOutput, calls=%fused_computation.6.clone.1 | convolution fusion | flops 807665664 | bytes 1703941 | tf_op jit(solution)/shard_map/while/body/eval_jaxpr/dot_general | solution.py:122
  229.1 1.0 dynamic-slice.8
  230.4 3.7 %fusion.47 = f32[1024,128]{1,0:T(8,128)S(1)} fusion(bf16[1024,64]{1,0:T(8,128)(2,1)S(1)} %get-tuple-element.180, f32[1024,128]{1,0:T(8,128)S(1)} %get-tuple-element.169, bf16[2048,64]{1,0:T(8,128)(2,1)S(1)} %copy.93, bf16[32768,128]{0,1:T(8,128)(2,1)} %get-tuple-element.179, s32[]{:T(128)S(6)} %select_n.73, pred[]{:T(512)S(6)} %compare.11), kind=kOutput, calls=%fused_computation.6.clone.1 | convolution fusion | flops 807665664 | bytes 1703941 | tf_op jit(solution)/shard_map/while/body/eval_jaxpr/dot_general | solution.py:122
  235.4 4.3 %all-to-all-start.1 = ((bf16[8,128,64]{1,2,0:T(8,128)(2,1)}), bf16[8,128,64]{1,2,0:T(8,128)(2,1)S(1)}, u32[]{:S(2)}, u32[]{:S(2)}) async-start(bf16[8,128,64]{1,2,0:T(8,128)(2,1)} %copy_bitcast_fusion.1), calls=%async_computation.1 | async-start | bytes 262144 | tf_op jit(solution)/shard_map/all_to_all | solution.py:133
  239.7 6.1 %all-to-all-done.1 = bf16[8,128,64]{1,2,0:T(8,128)(2,1)S(1)} async-done(((bf16[8,128,64]{1,2,0:T(8,128)(2,1)}), bf16[8,128,64]{1,2,0:T(8,128)(2,1)S(1)}, u32[]{:S(2)}, u32[]{:S(2)}) %all-to-all-start.1) | async-done | bytes 131104 | tf_op jit(solution)/shard_map/all_to_all | solution.py:133
  (107 shorter events, 19.6 us)
Async XLA Ops:
  6.5 100.9 %copy-start = (bf16[512,1024]{1,0:T(8,128)(2,1)S(1)}, bf16[512,1024]{1,0:T(8,128)(2,1)}, u32[]{:S(2)}) copy-start(bf16[512,1024]{1,0:T(8,128)(2,1)} %param.22) | copy-start | bytes 3145732
  6.5 2.8 %copy-start.11 = (f32[8]{0:T(128)S(1)}, f32[8]{0:T(128)}, u32[]{:S(2)}) copy-start(f32[8]{0:T(128)} %param.24) | copy-start | bytes 100
  6.5 61.5 %all-gather.3.cloned.1.call-start = ((), (), s32[]{:S(2)}) async-start(), calls=%async_computation.2 | async-start | bytes 2359296 | tf_op jit(solution)/shard_map/all_gather | solution.py:106
  7.6 2.1 copy-start.1
  7.6 2.1 copy-start.6
  9.7 1.0 copy-start.5
  10.1 1.0 copy-start.10
  25.1 62.4 %copy-start.2 = (bf16[1024,192]{0,1:T(8,128)(2,1)}, bf16[1024,192]{0,1:T(8,128)(2,1)S(1)}, u32[]{:S(2)}) copy-start(bf16[1024,192]{0,1:T(8,128)(2,1)S(1)} %copy_bitcast_fusion) | copy-start | bytes 1179652
  25.9 58.1 %copy-start.12 = (s32[1,1,12]{2,1,0:T(1,128)S(1)}, s32[1,1,12]{2,1,0:T(1,128)}, u32[]{:S(2)}) copy-start(s32[1,1,12]{2,1,0:T(1,128)} %param.16) | copy-start | bytes 148
  25.9 127.9 %all-gather.5.cloned.1.call-start = ((), (), s32[]{:S(2)}) async-start(), calls=%async_computation.3 | async-start | bytes 10485760 | tf_op jit(solution)/shard_map/all_gather | solution.py:107
  68.1 11.4 %collective-permute-start = (bf16[128,512]{1,0:T(8,128)(2,1)S(1)}, bf16[128,512]{1,0:T(8,128)(2,1)S(1)}, u32[]{:S(2)}, u32[]{:S(2)}) collective-permute-start(bf16[128,512]{1,0:T(8,128)(2,1)S(1)} %copy-done.1), channel_id=1, source_target_pairs={{0,4},{4,8},{8,12},{12,16},{16,20},{20,24},{24,28},{28,32},{32,36}... | collective-permute-start | bytes 393224 | tf_op jit(solution)/shard_map/ppermute | solution.py:29
  73.0 8.4 %collective-permute-start.1 = (bf16[128,512]{1,0:T(8,128)(2,1)S(1)}, bf16[128,512]{1,0:T(8,128)(2,1)S(1)}, u32[]{:S(2)}, u32[]{:S(2)}) collective-permute-start(bf16[128,512]{1,0:T(8,128)(2,1)S(1)} %copy-done.1), channel_id=1, source_target_pairs={{4,0},{8,4},{12,8},{16,12},{20,16},{24,20},{28,24},{32,28},{36,32}... | collective-permute-start | bytes 393224 | tf_op jit(solution)/shard_map/ppermute | solution.py:30
  81.4 18.5 %copy-start.4 = (bf16[384,512]{1,0:T(8,128)(2,1)}, bf16[384,512]{1,0:T(8,128)(2,1)S(1)}, u32[]{:S(2)}) copy-start(bf16[384,512]{1,0:T(8,128)(2,1)S(1)} %constant_dynamic-update-slice_fusion) | copy-start | bytes 1179652
  81.4 11.0 %collective-permute-start.2 = (bf16[384,512]{1,0:T(8,128)(2,1)S(1)}, bf16[384,512]{1,0:T(8,128)(2,1)}, u32[]{:S(2)}, u32[]{:S(2)}) collective-permute-start(bf16[384,512]{1,0:T(8,128)(2,1)S(1)} %constant_dynamic-update-slice_fusion), channel_id=1, source_target_pairs={{0,1},{1,2},{2,3},{3,0},{4,5},{5,6},{6,7},{7,4},{8,9},{9,10},{10,1... | collective-permute-start | bytes 1179656 | tf_op jit(solution)/shard_map/ppermute | solution.py:67
  81.5 12.1 %collective-permute-start.3 = (bf16[384,512]{1,0:T(8,128)(2,1)S(1)}, bf16[384,512]{1,0:T(8,128)(2,1)}, u32[]{:S(2)}, u32[]{:S(2)}) collective-permute-start(bf16[384,512]{1,0:T(8,128)(2,1)S(1)} %constant_dynamic-update-slice_fusion), channel_id=1, source_target_pairs={{0,2},{1,3},{2,0},{3,1},{4,6},{5,7},{6,4},{7,5},{8,10},{9,11},{10,... | collective-permute-start | bytes 1179656 | tf_op jit(solution)/shard_map/ppermute | solution.py:67
  82.7 17.3 %collective-permute-start.4 = (bf16[384,512]{1,0:T(8,128)(2,1)S(1)}, bf16[384,512]{1,0:T(8,128)(2,1)}, u32[]{:S(2)}, u32[]{:S(2)}) collective-permute-start(bf16[384,512]{1,0:T(8,128)(2,1)S(1)} %constant_dynamic-update-slice_fusion), channel_id=1, source_target_pairs={{0,3},{1,0},{2,1},{3,2},{4,7},{5,4},{6,5},{7,6},{8,11},{9,8},{10,9... | collective-permute-start | bytes 1179656 | tf_op jit(solution)/shard_map/ppermute | solution.py:67
  107.5 2.4 copy-start.3
  109.9 0.9 slice-start
  234.1 5.6 %copy-start.9 = (s32[8]{0:T(128)S(1)}, s32[8]{0:T(128)}, u32[]{:S(2)}) copy-start(s32[8]{0:T(128)} %constant.122) | copy-start | bytes 100
  234.2 12.3 %copy-start.7 = (bf16[512,512]{1,0:T(8,128)(2,1)S(1)}, bf16[512,512]{1,0:T(8,128)(2,1)}, u32[]{:S(2)}) copy-start(bf16[512,512]{1,0:T(8,128)(2,1)} %param.21) | copy-start | bytes 1572868
  234.4 12.4 %copy-start.8 = (f32[512]{0:T(512)S(1)}, f32[512]{0:T(512)}, u32[]{:S(2)}) copy-start(f32[512]{0:T(512)} %param.25) | copy-start | bytes 6148
  235.4 10.4 %all-to-all-start.1 = ((bf16[8,128,64]{1,2,0:T(8,128)(2,1)}), bf16[8,128,64]{1,2,0:T(8,128)(2,1)S(1)}, u32[]{:S(2)}, u32[]{:S(2)}) async-start(bf16[8,128,64]{1,2,0:T(8,128)(2,1)} %copy_bitcast_fusion.1), calls=%async_computation.1 | async-start | bytes 262144 | tf_op jit(solution)/shard_map/all_to_all | solution.py:133
Sparse Core Ops, SparseCore 0:
  26.0 42.0 all-gather.2
  69.9 83.9 all-gather.4

commit v4 on v3

--- a/solution.py
+++ b/solution.py
@@ -103,8 +103,7 @@
     local_term = jnp.dot(hidden, passing_outer_coefficients, preferred_element_type=jnp.float32)
 
     local_term, head_queries = lax.optimization_barrier((local_term, head_queries))
-    kv_in = lax.all_gather(key_values, COLUMN, axis=0, tiled=True)
-    kv_in = lax.all_gather(kv_in, ROW, axis=0, tiled=True)
+    kv_in = lax.all_gather(key_values, (ROW, COLUMN), axis=0, tiled=True)
     key_count = kv_in.shape[0]
     block_step = min(KEY_BLOCK, key_count)
     ones = jnp.ones((block_step, SUBSPACE_WIDTH), jnp.bfloat16)

time: 257 us -> 228 us (0.89)
  waiting for transfers between devices: 107 us -> 76.9 us
    all_gather x2 -> x1, waiting for transfers between devices: 85 us -> 54.4 us  [shards(): kv_in = lax.all_gather(key_values, (ROW, COLUMN), axis=0, tiled=True)]
  transfers between devices with their start and end apart: 8 -> 7, of which waited for: 8 -> 7; matrix products, arithmetic and copies ran while one was open for 5% -> 6% of each run, Pallas kernels for 0% -> 0%
where the time goes in v4:
time: 228 us; the launch traced here: 224 us
  waiting for transfers between devices  76.9 us (34%)
  matrix products  64.5 us (28%)
  local copies, waits for them, and re-layouts  34.2 us (15%)
  starting transfers between devices  17 us (7%)
  between operations  13.8 us (6%)
  blocking collectives  13.2 us (6%)
  other arithmetic  4.15 us (2%)
    dot_general x16, matrix products, accumulate(): jnp.dot(weights, widened, preferred_element_type=jnp.float32)  59.7 us
    all_gather x1, waiting for transfers between devices, shards(): kv_in = lax.all_gather(key_values, (ROW, COLUMN), axis=0, tiled=True)  54.4 us
    slice x16, local copies, waits for them, and re-layouts, accumulate(): widened = jnp.concatenate([block[:, SUBSPACE_WIDTH:], ones], axis=1)  15.6 us
    all_to_all x1, blocking collectives, shards(): lax.all_to_all(packed, GROUP, split_axis=1, concat_axis=0, tiled=True)  13.2 us
    ppermute x3, waiting for transfers between devices, shards(): gathered.append(lax.ppermute(halo_rows, 'head', pairs))  12.5 us
    ppermute x1, starting transfers between devices, extended(): after = lax.ppermute(first, DOM, down)  7.63 us
    all_to_all x1, waiting for transfers between devices, shards(): lax.all_to_all(merged, GROUP, split_axis=0, concat_axis=1, tiled=True)  6.12 us
    scatter x1, local copies, waits for them, and re-layouts, shards(): jnp.zeros_like(stacked).at[order].set(stacked)  4.75 us
  transfers between devices with their start and end apart: 7, of which 7 were waited for; matrix products, arithmetic and copies ran while one was open for 6% of the time, Pallas kernels for 0%

profile of v4, /device:TPU:4, one launch (start us, length us, event | category | flops | bytes accessed | tf_op | source)
XLA Modules:
  0.0 224.5 jit_solution(1230595181593717141)
XLA Ops:
  7.6 1.4 fusion.22
  11.8 13.2 %all_to_all.35 = bf16[128,8,192]{0,2,1:T(8,128)(2,1)S(1)} all-to-all(bf16[128,8,192]{0,2,1:T(8,128)(2,1)S(1)} %bitcast.63), channel_id=1, replica_groups=mesh['x'=4,'z'=8,'yhi'=2,'head'=4] {'yhi','head'}, dimensions={1} | all-to-all | bytes 786432 | tf_op jit(solution)/shard_map/all_to_all | solution.py:91
  25.9 2.7 %collective-permute-start = (bf16[128,512]{1,0:T(8,128)(2,1)S(1)}, bf16[128,512]{1,0:T(8,128)(2,1)S(1)}, u32[]{:S(2)}, u32[]{:S(2)}) collective-permute-start(bf16[128,512]{1,0:T(8,128)(2,1)S(1)} %copy-done.1), channel_id=1, source_target_pairs={{0,4},{4,8},{8,12},{12,16},{16,20},{20,24},{24,28},{28,32},{32,36}... | collective-permute-start | bytes 393224 | tf_op jit(solution)/shard_map/ppermute | solution.py:29
  28.6 7.6 %collective-permute-start.1 = (bf16[128,512]{1,0:T(8,128)(2,1)S(1)}, bf16[128,512]{1,0:T(8,128)(2,1)S(1)}, u32[]{:S(2)}, u32[]{:S(2)}) collective-permute-start(bf16[128,512]{1,0:T(8,128)(2,1)S(1)} %copy-done.1), channel_id=1, source_target_pairs={{4,0},{8,4},{12,8},{16,12},{20,16},{24,20},{28,24},{32,28},{36,32}... | collective-permute-start | bytes 393224 | tf_op jit(solution)/shard_map/ppermute | solution.py:30
  36.3 1.2 collective-permute-done
  37.5 2.7 %collective-permute-done.1 = bf16[128,512]{1,0:T(8,128)(2,1)S(1)} collective-permute-done((bf16[128,512]{1,0:T(8,128)(2,1)S(1)}, bf16[128,512]{1,0:T(8,128)(2,1)S(1)}, u32[]{:S(2)}, u32[]{:S(2)}) %collective-permute-start.1) | collective-permute-done | bytes 131104 | tf_op jit(solution)/shard_map/ppermute | solution.py:30
  41.2 1.4 collective-permute-start.4
  43.2 1.7 gather_fusion
  45.9 5.2 %collective-permute-done.2 = bf16[384,512]{1,0:T(8,128)(2,1)} collective-permute-done((bf16[384,512]{1,0:T(8,128)(2,1)S(1)}, bf16[384,512]{1,0:T(8,128)(2,1)}, u32[]{:S(2)}, u32[]{:S(2)}) %collective-permute-start.2) | collective-permute-done | bytes 393248 | tf_op jit(solution)/shard_map/ppermute | solution.py:67
  51.1 1.3 collective-permute-done.3
  52.4 6.1 %collective-permute-done.4 = bf16[384,512]{1,0:T(8,128)(2,1)} collective-permute-done((bf16[384,512]{1,0:T(8,128)(2,1)S(1)}, bf16[384,512]{1,0:T(8,128)(2,1)}, u32[]{:S(2)}, u32[]{:S(2)}) %collective-permute-start.4) | collective-permute-done | bytes 393248 | tf_op jit(solution)/shard_map/ppermute | solution.py:67
  58.5 1.6 pad_maximum_fusion
  60.0 1.3 broadcast_in_dim.47
  61.3 4.8 %scatter_fusion = bf16[4,384,512]{2,1,0:T(8,128)(2,1)} fusion(bf16[4,384,512]{2,1,0:T(8,128)(2,1)} %broadcast_in_dim.47, s32[4]{0:T(128)S(1)} %fusion.20, bf16[4,384,512]{2,1,0:T(8,128)(2,1)S(1)} %pad_maximum_fusion), kind=kCustom, calls=%fused_computation.3 | custom fusion | bytes 4718608 | tf_op jit(solution)/shard_map/scatter | solution.py:70
  66.1 2.3 %fusion.16 = bf16[128,1024]{1,0:T(8,128)(2,1)S(1)} fusion(bf16[512,1024]{1,0:T(8,128)(2,1)S(1)} %copy-done, bf16[128,1536]{0,1:T(8,128)(2,1)} %bitcast.72, bf16[1536,512]{1,0:T(8,128)(2,1)} %bitcast.62), kind=kOutput, calls=%fused_computation.23 | convolution fusion | flops 336789504 | bytes 3276800 | tf_op jit(solution)/shard_map/dot_general | solution.py:101
  69.5 54.4 %all-gather.2.cloned.1.call-done = bf16[32768,128]{0,1:T(8,128)(2,1)} async-done(((bf16[1024,128]{0,1:T(8,128)(2,1)}), bf16[32768,128]{0,1:T(8,128)(2,1)}) %all-gather.2.cloned.1.call-update) | async-done | bytes 8388624 | tf_op jit(solution)/shard_map/all_gather | solution.py:106
  123.9 80.3 %while.14 = (s32[]{:T(128)}, f32[1024,128]{1,0:T(8,128)S(1)}, bf16[32768,128]{0,1:T(8,128)(2,1)}, bf16[1024,64]{1,0:T(8,128)(2,1)S(1)}, s32[]{:T(128)}, /*index=5*/s32[]{:T(128)}, s32[]{:T(128)}, s32[]{:T(128)}, s32[]{}) while((s32[]{:T(128)}, f32[1024,128]{1,0:T(8,128)S(1)}, bf16[32768,128]{0,1:T(8,128)(2,1)}, ...), condition=%wide.region_4.5_spmd.clone, body=%wide.region_3.4_spmd.clone.sunk | while | flops 807665664 | bytes 2752681 | solution.py:123
  125.2 3.7 %fusion.47 = f32[1024,128]{1,0:T(8,128)S(1)} fusion(bf16[1024,64]{1,0:T(8,128)(2,1)S(1)} %get-tuple-element.180, f32[1024,128]{1,0:T(8,128)S(1)} %get-tuple-element.169, bf16[2048,64]{1,0:T(8,128)(2,1)S(1)} %copy.93, bf16[32768,128]{0,1:T(8,128)(2,1)} %get-tuple-element.179, s32[]{:T(128)S(6)} %select_n.73, pred[]{:T(512)S(6)} %compare.11), kind=kOutput, calls=%fused_computation.6.clone.1 | convolution fusion | flops 807665664 | bytes 1703941 | tf_op jit(solution)/shard_map/while/body/eval_jaxpr/dot_general | solution.py:121
  128.9 1.0 dynamic-slice.8
  130.2 3.7 %fusion.47 = f32[1024,128]{1,0:T(8,128)S(1)} fusion(bf16[1024,64]{1,0:T(8,128)(2,1)S(1)} %get-tuple-element.180, f32[1024,128]{1,0:T(8,128)S(1)} %get-tuple-element.169, bf16[2048,64]{1,0:T(8,128)(2,1)S(1)} %copy.93, bf16[32768,128]{0,1:T(8,128)(2,1)} %get-tuple-element.179, s32[]{:T(128)S(6)} %select_n.73, pred[]{:T(512)S(6)} %compare.11), kind=kOutput, calls=%fused_computation.6.clone.1 | convolution fusion | flops 807665664 | bytes 1703941 | tf_op jit(solution)/shard_map/while/body/eval_jaxpr/dot_general | solution.py:121
  133.9 1.0 dynamic-slice.8
  135.2 3.7 %fusion.47 = f32[1024,128]{1,0:T(8,128)S(1)} fusion(bf16[1024,64]{1,0:T(8,128)(2,1)S(1)} %get-tuple-element.180, f32[1024,128]{1,0:T(8,128)S(1)} %get-tuple-element.169, bf16[2048,64]{1,0:T(8,128)(2,1)S(1)} %copy.93, bf16[32768,128]{0,1:T(8,128)(2,1)} %get-tuple-element.179, s32[]{:T(128)S(6)} %select_n.73, pred[]{:T(512)S(6)} %compare.11), kind=kOutput, calls=%fused_computation.6.clone.1 | convolution fusion | flops 807665664 | bytes 1703941 | tf_op jit(solution)/shard_map/while/body/eval_jaxpr/dot_general | solution.py:121
  138.9 1.0 dynamic-slice.8
  140.2 3.7 %fusion.47 = f32[1024,128]{1,0:T(8,128)S(1)} fusion(bf16[1024,64]{1,0:T(8,128)(2,1)S(1)} %get-tuple-element.180, f32[1024,128]{1,0:T(8,128)S(1)} %get-tuple-element.169, bf16[2048,64]{1,0:T(8,128)(2,1)S(1)} %copy.93, bf16[32768,128]{0,1:T(8,128)(2,1)} %get-tuple-element.179, s32[]{:T(128)S(6)} %select_n.73, pred[]{:T(512)S(6)} %compare.11), kind=kOutput, calls=%fused_computation.6.clone.1 | convolution fusion | flops 807665664 | bytes 1703941 | tf_op jit(solution)/shard_map/while/body/eval_jaxpr/dot_general | solution.py:121
  144.0 1.0 dynamic-slice.8
  145.2 3.7 %fusion.47 = f32[1024,128]{1,0:T(8,128)S(1)} fusion(bf16[1024,64]{1,0:T(8,128)(2,1)S(1)} %get-tuple-element.180, f32[1024,128]{1,0:T(8,128)S(1)} %get-tuple-element.169, bf16[2048,64]{1,0:T(8,128)(2,1)S(1)} %copy.93, bf16[32768,128]{0,1:T(8,128)(2,1)} %get-tuple-element.179, s32[]{:T(128)S(6)} %select_n.73, pred[]{:T(512)S(6)} %compare.11), kind=kOutput, calls=%fused_computation.6.clone.1 | convolution fusion | flops 807665664 | bytes 1703941 | tf_op jit(solution)/shard_map/while/body/eval_jaxpr/dot_general | solution.py:121
  149.0 1.0 dynamic-slice.8
  150.2 3.7 %fusion.47 = f32[1024,128]{1,0:T(8,128)S(1)} fusion(bf16[1024,64]{1,0:T(8,128)(2,1)S(1)} %get-tuple-element.180, f32[1024,128]{1,0:T(8,128)S(1)} %get-tuple-element.169, bf16[2048,64]{1,0:T(8,128)(2,1)S(1)} %copy.93, bf16[32768,128]{0,1:T(8,128)(2,1)} %get-tuple-element.179, s32[]{:T(128)S(6)} %select_n.73, pred[]{:T(512)S(6)} %compare.11), kind=kOutput, calls=%fused_computation.6.clone.1 | convolution fusion | flops 807665664 | bytes 1703941 | tf_op jit(solution)/shard_map/while/body/eval_jaxpr/dot_general | solution.py:121
  154.0 1.0 dynamic-slice.8
  155.3 3.7 %fusion.47 = f32[1024,128]{1,0:T(8,128)S(1)} fusion(bf16[1024,64]{1,0:T(8,128)(2,1)S(1)} %get-tuple-element.180, f32[1024,128]{1,0:T(8,128)S(1)} %get-tuple-element.169, bf16[2048,64]{1,0:T(8,128)(2,1)S(1)} %copy.93, bf16[32768,128]{0,1:T(8,128)(2,1)} %get-tuple-element.179, s32[]{:T(128)S(6)} %select_n.73, pred[]{:T(512)S(6)} %compare.11), kind=kOutput, calls=%fused_computation.6.clone.1 | convolution fusion | flops 807665664 | bytes 1703941 | tf_op jit(solution)/shard_map/while/body/eval_jaxpr/dot_general | solution.py:121
  159.0 1.0 dynamic-slice.8
  160.3 3.7 %fusion.47 = f32[1024,128]{1,0:T(8,128)S(1)} fusion(bf16[1024,64]{1,0:T(8,128)(2,1)S(1)} %get-tuple-element.180, f32[1024,128]{1,0:T(8,128)S(1)} %get-tuple-element.169, bf16[2048,64]{1,0:T(8,128)(2,1)S(1)} %copy.93, bf16[32768,128]{0,1:T(8,128)(2,1)} %get-tuple-element.179, s32[]{:T(128)S(6)} %select_n.73, pred[]{:T(512)S(6)} %compare.11), kind=kOutput, calls=%fused_computation.6.clone.1 | convolution fusion | flops 807665664 | bytes 1703941 | tf_op jit(solution)/shard_map/while/body/eval_jaxpr/dot_general | solution.py:121
  164.0 1.0 dynamic-slice.8
  165.3 3.7 %fusion.47 = f32[1024,128]{1,0:T(8,128)S(1)} fusion(bf16[1024,64]{1,0:T(8,128)(2,1)S(1)} %get-tuple-element.180, f32[1024,128]{1,0:T(8,128)S(1)} %get-tuple-element.169, bf16[2048,64]{1,0:T(8,128)(2,1)S(1)} %copy.93, bf16[32768,128]{0,1:T(8,128)(2,1)} %get-tuple-element.179, s32[]{:T(128)S(6)} %select_n.73, pred[]{:T(512)S(6)} %compare.11), kind=kOutput, calls=%fused_computation.6.clone.1 | convolution fusion | flops 807665664 | bytes 1703941 | tf_op jit(solution)/shard_map/while/body/eval_jaxpr/dot_general | solution.py:121
  169.1 1.0 dynamic-slice.8
  170.3 3.7 %fusion.47 = f32[1024,128]{1,0:T(8,128)S(1)} fusion(bf16[1024,64]{1,0:T(8,128)(2,1)S(1)} %get-tuple-element.180, f32[1024,128]{1,0:T(8,128)S(1)} %get-tuple-element.169, bf16[2048,64]{1,0:T(8,128)(2,1)S(1)} %copy.93, bf16[32768,128]{0,1:T(8,128)(2,1)} %get-tuple-element.179, s32[]{:T(128)S(6)} %select_n.73, pred[]{:T(512)S(6)} %compare.11), kind=kOutput, calls=%fused_computation.6.clone.1 | convolution fusion | flops 807665664 | bytes 1703941 | tf_op jit(solution)/shard_map/while/body/eval_jaxpr/dot_general | solution.py:121
  174.1 1.0 dynamic-slice.8
  175.3 3.7 %fusion.47 = f32[1024,128]{1,0:T(8,128)S(1)} fusion(bf16[1024,64]{1,0:T(8,128)(2,1)S(1)} %get-tuple-element.180, f32[1024,128]{1,0:T(8,128)S(1)} %get-tuple-element.169, bf16[2048,64]{1,0:T(8,128)(2,1)S(1)} %copy.93, bf16[32768,128]{0,1:T(8,128)(2,1)} %get-tuple-element.179, s32[]{:T(128)S(6)} %select_n.73, pred[]{:T(512)S(6)} %compare.11), kind=kOutput, calls=%fused_computation.6.clone.1 | convolution fusion | flops 807665664 | bytes 1703941 | tf_op jit(solution)/shard_map/while/body/eval_jaxpr/dot_general | solution.py:121
  179.1 1.0 dynamic-slice.8
  180.4 3.7 %fusion.47 = f32[1024,128]{1,0:T(8,128)S(1)} fusion(bf16[1024,64]{1,0:T(8,128)(2,1)S(1)} %get-tuple-element.180, f32[1024,128]{1,0:T(8,128)S(1)} %get-tuple-element.169, bf16[2048,64]{1,0:T(8,128)(2,1)S(1)} %copy.93, bf16[32768,128]{0,1:T(8,128)(2,1)} %get-tuple-element.179, s32[]{:T(128)S(6)} %select_n.73, pred[]{:T(512)S(6)} %compare.11), kind=kOutput, calls=%fused_computation.6.clone.1 | convolution fusion | flops 807665664 | bytes 1703941 | tf_op jit(solution)/shard_map/while/body/eval_jaxpr/dot_general | solution.py:121
  184.1 1.0 dynamic-slice.8
  185.4 3.7 %fusion.47 = f32[1024,128]{1,0:T(8,128)S(1)} fusion(bf16[1024,64]{1,0:T(8,128)(2,1)S(1)} %get-tuple-element.180, f32[1024,128]{1,0:T(8,128)S(1)} %get-tuple-element.169, bf16[2048,64]{1,0:T(8,128)(2,1)S(1)} %copy.93, bf16[32768,128]{0,1:T(8,128)(2,1)} %get-tuple-element.179, s32[]{:T(128)S(6)} %select_n.73, pred[]{:T(512)S(6)} %compare.11), kind=kOutput, calls=%fused_computation.6.clone.1 | convolution fusion | flops 807665664 | bytes 1703941 | tf_op jit(solution)/shard_map/while/body/eval_jaxpr/dot_general | solution.py:121
  189.1 1.0 dynamic-slice.8
  190.4 3.7 %fusion.47 = f32[1024,128]{1,0:T(8,128)S(1)} fusion(bf16[1024,64]{1,0:T(8,128)(2,1)S(1)} %get-tuple-element.180, f32[1024,128]{1,0:T(8,128)S(1)} %get-tuple-element.169, bf16[2048,64]{1,0:T(8,128)(2,1)S(1)} %copy.93, bf16[32768,128]{0,1:T(8,128)(2,1)} %get-tuple-element.179, s32[]{:T(128)S(6)} %select_n.73, pred[]{:T(512)S(6)} %compare.11), kind=kOutput, calls=%fused_computation.6.clone.1 | convolution fusion | flops 807665664 | bytes 1703941 | tf_op jit(solution)/shard_map/while/body/eval_jaxpr/dot_general | solution.py:121
  195.4 3.7 %fusion.47 = f32[1024,128]{1,0:T(8,128)S(1)} fusion(bf16[1024,64]{1,0:T(8,128)(2,1)S(1)} %get-tuple-element.180, f32[1024,128]{1,0:T(8,128)S(1)} %get-tuple-element.169, bf16[2048,64]{1,0:T(8,128)(2,1)S(1)} %copy.93, bf16[32768,128]{0,1:T(8,128)(2,1)} %get-tuple-element.179, s32[]{:T(128)S(6)} %select_n.73, pred[]{:T(512)S(6)} %compare.11), kind=kOutput, calls=%fused_computation.6.clone.1 | convolution fusion | flops 807665664 | bytes 1703941 | tf_op jit(solution)/shard_map/while/body/eval_jaxpr/dot_general | solution.py:121
  200.4 3.7 %fusion.47 = f32[1024,128]{1,0:T(8,128)S(1)} fusion(bf16[1024,64]{1,0:T(8,128)(2,1)S(1)} %get-tuple-element.180, f32[1024,128]{1,0:T(8,128)S(1)} %get-tuple-element.169, bf16[2048,64]{1,0:T(8,128)(2,1)S(1)} %copy.93, bf16[32768,128]{0,1:T(8,128)(2,1)} %get-tuple-element.179, s32[]{:T(128)S(6)} %select_n.73, pred[]{:T(512)S(6)} %compare.11), kind=kOutput, calls=%fused_computation.6.clone.1 | convolution fusion | flops 807665664 | bytes 1703941 | tf_op jit(solution)/shard_map/while/body/eval_jaxpr/dot_general | solution.py:121
  205.5 4.3 %all-to-all-start.1 = ((bf16[8,128,64]{1,2,0:T(8,128)(2,1)}), bf16[8,128,64]{1,2,0:T(8,128)(2,1)S(1)}, u32[]{:S(2)}, u32[]{:S(2)}) async-start(bf16[8,128,64]{1,2,0:T(8,128)(2,1)} %copy_bitcast_fusion.1), calls=%async_computation.1 | async-start | bytes 262144 | tf_op jit(solution)/shard_map/all_to_all | solution.py:132
  209.8 6.1 %all-to-all-done.1 = bf16[8,128,64]{1,2,0:T(8,128)(2,1)S(1)} async-done(((bf16[8,128,64]{1,2,0:T(8,128)(2,1)}), bf16[8,128,64]{1,2,0:T(8,128)(2,1)S(1)}, u32[]{:S(2)}, u32[]{:S(2)}) %all-to-all-start.1) | async-done | bytes 131104 | tf_op jit(solution)/shard_map/all_to_all | solution.py:132
  (104 shorter events, 18.5 us)
Async XLA Ops:
  6.5 59.6 %copy-start = (bf16[512,1024]{1,0:T(8,128)(2,1)S(1)}, bf16[512,1024]{1,0:T(8,128)(2,1)}, u32[]{:S(2)}) copy-start(bf16[512,1024]{1,0:T(8,128)(2,1)} %param.22) | copy-start | bytes 3145732
  6.5 2.8 %copy-start.11 = (f32[8]{0:T(128)S(1)}, f32[8]{0:T(128)}, u32[]{:S(2)}) copy-start(f32[8]{0:T(128)} %param.24) | copy-start | bytes 100
  6.5 117.4 %all-gather.2.cloned.1.call-start = ((), (), s32[]{:S(2)}) async-start(), calls=%async_computation.2 | async-start | bytes 8650752 | tf_op jit(solution)/shard_map/all_gather | solution.py:106
  7.6 2.1 copy-start.1
  7.6 2.1 copy-start.6
  9.7 1.0 copy-start.5
  10.1 1.0 copy-start.10
  11.8 30.8 %copy-start.12 = (s32[1,1,12]{2,1,0:T(1,128)S(1)}, s32[1,1,12]{2,1,0:T(1,128)}, u32[]{:S(2)}) copy-start(s32[1,1,12]{2,1,0:T(1,128)} %param.16) | copy-start | bytes 148
  25.1 20.8 %copy-start.2 = (bf16[1024,192]{0,1:T(8,128)(2,1)}, bf16[1024,192]{0,1:T(8,128)(2,1)S(1)}, u32[]{:S(2)}) copy-start(bf16[1024,192]{0,1:T(8,128)(2,1)S(1)} %copy_bitcast_fusion) | copy-start | bytes 1179652
  25.9 11.6 %collective-permute-start = (bf16[128,512]{1,0:T(8,128)(2,1)S(1)}, bf16[128,512]{1,0:T(8,128)(2,1)S(1)}, u32[]{:S(2)}, u32[]{:S(2)}) collective-permute-start(bf16[128,512]{1,0:T(8,128)(2,1)S(1)} %copy-done.1), channel_id=1, source_target_pairs={{0,4},{4,8},{8,12},{12,16},{16,20},{20,24},{24,28},{28,32},{32,36}... | collective-permute-start | bytes 393224 | tf_op jit(solution)/shard_map/ppermute | solution.py:29
  28.6 11.5 %collective-permute-start.1 = (bf16[128,512]{1,0:T(8,128)(2,1)S(1)}, bf16[128,512]{1,0:T(8,128)(2,1)S(1)}, u32[]{:S(2)}, u32[]{:S(2)}) collective-permute-start(bf16[128,512]{1,0:T(8,128)(2,1)S(1)} %copy-done.1), channel_id=1, source_target_pairs={{4,0},{8,4},{12,8},{16,12},{20,16},{24,20},{28,24},{32,28},{36,32}... | collective-permute-start | bytes 393224 | tf_op jit(solution)/shard_map/ppermute | solution.py:30
  40.2 18.3 %copy-start.4 = (bf16[384,512]{1,0:T(8,128)(2,1)}, bf16[384,512]{1,0:T(8,128)(2,1)S(1)}, u32[]{:S(2)}) copy-start(bf16[384,512]{1,0:T(8,128)(2,1)S(1)} %constant_dynamic-update-slice_fusion) | copy-start | bytes 1179652
  40.2 11.0 %collective-permute-start.2 = (bf16[384,512]{1,0:T(8,128)(2,1)S(1)}, bf16[384,512]{1,0:T(8,128)(2,1)}, u32[]{:S(2)}, u32[]{:S(2)}) collective-permute-start(bf16[384,512]{1,0:T(8,128)(2,1)S(1)} %constant_dynamic-update-slice_fusion), channel_id=1, source_target_pairs={{0,1},{1,2},{2,3},{3,0},{4,5},{5,6},{6,7},{7,4},{8,9},{9,10},{10,1... | collective-permute-start | bytes 1179656 | tf_op jit(solution)/shard_map/ppermute | solution.py:67
  40.3 12.1 %collective-permute-start.3 = (bf16[384,512]{1,0:T(8,128)(2,1)S(1)}, bf16[384,512]{1,0:T(8,128)(2,1)}, u32[]{:S(2)}, u32[]{:S(2)}) collective-permute-start(bf16[384,512]{1,0:T(8,128)(2,1)S(1)} %constant_dynamic-update-slice_fusion), channel_id=1, source_target_pairs={{0,2},{1,3},{2,0},{3,1},{4,6},{5,7},{6,4},{7,5},{8,10},{9,11},{10,... | collective-permute-start | bytes 1179656 | tf_op jit(solution)/shard_map/ppermute | solution.py:67
  41.2 17.3 %collective-permute-start.4 = (bf16[384,512]{1,0:T(8,128)(2,1)S(1)}, bf16[384,512]{1,0:T(8,128)(2,1)}, u32[]{:S(2)}, u32[]{:S(2)}) collective-permute-start(bf16[384,512]{1,0:T(8,128)(2,1)S(1)} %constant_dynamic-update-slice_fusion), channel_id=1, source_target_pairs={{0,3},{1,0},{2,1},{3,2},{4,7},{5,4},{6,5},{7,6},{8,11},{9,8},{10,9... | collective-permute-start | bytes 1179656 | tf_op jit(solution)/shard_map/ppermute | solution.py:67
  66.1 2.3 %copy-start.3 = (bf16[1024,512]{1,0:T(8,128)(2,1)S(1)}, bf16[1024,512]{1,0:T(8,128)(2,1)}, u32[]{:S(2)}) copy-start(bf16[1024,512]{1,0:T(8,128)(2,1)} %param.23) | copy-start | bytes 3145732
  68.5 0.9 slice-start
  204.2 5.6 %copy-start.9 = (s32[8]{0:T(128)S(1)}, s32[8]{0:T(128)}, u32[]{:S(2)}) copy-start(s32[8]{0:T(128)} %constant.122) | copy-start | bytes 100
  204.2 12.3 %copy-start.7 = (bf16[512,512]{1,0:T(8,128)(2,1)S(1)}, bf16[512,512]{1,0:T(8,128)(2,1)}, u32[]{:S(2)}) copy-start(bf16[512,512]{1,0:T(8,128)(2,1)} %param.21) | copy-start | bytes 1572868
  204.4 12.4 %copy-start.8 = (f32[512]{0:T(512)S(1)}, f32[512]{0:T(512)}, u32[]{:S(2)}) copy-start(f32[512]{0:T(512)} %param.25) | copy-start | bytes 6148
  205.5 10.4 %all-to-all-start.1 = ((bf16[8,128,64]{1,2,0:T(8,128)(2,1)}), bf16[8,128,64]{1,2,0:T(8,128)(2,1)S(1)}, u32[]{:S(2)}, u32[]{:S(2)}) async-start(bf16[8,128,64]{1,2,0:T(8,128)(2,1)} %copy_bitcast_fusion.1), calls=%async_computation.1 | async-start | bytes 262144 | tf_op jit(solution)/shard_map/all_to_all | solution.py:132
Sparse Core Ops, SparseCore 0:
  26.0 97.8 all-gather.1

commit v5 on v4

--- a/solution.py
+++ b/solution.py
@@ -1,6 +1,8 @@
 import math
 
 import jax
+from jax.experimental import pallas as pl
+from jax.experimental.pallas import tpu as pltpu
 import jax.numpy as jnp
 from jax import lax
 from jax.sharding import Mesh
@@ -8,7 +10,9 @@
 
 NUM_SUBSPACES = 8
 SUBSPACE_WIDTH = 64
-KEY_BLOCK = 2048
+KEY_BLOCK = 8192
+KEY_STEP = 2048
+QUERY_STEP = 1024
 
 norm_eps = 1e-06
 
@@ -39,6 +43,53 @@
     if scales is not None:
         scaled = scaled * scales[None, :, None]
     return scaled.reshape(rows, -1).astype(jnp.bfloat16)
+
+
+def attention_kernel(q_ref, kv_ref, o_ref):
+    @pl.when(pl.program_id(0) == 0)
+    def _():
+        o_ref[...] = jnp.zeros_like(o_ref)
+
+    q_step = min(QUERY_STEP, q_ref.shape[0])
+    k_step = min(KEY_STEP, kv_ref.shape[0])
+    q_count = q_ref.shape[0] // q_step
+    k_count = kv_ref.shape[0] // k_step
+
+    def body(turn, carry):
+        rows = pl.ds(pl.multiple_of((turn // k_count) * q_step, q_step), q_step)
+        keys = pl.ds(pl.multiple_of((turn % k_count) * k_step, k_step), k_step)
+        block = kv_ref[keys, :]
+        scores = lax.dot_general(
+            q_ref[rows, :], block, (((1,), (1,)), ((), ())), preferred_element_type=jnp.float32
+        )
+        weights = jnp.exp(scores).astype(jnp.bfloat16)
+        lane = lax.broadcasted_iota(jnp.int32, block.shape, 1)
+        widened = jnp.where(lane < SUBSPACE_WIDTH, jnp.ones_like(block), block)
+        o_ref[rows, :] += jnp.dot(weights, widened, preferred_element_type=jnp.float32)
+        return carry
+
+    lax.fori_loop(0, q_count * k_count, body, 0)
+
+
+def attend(padded_queries, key_values):
+    rows, width = padded_queries.shape
+    keys = key_values.shape[0]
+    block = min(KEY_BLOCK, keys)
+    flops = 4 * rows * keys * width
+    return pl.pallas_call(
+        attention_kernel,
+        grid=(keys // block,),
+        in_specs=[
+            pl.BlockSpec((rows, width), lambda j: (0, 0)),
+            pl.BlockSpec((block, width), lambda j: (j, 0)),
+        ],
+        out_specs=pl.BlockSpec((rows, width), lambda j: (0, 0)),
+        out_shape=jax.ShapeDtypeStruct((rows, width), jnp.float32),
+        compiler_params=pltpu.CompilerParams(dimension_semantics=("arbitrary",)),
+        cost_estimate=pl.CostEstimate(
+            flops=flops, transcendentals=rows * keys, bytes_accessed=2 * keys * width + 6 * rows * width
+        ),
+    )(padded_queries, key_values)
 
 
 def shards(
@@ -104,31 +155,9 @@
 
     local_term, head_queries = lax.optimization_barrier((local_term, head_queries))
     kv_in = lax.all_gather(key_values, (ROW, COLUMN), axis=0, tiled=True)
-    key_count = kv_in.shape[0]
-    block_step = min(KEY_BLOCK, key_count)
-    ones = jnp.ones((block_step, SUBSPACE_WIDTH), jnp.bfloat16)
-
-    def accumulate(turn_index, totals):
-        block = lax.dynamic_slice_in_dim(kv_in, turn_index * block_step, block_step, 0)
-        scores = jnp.einsum(
-            "qd,kd->qk",
-            head_queries,
-            block[:, :SUBSPACE_WIDTH],
-            preferred_element_type=jnp.float32,
-        )
-        weights = jnp.exp(scores).astype(jnp.bfloat16)
-        widened = jnp.concatenate([block[:, SUBSPACE_WIDTH:], ones], axis=1)
-        return totals + jnp.dot(weights, widened, preferred_element_type=jnp.float32)
-
-    totals = lax.fori_loop(
-        0,
-        key_count // block_step,
-        accumulate,
-        jnp.zeros((query_rows, 2 * SUBSPACE_WIDTH), jnp.float32),
-    )
-    merged = (totals[:, :SUBSPACE_WIDTH] / totals[:, SUBSPACE_WIDTH : SUBSPACE_WIDTH + 1]).astype(
-        jnp.bfloat16
-    )
+    padded_queries = jnp.concatenate([head_queries, jnp.zeros_like(head_queries)], axis=1)
+    totals = attend(padded_queries, kv_in)
+    merged = (totals[:, SUBSPACE_WIDTH:] / totals[:, :1]).astype(jnp.bfloat16)
     back = lax.all_to_all(merged, GROUP, split_axis=0, concat_axis=1, tiled=True)
     node_heads = back.reshape(block_len, members, SUBSPACE_WIDTH)[:, jnp.array(member_of)]
     node_heads = node_heads.reshape(block_len, -1)

time: 228 us -> 189 us (0.83)
  matrix products: 64.5 us -> 4.72 us
  Pallas kernels: 0 us -> 40 us
  local copies, waits for them, and re-layouts: 34.2 us -> 15.1 us
    dot_general x16 -> x0, matrix products: 59.7 us -> none  [accumulate(): jnp.dot(weights, widened, preferred_element_type=jnp.float32)]
    pallas_call x0 -> x1, Pallas kernels: none -> 40 us  [attend(): pl.pallas_call(attention_kernel, grid=(keys // block,), in_specs=[pl.Bloc...]
    slice x17 -> x1, local copies, waits for them, and re-layouts: 15.9 us -> 1.3 us  [shards(): merged = (totals[:, SUBSPACE_WIDTH:] / totals[:, :1]).astype(jnp.bfloat16)]
    while x17 -> x0, local copies, waits for them, and re-layouts: 4.57 us -> none
  transfers between devices with their start and end apart: 7 -> 7, of which waited for: 7 -> 7; matrix products, arithmetic and copies ran while one was open for 6% -> 7% of each run, Pallas kernels for 0% -> 0%
where the time goes in v5:
time: 189 us; the launch traced here: 187 us
  waiting for transfers between devices  77.9 us (41%)
  Pallas kernels  40 us (21%)
  starting transfers between devices  17 us (9%)
  local copies, waits for them, and re-layouts  15.1 us (8%)
  between operations  13.8 us (7%)
  blocking collectives  13.3 us (7%)
  other arithmetic  4.72 us (2%)
  matrix products  4.72 us (2%)
    all_gather x1, waiting for transfers between devices, shards(): kv_in = lax.all_gather(key_values, (ROW, COLUMN), axis=0, tiled=True)  54.4 us
    pallas_call x1, Pallas kernels, attend(): pl.pallas_call(attention_kernel, grid=(keys // block,), in_specs=[pl.Bloc...  40 us
    ppermute x3, waiting for transfers between devices, shards(): gathered.append(lax.ppermute(halo_rows, 'head', pairs))  13.6 us
    all_to_all x1, blocking collectives, shards(): lax.all_to_all(packed, GROUP, split_axis=1, concat_axis=0, tiled=True)  13.3 us
    ppermute x1, starting transfers between devices, extended(): after = lax.ppermute(first, DOM, down)  7.63 us
    all_to_all x1, waiting for transfers between devices, shards(): lax.all_to_all(merged, GROUP, split_axis=0, concat_axis=1, tiled=True)  6.12 us
    scatter x1, local copies, waits for them, and re-layouts, shards(): jnp.zeros_like(stacked).at[order].set(stacked)  4.78 us
    all_to_all x1, starting transfers between devices, shards(): lax.all_to_all(merged, GROUP, split_axis=0, concat_axis=1, tiled=True)  4.29 us
  transfers between devices with their start and end apart: 7, of which 7 were waited for; matrix products, arithmetic and copies ran while one was open for 7% of the time, Pallas kernels for 0%

profile of v5, /device:TPU:4, one launch (start us, length us, event | category | flops | bytes accessed | tf_op | source)
XLA Modules:
  0.0 186.6 jit_solution(968220489497485144)
XLA Ops:
  6.5 0.8 maximum_reduce_fusion
  7.4 0.1 copy.34
  7.6 1.4 fusion.13
  9.0 0.1 copy.36
  9.2 0.1 copy.37
  9.5 0.1 copy.38
  9.7 0.2 fusion.12
  9.9 0.1 copy.39
  10.2 0.1 copy.40
  10.3 0.1 copy.41
  10.5 0.3 copy-done.3
  10.7 0.2 convolution_convert_fusion
  11.0 0.1 copy.42
  11.2 0.6 gather_fusion.1
  11.8 13.3 %all_to_all.35 = bf16[128,8,192]{0,2,1:T(8,128)(2,1)S(1)} all-to-all(bf16[128,8,192]{0,2,1:T(8,128)(2,1)S(1)} %bitcast.52), channel_id=1, replica_groups=mesh['x'=4,'z'=8,'yhi'=2,'head'=4] {'yhi','head'}, dimensions={1} | all-to-all | bytes 786432 | tf_op jit(solution)/shard_map/all_to_all | solution.py:142
  25.2 0.2 copy.46
  25.4 0.9 slice.23
  26.3 2.7 %collective-permute-start = (bf16[128,512]{1,0:T(8,128)(2,1)S(1)}, bf16[128,512]{1,0:T(8,128)(2,1)S(1)}, u32[]{:S(2)}, u32[]{:S(2)}) collective-permute-start(bf16[128,512]{1,0:T(8,128)(2,1)S(1)} %copy-done.1), channel_id=1, source_target_pairs={{0,4},{4,8},{8,12},{12,16},{16,20},{20,24},{24,28},{28,32},{32,36}... | collective-permute-start | bytes 393224 | tf_op jit(solution)/shard_map/ppermute | solution.py:33
  29.0 7.6 %collective-permute-start.1 = (bf16[128,512]{1,0:T(8,128)(2,1)S(1)}, bf16[128,512]{1,0:T(8,128)(2,1)S(1)}, u32[]{:S(2)}, u32[]{:S(2)}) collective-permute-start(bf16[128,512]{1,0:T(8,128)(2,1)S(1)} %copy-done.1), channel_id=1, source_target_pairs={{4,0},{8,4},{12,8},{16,12},{20,16},{24,20},{28,24},{32,28},{36,32}... | collective-permute-start | bytes 393224 | tf_op jit(solution)/shard_map/ppermute | solution.py:34
  36.6 1.2 collective-permute-done
  37.9 2.7 %collective-permute-done.1 = bf16[128,512]{1,0:T(8,128)(2,1)S(1)} collective-permute-done((bf16[128,512]{1,0:T(8,128)(2,1)S(1)}, bf16[128,512]{1,0:T(8,128)(2,1)S(1)}, u32[]{:S(2)}, u32[]{:S(2)}) %collective-permute-start.1) | collective-permute-done | bytes 131104 | tf_op jit(solution)/shard_map/ppermute | solution.py:34
  40.5 0.1 collective-permute-start.2
  40.6 0.9 collective-permute-start.3
  41.6 1.4 collective-permute-start.4
  43.0 0.1 copy.32
  43.3 0.1 copy.33
  43.5 0.6 gather_fusion
  44.2 0.1 select_bitcast_fusion
  44.3 0.9 copy.35
  45.3 6.2 %collective-permute-done.2 = bf16[384,512]{1,0:T(8,128)(2,1)} collective-permute-done((bf16[384,512]{1,0:T(8,128)(2,1)S(1)}, bf16[384,512]{1,0:T(8,128)(2,1)}, u32[]{:S(2)}, u32[]{:S(2)}) %collective-permute-start.2) | collective-permute-done | bytes 393248 | tf_op jit(solution)/shard_map/ppermute | solution.py:118
  51.5 1.3 collective-permute-done.3
  52.8 6.1 %collective-permute-done.4 = bf16[384,512]{1,0:T(8,128)(2,1)} collective-permute-done((bf16[384,512]{1,0:T(8,128)(2,1)S(1)}, bf16[384,512]{1,0:T(8,128)(2,1)}, u32[]{:S(2)}, u32[]{:S(2)}) %collective-permute-start.4) | collective-permute-done | bytes 393248 | tf_op jit(solution)/shard_map/ppermute | solution.py:118
  58.8 1.4 pad_maximum_fusion
  60.3 1.3 broadcast_in_dim.42
  61.6 4.8 %scatter_fusion = bf16[4,384,512]{2,1,0:T(8,128)(2,1)} fusion(bf16[4,384,512]{2,1,0:T(8,128)(2,1)} %broadcast_in_dim.42, s32[4]{0:T(128)S(1)} %fusion.11, bf16[4,384,512]{2,1,0:T(8,128)(2,1)S(1)} %pad_maximum_fusion), kind=kCustom, calls=%fused_computation.3 | custom fusion | bytes 4718608 | tf_op jit(solution)/shard_map/scatter | solution.py:121
  66.4 2.2 %fusion.8 = bf16[128,1024]{1,0:T(8,128)(2,1)S(1)} fusion(bf16[512,1024]{1,0:T(8,128)(2,1)S(1)} %copy-done, bf16[128,1536]{0,1:T(8,128)(2,1)S(1)} %bitcast.65, bf16[1536,512]{1,0:T(8,128)(2,1)} %bitcast.51), kind=kOutput, calls=%fused_computation.16 | convolution fusion | flops 336789504 | bytes 3276800 | tf_op jit(solution)/shard_map/dot_general | solution.py:152
  68.6 0.3 fusion.14
  68.9 0.8 concatenate.7.q_ref
  69.7 54.4 %all-gather.2.cloned.1.call-done.kv_ref = bf16[32768,128]{1,0:T(8,128)(2,1)} async-done(((bf16[1024,128]{1,0:T(8,128)(2,1)}), bf16[32768,128]{1,0:T(8,128)(2,1)}) %all-gather.2.cloned.1.call-update) | async-done | bytes 8388624 | tf_op jit(solution)/shard_map/all_gather | solution.py:157
  124.1 40.0 %shard_map.127 = f32[1024,128]{1,0:T(8,128)} custom-call(bf16[1024,128]{1,0:T(8,128)(2,1)} %concatenate.7.q_ref, bf16[32768,128]{1,0:T(8,128)(2,1)} %all-gather.2.cloned.1.call-done.kv_ref), custom_call_target="tpu_custom_call" | custom-call | flops 17179869184 | bytes 9175040 | tf_op jit(solution)/shard_map/pallas_call | solution.py:79
  164.1 1.3 slice_reduce_fusion
  165.4 1.4 fusion.9
  166.8 0.8 copy.47
  167.6 4.3 %all-to-all-start.1 = ((bf16[8,128,64]{1,2,0:T(8,128)(2,1)}), bf16[8,128,64]{1,2,0:T(8,128)(2,1)S(1)}, u32[]{:S(2)}, u32[]{:S(2)}) async-start(bf16[8,128,64]{1,2,0:T(8,128)(2,1)} %copy.47), calls=%async_computation.1 | async-start | bytes 262144 | tf_op jit(solution)/shard_map/all_to_all | solution.py:161
  171.9 6.1 %all-to-all-done.1 = bf16[8,128,64]{1,2,0:T(8,128)(2,1)S(1)} async-done(((bf16[8,128,64]{1,2,0:T(8,128)(2,1)}), bf16[8,128,64]{1,2,0:T(8,128)(2,1)S(1)}, u32[]{:S(2)}, u32[]{:S(2)}) %all-to-all-start.1) | async-done | bytes 131104 | tf_op jit(solution)/shard_map/all_to_all | solution.py:161
  178.0 0.6 gather_fusion.2
  178.6 0.3 multiply_reduce_fusion
  178.9 0.8 add_convert_fusion
  (54 shorter events, 1.1 us)
Async XLA Ops:
  6.5 59.9 %copy-start = (bf16[512,1024]{1,0:T(8,128)(2,1)S(1)}, bf16[512,1024]{1,0:T(8,128)(2,1)}, u32[]{:S(2)}) copy-start(bf16[512,1024]{1,0:T(8,128)(2,1)} %param.20) | copy-start | bytes 3145732
  6.5 2.8 %copy-start.11 = (f32[8]{0:T(128)S(1)}, f32[8]{0:T(128)}, u32[]{:S(2)}) copy-start(f32[8]{0:T(128)} %param.22) | copy-start | bytes 100
  6.5 117.5 %all-gather.2.cloned.1.call-start = ((), (), s32[]{:S(2)}) async-start(), calls=%async_computation.2 | async-start | bytes 8650752 | tf_op jit(solution)/shard_map/all_gather | solution.py:157
  7.6 2.1 %copy-start.1 = (bf16[128,512]{1,0:T(8,128)(2,1)S(1)}, bf16[128,512]{1,0:T(8,128)(2,1)}, u32[]{:S(2)}) copy-start(bf16[128,512]{1,0:T(8,128)(2,1)} %param.13) | copy-start | bytes 393220
  7.6 2.1 %copy-start.4 = (bf16[512,512]{1,0:T(8,128)(2,1)S(1)}, bf16[512,512]{1,0:T(8,128)(2,1)}, u32[]{:S(2)}) copy-start(bf16[512,512]{1,0:T(8,128)(2,1)} %param.17) | copy-start | bytes 1572868
  9.7 1.0 copy-start.3
  10.1 1.0 copy-start.10
  11.8 31.1 %copy-start.12 = (s32[1,1,12]{2,1,0:T(1,128)S(1)}, s32[1,1,12]{2,1,0:T(1,128)}, u32[]{:S(2)}) copy-start(s32[1,1,12]{2,1,0:T(1,128)} %param.14) | copy-start | bytes 148
  11.8 31.7 %copy-start.7 = (bf16[16,128,128]{2,1,0:T(8,128)(2,1)S(1)}, bf16[16,128,128]{2,1,0:T(8,128)(2,1)}, u32[]{:S(2)}) copy-start(bf16[16,128,128]{2,1,0:T(8,128)(2,1)} %param.15) | copy-start | bytes 1572868
  26.3 11.6 %collective-permute-start = (bf16[128,512]{1,0:T(8,128)(2,1)S(1)}, bf16[128,512]{1,0:T(8,128)(2,1)S(1)}, u32[]{:S(2)}, u32[]{:S(2)}) collective-permute-start(bf16[128,512]{1,0:T(8,128)(2,1)S(1)} %copy-done.1), channel_id=1, source_target_pairs={{0,4},{4,8},{8,12},{12,16},{16,20},{20,24},{24,28},{28,32},{32,36}... | collective-permute-start | bytes 393224 | tf_op jit(solution)/shard_map/ppermute | solution.py:33
  29.0 11.5 %collective-permute-start.1 = (bf16[128,512]{1,0:T(8,128)(2,1)S(1)}, bf16[128,512]{1,0:T(8,128)(2,1)S(1)}, u32[]{:S(2)}, u32[]{:S(2)}) collective-permute-start(bf16[128,512]{1,0:T(8,128)(2,1)S(1)} %copy-done.1), channel_id=1, source_target_pairs={{4,0},{8,4},{12,8},{16,12},{20,16},{24,20},{28,24},{32,28},{36,32}... | collective-permute-start | bytes 393224 | tf_op jit(solution)/shard_map/ppermute | solution.py:34
  40.5 11.0 %collective-permute-start.2 = (bf16[384,512]{1,0:T(8,128)(2,1)S(1)}, bf16[384,512]{1,0:T(8,128)(2,1)}, u32[]{:S(2)}, u32[]{:S(2)}) collective-permute-start(bf16[384,512]{1,0:T(8,128)(2,1)S(1)} %constant_dynamic-update-slice_fusion), channel_id=1, source_target_pairs={{0,1},{1,2},{2,3},{3,0},{4,5},{5,6},{6,7},{7,4},{8,9},{9,10},{10,1... | collective-permute-start | bytes 1179656 | tf_op jit(solution)/shard_map/ppermute | solution.py:118
  40.6 12.1 %collective-permute-start.3 = (bf16[384,512]{1,0:T(8,128)(2,1)S(1)}, bf16[384,512]{1,0:T(8,128)(2,1)}, u32[]{:S(2)}, u32[]{:S(2)}) collective-permute-start(bf16[384,512]{1,0:T(8,128)(2,1)S(1)} %constant_dynamic-update-slice_fusion), channel_id=1, source_target_pairs={{0,2},{1,3},{2,0},{3,1},{4,6},{5,7},{6,4},{7,5},{8,10},{9,11},{10,... | collective-permute-start | bytes 1179656 | tf_op jit(solution)/shard_map/ppermute | solution.py:118
  41.6 17.3 %collective-permute-start.4 = (bf16[384,512]{1,0:T(8,128)(2,1)S(1)}, bf16[384,512]{1,0:T(8,128)(2,1)}, u32[]{:S(2)}, u32[]{:S(2)}) collective-permute-start(bf16[384,512]{1,0:T(8,128)(2,1)S(1)} %constant_dynamic-update-slice_fusion), channel_id=1, source_target_pairs={{0,3},{1,0},{2,1},{3,2},{4,7},{5,4},{6,5},{7,6},{8,11},{9,8},{10,9... | collective-permute-start | bytes 1179656 | tf_op jit(solution)/shard_map/ppermute | solution.py:118
  61.6 4.8 %copy-start.6 = (bf16[128,12,128]{0,2,1:T(8,128)(2,1)S(1)}, bf16[128,12,128]{0,2,1:T(8,128)(2,1)}, u32[]{:S(2)}) copy-start(bf16[128,12,128]{0,2,1:T(8,128)(2,1)} %copy.35) | copy-start | bytes 1179652
  66.4 2.2 %copy-start.2 = (bf16[1024,512]{1,0:T(8,128)(2,1)S(1)}, bf16[1024,512]{1,0:T(8,128)(2,1)}, u32[]{:S(2)}) copy-start(bf16[1024,512]{1,0:T(8,128)(2,1)} %param.21) | copy-start | bytes 3145732
  164.1 7.8 %copy-start.9 = (s32[8]{0:T(128)S(1)}, s32[8]{0:T(128)}, u32[]{:S(2)}) copy-start(s32[8]{0:T(128)} %constant.87) | copy-start | bytes 100
  164.1 14.5 %copy-start.5 = (bf16[512,512]{1,0:T(8,128)(2,1)S(1)}, bf16[512,512]{1,0:T(8,128)(2,1)}, u32[]{:S(2)}) copy-start(bf16[512,512]{1,0:T(8,128)(2,1)} %param.19) | copy-start | bytes 1572868
  165.4 13.6 %copy-start.8 = (f32[512]{0:T(512)S(1)}, f32[512]{0:T(512)}, u32[]{:S(2)}) copy-start(f32[512]{0:T(512)} %param.23) | copy-start | bytes 6148
  167.6 10.4 %all-to-all-start.1 = ((bf16[8,128,64]{1,2,0:T(8,128)(2,1)}), bf16[8,128,64]{1,2,0:T(8,128)(2,1)S(1)}, u32[]{:S(2)}, u32[]{:S(2)}) async-start(bf16[8,128,64]{1,2,0:T(8,128)(2,1)} %copy.47), calls=%async_computation.1 | async-start | bytes 262144 | tf_op jit(solution)/shard_map/all_to_all | solution.py:161
Sparse Core Ops, SparseCore 0:
  26.4 97.6 all-gather.1

commit v6 on v5

--- a/solution.py
+++ b/solution.py
@@ -10,9 +10,6 @@
 
 NUM_SUBSPACES = 8
 SUBSPACE_WIDTH = 64
-KEY_BLOCK = 8192
-KEY_STEP = 2048
-QUERY_STEP = 1024
 
 norm_eps = 1e-06
 
@@ -45,49 +42,87 @@
     return scaled.reshape(rows, -1).astype(jnp.bfloat16)
 
 
-def attention_kernel(q_ref, kv_ref, o_ref):
-    @pl.when(pl.program_id(0) == 0)
-    def _():
-        o_ref[...] = jnp.zeros_like(o_ref)
-
-    q_step = min(QUERY_STEP, q_ref.shape[0])
-    k_step = min(KEY_STEP, kv_ref.shape[0])
-    q_count = q_ref.shape[0] // q_step
-    k_count = kv_ref.shape[0] // k_step
-
-    def body(turn, carry):
-        rows = pl.ds(pl.multiple_of((turn // k_count) * q_step, q_step), q_step)
-        keys = pl.ds(pl.multiple_of((turn % k_count) * k_step, k_step), k_step)
-        block = kv_ref[keys, :]
-        scores = lax.dot_general(
-            q_ref[rows, :], block, (((1,), (1,)), ((), ())), preferred_element_type=jnp.float32
+def accumulate(q_ref, block, o_ref):
+    scores = lax.dot_general(
+        q_ref[...], block, (((1,), (1,)), ((), ())), preferred_element_type=jnp.float32
+    )
+    weights = jnp.exp(scores).astype(jnp.bfloat16)
+    lane = lax.broadcasted_iota(jnp.int32, block.shape, 1)
+    widened = jnp.where(lane < SUBSPACE_WIDTH, jnp.ones_like(block), block)
+    o_ref[...] += jnp.dot(weights, widened, preferred_element_type=jnp.float32)
+
+
+def gathering_kernel(q_ref, kv_ref, o_ref, slots, send_sem, recv_sem):
+    columns = lax.axis_size(COLUMN)
+    positions = lax.axis_size(ROW) * columns
+    me = lax.axis_index(ROW) * columns + lax.axis_index(COLUMN)
+    pair = lax.axis_index(PAIR)
+    member = lax.axis_index("head")
+
+    def copy_with(offset):
+        target = lax.rem(me + offset, positions)
+        return pltpu.make_async_remote_copy(
+            src_ref=kv_ref,
+            dst_ref=slots.at[me],
+            send_sem=send_sem.at[offset],
+            recv_sem=recv_sem.at[me],
+            device_id=(target // columns, lax.rem(target, columns), pair, member),
+            device_id_type=pl.DeviceIdType.MESH,
         )
-        weights = jnp.exp(scores).astype(jnp.bfloat16)
-        lane = lax.broadcasted_iota(jnp.int32, block.shape, 1)
-        widened = jnp.where(lane < SUBSPACE_WIDTH, jnp.ones_like(block), block)
-        o_ref[rows, :] += jnp.dot(weights, widened, preferred_element_type=jnp.float32)
+
+    def arrival_from(offset):
+        source = lax.rem(me - offset + positions, positions)
+        return source, pltpu.make_async_remote_copy(
+            src_ref=kv_ref,
+            dst_ref=slots.at[source],
+            send_sem=send_sem.at[offset],
+            recv_sem=recv_sem.at[source],
+            device_id=(source // columns, lax.rem(source, columns), pair, member),
+            device_id_type=pl.DeviceIdType.MESH,
+        )
+
+    def send(offset, carry):
+        copy_with(offset).start()
         return carry
 
-    lax.fori_loop(0, q_count * k_count, body, 0)
-
-
-def attend(padded_queries, key_values):
+    lax.fori_loop(1, positions, send, 0)
+    o_ref[...] = jnp.zeros_like(o_ref)
+    accumulate(q_ref, kv_ref[...], o_ref)
+
+    def receive(offset, carry):
+        source, arrival = arrival_from(offset)
+        arrival.wait_recv()
+        accumulate(q_ref, slots[source], o_ref)
+        return carry
+
+    lax.fori_loop(1, positions, receive, 0)
+
+    def finish(offset, carry):
+        copy_with(offset).wait_send()
+        return carry
+
+    lax.fori_loop(1, positions, finish, 0)
+
+
+def gather_attend(padded_queries, key_values):
     rows, width = padded_queries.shape
-    keys = key_values.shape[0]
-    block = min(KEY_BLOCK, keys)
-    flops = 4 * rows * keys * width
+    positions = lax.axis_size(ROW) * lax.axis_size(COLUMN)
+    keys = positions * key_values.shape[0]
     return pl.pallas_call(
-        attention_kernel,
-        grid=(keys // block,),
-        in_specs=[
-            pl.BlockSpec((rows, width), lambda j: (0, 0)),
-            pl.BlockSpec((block, width), lambda j: (j, 0)),
+        gathering_kernel,
+        in_specs=[pl.BlockSpec(memory_space=pltpu.VMEM)] * 2,
+        out_specs=pl.BlockSpec(memory_space=pltpu.VMEM),
+        out_shape=jax.ShapeDtypeStruct((rows, width), jnp.float32),
+        scratch_shapes=[
+            pltpu.VMEM((positions,) + key_values.shape, key_values.dtype),
+            pltpu.SemaphoreType.DMA((positions,)),
+            pltpu.SemaphoreType.DMA((positions,)),
         ],
-        out_specs=pl.BlockSpec((rows, width), lambda j: (0, 0)),
-        out_shape=jax.ShapeDtypeStruct((rows, width), jnp.float32),
-        compiler_params=pltpu.CompilerParams(dimension_semantics=("arbitrary",)),
+        compiler_params=pltpu.CompilerParams(has_side_effects=True),
         cost_estimate=pl.CostEstimate(
-            flops=flops, transcendentals=rows * keys, bytes_accessed=2 * keys * width + 6 * rows * width
+            flops=4 * rows * keys * width,
+            transcendentals=rows * keys,
+            bytes_accessed=2 * keys * width + 6 * rows * width,
         ),
     )(padded_queries, key_values)
 
@@ -154,9 +189,8 @@
     local_term = jnp.dot(hidden, passing_outer_coefficients, preferred_element_type=jnp.float32)
 
     local_term, head_queries = lax.optimization_barrier((local_term, head_queries))
-    kv_in = lax.all_gather(key_values, (ROW, COLUMN), axis=0, tiled=True)
     padded_queries = jnp.concatenate([head_queries, jnp.zeros_like(head_queries)], axis=1)
-    totals = attend(padded_queries, kv_in)
+    totals = gather_attend(padded_queries, key_values)
     merged = (totals[:, SUBSPACE_WIDTH:] / totals[:, :1]).astype(jnp.bfloat16)
     back = lax.all_to_all(merged, GROUP, split_axis=0, concat_axis=1, tiled=True)
     node_heads = back.reshape(block_len, members, SUBSPACE_WIDTH)[:, jnp.array(member_of)]

time: 189 us -> 311 us (1.65)
  the two profiles are of different devices: /device:TPU:4 before, /device:TPU:68 now
where the time goes in v6:
time: 311 us
  Pallas kernels  245 us (79%)
  waiting for transfers between devices  19.3 us (6%)
  starting transfers between devices  18.9 us (6%)
  local copies, waits for them, and re-layouts  17.3 us (6%)
  matrix products  4.66 us (1%)
  other arithmetic  4.62 us (1%)
    pallas_call x1, Pallas kernels, gather_attend(): pl.pallas_call(gathering_kernel, in_specs=[pl.BlockSpec(memory_space=pltp...  245 us
    ppermute x3, waiting for transfers between devices, shards(): gathered.append(lax.ppermute(halo_rows, 'head', pairs))  11.6 us
  transfers between devices with their start and end apart: 7, of which 5 were waited for; matrix products, arithmetic and copies ran while one was open for 3% of the time, Pallas kernels for 0%

profile of v6, /device:TPU:68, one launch (start us, length us, event | category | flops | bytes accessed | tf_op | source)
XLA Modules:
  0.0 310.6 jit_solution(16702401472005966132)
XLA Ops:
  0.0 5.2 %collective-permute-start = (bf16[128,512]{1,0:T(8,128)(2,1)}, bf16[128,512]{1,0:T(8,128)(2,1)}, u32[]{:S(2)}, u32[]{:S(2)}) collective-permute-start(bf16[128,512]{1,0:T(8,128)(2,1)} %param.13), channel_id=1, source_target_pairs={{0,4},{4,8},{8,12},{12,16},{16,20},{20,24},{24,28},{28,32},{32,36}... | collective-permute-start | bytes 393224 | tf_op jit(solution)/shard_map/ppermute | solution.py:30
  5.3 3.1 %collective-permute-start.1 = (bf16[128,512]{1,0:T(8,128)(2,1)}, bf16[128,512]{1,0:T(8,128)(2,1)}, u32[]{:S(2)}, u32[]{:S(2)}) collective-permute-start(bf16[128,512]{1,0:T(8,128)(2,1)} %param.13), channel_id=1, source_target_pairs={{4,0},{8,4},{12,8},{16,12},{20,16},{24,20},{28,24},{32,28},{36,32}... | collective-permute-start | bytes 393224 | tf_op jit(solution)/shard_map/ppermute | solution.py:31
  8.4 0.7 maximum_reduce_fusion
  9.2 0.1 copy.34
  9.4 1.3 fusion.12
  10.7 0.1 copy.36
  10.9 0.1 copy.37
  11.2 0.2 fusion.11
  11.5 0.1 copy.39
  11.7 0.1 copy.40
  11.8 0.1 copy-done.3
  12.0 0.2 convolution_convert_fusion
  12.3 0.1 copy.38
  12.4 0.1 copy.41
  12.6 0.1 copy.42
  12.8 1.3 gather_fusion.1
  14.1 3.6 %all-to-all-start = ((bf16[128,8,192]{0,2,1:T(8,128)(2,1)}), bf16[128,8,192]{0,2,1:T(8,128)(2,1)S(1)}, u32[]{:S(2)}, u32[]{:S(2)}) async-start(bf16[128,8,192]{0,2,1:T(8,128)(2,1)} %bitcast.22), calls=%async_computation | async-start | bytes 786432 | tf_op jit(solution)/shard_map/all_to_all | solution.py:177
  17.7 0.9 constant_dynamic-update-slice_fusion.2
  18.6 0.9 constant_dynamic-update-slice_fusion
  19.6 0.6 collective-permute-start.2
  20.1 1.7 collective-permute-start.3
  21.8 1.3 collective-permute-start.4
  23.2 0.1 copy.32
  23.5 0.1 copy.33
  23.7 0.6 gather_fusion
  24.4 0.1 select_bitcast_fusion
  24.5 0.9 copy.35
  25.4 1.7 all-to-all-done
  27.1 0.2 copy.46
  27.4 0.9 slice.23.kv_ref
  28.2 5.0 %collective-permute-done.2 = bf16[384,512]{1,0:T(8,128)(2,1)} collective-permute-done((bf16[384,512]{1,0:T(8,128)(2,1)S(1)}, bf16[384,512]{1,0:T(8,128)(2,1)}, u32[]{:S(2)}, u32[]{:S(2)}) %collective-permute-start.2) | collective-permute-done | bytes 393248 | tf_op jit(solution)/shard_map/ppermute | solution.py:153
  33.2 0.9 collective-permute-done.3
  34.1 5.7 %collective-permute-done.4 = bf16[384,512]{1,0:T(8,128)(2,1)} collective-permute-done((bf16[384,512]{1,0:T(8,128)(2,1)S(1)}, bf16[384,512]{1,0:T(8,128)(2,1)}, u32[]{:S(2)}, u32[]{:S(2)}) %collective-permute-start.4) | collective-permute-done | bytes 393248 | tf_op jit(solution)/shard_map/ppermute | solution.py:153
  39.9 1.4 pad_maximum_fusion
  41.3 1.3 broadcast_in_dim.42
  42.6 4.6 %scatter_fusion = bf16[4,384,512]{2,1,0:T(8,128)(2,1)} fusion(bf16[4,384,512]{2,1,0:T(8,128)(2,1)} %broadcast_in_dim.42, s32[4]{0:T(128)S(1)} %fusion.10, bf16[4,384,512]{2,1,0:T(8,128)(2,1)S(1)} %pad_maximum_fusion), kind=kCustom, calls=%fused_computation.3 | custom fusion | bytes 4718608 | tf_op jit(solution)/shard_map/scatter | solution.py:156
  47.2 2.2 fusion.8
  49.5 0.3 fusion.13
  49.8 0.7 concatenate.7.q_ref
  50.5 245.4 %shard_map.127 = f32[1024,128]{1,0:T(8,128)} custom-call(bf16[1024,128]{1,0:T(8,128)(2,1)} %concatenate.7.q_ref, bf16[1024,128]{1,0:T(8,128)(2,1)} %slice.23.kv_ref), custom_call_target="tpu_custom_call" | custom-call | flops 17179869184 | bytes 9175040 | tf_op jit(solution)/shard_map/pallas_call | solution.py:111
  296.0 1.3 slice_reduce_fusion
  297.3 1.4 divide_convert_fusion
  298.7 0.8 copy.47
  299.5 3.4 %all-to-all-start.1 = ((bf16[8,128,64]{1,2,0:T(8,128)(2,1)}), bf16[8,128,64]{1,2,0:T(8,128)(2,1)S(1)}, u32[]{:S(2)}, u32[]{:S(2)}) async-start(bf16[8,128,64]{1,2,0:T(8,128)(2,1)} %copy.47), calls=%async_computation.1 | async-start | bytes 262144 | tf_op jit(solution)/shard_map/all_to_all | solution.py:195
  302.9 6.0 %all-to-all-done.1 = bf16[8,128,64]{1,2,0:T(8,128)(2,1)S(1)} async-done(((bf16[8,128,64]{1,2,0:T(8,128)(2,1)}), bf16[8,128,64]{1,2,0:T(8,128)(2,1)S(1)}, u32[]{:S(2)}, u32[]{:S(2)}) %all-to-all-start.1) | async-done | bytes 131104 | tf_op jit(solution)/shard_map/all_to_all | solution.py:195
  308.9 0.6 gather_fusion.2
  309.5 0.3 multiply_reduce_fusion
  309.9 0.8 add_convert_fusion
  (52 shorter events, 1.1 us)
Async XLA Ops:
  0.0 47.2 %copy-start = (bf16[512,1024]{1,0:T(8,128)(2,1)S(1)}, bf16[512,1024]{1,0:T(8,128)(2,1)}, u32[]{:S(2)}) copy-start(bf16[512,1024]{1,0:T(8,128)(2,1)} %param.20) | copy-start | bytes 3145732
  0.0 11.2 %copy-start.1 = (bf16[128,512]{1,0:T(8,128)(2,1)S(1)}, bf16[128,512]{1,0:T(8,128)(2,1)}, u32[]{:S(2)}) copy-start(bf16[128,512]{1,0:T(8,128)(2,1)} %param.13) | copy-start | bytes 393220
  0.0 11.1 %copy-start.11 = (f32[8]{0:T(128)S(1)}, f32[8]{0:T(128)}, u32[]{:S(2)}) copy-start(f32[8]{0:T(128)} %param.22) | copy-start | bytes 100
  0.0 11.2 %copy-start.4 = (bf16[512,512]{1,0:T(8,128)(2,1)S(1)}, bf16[512,512]{1,0:T(8,128)(2,1)}, u32[]{:S(2)}) copy-start(bf16[512,512]{1,0:T(8,128)(2,1)} %param.17) | copy-start | bytes 1572868
  0.0 17.7 %collective-permute-start = (bf16[128,512]{1,0:T(8,128)(2,1)}, bf16[128,512]{1,0:T(8,128)(2,1)}, u32[]{:S(2)}, u32[]{:S(2)}) collective-permute-start(bf16[128,512]{1,0:T(8,128)(2,1)} %param.13), channel_id=1, source_target_pairs={{0,4},{4,8},{8,12},{12,16},{16,20},{20,24},{24,28},{28,32},{32,36}... | collective-permute-start | bytes 393224 | tf_op jit(solution)/shard_map/ppermute | solution.py:30
  5.3 13.4 %collective-permute-start.1 = (bf16[128,512]{1,0:T(8,128)(2,1)}, bf16[128,512]{1,0:T(8,128)(2,1)}, u32[]{:S(2)}, u32[]{:S(2)}) collective-permute-start(bf16[128,512]{1,0:T(8,128)(2,1)} %param.13), channel_id=1, source_target_pairs={{4,0},{8,4},{12,8},{16,12},{20,16},{24,20},{28,24},{32,28},{36,32}... | collective-permute-start | bytes 393224 | tf_op jit(solution)/shard_map/ppermute | solution.py:31
  10.9 1.0 copy-start.3
  11.6 0.7 copy-start.10
  12.8 10.4 %copy-start.12 = (s32[1,1,12]{2,1,0:T(1,128)S(1)}, s32[1,1,12]{2,1,0:T(1,128)}, u32[]{:S(2)}) copy-start(s32[1,1,12]{2,1,0:T(1,128)} %param.14) | copy-start | bytes 148
  12.8 11.0 %copy-start.7 = (bf16[16,128,128]{2,1,0:T(8,128)(2,1)S(1)}, bf16[16,128,128]{2,1,0:T(8,128)(2,1)}, u32[]{:S(2)}) copy-start(bf16[16,128,128]{2,1,0:T(8,128)(2,1)} %param.15) | copy-start | bytes 1572868
  14.1 13.0 %all-to-all-start = ((bf16[128,8,192]{0,2,1:T(8,128)(2,1)}), bf16[128,8,192]{0,2,1:T(8,128)(2,1)S(1)}, u32[]{:S(2)}, u32[]{:S(2)}) async-start(bf16[128,8,192]{0,2,1:T(8,128)(2,1)} %bitcast.22), calls=%async_computation | async-start | bytes 786432 | tf_op jit(solution)/shard_map/all_to_all | solution.py:177
  19.6 13.6 %collective-permute-start.2 = (bf16[384,512]{1,0:T(8,128)(2,1)S(1)}, bf16[384,512]{1,0:T(8,128)(2,1)}, u32[]{:S(2)}, u32[]{:S(2)}) collective-permute-start(bf16[384,512]{1,0:T(8,128)(2,1)S(1)} %constant_dynamic-update-slice_fusion), channel_id=1, source_target_pairs={{0,1},{1,2},{2,3},{3,0},{4,5},{5,6},{6,7},{7,4},{8,9},{9,10},{10,1... | collective-permute-start | bytes 1179656 | tf_op jit(solution)/shard_map/ppermute | solution.py:153
  20.1 14.0 %collective-permute-start.3 = (bf16[384,512]{1,0:T(8,128)(2,1)S(1)}, bf16[384,512]{1,0:T(8,128)(2,1)}, u32[]{:S(2)}, u32[]{:S(2)}) collective-permute-start(bf16[384,512]{1,0:T(8,128)(2,1)S(1)} %constant_dynamic-update-slice_fusion), channel_id=1, source_target_pairs={{0,2},{1,3},{2,0},{3,1},{4,6},{5,7},{6,4},{7,5},{8,10},{9,11},{10,... | collective-permute-start | bytes 1179656 | tf_op jit(solution)/shard_map/ppermute | solution.py:153
  21.8 18.1 %collective-permute-start.4 = (bf16[384,512]{1,0:T(8,128)(2,1)S(1)}, bf16[384,512]{1,0:T(8,128)(2,1)}, u32[]{:S(2)}, u32[]{:S(2)}) collective-permute-start(bf16[384,512]{1,0:T(8,128)(2,1)S(1)} %constant_dynamic-update-slice_fusion), channel_id=1, source_target_pairs={{0,3},{1,0},{2,1},{3,2},{4,7},{5,4},{6,5},{7,6},{8,11},{9,8},{10,9... | collective-permute-start | bytes 1179656 | tf_op jit(solution)/shard_map/ppermute | solution.py:153
  42.6 4.6 %copy-start.6 = (bf16[128,12,128]{0,2,1:T(8,128)(2,1)S(1)}, bf16[128,12,128]{0,2,1:T(8,128)(2,1)}, u32[]{:S(2)}) copy-start(bf16[128,12,128]{0,2,1:T(8,128)(2,1)} %copy.35) | copy-start | bytes 1179652
  47.2 2.2 copy-start.2
  296.0 6.9 %copy-start.9 = (s32[8]{0:T(128)S(1)}, s32[8]{0:T(128)}, u32[]{:S(2)}) copy-start(s32[8]{0:T(128)} %constant.87) | copy-start | bytes 100
  296.0 13.5 %copy-start.5 = (bf16[512,512]{1,0:T(8,128)(2,1)S(1)}, bf16[512,512]{1,0:T(8,128)(2,1)}, u32[]{:S(2)}) copy-start(bf16[512,512]{1,0:T(8,128)(2,1)} %param.19) | copy-start | bytes 1572868
  297.3 12.6 %copy-start.8 = (f32[512]{0:T(512)S(1)}, f32[512]{0:T(512)}, u32[]{:S(2)}) copy-start(f32[512]{0:T(512)} %param.23) | copy-start | bytes 6148
  299.5 9.4 %all-to-all-start.1 = ((bf16[8,128,64]{1,2,0:T(8,128)(2,1)}), bf16[8,128,64]{1,2,0:T(8,128)(2,1)S(1)}, u32[]{:S(2)}, u32[]{:S(2)}) async-start(bf16[8,128,64]{1,2,0:T(8,128)(2,1)} %copy.47), calls=%async_computation.1 | async-start | bytes 262144 | tf_op jit(solution)/shard_map/all_to_all | solution.py:195

commit v7 on v5

--- a/solution.py
+++ b/solution.py
@@ -16,15 +16,16 @@
 
 norm_eps = 1e-06
 
-ROW = "x"
+ROW = "xhi"
+NEIGHBOUR = "xlo"
 COLUMN = "z"
 PAIR = "yhi"
-DOM = (ROW, COLUMN, PAIR)
+DOM = (ROW, NEIGHBOUR, COLUMN, PAIR)
 GROUP = (PAIR, "head")
 
 
 def extended(shard, width):
-    devices = lax.axis_size(ROW) * lax.axis_size(COLUMN) * lax.axis_size(PAIR)
+    devices = lax.axis_size(ROW) * lax.axis_size(NEIGHBOUR) * lax.axis_size(COLUMN) * lax.axis_size(PAIR)
     length = shard.shape[0]
     up = [(i, (i + 1) % devices) for i in range(devices - 1)]
     down = [(j, i) for i, j in up]
@@ -154,9 +155,14 @@
     local_term = jnp.dot(hidden, passing_outer_coefficients, preferred_element_type=jnp.float32)
 
     local_term, head_queries = lax.optimization_barrier((local_term, head_queries))
+    swap = [(0, 1), (1, 0)]
+    pair_queries = jnp.concatenate(
+        [head_queries, lax.ppermute(head_queries, NEIGHBOUR, swap)], axis=0
+    )
     kv_in = lax.all_gather(key_values, (ROW, COLUMN), axis=0, tiled=True)
-    padded_queries = jnp.concatenate([head_queries, jnp.zeros_like(head_queries)], axis=1)
+    padded_queries = jnp.concatenate([pair_queries, jnp.zeros_like(pair_queries)], axis=1)
     totals = attend(padded_queries, kv_in)
+    totals = totals[:query_rows] + lax.ppermute(totals[query_rows:], NEIGHBOUR, swap)
     merged = (totals[:, SUBSPACE_WIDTH:] / totals[:, :1]).astype(jnp.bfloat16)
     back = lax.all_to_all(merged, GROUP, split_axis=0, concat_axis=1, tiled=True)
     node_heads = back.reshape(block_len, members, SUBSPACE_WIDTH)[:, jnp.array(member_of)]
@@ -172,9 +178,11 @@
 
 def solution(mesh):
     n_dom, n_head = mesh.shape["dom"], mesh.shape["head"]
-    fine = Mesh(mesh.devices.reshape(n_dom // 16, 8, 2, n_head), (ROW, COLUMN, PAIR, "head"))
+    fine = Mesh(
+        mesh.devices.reshape(n_dom // 32, 2, 8, 2, n_head), (ROW, NEIGHBOUR, COLUMN, PAIR, "head")
+    )
     in_specs = (
-        P((ROW, COLUMN, PAIR, "head"), None),
+        P((ROW, NEIGHBOUR, COLUMN, PAIR, "head"), None),
         P(DOM, "head", None),
         P(),
         P(),
@@ -186,5 +194,5 @@
         P(),
         P(),
     )
-    out_specs = P((ROW, COLUMN, PAIR, "head"), None)
+    out_specs = P((ROW, NEIGHBOUR, COLUMN, PAIR, "head"), None)
     return jax.shard_map(shards, mesh=fine, in_specs=in_specs, out_specs=out_specs, check_vma=False)

time: 189 us -> 203 us (1.074)
  waiting for transfers between devices: 77.9 us -> 86 us
  starting transfers between devices: 17 us -> 21.2 us
    ppermute x0 -> x2, waiting for transfers between devices: none -> 15.9 us  [the longest x1 8.67 us: shards(): lax.ppermute(totals[query_rows:], NEIGHBOUR, swap)]
    all_gather x1, waiting for transfers between devices: 54.4 us -> 46.6 us  [shards(): kv_in = lax.all_gather(key_values, (ROW, COLUMN), axis=0, tiled=True)]
    ppermute x0 -> x2, starting transfers between devices: none -> 3.45 us  [the longest x1 2.17 us: shards(): lax.ppermute(totals[query_rows:], NEIGHBOUR, swap)]
  transfers between devices with their start and end apart: 7 -> 9, of which waited for: 7 -> 9; matrix products, arithmetic and copies ran while one was open for 7% -> 7% of each run, Pallas kernels for 0% -> 0%
where the time goes in v7:
time: 203 us; the launch traced here: 199 us
  waiting for transfers between devices  86 us (42%)
  Pallas kernels  40.2 us (20%)
  starting transfers between devices  21.2 us (10%)
  local copies, waits for them, and re-layouts  14.2 us (7%)
  between operations  13.8 us (7%)
  blocking collectives  13.3 us (7%)
  other arithmetic  5.77 us (3%)
  matrix products  4.72 us (2%)
    all_gather x1, waiting for transfers between devices, shards(): kv_in = lax.all_gather(key_values, (ROW, COLUMN), axis=0, tiled=True)  46.6 us
    pallas_call x1, Pallas kernels, attend(): pl.pallas_call(attention_kernel, grid=(keys // block,), in_specs=[pl.Bloc...  40.2 us
    ppermute x3, waiting for transfers between devices, shards(): gathered.append(lax.ppermute(halo_rows, 'head', pairs))  13.5 us
    all_to_all x1, blocking collectives, shards(): lax.all_to_all(packed, GROUP, split_axis=1, concat_axis=0, tiled=True)  13.3 us
    ppermute x1, waiting for transfers between devices, shards(): lax.ppermute(totals[query_rows:], NEIGHBOUR, swap)  8.67 us
    ppermute x1, starting transfers between devices, extended(): after = lax.ppermute(first, DOM, down)  7.63 us
    ppermute x1, waiting for transfers between devices, shards(): lax.ppermute(head_queries, NEIGHBOUR, swap)  7.19 us
    all_to_all x1, waiting for transfers between devices, shards(): lax.all_to_all(merged, GROUP, split_axis=0, concat_axis=1, tiled=True)  6.12 us
  transfers between devices with their start and end apart: 9, of which 9 were waited for; matrix products, arithmetic and copies ran while one was open for 7% of the time, Pallas kernels for 0%

profile of v7, /device:TPU:4, one launch (start us, length us, event | category | flops | bytes accessed | tf_op | source)
XLA Modules:
  0.0 199.2 jit_solution(15711987648047169229)
XLA Ops:
  6.5 0.8 maximum_reduce_fusion
  7.6 1.4 fusion.16
  9.0 0.1 copy.36
  9.2 0.1 copy.37
  9.7 0.2 fusion.15
  9.9 0.1 copy.39
  10.2 0.1 copy.40
  10.5 0.3 copy-done.3
  10.7 0.2 convolution_convert_fusion
  11.0 0.1 copy.42
  11.2 0.6 gather_fusion.1
  11.8 13.3 %all_to_all.35 = bf16[128,8,192]{0,2,1:T(8,128)(2,1)S(1)} all-to-all(bf16[128,8,192]{0,2,1:T(8,128)(2,1)S(1)} %bitcast.52), channel_id=1, replica_groups=mesh['xhi'=2,'xlo'=2,'z'=8,'yhi'=2,'head'=4] {'yhi','head'}, dimensions={1} | all-to-all | bytes 786432 | tf_op jit(solution)/shard_map/all_to_all | solution.py:143
  25.2 0.2 copy.46
  25.4 0.8 slice.31
  26.3 2.7 %collective-permute-start = (bf16[128,512]{1,0:T(8,128)(2,1)S(1)}, bf16[128,512]{1,0:T(8,128)(2,1)S(1)}, u32[]{:S(2)}, u32[]{:S(2)}) collective-permute-start(bf16[128,512]{1,0:T(8,128)(2,1)S(1)} %copy-done.1), channel_id=1, source_target_pairs={{0,4},{4,8},{8,12},{12,16},{16,20},{20,24},{24,28},{28,32},{32,36}... | collective-permute-start | bytes 393224 | tf_op jit(solution)/shard_map/ppermute | solution.py:34
  29.0 7.6 %collective-permute-start.1 = (bf16[128,512]{1,0:T(8,128)(2,1)S(1)}, bf16[128,512]{1,0:T(8,128)(2,1)S(1)}, u32[]{:S(2)}, u32[]{:S(2)}) collective-permute-start(bf16[128,512]{1,0:T(8,128)(2,1)S(1)} %copy-done.1), channel_id=1, source_target_pairs={{4,0},{8,4},{12,8},{16,12},{20,16},{24,20},{28,24},{32,28},{36,32}... | collective-permute-start | bytes 393224 | tf_op jit(solution)/shard_map/ppermute | solution.py:35
  36.6 1.2 collective-permute-done
  37.8 2.7 %collective-permute-done.1 = bf16[128,512]{1,0:T(8,128)(2,1)S(1)} collective-permute-done((bf16[128,512]{1,0:T(8,128)(2,1)S(1)}, bf16[128,512]{1,0:T(8,128)(2,1)S(1)}, u32[]{:S(2)}, u32[]{:S(2)}) %collective-permute-start.1) | collective-permute-done | bytes 131104 | tf_op jit(solution)/shard_map/ppermute | solution.py:35
  40.6 0.9 collective-permute-start.3
  41.6 1.4 collective-permute-start.4
  43.5 0.6 gather_fusion
  44.2 0.1 select_bitcast_fusion
  44.3 0.9 copy.35
  45.3 6.2 %collective-permute-done.2 = bf16[384,512]{1,0:T(8,128)(2,1)} collective-permute-done((bf16[384,512]{1,0:T(8,128)(2,1)S(1)}, bf16[384,512]{1,0:T(8,128)(2,1)}, u32[]{:S(2)}, u32[]{:S(2)}) %collective-permute-start.2) | collective-permute-done | bytes 393248 | tf_op jit(solution)/shard_map/ppermute | solution.py:119
  51.5 1.3 collective-permute-done.3
  52.8 6.1 %collective-permute-done.4 = bf16[384,512]{1,0:T(8,128)(2,1)} collective-permute-done((bf16[384,512]{1,0:T(8,128)(2,1)S(1)}, bf16[384,512]{1,0:T(8,128)(2,1)}, u32[]{:S(2)}, u32[]{:S(2)}) %collective-permute-start.4) | collective-permute-done | bytes 393248 | tf_op jit(solution)/shard_map/ppermute | solution.py:119
  58.8 1.4 pad_maximum_fusion
  60.3 1.3 broadcast_in_dim.42
  61.5 4.7 %scatter_fusion = bf16[4,384,512]{2,1,0:T(8,128)(2,1)} fusion(bf16[4,384,512]{2,1,0:T(8,128)(2,1)} %broadcast_in_dim.42, s32[4]{0:T(128)S(1)} %fusion.14, bf16[4,384,512]{2,1,0:T(8,128)(2,1)S(1)} %pad_maximum_fusion), kind=kCustom, calls=%fused_computation.3 | custom fusion | bytes 4718608 | tf_op jit(solution)/shard_map/scatter | solution.py:122
  66.3 2.2 %fusion.10 = bf16[128,1024]{1,0:T(8,128)(2,1)S(1)} fusion(bf16[512,1024]{1,0:T(8,128)(2,1)S(1)} %copy-done, bf16[128,1536]{0,1:T(8,128)(2,1)S(1)} %bitcast.65, bf16[1536,512]{1,0:T(8,128)(2,1)} %bitcast.51), kind=kOutput, calls=%fused_computation.19 | convolution fusion | flops 336789504 | bytes 3276800 | tf_op jit(solution)/shard_map/dot_general | solution.py:153
  68.5 0.3 fusion.17
  68.8 1.3 collective-permute-start.5
  70.1 7.2 %collective-permute-done.5 = bf16[1024,64]{1,0:T(8,128)(2,1)S(1)} collective-permute-done((bf16[1024,64]{1,0:T(8,128)(2,1)S(1)}, bf16[1024,64]{1,0:T(8,128)(2,1)S(1)}, u32[]{:S(2)}, u32[]{:S(2)}) %collective-permute-start.5) | collective-permute-done | bytes 131104 | tf_op jit(solution)/shard_map/ppermute | solution.py:160
  77.3 1.0 fusion.11.q_ref
  78.3 46.6 %all-gather.2.cloned.1.call-done.kv_ref = bf16[16384,128]{1,0:T(8,128)(2,1)} async-done(((bf16[1024,128]{1,0:T(8,128)(2,1)}), bf16[16384,128]{1,0:T(8,128)(2,1)}) %all-gather.2.cloned.1.call-update) | async-done | bytes 4194320 | tf_op jit(solution)/shard_map/all_gather | solution.py:162
  124.9 40.2 %shard_map.127 = f32[2048,128]{1,0:T(8,128)} custom-call(bf16[2048,128]{1,0:T(8,128)(2,1)} %fusion.11.q_ref, bf16[16384,128]{1,0:T(8,128)(2,1)} %all-gather.2.cloned.1.call-done.kv_ref), custom_call_target="tpu_custom_call" | custom-call | flops 17179869184 | bytes 5767168 | tf_op jit(solution)/shard_map/pallas_call | solution.py:80
  165.1 1.1 slice.33
  166.2 2.2 %collective-permute-start.6 = (f32[1024,128]{1,0:T(8,128)S(1)}, f32[1024,128]{1,0:T(8,128)S(1)}, u32[]{:S(2)}, u32[]{:S(2)}) collective-permute-start(f32[1024,128]{1,0:T(8,128)S(1)} %slice.33), channel_id=1, source_target_pairs={{0,64},{64,0},{1,65},{65,1},{2,66},{66,2},{3,67},{67,3},{4,68},{68... | collective-permute-start | bytes 1572872 | tf_op jit(solution)/shard_map/ppermute | solution.py:165
  168.3 8.7 %collective-permute-done.6 = f32[1024,128]{1,0:T(8,128)S(1)} collective-permute-done((f32[1024,128]{1,0:T(8,128)S(1)}, f32[1024,128]{1,0:T(8,128)S(1)}, u32[]{:S(2)}, u32[]{:S(2)}) %collective-permute-start.6) | collective-permute-done | bytes 524320 | tf_op jit(solution)/shard_map/ppermute | solution.py:165
  177.0 1.1 slice_add_fusion
  178.1 0.2 slice_reduce_fusion
  178.4 0.3 fusion.12
  178.7 0.8 copy.47
  179.5 5.0 %all-to-all-start.1 = ((bf16[8,128,64]{1,2,0:T(8,128)(2,1)}), bf16[8,128,64]{1,2,0:T(8,128)(2,1)S(1)}, u32[]{:S(2)}, u32[]{:S(2)}) async-start(bf16[8,128,64]{1,2,0:T(8,128)(2,1)} %copy.47), calls=%async_computation.1 | async-start | bytes 262144 | tf_op jit(solution)/shard_map/all_to_all | solution.py:167
  184.5 6.1 %all-to-all-done.1 = bf16[8,128,64]{1,2,0:T(8,128)(2,1)S(1)} async-done(((bf16[8,128,64]{1,2,0:T(8,128)(2,1)}), bf16[8,128,64]{1,2,0:T(8,128)(2,1)S(1)}, u32[]{:S(2)}, u32[]{:S(2)}) %all-to-all-start.1) | async-done | bytes 131104 | tf_op jit(solution)/shard_map/all_to_all | solution.py:167
  190.6 0.6 gather_fusion.2
  191.2 0.3 multiply_reduce_fusion
  191.6 0.8 add_convert_fusion
  (60 shorter events, 1.7 us)
Async XLA Ops:
  6.5 59.7 %copy-start = (bf16[512,1024]{1,0:T(8,128)(2,1)S(1)}, bf16[512,1024]{1,0:T(8,128)(2,1)}, u32[]{:S(2)}) copy-start(bf16[512,1024]{1,0:T(8,128)(2,1)} %param.20) | copy-start | bytes 3145732
  6.5 2.8 %copy-start.11 = (f32[8]{0:T(128)S(1)}, f32[8]{0:T(128)}, u32[]{:S(2)}) copy-start(f32[8]{0:T(128)} %param.22) | copy-start | bytes 100
  6.5 118.4 %all-gather.2.cloned.1.call-start = ((), (), s32[]{:S(2)}) async-start(), calls=%async_computation.2 | async-start | bytes 4456448 | tf_op jit(solution)/shard_map/all_gather | solution.py:162
  7.6 2.1 %copy-start.1 = (bf16[128,512]{1,0:T(8,128)(2,1)S(1)}, bf16[128,512]{1,0:T(8,128)(2,1)}, u32[]{:S(2)}) copy-start(bf16[128,512]{1,0:T(8,128)(2,1)} %param.13) | copy-start | bytes 393220
  7.6 2.1 %copy-start.4 = (bf16[512,512]{1,0:T(8,128)(2,1)S(1)}, bf16[512,512]{1,0:T(8,128)(2,1)}, u32[]{:S(2)}) copy-start(bf16[512,512]{1,0:T(8,128)(2,1)} %param.17) | copy-start | bytes 1572868
  9.7 1.0 copy-start.3
  10.1 1.0 copy-start.10
  11.8 31.1 %copy-start.12 = (s32[1,1,12]{2,1,0:T(1,128)S(1)}, s32[1,1,12]{2,1,0:T(1,128)}, u32[]{:S(2)}) copy-start(s32[1,1,12]{2,1,0:T(1,128)} %param.14) | copy-start | bytes 148
  11.8 31.7 %copy-start.7 = (bf16[16,128,128]{2,1,0:T(8,128)(2,1)S(1)}, bf16[16,128,128]{2,1,0:T(8,128)(2,1)}, u32[]{:S(2)}) copy-start(bf16[16,128,128]{2,1,0:T(8,128)(2,1)} %param.15) | copy-start | bytes 1572868
  26.3 11.6 %collective-permute-start = (bf16[128,512]{1,0:T(8,128)(2,1)S(1)}, bf16[128,512]{1,0:T(8,128)(2,1)S(1)}, u32[]{:S(2)}, u32[]{:S(2)}) collective-permute-start(bf16[128,512]{1,0:T(8,128)(2,1)S(1)} %copy-done.1), channel_id=1, source_target_pairs={{0,4},{4,8},{8,12},{12,16},{16,20},{20,24},{24,28},{28,32},{32,36}... | collective-permute-start | bytes 393224 | tf_op jit(solution)/shard_map/ppermute | solution.py:34
  29.0 11.5 %collective-permute-start.1 = (bf16[128,512]{1,0:T(8,128)(2,1)S(1)}, bf16[128,512]{1,0:T(8,128)(2,1)S(1)}, u32[]{:S(2)}, u32[]{:S(2)}) collective-permute-start(bf16[128,512]{1,0:T(8,128)(2,1)S(1)} %copy-done.1), channel_id=1, source_target_pairs={{4,0},{8,4},{12,8},{16,12},{20,16},{24,20},{28,24},{32,28},{36,32}... | collective-permute-start | bytes 393224 | tf_op jit(solution)/shard_map/ppermute | solution.py:35
  40.5 11.0 %collective-permute-start.2 = (bf16[384,512]{1,0:T(8,128)(2,1)S(1)}, bf16[384,512]{1,0:T(8,128)(2,1)}, u32[]{:S(2)}, u32[]{:S(2)}) collective-permute-start(bf16[384,512]{1,0:T(8,128)(2,1)S(1)} %constant_dynamic-update-slice_fusion), channel_id=1, source_target_pairs={{0,1},{1,2},{2,3},{3,0},{4,5},{5,6},{6,7},{7,4},{8,9},{9,10},{10,1... | collective-permute-start | bytes 1179656 | tf_op jit(solution)/shard_map/ppermute | solution.py:119
  40.6 12.1 %collective-permute-start.3 = (bf16[384,512]{1,0:T(8,128)(2,1)S(1)}, bf16[384,512]{1,0:T(8,128)(2,1)}, u32[]{:S(2)}, u32[]{:S(2)}) collective-permute-start(bf16[384,512]{1,0:T(8,128)(2,1)S(1)} %constant_dynamic-update-slice_fusion), channel_id=1, source_target_pairs={{0,2},{1,3},{2,0},{3,1},{4,6},{5,7},{6,4},{7,5},{8,10},{9,11},{10,... | collective-permute-start | bytes 1179656 | tf_op jit(solution)/shard_map/ppermute | solution.py:119
  41.6 17.3 %collective-permute-start.4 = (bf16[384,512]{1,0:T(8,128)(2,1)S(1)}, bf16[384,512]{1,0:T(8,128)(2,1)}, u32[]{:S(2)}, u32[]{:S(2)}) collective-permute-start(bf16[384,512]{1,0:T(8,128)(2,1)S(1)} %constant_dynamic-update-slice_fusion), channel_id=1, source_target_pairs={{0,3},{1,0},{2,1},{3,2},{4,7},{5,4},{6,5},{7,6},{8,11},{9,8},{10,9... | collective-permute-start | bytes 1179656 | tf_op jit(solution)/shard_map/ppermute | solution.py:119
  61.5 4.7 %copy-start.6 = (bf16[128,12,128]{0,2,1:T(8,128)(2,1)S(1)}, bf16[128,12,128]{0,2,1:T(8,128)(2,1)}, u32[]{:S(2)}) copy-start(bf16[128,12,128]{0,2,1:T(8,128)(2,1)} %copy.35) | copy-start | bytes 1179652
  66.3 2.2 %copy-start.2 = (bf16[1024,512]{1,0:T(8,128)(2,1)S(1)}, bf16[1024,512]{1,0:T(8,128)(2,1)}, u32[]{:S(2)}) copy-start(bf16[1024,512]{1,0:T(8,128)(2,1)} %param.21) | copy-start | bytes 3145732
  68.8 8.5 %collective-permute-start.5 = (bf16[1024,64]{1,0:T(8,128)(2,1)S(1)}, bf16[1024,64]{1,0:T(8,128)(2,1)S(1)}, u32[]{:S(2)}, u32[]{:S(2)}) collective-permute-start(bf16[1024,64]{1,0:T(8,128)(2,1)S(1)} %slice.30), channel_id=1, source_target_pairs={{0,64},{64,0},{1,65},{65,1},{2,66},{66,2},{3,67},{67,3},{4,68},{68... | collective-permute-start | bytes 393224 | tf_op jit(solution)/shard_map/ppermute | solution.py:160
  166.2 18.3 %copy-start.9 = (s32[8]{0:T(128)S(1)}, s32[8]{0:T(128)}, u32[]{:S(2)}) copy-start(s32[8]{0:T(128)} %constant.87) | copy-start | bytes 100
  166.2 10.8 %collective-permute-start.6 = (f32[1024,128]{1,0:T(8,128)S(1)}, f32[1024,128]{1,0:T(8,128)S(1)}, u32[]{:S(2)}, u32[]{:S(2)}) collective-permute-start(f32[1024,128]{1,0:T(8,128)S(1)} %slice.33), channel_id=1, source_target_pairs={{0,64},{64,0},{1,65},{65,1},{2,66},{66,2},{3,67},{67,3},{4,68},{68... | collective-permute-start | bytes 1572872 | tf_op jit(solution)/shard_map/ppermute | solution.py:165
  178.1 13.1 %copy-start.5 = (bf16[512,512]{1,0:T(8,128)(2,1)S(1)}, bf16[512,512]{1,0:T(8,128)(2,1)}, u32[]{:S(2)}) copy-start(bf16[512,512]{1,0:T(8,128)(2,1)} %param.19) | copy-start | bytes 1572868
  178.3 13.2 %copy-start.8 = (f32[512]{0:T(512)S(1)}, f32[512]{0:T(512)}, u32[]{:S(2)}) copy-start(f32[512]{0:T(512)} %param.23) | copy-start | bytes 6148
  179.5 11.1 %all-to-all-start.1 = ((bf16[8,128,64]{1,2,0:T(8,128)(2,1)}), bf16[8,128,64]{1,2,0:T(8,128)(2,1)S(1)}, u32[]{:S(2)}, u32[]{:S(2)}) async-start(bf16[8,128,64]{1,2,0:T(8,128)(2,1)} %copy.47), calls=%async_computation.1 | async-start | bytes 262144 | tf_op jit(solution)/shard_map/all_to_all | solution.py:167
Sparse Core Ops, SparseCore 0:
  26.4 98.4 all-gather.1

commit v8 on v5

--- a/solution.py
+++ b/solution.py
@@ -121,10 +121,6 @@
     nearby = jnp.zeros_like(stacked).at[order].set(stacked).reshape(-1, halo_rows.shape[1])
     slot_order = slot_ids.reshape(3, group_size).T.reshape(-1)
     asking_vector_multiplier = softness_per_subspace / math.sqrt(SUBSPACE_WIDTH)
-    queries = head_norm(
-        jnp.dot(vertex_embeddings, asking_projector, preferred_element_type=jnp.float32),
-        asking_vector_multiplier,
-    )
     keys_all = head_norm(
         jnp.dot(vertex_embeddings, lookup_projector, preferred_element_type=jnp.float32), None
     )
@@ -134,15 +130,23 @@
 
     head_of = [(j % group_size) * pair_size + j // group_size for j in range(members)]
     member_of = [head_of.index(h) for h in range(NUM_SUBSPACES)]
-    packed = jnp.stack(
-        [t.reshape(block_len, NUM_SUBSPACES, SUBSPACE_WIDTH) for t in (queries, keys_all, values_all)],
-        axis=2,
-    )[:, jnp.array(head_of)]
-    packed = packed.reshape(block_len, -1)
-    mine = lax.all_to_all(packed, GROUP, split_axis=1, concat_axis=0, tiled=True)
-    query_rows = mine.shape[0]
-    head_queries = mine[:, :SUBSPACE_WIDTH]
-    key_values = mine[:, SUBSPACE_WIDTH:]
+
+    def to_members(parts):
+        packed = jnp.stack(
+            [t.reshape(block_len, NUM_SUBSPACES, SUBSPACE_WIDTH) for t in parts], axis=2
+        )[:, jnp.array(head_of)]
+        return lax.all_to_all(
+            packed.reshape(block_len, -1), GROUP, split_axis=1, concat_axis=0, tiled=True
+        )
+
+    key_values = to_members((keys_all, values_all))
+    kv_in = lax.all_gather(key_values, (ROW, COLUMN), axis=0, tiled=True)
+    queries = head_norm(
+        jnp.dot(vertex_embeddings, asking_projector, preferred_element_type=jnp.float32),
+        asking_vector_multiplier,
+    )
+    head_queries = to_members((queries,))
+    query_rows = head_queries.shape[0]
 
     selected = jnp.take(coupling_strength_panels, jnp.maximum(slot_order, 0), axis=0)
     selected = jnp.where((slot_order >= 0)[:, None, None], selected, jnp.zeros_like(selected))
@@ -154,7 +158,6 @@
     local_term = jnp.dot(hidden, passing_outer_coefficients, preferred_element_type=jnp.float32)
 
     local_term, head_queries = lax.optimization_barrier((local_term, head_queries))
-    kv_in = lax.all_gather(key_values, (ROW, COLUMN), axis=0, tiled=True)
     padded_queries = jnp.concatenate([head_queries, jnp.zeros_like(head_queries)], axis=1)
     totals = attend(padded_queries, kv_in)
     merged = (totals[:, SUBSPACE_WIDTH:] / totals[:, :1]).astype(jnp.bfloat16)

time: 189 us -> 187 us (0.989)
  waiting for transfers between devices: 77.9 us -> 69.4 us
  starting transfers between devices: 17 us -> 21.5 us
  local copies, waits for them, and re-layouts: 15.1 us -> 17.8 us
    all_gather x1, waiting for transfers between devices: 54.4 us -> 51 us  [shards(): kv_in = lax.all_gather(key_values, (ROW, COLUMN), axis=0, tiled=True)]
    all_to_all x0 -> x1, starting transfers between devices: none -> 3.37 us  [to_members(): lax.all_to_all(packed.reshape(block_len, -1), GROUP, split_axis=1, concat...]
    ppermute x1, waiting for transfers between devices: 2.68 us -> 0.01 us  [extended(): after = lax.ppermute(first, DOM, down)]
  transfers between devices with their start and end apart: 7 -> 8, of which waited for: 7 -> 5; matrix products, arithmetic and copies ran while one was open for 7% -> 9% of each run, Pallas kernels for 0% -> 0%
where the time goes in v8:
time: 187 us; the launch traced here: 184 us
  waiting for transfers between devices  69.4 us (37%)
  Pallas kernels  40 us (21%)
  starting transfers between devices  21.5 us (11%)
  local copies, waits for them, and re-layouts  17.8 us (10%)
  between operations  13.8 us (7%)
  blocking collectives  11.8 us (6%)
  matrix products  4.72 us (3%)
  other arithmetic  4.69 us (3%)
    all_gather x1, waiting for transfers between devices, shards(): kv_in = lax.all_gather(key_values, (ROW, COLUMN), axis=0, tiled=True)  51 us
    pallas_call x1, Pallas kernels, attend(): pl.pallas_call(attention_kernel, grid=(keys // block,), in_specs=[pl.Bloc...  40 us
    ppermute x3, waiting for transfers between devices, shards(): gathered.append(lax.ppermute(halo_rows, 'head', pairs))  12.3 us
    all_to_all x1, blocking collectives, to_members(): lax.all_to_all(packed.reshape(block_len, -1), GROUP, split_axis=1, concat...  11.8 us
    ppermute x1, starting transfers between devices, extended(): after = lax.ppermute(first, DOM, down)  8.08 us
    all_to_all x1, waiting for transfers between devices, shards(): lax.all_to_all(merged, GROUP, split_axis=0, concat_axis=1, tiled=True)  6.12 us
    scatter x1, local copies, waits for them, and re-layouts, shards(): jnp.zeros_like(stacked).at[order].set(stacked)  4.75 us
    all_to_all x1, starting transfers between devices, shards(): lax.all_to_all(merged, GROUP, split_axis=0, concat_axis=1, tiled=True)  4.29 us
  transfers between devices with their start and end apart: 8, of which 5 were waited for; matrix products, arithmetic and copies ran while one was open for 9% of the time, Pallas kernels for 0%

profile of v8, /device:TPU:4, one launch (start us, length us, event | category | flops | bytes accessed | tf_op | source)
XLA Modules:
  0.0 183.7 jit_solution(2088662099383351241)
XLA Ops:
  6.5 0.8 maximum_reduce_fusion
  7.4 0.1 copy.35
  7.6 1.4 fusion.13
  9.0 0.1 copy.41
  9.2 0.1 copy.42
  9.4 0.1 copy.43
  9.5 0.2 convolution_convert_fusion
  9.8 0.1 copy.44
  10.0 0.6 gather_fusion.2
  10.6 11.8 %all_to_all.54 = bf16[128,8,128]{0,2,1:T(8,128)(2,1)S(1)} all-to-all(bf16[128,8,128]{0,2,1:T(8,128)(2,1)S(1)} %bitcast.53), channel_id=1, replica_groups=mesh['x'=4,'z'=8,'yhi'=2,'head'=4] {'yhi','head'}, dimensions={1} | all-to-all | bytes 524288 | tf_op jit(solution)/shard_map/all_to_all | solution.py:138
  22.4 0.9 copy.47
  23.3 2.3 %collective-permute-start = (bf16[128,512]{1,0:T(8,128)(2,1)S(1)}, bf16[128,512]{1,0:T(8,128)(2,1)S(1)}, u32[]{:S(2)}, u32[]{:S(2)}) collective-permute-start(bf16[128,512]{1,0:T(8,128)(2,1)S(1)} %copy-done.1), channel_id=1, source_target_pairs={{0,4},{4,8},{8,12},{12,16},{16,20},{20,24},{24,28},{28,32},{32,36}... | collective-permute-start | bytes 393224 | tf_op jit(solution)/shard_map/ppermute | solution.py:33
  25.6 8.1 %collective-permute-start.1 = (bf16[128,512]{1,0:T(8,128)(2,1)S(1)}, bf16[128,512]{1,0:T(8,128)(2,1)S(1)}, u32[]{:S(2)}, u32[]{:S(2)}) collective-permute-start(bf16[128,512]{1,0:T(8,128)(2,1)S(1)} %copy-done.1), channel_id=1, source_target_pairs={{4,0},{8,4},{12,8},{16,12},{20,16},{24,20},{28,24},{32,28},{36,32}... | collective-permute-start | bytes 393224 | tf_op jit(solution)/shard_map/ppermute | solution.py:34
  33.7 0.2 fusion.12
  33.9 0.1 copy.37
  34.1 0.1 copy.38
  34.5 0.1 copy.39
  34.6 1.2 gather_fusion.1
  35.8 3.4 %all-to-all-start = ((bf16[128,8,64]{0,2,1:T(8,128)(2,1)}), bf16[128,8,64]{0,2,1:T(8,128)(2,1)S(1)}, u32[]{:S(2)}, u32[]{:S(2)}) async-start(bf16[128,8,64]{0,2,1:T(8,128)(2,1)} %bitcast.14), calls=%async_computation | async-start | bytes 262144 | tf_op jit(solution)/shard_map/all_to_all | solution.py:138
  39.3 0.5 collective-permute-start.2
  39.7 1.7 collective-permute-start.3
  41.4 1.3 collective-permute-start.4
  42.8 0.1 copy.33
  43.1 0.1 copy.34
  43.3 1.7 gather_fusion
  45.0 0.1 select_bitcast_fusion
  45.1 0.9 copy.36
  46.1 0.2 copy.40
  46.3 5.4 %collective-permute-done.2 = bf16[384,512]{1,0:T(8,128)(2,1)S(1)} collective-permute-done((bf16[384,512]{1,0:T(8,128)(2,1)S(1)}, bf16[384,512]{1,0:T(8,128)(2,1)S(1)}, u32[]{:S(2)}, u32[]{:S(2)}) %collective-permute-start.2) | collective-permute-done | bytes 393248 | tf_op jit(solution)/shard_map/ppermute | solution.py:118
  51.7 1.1 collective-permute-done.3
  52.7 5.9 %collective-permute-done.4 = bf16[384,512]{1,0:T(8,128)(2,1)S(1)} collective-permute-done((bf16[384,512]{1,0:T(8,128)(2,1)S(1)}, bf16[384,512]{1,0:T(8,128)(2,1)S(1)}, u32[]{:S(2)}, u32[]{:S(2)}) %collective-permute-start.4) | collective-permute-done | bytes 393248 | tf_op jit(solution)/shard_map/ppermute | solution.py:118
  58.6 0.8 copy-done.7
  59.4 1.4 pad_maximum_fusion
  60.9 1.3 broadcast_in_dim.45
  62.2 4.7 %scatter_fusion = bf16[4,384,512]{2,1,0:T(8,128)(2,1)} fusion(bf16[4,384,512]{2,1,0:T(8,128)(2,1)} %broadcast_in_dim.45, s32[4]{0:T(128)S(1)} %fusion.11, bf16[4,384,512]{2,1,0:T(8,128)(2,1)S(1)} %pad_maximum_fusion), kind=kCustom, calls=%fused_computation.4 | custom fusion | bytes 4718608 | tf_op jit(solution)/shard_map/scatter | solution.py:121
  66.9 2.2 %fusion.8 = bf16[128,1024]{1,0:T(8,128)(2,1)S(1)} fusion(bf16[512,1024]{1,0:T(8,128)(2,1)S(1)} %copy-done, bf16[128,1536]{0,1:T(8,128)(2,1)S(1)} %bitcast.69, bf16[1536,512]{1,0:T(8,128)(2,1)} %bitcast.52), kind=kOutput, calls=%fused_computation.17 | convolution fusion | flops 336789504 | bytes 3276800 | tf_op jit(solution)/shard_map/dot_general | solution.py:156
  69.2 0.3 fusion.14
  69.5 0.8 concatenate.7.q_ref
  70.3 51.0 %all-gather.2.cloned.1.call-done.kv_ref = bf16[32768,128]{1,0:T(8,128)(2,1)} async-done(((bf16[1024,128]{1,0:T(8,128)(2,1)}), bf16[32768,128]{1,0:T(8,128)(2,1)}) %all-gather.2.cloned.1.call-update) | async-done | bytes 8388624 | tf_op jit(solution)/shard_map/all_gather | solution.py:143
  121.3 40.0 %shard_map.136 = f32[1024,128]{1,0:T(8,128)} custom-call(bf16[1024,128]{1,0:T(8,128)(2,1)} %concatenate.7.q_ref, bf16[32768,128]{1,0:T(8,128)(2,1)} %all-gather.2.cloned.1.call-done.kv_ref), custom_call_target="tpu_custom_call" | custom-call | flops 17179869184 | bytes 9175040 | tf_op jit(solution)/shard_map/pallas_call | solution.py:79
  161.3 1.3 slice_reduce_fusion
  162.6 1.4 fusion.9
  164.0 0.8 copy.48
  164.8 4.3 %all-to-all-start.2 = ((bf16[8,128,64]{1,2,0:T(8,128)(2,1)}), bf16[8,128,64]{1,2,0:T(8,128)(2,1)S(1)}, u32[]{:S(2)}, u32[]{:S(2)}) async-start(bf16[8,128,64]{1,2,0:T(8,128)(2,1)} %copy.48), calls=%async_computation.2 | async-start | bytes 262144 | tf_op jit(solution)/shard_map/all_to_all | solution.py:164
  169.1 6.1 %all-to-all-done.2 = bf16[8,128,64]{1,2,0:T(8,128)(2,1)S(1)} async-done(((bf16[8,128,64]{1,2,0:T(8,128)(2,1)}), bf16[8,128,64]{1,2,0:T(8,128)(2,1)S(1)}, u32[]{:S(2)}, u32[]{:S(2)}) %all-to-all-start.2) | async-done | bytes 131104 | tf_op jit(solution)/shard_map/all_to_all | solution.py:164
  175.2 0.6 gather_fusion.3
  175.8 0.3 multiply_reduce_fusion
  176.1 0.8 add_convert_fusion
  (58 shorter events, 1.1 us)
Async XLA Ops:
  6.5 60.4 %copy-start = (bf16[512,1024]{1,0:T(8,128)(2,1)S(1)}, bf16[512,1024]{1,0:T(8,128)(2,1)}, u32[]{:S(2)}) copy-start(bf16[512,1024]{1,0:T(8,128)(2,1)} %param.21) | copy-start | bytes 3145732
  6.5 114.7 %all-gather.2.cloned.1.call-start = ((), (), s32[]{:S(2)}) async-start(), calls=%async_computation.3 | async-start | bytes 8650752 | tf_op jit(solution)/shard_map/all_gather | solution.py:143
  7.6 1.9 %copy-start.1 = (bf16[128,512]{1,0:T(8,128)(2,1)S(1)}, bf16[128,512]{1,0:T(8,128)(2,1)}, u32[]{:S(2)}) copy-start(bf16[128,512]{1,0:T(8,128)(2,1)} %param.14) | copy-start | bytes 393220
  7.6 1.9 %copy-start.3 = (bf16[512,512]{1,0:T(8,128)(2,1)S(1)}, bf16[512,512]{1,0:T(8,128)(2,1)}, u32[]{:S(2)}) copy-start(bf16[512,512]{1,0:T(8,128)(2,1)} %param.19) | copy-start | bytes 1572868
  9.1 0.8 copy-start.11
  9.8 23.9 %copy-start.4 = (bf16[512,512]{1,0:T(8,128)(2,1)S(1)}, bf16[512,512]{1,0:T(8,128)(2,1)}, u32[]{:S(2)}) copy-start(bf16[512,512]{1,0:T(8,128)(2,1)} %param.17) | copy-start | bytes 1572868
  23.2 11.0 %copy-start.12 = (f32[8]{0:T(128)S(1)}, f32[8]{0:T(128)}, u32[]{:S(2)}) copy-start(f32[8]{0:T(128)} %param.23) | copy-start | bytes 100
  23.3 15.9 %collective-permute-start = (bf16[128,512]{1,0:T(8,128)(2,1)S(1)}, bf16[128,512]{1,0:T(8,128)(2,1)S(1)}, u32[]{:S(2)}, u32[]{:S(2)}) collective-permute-start(bf16[128,512]{1,0:T(8,128)(2,1)S(1)} %copy-done.1), channel_id=1, source_target_pairs={{0,4},{4,8},{8,12},{12,16},{16,20},{20,24},{24,28},{28,32},{32,36}... | collective-permute-start | bytes 393224 | tf_op jit(solution)/shard_map/ppermute | solution.py:33
  25.6 13.7 %collective-permute-start.1 = (bf16[128,512]{1,0:T(8,128)(2,1)S(1)}, bf16[128,512]{1,0:T(8,128)(2,1)S(1)}, u32[]{:S(2)}, u32[]{:S(2)}) collective-permute-start(bf16[128,512]{1,0:T(8,128)(2,1)S(1)} %copy-done.1), channel_id=1, source_target_pairs={{4,0},{8,4},{12,8},{16,12},{20,16},{24,20},{28,24},{32,28},{36,32}... | collective-permute-start | bytes 393224 | tf_op jit(solution)/shard_map/ppermute | solution.py:34
  34.1 8.6 %copy-start.13 = (s32[1,1,12]{2,1,0:T(1,128)S(1)}, s32[1,1,12]{2,1,0:T(1,128)}, u32[]{:S(2)}) copy-start(s32[1,1,12]{2,1,0:T(1,128)} %param.15) | copy-start | bytes 148
  35.8 10.3 %all-to-all-start = ((bf16[128,8,64]{0,2,1:T(8,128)(2,1)}), bf16[128,8,64]{0,2,1:T(8,128)(2,1)S(1)}, u32[]{:S(2)}, u32[]{:S(2)}) async-start(bf16[128,8,64]{0,2,1:T(8,128)(2,1)} %bitcast.14), calls=%async_computation | async-start | bytes 262144 | tf_op jit(solution)/shard_map/all_to_all | solution.py:138
  39.3 12.4 %collective-permute-start.2 = (bf16[384,512]{1,0:T(8,128)(2,1)S(1)}, bf16[384,512]{1,0:T(8,128)(2,1)S(1)}, u32[]{:S(2)}, u32[]{:S(2)}) collective-permute-start(bf16[384,512]{1,0:T(8,128)(2,1)S(1)} %constant_dynamic-update-slice_fusion), channel_id=1, source_target_pairs={{0,1},{1,2},{2,3},{3,0},{4,5},{5,6},{6,7},{7,4},{8,9},{9,10},{10,1... | collective-permute-start | bytes 1179656 | tf_op jit(solution)/shard_map/ppermute | solution.py:118
  39.7 13.0 %collective-permute-start.3 = (bf16[384,512]{1,0:T(8,128)(2,1)S(1)}, bf16[384,512]{1,0:T(8,128)(2,1)}, u32[]{:S(2)}, u32[]{:S(2)}) collective-permute-start(bf16[384,512]{1,0:T(8,128)(2,1)S(1)} %constant_dynamic-update-slice_fusion), channel_id=1, source_target_pairs={{0,2},{1,3},{2,0},{3,1},{4,6},{5,7},{6,4},{7,5},{8,10},{9,11},{10,... | collective-permute-start | bytes 1179656 | tf_op jit(solution)/shard_map/ppermute | solution.py:118
  41.4 17.2 %collective-permute-start.4 = (bf16[384,512]{1,0:T(8,128)(2,1)S(1)}, bf16[384,512]{1,0:T(8,128)(2,1)S(1)}, u32[]{:S(2)}, u32[]{:S(2)}) collective-permute-start(bf16[384,512]{1,0:T(8,128)(2,1)S(1)} %constant_dynamic-update-slice_fusion), channel_id=1, source_target_pairs={{0,3},{1,0},{2,1},{3,2},{4,7},{5,4},{6,5},{7,6},{8,11},{9,8},{10,9... | collective-permute-start | bytes 1179656 | tf_op jit(solution)/shard_map/ppermute | solution.py:118
  51.7 7.0 %copy-start.6 = (bf16[384,512]{1,0:T(8,128)(2,1)}, bf16[384,512]{1,0:T(8,128)(2,1)S(1)}, u32[]{:S(2)}) copy-start(bf16[384,512]{1,0:T(8,128)(2,1)S(1)} %collective-permute-done.2) | copy-start | bytes 1179652
  58.6 0.8 copy-start.7
  62.2 4.8 %copy-start.8 = (bf16[128,12,128]{0,2,1:T(8,128)(2,1)S(1)}, bf16[128,12,128]{0,2,1:T(8,128)(2,1)}, u32[]{:S(2)}) copy-start(bf16[128,12,128]{0,2,1:T(8,128)(2,1)} %copy.36) | copy-start | bytes 1179652
  66.9 2.2 %copy-start.2 = (bf16[1024,512]{1,0:T(8,128)(2,1)S(1)}, bf16[1024,512]{1,0:T(8,128)(2,1)}, u32[]{:S(2)}) copy-start(bf16[1024,512]{1,0:T(8,128)(2,1)} %param.22) | copy-start | bytes 3145732
  161.3 7.8 %copy-start.10 = (s32[8]{0:T(128)S(1)}, s32[8]{0:T(128)}, u32[]{:S(2)}) copy-start(s32[8]{0:T(128)} %constant.88) | copy-start | bytes 100
  161.3 14.5 %copy-start.5 = (bf16[512,512]{1,0:T(8,128)(2,1)S(1)}, bf16[512,512]{1,0:T(8,128)(2,1)}, u32[]{:S(2)}) copy-start(bf16[512,512]{1,0:T(8,128)(2,1)} %param.20) | copy-start | bytes 1572868
  162.6 13.6 %copy-start.9 = (f32[512]{0:T(512)S(1)}, f32[512]{0:T(512)}, u32[]{:S(2)}) copy-start(f32[512]{0:T(512)} %param.24) | copy-start | bytes 6148
  164.8 10.4 %all-to-all-start.2 = ((bf16[8,128,64]{1,2,0:T(8,128)(2,1)}), bf16[8,128,64]{1,2,0:T(8,128)(2,1)S(1)}, u32[]{:S(2)}, u32[]{:S(2)}) async-start(bf16[8,128,64]{1,2,0:T(8,128)(2,1)} %copy.48), calls=%async_computation.2 | async-start | bytes 262144 | tf_op jit(solution)/shard_map/all_to_all | solution.py:164
Sparse Core Ops, SparseCore 0:
  23.4 97.8 all-gather.1

commit v9 on v8

--- a/solution.py
+++ b/solution.py
@@ -11,7 +11,7 @@
 NUM_SUBSPACES = 8
 SUBSPACE_WIDTH = 64
 KEY_BLOCK = 8192
-KEY_STEP = 2048
+KEY_STEP = 4096
 QUERY_STEP = 1024
 
 norm_eps = 1e-06
@@ -139,7 +139,17 @@
             packed.reshape(block_len, -1), GROUP, split_axis=1, concat_axis=0, tiled=True
         )
 
-    key_values = to_members((keys_all, values_all))
+    me = lax.axis_index(PAIR) * group_size + lax.axis_index("head")
+    kv_packed = jnp.stack(
+        [t.reshape(block_len, NUM_SUBSPACES, SUBSPACE_WIDTH) for t in (keys_all, values_all)],
+        axis=2,
+    )[:, jnp.array(head_of)]
+    pieces = [jnp.take(kv_packed, me, axis=1).reshape(block_len, -1)]
+    for shift in range(1, members):
+        chunk = jnp.take(kv_packed, lax.rem(me + shift, members), axis=1).reshape(block_len, -1)
+        pairs = [(i, (i + shift) % members) for i in range(members)]
+        pieces.append(lax.ppermute(chunk, GROUP, pairs))
+    key_values = jnp.concatenate(pieces, axis=0)
     kv_in = lax.all_gather(key_values, (ROW, COLUMN), axis=0, tiled=True)
     queries = head_norm(
         jnp.dot(vertex_embeddings, asking_projector, preferred_element_type=jnp.float32),

time: 187 us -> 188 us (level)
  blocking collectives: 11.8 us -> 0 us
  starting transfers between devices: 21.5 us -> 29.7 us
  waiting for transfers between devices: 69.4 us -> 74 us
    all_to_all x1 -> x0, blocking collectives: 11.8 us -> none  [to_members(): lax.all_to_all(packed.reshape(block_len, -1), GROUP, split_axis=1, concat...]
    ppermute x0 -> x7, starting transfers between devices: none -> 9.24 us  [shards(): pieces.append(lax.ppermute(chunk, GROUP, pairs))]
    ppermute x3, waiting for transfers between devices: 12.3 us -> 15 us  [shards(): gathered.append(lax.ppermute(halo_rows, 'head', pairs))]
    ppermute x0 -> x7, waiting for transfers between devices: none -> 2.44 us  [shards(): pieces.append(lax.ppermute(chunk, GROUP, pairs))]
  transfers between devices with their start and end apart: 8 -> 15, of which waited for: 5 -> 6; matrix products, arithmetic and copies ran while one was open for 9% -> 9% of each run, Pallas kernels for 0% -> 0%
where the time goes in v9:
time: 188 us; the launch traced here: 185 us
  waiting for transfers between devices  74 us (39%)
  Pallas kernels  38.7 us (21%)
  starting transfers between devices  29.7 us (16%)
  local copies, waits for them, and re-layouts  18.5 us (10%)
  between operations  14 us (7%)
  matrix products  5.58 us (3%)
  other arithmetic  4.77 us (3%)
    all_gather x1, waiting for transfers between devices, shards(): kv_in = lax.all_gather(key_values, (ROW, COLUMN), axis=0, tiled=True)  49.9 us
    pallas_call x1, Pallas kernels, attend(): pl.pallas_call(attention_kernel, grid=(keys // block,), in_specs=[pl.Bloc...  38.7 us
    ppermute x3, waiting for transfers between devices, shards(): gathered.append(lax.ppermute(halo_rows, 'head', pairs))  15 us
    ppermute x7, starting transfers between devices, shards(): pieces.append(lax.ppermute(chunk, GROUP, pairs))  9.24 us
    ppermute x1, starting transfers between devices, extended(): after = lax.ppermute(first, DOM, down)  7.43 us
    all_to_all x1, waiting for transfers between devices, shards(): lax.all_to_all(merged, GROUP, split_axis=0, concat_axis=1, tiled=True)  6.12 us
    scatter x1, local copies, waits for them, and re-layouts, shards(): jnp.zeros_like(stacked).at[order].set(stacked)  4.75 us
    all_to_all x1, starting transfers between devices, shards(): lax.all_to_all(merged, GROUP, split_axis=0, concat_axis=1, tiled=True)  4.29 us
  transfers between devices with their start and end apart: 15, of which 6 were waited for; matrix products, arithmetic and copies ran while one was open for 9% of the time, Pallas kernels for 0%

profile of v9, /device:TPU:4, one launch (start us, length us, event | category | flops | bytes accessed | tf_op | source)
XLA Modules:
  0.0 185.2 jit_solution(13376539011865632570)
XLA Ops:
  6.5 0.8 maximum_reduce_fusion
  7.6 1.3 convolution_convert_fusion
  9.1 1.1 fusion.13
  10.2 0.1 copy.47
  10.4 0.1 copy.48
  10.8 0.6 gather_fusion.2
  11.8 1.7 collective-permute-start.6
  13.6 2.4 %collective-permute-start.7 = (bf16[128,128]{1,0:T(8,128)(2,1)S(1)}, bf16[128,128]{1,0:T(8,128)(2,1)S(1)}, u32[]{:S(2)}, u32[]{:S(2)}) collective-permute-start(bf16[128,128]{1,0:T(8,128)(2,1)S(1)} %copy.55), channel_id=1, source_target_pairs={{0,3},{1,4},{2,5},{3,6},{4,7},{5,0},{6,1},{7,2},{8,11},{9,12},{10,... | collective-permute-start | bytes 98312 | tf_op jit(solution)/shard_map/ppermute | solution.py:151
  16.0 1.9 %collective-permute-start.8 = (bf16[128,128]{1,0:T(8,128)(2,1)S(1)}, bf16[128,128]{1,0:T(8,128)(2,1)S(1)}, u32[]{:S(2)}, u32[]{:S(2)}) collective-permute-start(bf16[128,128]{1,0:T(8,128)(2,1)S(1)} %copy.56), channel_id=1, source_target_pairs={{0,4},{1,5},{2,6},{3,7},{4,0},{5,1},{6,2},{7,3},{8,12},{9,13},{10,... | collective-permute-start | bytes 98312 | tf_op jit(solution)/shard_map/ppermute | solution.py:151
  18.1 1.8 collective-permute-start.9
  20.1 0.1 copy.59
  20.3 1.4 collective-permute-start.10
  21.9 2.4 %collective-permute-done.10 = bf16[128,128]{1,0:T(8,128)(2,1)S(1)} collective-permute-done((bf16[128,128]{1,0:T(8,128)(2,1)S(1)}, bf16[128,128]{1,0:T(8,128)(2,1)S(1)}, u32[]{:S(2)}, u32[]{:S(2)}) %collective-permute-start.10) | collective-permute-done | bytes 32800 | tf_op jit(solution)/shard_map/ppermute | solution.py:151
  24.3 0.7 copy-done.9
  25.1 2.9 %collective-permute-start = (bf16[128,512]{1,0:T(8,128)(2,1)S(1)}, bf16[128,512]{1,0:T(8,128)(2,1)S(1)}, u32[]{:S(2)}, u32[]{:S(2)}) collective-permute-start(bf16[128,512]{1,0:T(8,128)(2,1)S(1)} %copy-done.1), channel_id=1, source_target_pairs={{0,4},{4,8},{8,12},{12,16},{16,20},{20,24},{24,28},{28,32},{32,36}... | collective-permute-start | bytes 393224 | tf_op jit(solution)/shard_map/ppermute | solution.py:33
  28.0 7.4 %collective-permute-start.1 = (bf16[128,512]{1,0:T(8,128)(2,1)S(1)}, bf16[128,512]{1,0:T(8,128)(2,1)S(1)}, u32[]{:S(2)}, u32[]{:S(2)}) collective-permute-start(bf16[128,512]{1,0:T(8,128)(2,1)S(1)} %copy-done.1), channel_id=1, source_target_pairs={{4,0},{8,4},{12,8},{16,12},{20,16},{24,20},{28,24},{32,28},{36,32}... | collective-permute-start | bytes 393224 | tf_op jit(solution)/shard_map/ppermute | solution.py:34
  35.4 0.2 fusion.12
  35.7 0.1 copy.43
  35.9 0.1 copy.44
  36.4 1.2 gather_fusion.1
  37.6 3.4 %all-to-all-start = ((bf16[128,8,64]{0,2,1:T(8,128)(2,1)}), bf16[128,8,64]{0,2,1:T(8,128)(2,1)S(1)}, u32[]{:S(2)}, u32[]{:S(2)}) async-start(bf16[128,8,64]{0,2,1:T(8,128)(2,1)} %bitcast.14), calls=%async_computation | async-start | bytes 262144 | tf_op jit(solution)/shard_map/all_to_all | solution.py:138
  41.1 1.8 collective-permute-start.4
  42.9 0.4 collective-permute-start.3
  43.3 0.1 collective-permute-start.2
  44.1 1.7 gather_fusion
  45.8 0.1 select_bitcast_fusion
  45.9 0.9 copy.42
  46.8 0.6 all-to-all-done
  47.4 0.2 copy.46
  47.6 4.8 %collective-permute-done.4 = bf16[384,512]{1,0:T(8,128)(2,1)S(1)} collective-permute-done((bf16[384,512]{1,0:T(8,128)(2,1)S(1)}, bf16[384,512]{1,0:T(8,128)(2,1)S(1)}, u32[]{:S(2)}, u32[]{:S(2)}) %collective-permute-start.4) | collective-permute-done | bytes 393248 | tf_op jit(solution)/shard_map/ppermute | solution.py:118
  52.5 10.2 %collective-permute-done.3 = bf16[384,512]{1,0:T(8,128)(2,1)} collective-permute-done((bf16[384,512]{1,0:T(8,128)(2,1)S(1)}, bf16[384,512]{1,0:T(8,128)(2,1)}, u32[]{:S(2)}, u32[]{:S(2)}) %collective-permute-start.3) | collective-permute-done | bytes 393248 | tf_op jit(solution)/shard_map/ppermute | solution.py:118
  62.6 0.7 copy-done.7
  63.4 1.4 pad_maximum_fusion
  64.8 1.3 broadcast_in_dim.54
  66.1 4.7 %scatter_fusion = bf16[4,384,512]{2,1,0:T(8,128)(2,1)} fusion(bf16[4,384,512]{2,1,0:T(8,128)(2,1)} %broadcast_in_dim.54, s32[4]{0:T(128)S(1)} %fusion.11, bf16[4,384,512]{2,1,0:T(8,128)(2,1)S(1)} %pad_maximum_fusion), kind=kCustom, calls=%fused_computation.4 | custom fusion | bytes 4718608 | tf_op jit(solution)/shard_map/scatter | solution.py:121
  70.9 2.2 %fusion.8 = bf16[128,1024]{1,0:T(8,128)(2,1)S(1)} fusion(bf16[512,1024]{1,0:T(8,128)(2,1)S(1)} %copy-done, bf16[128,1536]{0,1:T(8,128)(2,1)S(1)} %bitcast.87, bf16[1536,512]{1,0:T(8,128)(2,1)} %bitcast.72), kind=kOutput, calls=%fused_computation.17 | convolution fusion | flops 336789504 | bytes 3276800 | tf_op jit(solution)/shard_map/dot_general | solution.py:166
  73.1 0.3 fusion.14
  73.4 0.8 concatenate.10.q_ref
  74.2 49.9 %all-gather.2.cloned.1.call-done.kv_ref = bf16[32768,128]{1,0:T(8,128)(2,1)} async-done(((bf16[1024,128]{1,0:T(8,128)(2,1)}), bf16[32768,128]{1,0:T(8,128)(2,1)}) %all-gather.2.cloned.1.call-update) | async-done | bytes 8388624 | tf_op jit(solution)/shard_map/all_gather | solution.py:153
  124.1 38.7 %shard_map.136 = f32[1024,128]{1,0:T(8,128)} custom-call(bf16[1024,128]{1,0:T(8,128)(2,1)} %concatenate.10.q_ref, bf16[32768,128]{1,0:T(8,128)(2,1)} %all-gather.2.cloned.1.call-done.kv_ref), custom_call_target="tpu_custom_call" | custom-call | flops 17179869184 | bytes 9175040 | tf_op jit(solution)/shard_map/pallas_call | solution.py:79
  162.7 1.3 slice_reduce_fusion
  164.1 1.4 fusion.9
  165.4 0.8 copy.61
  166.2 4.3 %all-to-all-start.1 = ((bf16[8,128,64]{1,2,0:T(8,128)(2,1)}), bf16[8,128,64]{1,2,0:T(8,128)(2,1)S(1)}, u32[]{:S(2)}, u32[]{:S(2)}) async-start(bf16[8,128,64]{1,2,0:T(8,128)(2,1)} %copy.61), calls=%async_computation.1 | async-start | bytes 262144 | tf_op jit(solution)/shard_map/all_to_all | solution.py:174
  170.5 6.1 %all-to-all-done.1 = bf16[8,128,64]{1,2,0:T(8,128)(2,1)S(1)} async-done(((bf16[8,128,64]{1,2,0:T(8,128)(2,1)}), bf16[8,128,64]{1,2,0:T(8,128)(2,1)S(1)}, u32[]{:S(2)}, u32[]{:S(2)}) %all-to-all-start.1) | async-done | bytes 131104 | tf_op jit(solution)/shard_map/all_to_all | solution.py:174
  176.7 0.6 gather_fusion.3
  177.2 0.3 multiply_reduce_fusion
  177.6 0.8 add_convert_fusion
  (89 shorter events, 2.7 us)
Async XLA Ops:
  6.5 64.4 %copy-start = (bf16[512,1024]{1,0:T(8,128)(2,1)S(1)}, bf16[512,1024]{1,0:T(8,128)(2,1)}, u32[]{:S(2)}) copy-start(bf16[512,1024]{1,0:T(8,128)(2,1)} %param.23) | copy-start | bytes 3145732
  6.5 2.5 %copy-start.3 = (bf16[512,512]{1,0:T(8,128)(2,1)S(1)}, bf16[512,512]{1,0:T(8,128)(2,1)}, u32[]{:S(2)}) copy-start(bf16[512,512]{1,0:T(8,128)(2,1)} %param.20) | copy-start | bytes 1572868
  6.5 117.5 %all-gather.2.cloned.1.call-start = ((), (), s32[]{:S(2)}) async-start(), calls=%async_computation.2 | async-start | bytes 8650752 | tf_op jit(solution)/shard_map/all_gather | solution.py:153
  9.1 1.7 copy-start.12
  10.8 14.2 %copy-start.1 = (bf16[128,512]{1,0:T(8,128)(2,1)S(1)}, bf16[128,512]{1,0:T(8,128)(2,1)}, u32[]{:S(2)}) copy-start(bf16[128,512]{1,0:T(8,128)(2,1)} %param.16) | copy-start | bytes 393220
  10.8 24.6 %copy-start.4 = (bf16[512,512]{1,0:T(8,128)(2,1)S(1)}, bf16[512,512]{1,0:T(8,128)(2,1)}, u32[]{:S(2)}) copy-start(bf16[512,512]{1,0:T(8,128)(2,1)} %param.19) | copy-start | bytes 1572868
  11.6 8.6 %collective-permute-start.5 = (bf16[128,128]{1,0:T(8,128)(2,1)S(1)}, bf16[128,128]{1,0:T(8,128)(2,1)S(1)}, u32[]{:S(2)}, u32[]{:S(2)}) collective-permute-start(bf16[128,128]{1,0:T(8,128)(2,1)S(1)} %copy.53), channel_id=1, source_target_pairs={{0,1},{1,2},{2,3},{3,4},{4,5},{5,6},{6,7},{7,0},{8,9},{9,10},{10,1... | collective-permute-start | bytes 98312 | tf_op jit(solution)/shard_map/ppermute | solution.py:151
  11.8 9.9 %collective-permute-start.6 = (bf16[128,128]{1,0:T(8,128)(2,1)S(1)}, bf16[128,128]{1,0:T(8,128)(2,1)S(1)}, u32[]{:S(2)}, u32[]{:S(2)}) collective-permute-start(bf16[128,128]{1,0:T(8,128)(2,1)S(1)} %copy.54), channel_id=1, source_target_pairs={{0,2},{1,3},{2,4},{3,5},{4,6},{5,7},{6,0},{7,1},{8,10},{9,11},{10,... | collective-permute-start | bytes 98312 | tf_op jit(solution)/shard_map/ppermute | solution.py:151
  13.6 8.2 %collective-permute-start.7 = (bf16[128,128]{1,0:T(8,128)(2,1)S(1)}, bf16[128,128]{1,0:T(8,128)(2,1)S(1)}, u32[]{:S(2)}, u32[]{:S(2)}) collective-permute-start(bf16[128,128]{1,0:T(8,128)(2,1)S(1)} %copy.55), channel_id=1, source_target_pairs={{0,3},{1,4},{2,5},{3,6},{4,7},{5,0},{6,1},{7,2},{8,11},{9,12},{10,... | collective-permute-start | bytes 98312 | tf_op jit(solution)/shard_map/ppermute | solution.py:151
  16.0 5.8 %collective-permute-start.8 = (bf16[128,128]{1,0:T(8,128)(2,1)S(1)}, bf16[128,128]{1,0:T(8,128)(2,1)S(1)}, u32[]{:S(2)}, u32[]{:S(2)}) collective-permute-start(bf16[128,128]{1,0:T(8,128)(2,1)S(1)} %copy.56), channel_id=1, source_target_pairs={{0,4},{1,5},{2,6},{3,7},{4,0},{5,1},{6,2},{7,3},{8,12},{9,13},{10,... | collective-permute-start | bytes 98312 | tf_op jit(solution)/shard_map/ppermute | solution.py:151
  18.1 3.8 %collective-permute-start.9 = (bf16[128,128]{1,0:T(8,128)(2,1)S(1)}, bf16[128,128]{1,0:T(8,128)(2,1)S(1)}, u32[]{:S(2)}, u32[]{:S(2)}) collective-permute-start(bf16[128,128]{1,0:T(8,128)(2,1)S(1)} %copy.57), channel_id=1, source_target_pairs={{0,5},{1,6},{2,7},{3,0},{4,1},{5,2},{6,3},{7,4},{8,13},{9,14},{10,... | collective-permute-start | bytes 98312 | tf_op jit(solution)/shard_map/ppermute | solution.py:151
  20.3 4.0 %collective-permute-start.10 = (bf16[128,128]{1,0:T(8,128)(2,1)S(1)}, bf16[128,128]{1,0:T(8,128)(2,1)S(1)}, u32[]{:S(2)}, u32[]{:S(2)}) collective-permute-start(bf16[128,128]{1,0:T(8,128)(2,1)S(1)} %copy.58), channel_id=1, source_target_pairs={{0,6},{1,7},{2,0},{3,1},{4,2},{5,3},{6,4},{7,5},{8,14},{9,15},{10,... | collective-permute-start | bytes 98312 | tf_op jit(solution)/shard_map/ppermute | solution.py:151
  21.7 2.6 %collective-permute-start.11 = (bf16[128,128]{1,0:T(8,128)(2,1)S(1)}, bf16[128,128]{1,0:T(8,128)(2,1)S(1)}, u32[]{:S(2)}, u32[]{:S(2)}) collective-permute-start(bf16[128,128]{1,0:T(8,128)(2,1)S(1)} %copy.59), channel_id=1, source_target_pairs={{0,7},{1,0},{2,1},{3,2},{4,3},{5,4},{6,5},{7,6},{8,15},{9,8},{10,9... | collective-permute-start | bytes 98312 | tf_op jit(solution)/shard_map/ppermute | solution.py:151
  21.9 14.2 %copy-start.13 = (f32[8]{0:T(128)S(1)}, f32[8]{0:T(128)}, u32[]{:S(2)}) copy-start(f32[8]{0:T(128)} %param.25) | copy-start | bytes 100
  24.3 0.7 copy-start.9
  25.1 16.0 %collective-permute-start = (bf16[128,512]{1,0:T(8,128)(2,1)S(1)}, bf16[128,512]{1,0:T(8,128)(2,1)S(1)}, u32[]{:S(2)}, u32[]{:S(2)}) collective-permute-start(bf16[128,512]{1,0:T(8,128)(2,1)S(1)} %copy-done.1), channel_id=1, source_target_pairs={{0,4},{4,8},{8,12},{12,16},{16,20},{20,24},{24,28},{28,32},{32,36}... | collective-permute-start | bytes 393224 | tf_op jit(solution)/shard_map/ppermute | solution.py:33
  28.0 13.1 %collective-permute-start.1 = (bf16[128,512]{1,0:T(8,128)(2,1)S(1)}, bf16[128,512]{1,0:T(8,128)(2,1)S(1)}, u32[]{:S(2)}, u32[]{:S(2)}) collective-permute-start(bf16[128,512]{1,0:T(8,128)(2,1)S(1)} %copy-done.1), channel_id=1, source_target_pairs={{4,0},{8,4},{12,8},{16,12},{20,16},{24,20},{28,24},{32,28},{36,32}... | collective-permute-start | bytes 393224 | tf_op jit(solution)/shard_map/ppermute | solution.py:34
  35.9 7.6 %copy-start.14 = (s32[1,1,12]{2,1,0:T(1,128)S(1)}, s32[1,1,12]{2,1,0:T(1,128)}, u32[]{:S(2)}) copy-start(s32[1,1,12]{2,1,0:T(1,128)} %param.17) | copy-start | bytes 148
  37.6 9.8 %all-to-all-start = ((bf16[128,8,64]{0,2,1:T(8,128)(2,1)}), bf16[128,8,64]{0,2,1:T(8,128)(2,1)S(1)}, u32[]{:S(2)}, u32[]{:S(2)}) async-start(bf16[128,8,64]{0,2,1:T(8,128)(2,1)} %bitcast.14), calls=%async_computation | async-start | bytes 262144 | tf_op jit(solution)/shard_map/all_to_all | solution.py:138
  41.1 11.4 %collective-permute-start.4 = (bf16[384,512]{1,0:T(8,128)(2,1)S(1)}, bf16[384,512]{1,0:T(8,128)(2,1)S(1)}, u32[]{:S(2)}, u32[]{:S(2)}) collective-permute-start(bf16[384,512]{1,0:T(8,128)(2,1)S(1)} %constant_dynamic-update-slice_fusion), channel_id=1, source_target_pairs={{0,3},{1,0},{2,1},{3,2},{4,7},{5,4},{6,5},{7,6},{8,11},{9,8},{10,9... | collective-permute-start | bytes 1179656 | tf_op jit(solution)/shard_map/ppermute | solution.py:118
  42.9 19.7 %collective-permute-start.3 = (bf16[384,512]{1,0:T(8,128)(2,1)S(1)}, bf16[384,512]{1,0:T(8,128)(2,1)}, u32[]{:S(2)}, u32[]{:S(2)}) collective-permute-start(bf16[384,512]{1,0:T(8,128)(2,1)S(1)} %constant_dynamic-update-slice_fusion), channel_id=1, source_target_pairs={{0,2},{1,3},{2,0},{3,1},{4,6},{5,7},{6,4},{7,5},{8,10},{9,11},{10,... | collective-permute-start | bytes 1179656 | tf_op jit(solution)/shard_map/ppermute | solution.py:118
  43.3 19.3 %collective-permute-start.2 = (bf16[384,512]{1,0:T(8,128)(2,1)S(1)}, bf16[384,512]{1,0:T(8,128)(2,1)S(1)}, u32[]{:S(2)}, u32[]{:S(2)}) collective-permute-start(bf16[384,512]{1,0:T(8,128)(2,1)S(1)} %constant_dynamic-update-slice_fusion), channel_id=1, source_target_pairs={{0,1},{1,2},{2,3},{3,0},{4,5},{5,6},{6,7},{7,4},{8,9},{9,10},{10,1... | collective-permute-start | bytes 1179656 | tf_op jit(solution)/shard_map/ppermute | solution.py:118
  52.5 10.2 %copy-start.6 = (bf16[384,512]{1,0:T(8,128)(2,1)}, bf16[384,512]{1,0:T(8,128)(2,1)S(1)}, u32[]{:S(2)}) copy-start(bf16[384,512]{1,0:T(8,128)(2,1)S(1)} %collective-permute-done.4) | copy-start | bytes 1179652
  62.6 0.7 copy-start.7
  66.1 4.8 %copy-start.8 = (bf16[128,12,128]{0,2,1:T(8,128)(2,1)S(1)}, bf16[128,12,128]{0,2,1:T(8,128)(2,1)}, u32[]{:S(2)}) copy-start(bf16[128,12,128]{0,2,1:T(8,128)(2,1)} %copy.42) | copy-start | bytes 1179652
  70.9 2.2 %copy-start.2 = (bf16[1024,512]{1,0:T(8,128)(2,1)S(1)}, bf16[1024,512]{1,0:T(8,128)(2,1)}, u32[]{:S(2)}) copy-start(bf16[1024,512]{1,0:T(8,128)(2,1)} %param.24) | copy-start | bytes 3145732
  162.7 7.8 %copy-start.11 = (s32[8]{0:T(128)S(1)}, s32[8]{0:T(128)}, u32[]{:S(2)}) copy-start(s32[8]{0:T(128)} %constant.165) | copy-start | bytes 100
  162.7 14.5 %copy-start.5 = (bf16[512,512]{1,0:T(8,128)(2,1)S(1)}, bf16[512,512]{1,0:T(8,128)(2,1)}, u32[]{:S(2)}) copy-start(bf16[512,512]{1,0:T(8,128)(2,1)} %param.22) | copy-start | bytes 1572868
  164.0 13.6 %copy-start.10 = (f32[512]{0:T(512)S(1)}, f32[512]{0:T(512)}, u32[]{:S(2)}) copy-start(f32[512]{0:T(512)} %param.26) | copy-start | bytes 6148
  166.2 10.4 %all-to-all-start.1 = ((bf16[8,128,64]{1,2,0:T(8,128)(2,1)}), bf16[8,128,64]{1,2,0:T(8,128)(2,1)S(1)}, u32[]{:S(2)}, u32[]{:S(2)}) async-start(bf16[8,128,64]{1,2,0:T(8,128)(2,1)} %copy.61), calls=%async_computation.1 | async-start | bytes 262144 | tf_op jit(solution)/shard_map/all_to_all | solution.py:174
Sparse Core Ops, SparseCore 0:
  25.2 98.8 all-gather.1

commit v10 on v8

--- a/solution.py
+++ b/solution.py
@@ -140,7 +140,7 @@
         )
 
     key_values = to_members((keys_all, values_all))
-    kv_in = lax.all_gather(key_values, (ROW, COLUMN), axis=0, tiled=True)
+    kv_in = lax.all_gather(key_values, (COLUMN, ROW), axis=0, tiled=True)
     queries = head_norm(
         jnp.dot(vertex_embeddings, asking_projector, preferred_element_type=jnp.float32),
         asking_vector_multiplier,

time: 187 us -> 186 us (level)
  no operation moved by 1% of the time
where the time goes in v10:
time: 186 us; the launch traced here: 184 us
  waiting for transfers between devices  69.3 us (37%)
  Pallas kernels  40 us (22%)
  starting transfers between devices  21.5 us (12%)
  local copies, waits for them, and re-layouts  17.8 us (10%)
  between operations  13.8 us (7%)
  blocking collectives  11.8 us (6%)
  matrix products  4.72 us (3%)
  other arithmetic  4.69 us (3%)
    all_gather x1, waiting for transfers between devices, shards(): kv_in = lax.all_gather(key_values, (COLUMN, ROW), axis=0, tiled=True)  50.8 us
    pallas_call x1, Pallas kernels, attend(): pl.pallas_call(attention_kernel, grid=(keys // block,), in_specs=[pl.Bloc...  40 us
    ppermute x3, waiting for transfers between devices, shards(): gathered.append(lax.ppermute(halo_rows, 'head', pairs))  12.3 us
    all_to_all x1, blocking collectives, to_members(): lax.all_to_all(packed.reshape(block_len, -1), GROUP, split_axis=1, concat...  11.8 us
    ppermute x1, starting transfers between devices, extended(): after = lax.ppermute(first, DOM, down)  8.08 us
    all_to_all x1, waiting for transfers between devices, shards(): lax.all_to_all(merged, GROUP, split_axis=0, concat_axis=1, tiled=True)  6.12 us
    scatter x1, local copies, waits for them, and re-layouts, shards(): jnp.zeros_like(stacked).at[order].set(stacked)  4.75 us
    all_to_all x1, starting transfers between devices, shards(): lax.all_to_all(merged, GROUP, split_axis=0, concat_axis=1, tiled=True)  4.29 us
  transfers between devices with their start and end apart: 8, of which 5 were waited for; matrix products, arithmetic and copies ran while one was open for 9% of the time, Pallas kernels for 0%

profile of v10, /device:TPU:4, one launch (start us, length us, event | category | flops | bytes accessed | tf_op | source)
XLA Modules:
  0.0 183.6 jit_solution(7698978190548794624)
XLA Ops:
  6.5 0.8 maximum_reduce_fusion
  7.4 0.1 copy.35
  7.6 1.4 fusion.13
  9.0 0.1 copy.41
  9.2 0.1 copy.42
  9.4 0.1 copy.43
  9.5 0.2 convolution_convert_fusion
  9.8 0.1 copy.44
  10.0 0.6 gather_fusion.2
  10.6 11.8 %all_to_all.54 = bf16[128,8,128]{0,2,1:T(8,128)(2,1)S(1)} all-to-all(bf16[128,8,128]{0,2,1:T(8,128)(2,1)S(1)} %bitcast.53), channel_id=1, replica_groups=mesh['x'=4,'z'=8,'yhi'=2,'head'=4] {'yhi','head'}, dimensions={1} | all-to-all | bytes 524288 | tf_op jit(solution)/shard_map/all_to_all | solution.py:138
  22.4 0.9 copy.47
  23.3 2.3 %collective-permute-start = (bf16[128,512]{1,0:T(8,128)(2,1)S(1)}, bf16[128,512]{1,0:T(8,128)(2,1)S(1)}, u32[]{:S(2)}, u32[]{:S(2)}) collective-permute-start(bf16[128,512]{1,0:T(8,128)(2,1)S(1)} %copy-done.1), channel_id=1, source_target_pairs={{0,4},{4,8},{8,12},{12,16},{16,20},{20,24},{24,28},{28,32},{32,36}... | collective-permute-start | bytes 393224 | tf_op jit(solution)/shard_map/ppermute | solution.py:33
  25.6 8.1 %collective-permute-start.1 = (bf16[128,512]{1,0:T(8,128)(2,1)S(1)}, bf16[128,512]{1,0:T(8,128)(2,1)S(1)}, u32[]{:S(2)}, u32[]{:S(2)}) collective-permute-start(bf16[128,512]{1,0:T(8,128)(2,1)S(1)} %copy-done.1), channel_id=1, source_target_pairs={{4,0},{8,4},{12,8},{16,12},{20,16},{24,20},{28,24},{32,28},{36,32}... | collective-permute-start | bytes 393224 | tf_op jit(solution)/shard_map/ppermute | solution.py:34
  33.7 0.2 fusion.12
  33.9 0.1 copy.37
  34.1 0.1 copy.38
  34.5 0.1 copy.39
  34.6 1.2 gather_fusion.1
  35.8 3.4 %all-to-all-start = ((bf16[128,8,64]{0,2,1:T(8,128)(2,1)}), bf16[128,8,64]{0,2,1:T(8,128)(2,1)S(1)}, u32[]{:S(2)}, u32[]{:S(2)}) async-start(bf16[128,8,64]{0,2,1:T(8,128)(2,1)} %bitcast.14), calls=%async_computation | async-start | bytes 262144 | tf_op jit(solution)/shard_map/all_to_all | solution.py:138
  39.3 0.5 collective-permute-start.2
  39.7 1.7 collective-permute-start.3
  41.4 1.3 collective-permute-start.4
  42.8 0.1 copy.33
  43.1 0.1 copy.34
  43.3 1.7 gather_fusion
  45.0 0.1 select_bitcast_fusion
  45.1 0.9 copy.36
  46.1 0.2 copy.40
  46.3 5.4 %collective-permute-done.2 = bf16[384,512]{1,0:T(8,128)(2,1)S(1)} collective-permute-done((bf16[384,512]{1,0:T(8,128)(2,1)S(1)}, bf16[384,512]{1,0:T(8,128)(2,1)S(1)}, u32[]{:S(2)}, u32[]{:S(2)}) %collective-permute-start.2) | collective-permute-done | bytes 393248 | tf_op jit(solution)/shard_map/ppermute | solution.py:118
  51.7 1.1 collective-permute-done.3
  52.7 5.9 %collective-permute-done.4 = bf16[384,512]{1,0:T(8,128)(2,1)S(1)} collective-permute-done((bf16[384,512]{1,0:T(8,128)(2,1)S(1)}, bf16[384,512]{1,0:T(8,128)(2,1)S(1)}, u32[]{:S(2)}, u32[]{:S(2)}) %collective-permute-start.4) | collective-permute-done | bytes 393248 | tf_op jit(solution)/shard_map/ppermute | solution.py:118
  58.6 0.8 copy-done.7
  59.4 1.4 pad_maximum_fusion
  60.9 1.3 broadcast_in_dim.45
  62.2 4.7 %scatter_fusion = bf16[4,384,512]{2,1,0:T(8,128)(2,1)} fusion(bf16[4,384,512]{2,1,0:T(8,128)(2,1)} %broadcast_in_dim.45, s32[4]{0:T(128)S(1)} %fusion.11, bf16[4,384,512]{2,1,0:T(8,128)(2,1)S(1)} %pad_maximum_fusion), kind=kCustom, calls=%fused_computation.4 | custom fusion | bytes 4718608 | tf_op jit(solution)/shard_map/scatter | solution.py:121
  66.9 2.2 %fusion.8 = bf16[128,1024]{1,0:T(8,128)(2,1)S(1)} fusion(bf16[512,1024]{1,0:T(8,128)(2,1)S(1)} %copy-done, bf16[128,1536]{0,1:T(8,128)(2,1)S(1)} %bitcast.69, bf16[1536,512]{1,0:T(8,128)(2,1)} %bitcast.52), kind=kOutput, calls=%fused_computation.17 | convolution fusion | flops 336789504 | bytes 3276800 | tf_op jit(solution)/shard_map/dot_general | solution.py:156
  69.2 0.3 fusion.14
  69.5 0.8 concatenate.7.q_ref
  70.3 50.8 %all-gather.2.cloned.1.call-done.kv_ref = bf16[32768,128]{1,0:T(8,128)(2,1)} async-done(((bf16[1024,128]{1,0:T(8,128)(2,1)}), bf16[32768,128]{1,0:T(8,128)(2,1)}) %all-gather.2.cloned.1.call-update) | async-done | bytes 8388624 | tf_op jit(solution)/shard_map/all_gather | solution.py:143
  121.1 40.0 %shard_map.136 = f32[1024,128]{1,0:T(8,128)} custom-call(bf16[1024,128]{1,0:T(8,128)(2,1)} %concatenate.7.q_ref, bf16[32768,128]{1,0:T(8,128)(2,1)} %all-gather.2.cloned.1.call-done.kv_ref), custom_call_target="tpu_custom_call" | custom-call | flops 17179869184 | bytes 9175040 | tf_op jit(solution)/shard_map/pallas_call | solution.py:79
  161.1 1.3 slice_reduce_fusion
  162.4 1.4 fusion.9
  163.8 0.8 copy.48
  164.6 4.3 %all-to-all-start.2 = ((bf16[8,128,64]{1,2,0:T(8,128)(2,1)}), bf16[8,128,64]{1,2,0:T(8,128)(2,1)S(1)}, u32[]{:S(2)}, u32[]{:S(2)}) async-start(bf16[8,128,64]{1,2,0:T(8,128)(2,1)} %copy.48), calls=%async_computation.2 | async-start | bytes 262144 | tf_op jit(solution)/shard_map/all_to_all | solution.py:164
  168.9 6.1 %all-to-all-done.2 = bf16[8,128,64]{1,2,0:T(8,128)(2,1)S(1)} async-done(((bf16[8,128,64]{1,2,0:T(8,128)(2,1)}), bf16[8,128,64]{1,2,0:T(8,128)(2,1)S(1)}, u32[]{:S(2)}, u32[]{:S(2)}) %all-to-all-start.2) | async-done | bytes 131104 | tf_op jit(solution)/shard_map/all_to_all | solution.py:164
  175.0 0.6 gather_fusion.3
  175.6 0.3 multiply_reduce_fusion
  176.0 0.8 add_convert_fusion
  (58 shorter events, 1.1 us)
Async XLA Ops:
  6.5 60.4 %copy-start = (bf16[512,1024]{1,0:T(8,128)(2,1)S(1)}, bf16[512,1024]{1,0:T(8,128)(2,1)}, u32[]{:S(2)}) copy-start(bf16[512,1024]{1,0:T(8,128)(2,1)} %param.21) | copy-start | bytes 3145732
  6.5 114.6 %all-gather.2.cloned.1.call-start = ((), (), s32[]{:S(2)}) async-start(), calls=%async_computation.3 | async-start | bytes 8650752 | tf_op jit(solution)/shard_map/all_gather | solution.py:143
  7.6 1.9 %copy-start.1 = (bf16[128,512]{1,0:T(8,128)(2,1)S(1)}, bf16[128,512]{1,0:T(8,128)(2,1)}, u32[]{:S(2)}) copy-start(bf16[128,512]{1,0:T(8,128)(2,1)} %param.14) | copy-start | bytes 393220
  7.6 1.9 %copy-start.3 = (bf16[512,512]{1,0:T(8,128)(2,1)S(1)}, bf16[512,512]{1,0:T(8,128)(2,1)}, u32[]{:S(2)}) copy-start(bf16[512,512]{1,0:T(8,128)(2,1)} %param.19) | copy-start | bytes 1572868
  9.1 0.8 copy-start.11
  9.8 23.9 %copy-start.4 = (bf16[512,512]{1,0:T(8,128)(2,1)S(1)}, bf16[512,512]{1,0:T(8,128)(2,1)}, u32[]{:S(2)}) copy-start(bf16[512,512]{1,0:T(8,128)(2,1)} %param.17) | copy-start | bytes 1572868
  23.2 11.0 %copy-start.12 = (f32[8]{0:T(128)S(1)}, f32[8]{0:T(128)}, u32[]{:S(2)}) copy-start(f32[8]{0:T(128)} %param.23) | copy-start | bytes 100
  23.3 15.9 %collective-permute-start = (bf16[128,512]{1,0:T(8,128)(2,1)S(1)}, bf16[128,512]{1,0:T(8,128)(2,1)S(1)}, u32[]{:S(2)}, u32[]{:S(2)}) collective-permute-start(bf16[128,512]{1,0:T(8,128)(2,1)S(1)} %copy-done.1), channel_id=1, source_target_pairs={{0,4},{4,8},{8,12},{12,16},{16,20},{20,24},{24,28},{28,32},{32,36}... | collective-permute-start | bytes 393224 | tf_op jit(solution)/shard_map/ppermute | solution.py:33
  25.6 13.7 %collective-permute-start.1 = (bf16[128,512]{1,0:T(8,128)(2,1)S(1)}, bf16[128,512]{1,0:T(8,128)(2,1)S(1)}, u32[]{:S(2)}, u32[]{:S(2)}) collective-permute-start(bf16[128,512]{1,0:T(8,128)(2,1)S(1)} %copy-done.1), channel_id=1, source_target_pairs={{4,0},{8,4},{12,8},{16,12},{20,16},{24,20},{28,24},{32,28},{36,32}... | collective-permute-start | bytes 393224 | tf_op jit(solution)/shard_map/ppermute | solution.py:34
  34.1 8.6 %copy-start.13 = (s32[1,1,12]{2,1,0:T(1,128)S(1)}, s32[1,1,12]{2,1,0:T(1,128)}, u32[]{:S(2)}) copy-start(s32[1,1,12]{2,1,0:T(1,128)} %param.15) | copy-start | bytes 148
  35.8 10.3 %all-to-all-start = ((bf16[128,8,64]{0,2,1:T(8,128)(2,1)}), bf16[128,8,64]{0,2,1:T(8,128)(2,1)S(1)}, u32[]{:S(2)}, u32[]{:S(2)}) async-start(bf16[128,8,64]{0,2,1:T(8,128)(2,1)} %bitcast.14), calls=%async_computation | async-start | bytes 262144 | tf_op jit(solution)/shard_map/all_to_all | solution.py:138
  39.3 12.4 %collective-permute-start.2 = (bf16[384,512]{1,0:T(8,128)(2,1)S(1)}, bf16[384,512]{1,0:T(8,128)(2,1)S(1)}, u32[]{:S(2)}, u32[]{:S(2)}) collective-permute-start(bf16[384,512]{1,0:T(8,128)(2,1)S(1)} %constant_dynamic-update-slice_fusion), channel_id=1, source_target_pairs={{0,1},{1,2},{2,3},{3,0},{4,5},{5,6},{6,7},{7,4},{8,9},{9,10},{10,1... | collective-permute-start | bytes 1179656 | tf_op jit(solution)/shard_map/ppermute | solution.py:118
  39.7 13.0 %collective-permute-start.3 = (bf16[384,512]{1,0:T(8,128)(2,1)S(1)}, bf16[384,512]{1,0:T(8,128)(2,1)}, u32[]{:S(2)}, u32[]{:S(2)}) collective-permute-start(bf16[384,512]{1,0:T(8,128)(2,1)S(1)} %constant_dynamic-update-slice_fusion), channel_id=1, source_target_pairs={{0,2},{1,3},{2,0},{3,1},{4,6},{5,7},{6,4},{7,5},{8,10},{9,11},{10,... | collective-permute-start | bytes 1179656 | tf_op jit(solution)/shard_map/ppermute | solution.py:118
  41.4 17.2 %collective-permute-start.4 = (bf16[384,512]{1,0:T(8,128)(2,1)S(1)}, bf16[384,512]{1,0:T(8,128)(2,1)S(1)}, u32[]{:S(2)}, u32[]{:S(2)}) collective-permute-start(bf16[384,512]{1,0:T(8,128)(2,1)S(1)} %constant_dynamic-update-slice_fusion), channel_id=1, source_target_pairs={{0,3},{1,0},{2,1},{3,2},{4,7},{5,4},{6,5},{7,6},{8,11},{9,8},{10,9... | collective-permute-start | bytes 1179656 | tf_op jit(solution)/shard_map/ppermute | solution.py:118
  51.7 7.0 %copy-start.6 = (bf16[384,512]{1,0:T(8,128)(2,1)}, bf16[384,512]{1,0:T(8,128)(2,1)S(1)}, u32[]{:S(2)}) copy-start(bf16[384,512]{1,0:T(8,128)(2,1)S(1)} %collective-permute-done.2) | copy-start | bytes 1179652
  58.6 0.8 copy-start.7
  62.2 4.8 %copy-start.8 = (bf16[128,12,128]{0,2,1:T(8,128)(2,1)S(1)}, bf16[128,12,128]{0,2,1:T(8,128)(2,1)}, u32[]{:S(2)}) copy-start(bf16[128,12,128]{0,2,1:T(8,128)(2,1)} %copy.36) | copy-start | bytes 1179652
  66.9 2.2 %copy-start.2 = (bf16[1024,512]{1,0:T(8,128)(2,1)S(1)}, bf16[1024,512]{1,0:T(8,128)(2,1)}, u32[]{:S(2)}) copy-start(bf16[1024,512]{1,0:T(8,128)(2,1)} %param.22) | copy-start | bytes 3145732
  161.1 7.8 %copy-start.10 = (s32[8]{0:T(128)S(1)}, s32[8]{0:T(128)}, u32[]{:S(2)}) copy-start(s32[8]{0:T(128)} %constant.88) | copy-start | bytes 100
  161.1 14.5 %copy-start.5 = (bf16[512,512]{1,0:T(8,128)(2,1)S(1)}, bf16[512,512]{1,0:T(8,128)(2,1)}, u32[]{:S(2)}) copy-start(bf16[512,512]{1,0:T(8,128)(2,1)} %param.20) | copy-start | bytes 1572868
  162.4 13.6 %copy-start.9 = (f32[512]{0:T(512)S(1)}, f32[512]{0:T(512)}, u32[]{:S(2)}) copy-start(f32[512]{0:T(512)} %param.24) | copy-start | bytes 6148
  164.6 10.4 %all-to-all-start.2 = ((bf16[8,128,64]{1,2,0:T(8,128)(2,1)}), bf16[8,128,64]{1,2,0:T(8,128)(2,1)S(1)}, u32[]{:S(2)}, u32[]{:S(2)}) async-start(bf16[8,128,64]{1,2,0:T(8,128)(2,1)} %copy.48), calls=%async_computation.2 | async-start | bytes 262144 | tf_op jit(solution)/shard_map/all_to_all | solution.py:164
Sparse Core Ops, SparseCore 0:
  23.4 97.6 all-gather.1

commit v11 on v10

--- a/solution.py
+++ b/solution.py
@@ -10,9 +10,7 @@
 
 NUM_SUBSPACES = 8
 SUBSPACE_WIDTH = 64
-KEY_BLOCK = 8192
 KEY_STEP = 2048
-QUERY_STEP = 1024
 
 norm_eps = 1e-06
 
@@ -45,49 +43,85 @@
     return scaled.reshape(rows, -1).astype(jnp.bfloat16)
 
 
-def attention_kernel(q_ref, kv_ref, o_ref):
-    @pl.when(pl.program_id(0) == 0)
-    def _():
-        o_ref[...] = jnp.zeros_like(o_ref)
-
-    q_step = min(QUERY_STEP, q_ref.shape[0])
-    k_step = min(KEY_STEP, kv_ref.shape[0])
-    q_count = q_ref.shape[0] // q_step
-    k_count = kv_ref.shape[0] // k_step
+def accumulate(q_ref, block, o_ref):
+    step = min(KEY_STEP, block.shape[0])
 
     def body(turn, carry):
-        rows = pl.ds(pl.multiple_of((turn // k_count) * q_step, q_step), q_step)
-        keys = pl.ds(pl.multiple_of((turn % k_count) * k_step, k_step), k_step)
-        block = kv_ref[keys, :]
+        keys = pl.ds(pl.multiple_of(turn * step, step), step)
+        part = block[keys, :]
         scores = lax.dot_general(
-            q_ref[rows, :], block, (((1,), (1,)), ((), ())), preferred_element_type=jnp.float32
+            q_ref[...], part, (((1,), (1,)), ((), ())), preferred_element_type=jnp.float32
         )
         weights = jnp.exp(scores).astype(jnp.bfloat16)
-        lane = lax.broadcasted_iota(jnp.int32, block.shape, 1)
-        widened = jnp.where(lane < SUBSPACE_WIDTH, jnp.ones_like(block), block)
-        o_ref[rows, :] += jnp.dot(weights, widened, preferred_element_type=jnp.float32)
+        lane = lax.broadcasted_iota(jnp.int32, part.shape, 1)
+        widened = jnp.where(lane < SUBSPACE_WIDTH, jnp.ones_like(part), part)
+        o_ref[...] += jnp.dot(weights, widened, preferred_element_type=jnp.float32)
         return carry
 
-    lax.fori_loop(0, q_count * k_count, body, 0)
-
-
-def attend(padded_queries, key_values):
+    lax.fori_loop(0, block.shape[0] // step, body, 0)
+
+
+def ring_kernel(q_ref, kv_ref, o_ref, slots, send_sem, recv_sem):
+    positions = lax.axis_size(ROW)
+    me = lax.axis_index(ROW)
+    column = lax.axis_index(COLUMN)
+    pair = lax.axis_index(PAIR)
+    member = lax.axis_index("head")
+    offsets = [1, positions - 1] + list(range(2, positions - 1))
+
+    def copy_to(offset):
+        target = lax.rem(me + offset, positions)
+        return pltpu.make_async_remote_copy(
+            src_ref=kv_ref,
+            dst_ref=slots.at[me],
+            send_sem=send_sem.at[offset],
+            recv_sem=recv_sem.at[me],
+            device_id=(target, column, pair, member),
+            device_id_type=pl.DeviceIdType.MESH,
+        )
+
+    def arrival(offset):
+        source = lax.rem(me - offset + positions, positions)
+        return source, pltpu.make_async_remote_copy(
+            src_ref=kv_ref,
+            dst_ref=slots.at[source],
+            send_sem=send_sem.at[offset],
+            recv_sem=recv_sem.at[source],
+            device_id=(source, column, pair, member),
+            device_id_type=pl.DeviceIdType.MESH,
+        )
+
+    for offset in offsets:
+        copy_to(offset).start()
+    o_ref[...] = jnp.zeros_like(o_ref)
+    accumulate(q_ref, kv_ref, o_ref)
+    for offset in offsets:
+        source, landing = arrival(offset)
+        landing.wait_recv()
+        accumulate(q_ref, slots.at[source], o_ref)
+    for offset in offsets:
+        copy_to(offset).wait_send()
+
+
+def ring_attend(padded_queries, key_values):
     rows, width = padded_queries.shape
-    keys = key_values.shape[0]
-    block = min(KEY_BLOCK, keys)
-    flops = 4 * rows * keys * width
+    positions = lax.axis_size(ROW)
+    keys = positions * key_values.shape[0]
     return pl.pallas_call(
-        attention_kernel,
-        grid=(keys // block,),
-        in_specs=[
-            pl.BlockSpec((rows, width), lambda j: (0, 0)),
-            pl.BlockSpec((block, width), lambda j: (j, 0)),
+        ring_kernel,
+        in_specs=[pl.BlockSpec(memory_space=pltpu.VMEM)] * 2,
+        out_specs=pl.BlockSpec(memory_space=pltpu.VMEM),
+        out_shape=jax.ShapeDtypeStruct((rows, width), jnp.float32),
+        scratch_shapes=[
+            pltpu.VMEM((positions,) + key_values.shape, key_values.dtype),
+            pltpu.SemaphoreType.DMA((positions,)),
+            pltpu.SemaphoreType.DMA((positions,)),
         ],
-        out_specs=pl.BlockSpec((rows, width), lambda j: (0, 0)),
-        out_shape=jax.ShapeDtypeStruct((rows, width), jnp.float32),
-        compiler_params=pltpu.CompilerParams(dimension_semantics=("arbitrary",)),
+        compiler_params=pltpu.CompilerParams(has_side_effects=True),
         cost_estimate=pl.CostEstimate(
-            flops=flops, transcendentals=rows * keys, bytes_accessed=2 * keys * width + 6 * rows * width
+            flops=4 * rows * keys * width,
+            transcendentals=rows * keys,
+            bytes_accessed=2 * keys * width + 6 * rows * width,
         ),
     )(padded_queries, key_values)
 
@@ -140,7 +174,7 @@
         )
 
     key_values = to_members((keys_all, values_all))
-    kv_in = lax.all_gather(key_values, (COLUMN, ROW), axis=0, tiled=True)
+    kv_in = lax.all_gather(key_values, COLUMN, axis=0, tiled=True)
     queries = head_norm(
         jnp.dot(vertex_embeddings, asking_projector, preferred_element_type=jnp.float32),
         asking_vector_multiplier,
@@ -159,7 +193,7 @@
 
     local_term, head_queries = lax.optimization_barrier((local_term, head_queries))
     padded_queries = jnp.concatenate([head_queries, jnp.zeros_like(head_queries)], axis=1)
-    totals = attend(padded_queries, kv_in)
+    totals = ring_attend(padded_queries, kv_in)
     merged = (totals[:, SUBSPACE_WIDTH:] / totals[:, :1]).astype(jnp.bfloat16)
     back = lax.all_to_all(merged, GROUP, split_axis=0, concat_axis=1, tiled=True)
     node_heads = back.reshape(block_len, members, SUBSPACE_WIDTH)[:, jnp.array(member_of)]

time: 186 us -> 227 us (1.22)
  Pallas kernels: 40 us -> 135 us
  waiting for transfers between devices: 69.3 us -> 18.4 us
    pallas_call x1, Pallas kernels: 40 us -> 135 us  [ring_attend(): pl.pallas_call(ring_kernel, in_specs=[pl.BlockSpec(memory_space=pltpu.VME...]
    all_gather x1, waiting for transfers between devices: 50.8 us -> 0.01 us  [shards(): kv_in = lax.all_gather(key_values, COLUMN, axis=0, tiled=True)]
  transfers between devices with their start and end apart: 8 -> 8, of which waited for: 5 -> 4; matrix products, arithmetic and copies ran while one was open for 9% -> 7% of each run, Pallas kernels for 0% -> 0%
where the time goes in v11:
time: 227 us
  Pallas kernels  135 us (59%)
  starting transfers between devices  20.6 us (9%)
  waiting for transfers between devices  18.4 us (8%)
  local copies, waits for them, and re-layouts  17.6 us (8%)
  between operations  13.8 us (6%)
  blocking collectives  11.8 us (5%)
  matrix products  4.73 us (2%)
  other arithmetic  4.69 us (2%)
    pallas_call x1, Pallas kernels, ring_attend(): pl.pallas_call(ring_kernel, in_specs=[pl.BlockSpec(memory_space=pltpu.VME...  135 us
    ppermute x3, waiting for transfers between devices, shards(): gathered.append(lax.ppermute(halo_rows, 'head', pairs))  12.3 us
    all_to_all x1, blocking collectives, to_members(): lax.all_to_all(packed.reshape(block_len, -1), GROUP, split_axis=1, concat...  11.8 us
    ppermute x1, starting transfers between devices, extended(): after = lax.ppermute(first, DOM, down)  8.08 us
    all_to_all x1, waiting for transfers between devices, shards(): lax.all_to_all(merged, GROUP, split_axis=0, concat_axis=1, tiled=True)  6.03 us
    scatter x1, local copies, waits for them, and re-layouts, shards(): jnp.zeros_like(stacked).at[order].set(stacked)  4.72 us
  transfers between devices with their start and end apart: 8, of which 4 were waited for; matrix products, arithmetic and copies ran while one was open for 7% of the time, Pallas kernels for 0%

profile of v11, /device:TPU:4, one launch (start us, length us, event | category | flops | bytes accessed | tf_op | source)
XLA Modules:
  0.0 226.8 jit_solution(14116715374892716619)
XLA Ops:
  6.5 0.8 maximum_reduce_fusion
  7.4 0.1 copy.35
  7.6 1.4 fusion.12
  9.0 0.1 copy.41
  9.2 0.1 copy.42
  9.4 0.1 copy.43
  9.5 0.2 convolution_convert_fusion
  9.8 0.1 copy.44
  10.0 0.6 gather_fusion.2
  10.6 11.8 %all_to_all.54 = bf16[128,8,128]{0,2,1:T(8,128)(2,1)S(1)} all-to-all(bf16[128,8,128]{0,2,1:T(8,128)(2,1)S(1)} %bitcast.53), channel_id=1, replica_groups=mesh['x'=4,'z'=8,'yhi'=2,'head'=4] {'yhi','head'}, dimensions={1} | all-to-all | bytes 524288 | tf_op jit(solution)/shard_map/all_to_all | solution.py:172
  22.4 0.8 copy.47
  23.2 2.3 %collective-permute-start = (bf16[128,512]{1,0:T(8,128)(2,1)S(1)}, bf16[128,512]{1,0:T(8,128)(2,1)S(1)}, u32[]{:S(2)}, u32[]{:S(2)}) collective-permute-start(bf16[128,512]{1,0:T(8,128)(2,1)S(1)} %copy-done.1), channel_id=1, source_target_pairs={{0,4},{4,8},{8,12},{12,16},{16,20},{20,24},{24,28},{28,32},{32,36}... | collective-permute-start | bytes 393224 | tf_op jit(solution)/shard_map/ppermute | solution.py:31
  25.5 8.1 %collective-permute-start.1 = (bf16[128,512]{1,0:T(8,128)(2,1)S(1)}, bf16[128,512]{1,0:T(8,128)(2,1)S(1)}, u32[]{:S(2)}, u32[]{:S(2)}) collective-permute-start(bf16[128,512]{1,0:T(8,128)(2,1)S(1)} %copy-done.1), channel_id=1, source_target_pairs={{4,0},{8,4},{12,8},{16,12},{20,16},{24,20},{28,24},{32,28},{36,32}... | collective-permute-start | bytes 393224 | tf_op jit(solution)/shard_map/ppermute | solution.py:32
  33.6 0.2 fusion.11
  33.9 0.1 copy.37
  34.1 0.1 copy.38
  34.4 0.1 copy.39
  34.5 1.2 gather_fusion.1
  35.8 3.4 %all-to-all-start = ((bf16[128,8,64]{0,2,1:T(8,128)(2,1)}), bf16[128,8,64]{0,2,1:T(8,128)(2,1)S(1)}, u32[]{:S(2)}, u32[]{:S(2)}) async-start(bf16[128,8,64]{0,2,1:T(8,128)(2,1)} %bitcast.14), calls=%async_computation | async-start | bytes 262144 | tf_op jit(solution)/shard_map/all_to_all | solution.py:172
  39.2 0.5 collective-permute-start.2
  39.7 1.7 collective-permute-start.3
  41.4 1.3 collective-permute-start.4
  42.8 0.1 copy.33
  42.9 0.1 ge.24
  43.1 0.1 copy.34
  43.3 1.7 gather_fusion
  45.0 0.1 select_bitcast_fusion
  45.1 0.9 copy.36
  46.1 0.2 copy.40
  46.2 5.4 %collective-permute-done.2 = bf16[384,512]{1,0:T(8,128)(2,1)S(1)} collective-permute-done((bf16[384,512]{1,0:T(8,128)(2,1)S(1)}, bf16[384,512]{1,0:T(8,128)(2,1)S(1)}, u32[]{:S(2)}, u32[]{:S(2)}) %collective-permute-start.2) | collective-permute-done | bytes 393248 | tf_op jit(solution)/shard_map/ppermute | solution.py:152
  51.6 1.1 collective-permute-done.3
  52.7 5.9 %collective-permute-done.4 = bf16[384,512]{1,0:T(8,128)(2,1)S(1)} collective-permute-done((bf16[384,512]{1,0:T(8,128)(2,1)S(1)}, bf16[384,512]{1,0:T(8,128)(2,1)S(1)}, u32[]{:S(2)}, u32[]{:S(2)}) %collective-permute-start.4) | collective-permute-done | bytes 393248 | tf_op jit(solution)/shard_map/ppermute | solution.py:152
  58.6 0.7 copy-done.7
  59.3 1.4 pad_maximum_fusion
  60.8 1.3 broadcast_in_dim.45
  62.0 4.7 %scatter_fusion = bf16[4,384,512]{2,1,0:T(8,128)(2,1)} fusion(bf16[4,384,512]{2,1,0:T(8,128)(2,1)} %broadcast_in_dim.45, s32[4]{0:T(128)S(1)} %fusion.10, bf16[4,384,512]{2,1,0:T(8,128)(2,1)S(1)} %pad_maximum_fusion), kind=kCustom, calls=%fused_computation.4 | custom fusion | bytes 4718608 | tf_op jit(solution)/shard_map/scatter | solution.py:155
  66.8 2.2 fusion.8
  69.0 0.3 fusion.13
  69.3 0.8 concatenate.7.q_ref
  70.1 135.2 %shard_map.136 = f32[1024,128]{1,0:T(8,128)} custom-call(bf16[1024,128]{1,0:T(8,128)(2,1)} %concatenate.7.q_ref, bf16[8192,128]{1,0:T(8,128)(2,1)} %all-gather.2.cloned.1.call-done.kv_ref), custom_call_target="tpu_custom_call" | custom-call | flops 17179869184 | bytes 9175040 | tf_op jit(solution)/shard_map/pallas_call | solution.py:110
  205.3 1.3 slice_reduce_fusion
  206.7 1.4 divide_convert_fusion
  208.1 0.8 copy.48
  208.8 3.4 %all-to-all-start.2 = ((bf16[8,128,64]{1,2,0:T(8,128)(2,1)}), bf16[8,128,64]{1,2,0:T(8,128)(2,1)S(1)}, u32[]{:S(2)}, u32[]{:S(2)}) async-start(bf16[8,128,64]{1,2,0:T(8,128)(2,1)} %copy.48), calls=%async_computation.2 | async-start | bytes 262144 | tf_op jit(solution)/shard_map/all_to_all | solution.py:198
  212.3 6.0 %all-to-all-done.2 = bf16[8,128,64]{1,2,0:T(8,128)(2,1)S(1)} async-done(((bf16[8,128,64]{1,2,0:T(8,128)(2,1)}), bf16[8,128,64]{1,2,0:T(8,128)(2,1)S(1)}, u32[]{:S(2)}, u32[]{:S(2)}) %all-to-all-start.2) | async-done | bytes 131104 | tf_op jit(solution)/shard_map/all_to_all | solution.py:198
  218.3 0.6 gather_fusion.3
  218.9 0.3 multiply_reduce_fusion
  219.2 0.8 add_convert_fusion
  (58 shorter events, 1.0 us)
Async XLA Ops:
  6.5 60.2 %copy-start = (bf16[512,1024]{1,0:T(8,128)(2,1)S(1)}, bf16[512,1024]{1,0:T(8,128)(2,1)}, u32[]{:S(2)}) copy-start(bf16[512,1024]{1,0:T(8,128)(2,1)} %param.21) | copy-start | bytes 3145732
  6.5 63.5 %all-gather.2.cloned.1.call-start = ((), (), s32[]{:S(2)}) async-start(), calls=%async_computation.3 | async-start | bytes 2359296 | tf_op jit(solution)/shard_map/all_gather | solution.py:177
  7.6 1.9 copy-start.1
  7.6 1.9 copy-start.3
  9.1 0.8 copy-start.11
  9.8 23.8 %copy-start.4 = (bf16[512,512]{1,0:T(8,128)(2,1)S(1)}, bf16[512,512]{1,0:T(8,128)(2,1)}, u32[]{:S(2)}) copy-start(bf16[512,512]{1,0:T(8,128)(2,1)} %param.17) | copy-start | bytes 1572868
  23.2 11.0 %copy-start.12 = (f32[8]{0:T(128)S(1)}, f32[8]{0:T(128)}, u32[]{:S(2)}) copy-start(f32[8]{0:T(128)} %param.23) | copy-start | bytes 100
  23.2 15.9 %collective-permute-start = (bf16[128,512]{1,0:T(8,128)(2,1)S(1)}, bf16[128,512]{1,0:T(8,128)(2,1)S(1)}, u32[]{:S(2)}, u32[]{:S(2)}) collective-permute-start(bf16[128,512]{1,0:T(8,128)(2,1)S(1)} %copy-done.1), channel_id=1, source_target_pairs={{0,4},{4,8},{8,12},{12,16},{16,20},{20,24},{24,28},{28,32},{32,36}... | collective-permute-start | bytes 393224 | tf_op jit(solution)/shard_map/ppermute | solution.py:31
  25.5 13.7 %collective-permute-start.1 = (bf16[128,512]{1,0:T(8,128)(2,1)S(1)}, bf16[128,512]{1,0:T(8,128)(2,1)S(1)}, u32[]{:S(2)}, u32[]{:S(2)}) collective-permute-start(bf16[128,512]{1,0:T(8,128)(2,1)S(1)} %copy-done.1), channel_id=1, source_target_pairs={{4,0},{8,4},{12,8},{16,12},{20,16},{24,20},{28,24},{32,28},{36,32}... | collective-permute-start | bytes 393224 | tf_op jit(solution)/shard_map/ppermute | solution.py:32
  34.1 8.6 %copy-start.13 = (s32[1,1,12]{2,1,0:T(1,128)S(1)}, s32[1,1,12]{2,1,0:T(1,128)}, u32[]{:S(2)}) copy-start(s32[1,1,12]{2,1,0:T(1,128)} %param.15) | copy-start | bytes 148
  35.8 10.3 %all-to-all-start = ((bf16[128,8,64]{0,2,1:T(8,128)(2,1)}), bf16[128,8,64]{0,2,1:T(8,128)(2,1)S(1)}, u32[]{:S(2)}, u32[]{:S(2)}) async-start(bf16[128,8,64]{0,2,1:T(8,128)(2,1)} %bitcast.14), calls=%async_computation | async-start | bytes 262144 | tf_op jit(solution)/shard_map/all_to_all | solution.py:172
  39.2 12.4 %collective-permute-start.2 = (bf16[384,512]{1,0:T(8,128)(2,1)S(1)}, bf16[384,512]{1,0:T(8,128)(2,1)S(1)}, u32[]{:S(2)}, u32[]{:S(2)}) collective-permute-start(bf16[384,512]{1,0:T(8,128)(2,1)S(1)} %constant_dynamic-update-slice_fusion), channel_id=1, source_target_pairs={{0,1},{1,2},{2,3},{3,0},{4,5},{5,6},{6,7},{7,4},{8,9},{9,10},{10,1... | collective-permute-start | bytes 1179656 | tf_op jit(solution)/shard_map/ppermute | solution.py:152
  39.7 13.0 %collective-permute-start.3 = (bf16[384,512]{1,0:T(8,128)(2,1)S(1)}, bf16[384,512]{1,0:T(8,128)(2,1)}, u32[]{:S(2)}, u32[]{:S(2)}) collective-permute-start(bf16[384,512]{1,0:T(8,128)(2,1)S(1)} %constant_dynamic-update-slice_fusion), channel_id=1, source_target_pairs={{0,2},{1,3},{2,0},{3,1},{4,6},{5,7},{6,4},{7,5},{8,10},{9,11},{10,... | collective-permute-start | bytes 1179656 | tf_op jit(solution)/shard_map/ppermute | solution.py:152
  41.4 17.2 %collective-permute-start.4 = (bf16[384,512]{1,0:T(8,128)(2,1)S(1)}, bf16[384,512]{1,0:T(8,128)(2,1)S(1)}, u32[]{:S(2)}, u32[]{:S(2)}) collective-permute-start(bf16[384,512]{1,0:T(8,128)(2,1)S(1)} %constant_dynamic-update-slice_fusion), channel_id=1, source_target_pairs={{0,3},{1,0},{2,1},{3,2},{4,7},{5,4},{6,5},{7,6},{8,11},{9,8},{10,9... | collective-permute-start | bytes 1179656 | tf_op jit(solution)/shard_map/ppermute | solution.py:152
  51.6 7.0 %copy-start.6 = (bf16[384,512]{1,0:T(8,128)(2,1)}, bf16[384,512]{1,0:T(8,128)(2,1)S(1)}, u32[]{:S(2)}) copy-start(bf16[384,512]{1,0:T(8,128)(2,1)S(1)} %collective-permute-done.2) | copy-start | bytes 1179652
  58.6 0.7 copy-start.7
  62.0 4.7 %copy-start.8 = (bf16[128,12,128]{0,2,1:T(8,128)(2,1)S(1)}, bf16[128,12,128]{0,2,1:T(8,128)(2,1)}, u32[]{:S(2)}) copy-start(bf16[128,12,128]{0,2,1:T(8,128)(2,1)} %copy.36) | copy-start | bytes 1179652
  66.8 2.2 copy-start.2
  205.3 6.9 %copy-start.10 = (s32[8]{0:T(128)S(1)}, s32[8]{0:T(128)}, u32[]{:S(2)}) copy-start(s32[8]{0:T(128)} %constant.88) | copy-start | bytes 100
  205.3 13.5 %copy-start.5 = (bf16[512,512]{1,0:T(8,128)(2,1)S(1)}, bf16[512,512]{1,0:T(8,128)(2,1)}, u32[]{:S(2)}) copy-start(bf16[512,512]{1,0:T(8,128)(2,1)} %param.20) | copy-start | bytes 1572868
  206.7 12.6 %copy-start.9 = (f32[512]{0:T(512)S(1)}, f32[512]{0:T(512)}, u32[]{:S(2)}) copy-start(f32[512]{0:T(512)} %param.24) | copy-start | bytes 6148
  208.8 9.4 %all-to-all-start.2 = ((bf16[8,128,64]{1,2,0:T(8,128)(2,1)}), bf16[8,128,64]{1,2,0:T(8,128)(2,1)S(1)}, u32[]{:S(2)}, u32[]{:S(2)}) async-start(bf16[8,128,64]{1,2,0:T(8,128)(2,1)} %copy.48), calls=%async_computation.2 | async-start | bytes 262144 | tf_op jit(solution)/shard_map/all_to_all | solution.py:198
Sparse Core Ops, SparseCore 0:
  23.4 42.5 all-gather.1

commit v12 on v10

--- a/solution.py
+++ b/solution.py
@@ -45,10 +45,10 @@
     return scaled.reshape(rows, -1).astype(jnp.bfloat16)
 
 
-def attention_kernel(q_ref, kv_ref, o_ref):
+def attention_kernel(q_ref, kv_ref, o_ref, acc_ref):
     @pl.when(pl.program_id(0) == 0)
     def _():
-        o_ref[...] = jnp.zeros_like(o_ref)
+        acc_ref[...] = jnp.zeros_like(acc_ref)
 
     q_step = min(QUERY_STEP, q_ref.shape[0])
     k_step = min(KEY_STEP, kv_ref.shape[0])
@@ -65,10 +65,15 @@
         weights = jnp.exp(scores).astype(jnp.bfloat16)
         lane = lax.broadcasted_iota(jnp.int32, block.shape, 1)
         widened = jnp.where(lane < SUBSPACE_WIDTH, jnp.ones_like(block), block)
-        o_ref[rows, :] += jnp.dot(weights, widened, preferred_element_type=jnp.float32)
+        acc_ref[rows, :] += jnp.dot(weights, widened, preferred_element_type=jnp.float32)
         return carry
 
     lax.fori_loop(0, q_count * k_count, body, 0)
+
+    @pl.when(pl.program_id(0) == pl.num_programs(0) - 1)
+    def _():
+        totals = acc_ref[...]
+        o_ref[...] = (totals[:, SUBSPACE_WIDTH:] / totals[:, :1]).astype(o_ref.dtype)
 
 
 def attend(padded_queries, key_values):
@@ -83,8 +88,9 @@
             pl.BlockSpec((rows, width), lambda j: (0, 0)),
             pl.BlockSpec((block, width), lambda j: (j, 0)),
         ],
-        out_specs=pl.BlockSpec((rows, width), lambda j: (0, 0)),
-        out_shape=jax.ShapeDtypeStruct((rows, width), jnp.float32),
+        out_specs=pl.BlockSpec((rows, SUBSPACE_WIDTH), lambda j: (0, 0)),
+        out_shape=jax.ShapeDtypeStruct((rows, SUBSPACE_WIDTH), jnp.bfloat16),
+        scratch_shapes=[pltpu.VMEM((rows, width), jnp.float32)],
         compiler_params=pltpu.CompilerParams(dimension_semantics=("arbitrary",)),
         cost_estimate=pl.CostEstimate(
             flops=flops, transcendentals=rows * keys, bytes_accessed=2 * keys * width + 6 * rows * width
@@ -159,8 +165,7 @@
 
     local_term, head_queries = lax.optimization_barrier((local_term, head_queries))
     padded_queries = jnp.concatenate([head_queries, jnp.zeros_like(head_queries)], axis=1)
-    totals = attend(padded_queries, kv_in)
-    merged = (totals[:, SUBSPACE_WIDTH:] / totals[:, :1]).astype(jnp.bfloat16)
+    merged = attend(padded_queries, kv_in)
     back = lax.all_to_all(merged, GROUP, split_axis=0, concat_axis=1, tiled=True)
     node_heads = back.reshape(block_len, members, SUBSPACE_WIDTH)[:, jnp.array(member_of)]
     node_heads = node_heads.reshape(block_len, -1)

time: 186 us -> 185 us (level)
  local copies, waits for them, and re-layouts: 17.8 us -> 15.5 us
  waiting for transfers between devices: 69.3 us -> 71.2 us
  transfers between devices with their start and end apart: 8 -> 8, of which waited for: 5 -> 6; matrix products, arithmetic and copies ran while one was open for 9% -> 8% of each run, Pallas kernels for 0% -> 0%
where the time goes in v12:
time: 185 us; the launch traced here: 182 us
  waiting for transfers between devices  71.2 us (38%)
  Pallas kernels  40.2 us (22%)
  starting transfers between devices  21.5 us (12%)
  local copies, waits for them, and re-layouts  15.5 us (8%)
  between operations  13.8 us (7%)
  blocking collectives  11.8 us (6%)
  matrix products  4.73 us (3%)
  other arithmetic  3.31 us (2%)
    all_gather x1, waiting for transfers between devices, shards(): kv_in = lax.all_gather(key_values, (COLUMN, ROW), axis=0, tiled=True)  51.7 us
    pallas_call x1, Pallas kernels, attend(): pl.pallas_call(attention_kernel, grid=(keys // block,), in_specs=[pl.Bloc...  40.2 us
    ppermute x3, waiting for transfers between devices, shards(): gathered.append(lax.ppermute(halo_rows, 'head', pairs))  12.8 us
    all_to_all x1, blocking collectives, to_members(): lax.all_to_all(packed.reshape(block_len, -1), GROUP, split_axis=1, concat...  11.8 us
    ppermute x1, starting transfers between devices, extended(): after = lax.ppermute(first, DOM, down)  8.08 us
    all_to_all x1, waiting for transfers between devices, shards(): lax.all_to_all(merged, GROUP, split_axis=0, concat_axis=1, tiled=True)  6.12 us
    scatter x1, local copies, waits for them, and re-layouts, shards(): jnp.zeros_like(stacked).at[order].set(stacked)  4.72 us
    all_to_all x1, starting transfers between devices, shards(): lax.all_to_all(merged, GROUP, split_axis=0, concat_axis=1, tiled=True)  4.3 us
  transfers between devices with their start and end apart: 8, of which 6 were waited for; matrix products, arithmetic and copies ran while one was open for 8% of the time, Pallas kernels for 0%

profile of v12, /device:TPU:4, one launch (start us, length us, event | category | flops | bytes accessed | tf_op | source)
XLA Modules:
  0.0 182.0 jit_solution(3877713266580032156)
XLA Ops:
  6.5 0.8 maximum_reduce_fusion
  7.4 0.1 copy.35
  7.6 1.4 fusion.12
  9.0 0.1 copy.41
  9.2 0.1 copy.42
  9.4 0.1 copy.43
  9.5 0.2 convolution_convert_fusion
  9.8 0.1 copy.44
  10.0 0.6 gather_fusion.2
  10.6 11.8 %all_to_all.54 = bf16[128,8,128]{0,2,1:T(8,128)(2,1)S(1)} all-to-all(bf16[128,8,128]{0,2,1:T(8,128)(2,1)S(1)} %bitcast.53), channel_id=1, replica_groups=mesh['x'=4,'z'=8,'yhi'=2,'head'=4] {'yhi','head'}, dimensions={1} | all-to-all | bytes 524288 | tf_op jit(solution)/shard_map/all_to_all | solution.py:144
  22.4 0.9 copy.47
  23.2 2.3 %collective-permute-start = (bf16[128,512]{1,0:T(8,128)(2,1)S(1)}, bf16[128,512]{1,0:T(8,128)(2,1)S(1)}, u32[]{:S(2)}, u32[]{:S(2)}) collective-permute-start(bf16[128,512]{1,0:T(8,128)(2,1)S(1)} %copy-done.1), channel_id=1, source_target_pairs={{0,4},{4,8},{8,12},{12,16},{16,20},{20,24},{24,28},{28,32},{32,36}... | collective-permute-start | bytes 393224 | tf_op jit(solution)/shard_map/ppermute | solution.py:33
  25.5 8.1 %collective-permute-start.1 = (bf16[128,512]{1,0:T(8,128)(2,1)S(1)}, bf16[128,512]{1,0:T(8,128)(2,1)S(1)}, u32[]{:S(2)}, u32[]{:S(2)}) collective-permute-start(bf16[128,512]{1,0:T(8,128)(2,1)S(1)} %copy-done.1), channel_id=1, source_target_pairs={{4,0},{8,4},{12,8},{16,12},{20,16},{24,20},{28,24},{32,28},{36,32}... | collective-permute-start | bytes 393224 | tf_op jit(solution)/shard_map/ppermute | solution.py:34
  33.6 0.2 fusion.11
  33.9 0.1 copy.37
  34.1 0.1 copy.38
  34.4 0.1 copy.39
  34.6 1.2 gather_fusion.1
  35.8 3.4 %all-to-all-start = ((bf16[128,8,64]{0,2,1:T(8,128)(2,1)}), bf16[128,8,64]{0,2,1:T(8,128)(2,1)S(1)}, u32[]{:S(2)}, u32[]{:S(2)}) async-start(bf16[128,8,64]{0,2,1:T(8,128)(2,1)} %bitcast.14), calls=%async_computation | async-start | bytes 262144 | tf_op jit(solution)/shard_map/all_to_all | solution.py:144
  39.3 0.5 collective-permute-start.2
  39.7 1.7 collective-permute-start.3
  41.4 1.3 collective-permute-start.4
  42.8 0.1 copy.33
  42.9 0.1 ge.24
  43.1 0.1 copy.34
  43.2 0.1 le.19
  43.3 0.6 gather_fusion
  43.9 0.1 select_bitcast_fusion
  44.1 0.9 copy.36
  45.0 0.6 all-to-all-done
  45.6 0.2 copy.40
  45.8 5.9 %collective-permute-done.2 = bf16[384,512]{1,0:T(8,128)(2,1)S(1)} collective-permute-done((bf16[384,512]{1,0:T(8,128)(2,1)S(1)}, bf16[384,512]{1,0:T(8,128)(2,1)S(1)}, u32[]{:S(2)}, u32[]{:S(2)}) %collective-permute-start.2) | collective-permute-done | bytes 393248 | tf_op jit(solution)/shard_map/ppermute | solution.py:124
  51.7 1.1 collective-permute-done.3
  52.7 5.9 %collective-permute-done.4 = bf16[384,512]{1,0:T(8,128)(2,1)} collective-permute-done((bf16[384,512]{1,0:T(8,128)(2,1)S(1)}, bf16[384,512]{1,0:T(8,128)(2,1)}, u32[]{:S(2)}, u32[]{:S(2)}) %collective-permute-start.4) | collective-permute-done | bytes 393248 | tf_op jit(solution)/shard_map/ppermute | solution.py:124
  58.6 1.4 pad_maximum_fusion
  60.0 1.3 broadcast_in_dim.45
  61.4 4.7 %scatter_fusion = bf16[4,384,512]{2,1,0:T(8,128)(2,1)} fusion(bf16[4,384,512]{2,1,0:T(8,128)(2,1)} %broadcast_in_dim.45, s32[4]{0:T(128)S(1)} %fusion.10, bf16[4,384,512]{2,1,0:T(8,128)(2,1)S(1)} %pad_maximum_fusion), kind=kCustom, calls=%fused_computation.4 | custom fusion | bytes 4718608 | tf_op jit(solution)/shard_map/scatter | solution.py:127
  66.1 2.2 %fusion.8 = bf16[128,1024]{1,0:T(8,128)(2,1)S(1)} fusion(bf16[512,1024]{1,0:T(8,128)(2,1)S(1)} %copy-done, bf16[128,1536]{0,1:T(8,128)(2,1)S(1)} %bitcast.67, bf16[1536,512]{1,0:T(8,128)(2,1)} %bitcast.52), kind=kOutput, calls=%fused_computation.17 | convolution fusion | flops 336789504 | bytes 3276800 | tf_op jit(solution)/shard_map/dot_general | solution.py:162
  68.3 0.3 fusion.13
  68.6 0.8 concatenate.7.q_ref
  69.4 51.7 %all-gather.2.cloned.1.call-done.kv_ref = bf16[32768,128]{1,0:T(8,128)(2,1)} async-done(((bf16[1024,128]{1,0:T(8,128)(2,1)}), bf16[32768,128]{1,0:T(8,128)(2,1)}) %all-gather.2.cloned.1.call-update) | async-done | bytes 8388624 | tf_op jit(solution)/shard_map/all_gather | solution.py:149
  121.1 40.2 %shard_map.136 = bf16[1024,64]{1,0:T(8,128)(2,1)} custom-call(bf16[1024,128]{1,0:T(8,128)(2,1)} %concatenate.7.q_ref, bf16[32768,128]{1,0:T(8,128)(2,1)} %all-gather.2.cloned.1.call-done.kv_ref), custom_call_target="tpu_custom_call" | custom-call | flops 17179869184 | bytes 9175040 | tf_op jit(solution)/shard_map/pallas_call | solution.py:84
  161.3 1.7 copy.48
  163.0 4.3 %all-to-all-start.2 = ((bf16[8,128,64]{1,2,0:T(8,128)(2,1)}), bf16[8,128,64]{1,2,0:T(8,128)(2,1)S(1)}, u32[]{:S(2)}, u32[]{:S(2)}) async-start(bf16[8,128,64]{1,2,0:T(8,128)(2,1)} %copy.48), calls=%async_computation.2 | async-start | bytes 262144 | tf_op jit(solution)/shard_map/all_to_all | solution.py:169
  167.4 6.1 %all-to-all-done.2 = bf16[8,128,64]{1,2,0:T(8,128)(2,1)S(1)} async-done(((bf16[8,128,64]{1,2,0:T(8,128)(2,1)}), bf16[8,128,64]{1,2,0:T(8,128)(2,1)S(1)}, u32[]{:S(2)}, u32[]{:S(2)}) %all-to-all-start.2) | async-done | bytes 131104 | tf_op jit(solution)/shard_map/all_to_all | solution.py:169
  173.5 0.6 gather_fusion.3
  174.1 0.3 multiply_reduce_fusion
  174.4 0.8 add_convert_fusion
  (56 shorter events, 0.9 us)
Async XLA Ops:
  6.5 59.5 %copy-start = (bf16[512,1024]{1,0:T(8,128)(2,1)S(1)}, bf16[512,1024]{1,0:T(8,128)(2,1)}, u32[]{:S(2)}) copy-start(bf16[512,1024]{1,0:T(8,128)(2,1)} %param.21) | copy-start | bytes 3145732
  6.5 114.6 %all-gather.2.cloned.1.call-start = ((), (), s32[]{:S(2)}) async-start(), calls=%async_computation.3 | async-start | bytes 8650752 | tf_op jit(solution)/shard_map/all_gather | solution.py:149
  7.6 1.9 %copy-start.1 = (bf16[128,512]{1,0:T(8,128)(2,1)S(1)}, bf16[128,512]{1,0:T(8,128)(2,1)}, u32[]{:S(2)}) copy-start(bf16[128,512]{1,0:T(8,128)(2,1)} %param.14) | copy-start | bytes 393220
  7.6 1.9 %copy-start.3 = (bf16[512,512]{1,0:T(8,128)(2,1)S(1)}, bf16[512,512]{1,0:T(8,128)(2,1)}, u32[]{:S(2)}) copy-start(bf16[512,512]{1,0:T(8,128)(2,1)} %param.19) | copy-start | bytes 1572868
  9.1 0.8 copy-start.11
  9.8 23.9 %copy-start.4 = (bf16[512,512]{1,0:T(8,128)(2,1)S(1)}, bf16[512,512]{1,0:T(8,128)(2,1)}, u32[]{:S(2)}) copy-start(bf16[512,512]{1,0:T(8,128)(2,1)} %param.17) | copy-start | bytes 1572868
  23.2 11.0 %copy-start.12 = (f32[8]{0:T(128)S(1)}, f32[8]{0:T(128)}, u32[]{:S(2)}) copy-start(f32[8]{0:T(128)} %param.23) | copy-start | bytes 100
  23.2 15.9 %collective-permute-start = (bf16[128,512]{1,0:T(8,128)(2,1)S(1)}, bf16[128,512]{1,0:T(8,128)(2,1)S(1)}, u32[]{:S(2)}, u32[]{:S(2)}) collective-permute-start(bf16[128,512]{1,0:T(8,128)(2,1)S(1)} %copy-done.1), channel_id=1, source_target_pairs={{0,4},{4,8},{8,12},{12,16},{16,20},{20,24},{24,28},{28,32},{32,36}... | collective-permute-start | bytes 393224 | tf_op jit(solution)/shard_map/ppermute | solution.py:33
  25.5 13.7 %collective-permute-start.1 = (bf16[128,512]{1,0:T(8,128)(2,1)S(1)}, bf16[128,512]{1,0:T(8,128)(2,1)S(1)}, u32[]{:S(2)}, u32[]{:S(2)}) collective-permute-start(bf16[128,512]{1,0:T(8,128)(2,1)S(1)} %copy-done.1), channel_id=1, source_target_pairs={{4,0},{8,4},{12,8},{16,12},{20,16},{24,20},{28,24},{32,28},{36,32}... | collective-permute-start | bytes 393224 | tf_op jit(solution)/shard_map/ppermute | solution.py:34
  34.1 8.6 %copy-start.13 = (s32[1,1,12]{2,1,0:T(1,128)S(1)}, s32[1,1,12]{2,1,0:T(1,128)}, u32[]{:S(2)}) copy-start(s32[1,1,12]{2,1,0:T(1,128)} %param.15) | copy-start | bytes 148
  34.1 9.2 %copy-start.8 = (bf16[16,128,128]{2,1,0:T(8,128)(2,1)S(1)}, bf16[16,128,128]{2,1,0:T(8,128)(2,1)}, u32[]{:S(2)}) copy-start(bf16[16,128,128]{2,1,0:T(8,128)(2,1)} %param.16) | copy-start | bytes 1572868
  35.8 9.8 %all-to-all-start = ((bf16[128,8,64]{0,2,1:T(8,128)(2,1)}), bf16[128,8,64]{0,2,1:T(8,128)(2,1)S(1)}, u32[]{:S(2)}, u32[]{:S(2)}) async-start(bf16[128,8,64]{0,2,1:T(8,128)(2,1)} %bitcast.14), calls=%async_computation | async-start | bytes 262144 | tf_op jit(solution)/shard_map/all_to_all | solution.py:144
  39.3 12.4 %collective-permute-start.2 = (bf16[384,512]{1,0:T(8,128)(2,1)S(1)}, bf16[384,512]{1,0:T(8,128)(2,1)S(1)}, u32[]{:S(2)}, u32[]{:S(2)}) collective-permute-start(bf16[384,512]{1,0:T(8,128)(2,1)S(1)} %constant_dynamic-update-slice_fusion), channel_id=1, source_target_pairs={{0,1},{1,2},{2,3},{3,0},{4,5},{5,6},{6,7},{7,4},{8,9},{9,10},{10,1... | collective-permute-start | bytes 1179656 | tf_op jit(solution)/shard_map/ppermute | solution.py:124
  39.7 13.0 %collective-permute-start.3 = (bf16[384,512]{1,0:T(8,128)(2,1)S(1)}, bf16[384,512]{1,0:T(8,128)(2,1)}, u32[]{:S(2)}, u32[]{:S(2)}) collective-permute-start(bf16[384,512]{1,0:T(8,128)(2,1)S(1)} %constant_dynamic-update-slice_fusion), channel_id=1, source_target_pairs={{0,2},{1,3},{2,0},{3,1},{4,6},{5,7},{6,4},{7,5},{8,10},{9,11},{10,... | collective-permute-start | bytes 1179656 | tf_op jit(solution)/shard_map/ppermute | solution.py:124
  41.4 17.2 %collective-permute-start.4 = (bf16[384,512]{1,0:T(8,128)(2,1)S(1)}, bf16[384,512]{1,0:T(8,128)(2,1)}, u32[]{:S(2)}, u32[]{:S(2)}) collective-permute-start(bf16[384,512]{1,0:T(8,128)(2,1)S(1)} %constant_dynamic-update-slice_fusion), channel_id=1, source_target_pairs={{0,3},{1,0},{2,1},{3,2},{4,7},{5,4},{6,5},{7,6},{8,11},{9,8},{10,9... | collective-permute-start | bytes 1179656 | tf_op jit(solution)/shard_map/ppermute | solution.py:124
  51.7 6.9 %copy-start.6 = (bf16[384,512]{1,0:T(8,128)(2,1)}, bf16[384,512]{1,0:T(8,128)(2,1)S(1)}, u32[]{:S(2)}) copy-start(bf16[384,512]{1,0:T(8,128)(2,1)S(1)} %collective-permute-done.2) | copy-start | bytes 1179652
  61.4 4.7 %copy-start.7 = (bf16[128,12,128]{0,2,1:T(8,128)(2,1)S(1)}, bf16[128,12,128]{0,2,1:T(8,128)(2,1)}, u32[]{:S(2)}) copy-start(bf16[128,12,128]{0,2,1:T(8,128)(2,1)} %copy.36) | copy-start | bytes 1179652
  66.1 2.2 %copy-start.2 = (bf16[1024,512]{1,0:T(8,128)(2,1)S(1)}, bf16[1024,512]{1,0:T(8,128)(2,1)}, u32[]{:S(2)}) copy-start(bf16[1024,512]{1,0:T(8,128)(2,1)} %param.22) | copy-start | bytes 3145732
  69.4 97.9 %copy-start.10 = (s32[8]{0:T(128)S(1)}, s32[8]{0:T(128)}, u32[]{:S(2)}) copy-start(s32[8]{0:T(128)} %constant.88) | copy-start | bytes 100
  69.4 104.6 %copy-start.5 = (bf16[512,512]{1,0:T(8,128)(2,1)S(1)}, bf16[512,512]{1,0:T(8,128)(2,1)}, u32[]{:S(2)}) copy-start(bf16[512,512]{1,0:T(8,128)(2,1)} %param.20) | copy-start | bytes 1572868
  161.3 13.1 %copy-start.9 = (f32[512]{0:T(512)S(1)}, f32[512]{0:T(512)}, u32[]{:S(2)}) copy-start(f32[512]{0:T(512)} %param.24) | copy-start | bytes 6148
  163.0 10.4 %all-to-all-start.2 = ((bf16[8,128,64]{1,2,0:T(8,128)(2,1)}), bf16[8,128,64]{1,2,0:T(8,128)(2,1)S(1)}, u32[]{:S(2)}, u32[]{:S(2)}) async-start(bf16[8,128,64]{1,2,0:T(8,128)(2,1)} %copy.48), calls=%async_computation.2 | async-start | bytes 262144 | tf_op jit(solution)/shard_map/all_to_all | solution.py:169
Sparse Core Ops, SparseCore 0:
  23.4 97.6 all-gather.1

commit v13 on v12

--- a/solution.py
+++ b/solution.py
@@ -11,7 +11,7 @@
 NUM_SUBSPACES = 8
 SUBSPACE_WIDTH = 64
 KEY_BLOCK = 8192
-KEY_STEP = 2048
+KEY_STEP = 4096
 QUERY_STEP = 1024
 
 norm_eps = 1e-06

time: 185 us -> 183 us (0.989)
  no operation moved by 1% of the time
where the time goes in v13:
time: 183 us; the launch traced here: 181 us
  waiting for transfers between devices  71.2 us (39%)
  Pallas kernels  38.9 us (21%)
  starting transfers between devices  21.5 us (12%)
  local copies, waits for them, and re-layouts  15.5 us (8%)
  between operations  13.8 us (8%)
  blocking collectives  11.8 us (6%)
  matrix products  4.73 us (3%)
  other arithmetic  3.31 us (2%)
    all_gather x1, waiting for transfers between devices, shards(): kv_in = lax.all_gather(key_values, (COLUMN, ROW), axis=0, tiled=True)  51.7 us
    pallas_call x1, Pallas kernels, attend(): pl.pallas_call(attention_kernel, grid=(keys // block,), in_specs=[pl.Bloc...  38.9 us
    ppermute x3, waiting for transfers between devices, shards(): gathered.append(lax.ppermute(halo_rows, 'head', pairs))  12.8 us
    all_to_all x1, blocking collectives, to_members(): lax.all_to_all(packed.reshape(block_len, -1), GROUP, split_axis=1, concat...  11.8 us
    ppermute x1, starting transfers between devices, extended(): after = lax.ppermute(first, DOM, down)  8.08 us
    all_to_all x1, waiting for transfers between devices, shards(): lax.all_to_all(merged, GROUP, split_axis=0, concat_axis=1, tiled=True)  6.12 us
    scatter x1, local copies, waits for them, and re-layouts, shards(): jnp.zeros_like(stacked).at[order].set(stacked)  4.72 us
    all_to_all x1, starting transfers between devices, shards(): lax.all_to_all(merged, GROUP, split_axis=0, concat_axis=1, tiled=True)  4.29 us
  transfers between devices with their start and end apart: 8, of which 6 were waited for; matrix products, arithmetic and copies ran while one was open for 8% of the time, Pallas kernels for 0%

profile of v13, /device:TPU:4, one launch (start us, length us, event | category | flops | bytes accessed | tf_op | source)
XLA Modules:
  0.0 180.7 jit_solution(10772119263309396906)
XLA Ops:
  6.5 0.8 maximum_reduce_fusion
  7.4 0.1 copy.35
  7.6 1.4 fusion.12
  9.0 0.1 copy.41
  9.2 0.1 copy.42
  9.4 0.1 copy.43
  9.5 0.2 convolution_convert_fusion
  9.8 0.1 copy.44
  10.0 0.6 gather_fusion.2
  10.6 11.8 %all_to_all.54 = bf16[128,8,128]{0,2,1:T(8,128)(2,1)S(1)} all-to-all(bf16[128,8,128]{0,2,1:T(8,128)(2,1)S(1)} %bitcast.53), channel_id=1, replica_groups=mesh['x'=4,'z'=8,'yhi'=2,'head'=4] {'yhi','head'}, dimensions={1} | all-to-all | bytes 524288 | tf_op jit(solution)/shard_map/all_to_all | solution.py:144
  22.4 0.9 copy.47
  23.2 2.3 %collective-permute-start = (bf16[128,512]{1,0:T(8,128)(2,1)S(1)}, bf16[128,512]{1,0:T(8,128)(2,1)S(1)}, u32[]{:S(2)}, u32[]{:S(2)}) collective-permute-start(bf16[128,512]{1,0:T(8,128)(2,1)S(1)} %copy-done.1), channel_id=1, source_target_pairs={{0,4},{4,8},{8,12},{12,16},{16,20},{20,24},{24,28},{28,32},{32,36}... | collective-permute-start | bytes 393224 | tf_op jit(solution)/shard_map/ppermute | solution.py:33
  25.5 8.1 %collective-permute-start.1 = (bf16[128,512]{1,0:T(8,128)(2,1)S(1)}, bf16[128,512]{1,0:T(8,128)(2,1)S(1)}, u32[]{:S(2)}, u32[]{:S(2)}) collective-permute-start(bf16[128,512]{1,0:T(8,128)(2,1)S(1)} %copy-done.1), channel_id=1, source_target_pairs={{4,0},{8,4},{12,8},{16,12},{20,16},{24,20},{28,24},{32,28},{36,32}... | collective-permute-start | bytes 393224 | tf_op jit(solution)/shard_map/ppermute | solution.py:34
  33.6 0.2 fusion.11
  33.9 0.1 copy.37
  34.1 0.1 copy.38
  34.4 0.1 copy.39
  34.6 1.2 gather_fusion.1
  35.8 3.4 %all-to-all-start = ((bf16[128,8,64]{0,2,1:T(8,128)(2,1)}), bf16[128,8,64]{0,2,1:T(8,128)(2,1)S(1)}, u32[]{:S(2)}, u32[]{:S(2)}) async-start(bf16[128,8,64]{0,2,1:T(8,128)(2,1)} %bitcast.14), calls=%async_computation | async-start | bytes 262144 | tf_op jit(solution)/shard_map/all_to_all | solution.py:144
  39.3 0.5 collective-permute-start.2
  39.7 1.7 collective-permute-start.3
  41.4 1.3 collective-permute-start.4
  42.8 0.1 copy.33
  42.9 0.1 ge.24
  43.1 0.1 copy.34
  43.2 0.1 le.19
  43.3 0.6 gather_fusion
  43.9 0.1 select_bitcast_fusion
  44.1 0.9 copy.36
  45.0 0.6 all-to-all-done
  45.6 0.2 copy.40
  45.8 5.9 %collective-permute-done.2 = bf16[384,512]{1,0:T(8,128)(2,1)S(1)} collective-permute-done((bf16[384,512]{1,0:T(8,128)(2,1)S(1)}, bf16[384,512]{1,0:T(8,128)(2,1)S(1)}, u32[]{:S(2)}, u32[]{:S(2)}) %collective-permute-start.2) | collective-permute-done | bytes 393248 | tf_op jit(solution)/shard_map/ppermute | solution.py:124
  51.7 1.1 collective-permute-done.3
  52.7 5.9 %collective-permute-done.4 = bf16[384,512]{1,0:T(8,128)(2,1)} collective-permute-done((bf16[384,512]{1,0:T(8,128)(2,1)S(1)}, bf16[384,512]{1,0:T(8,128)(2,1)}, u32[]{:S(2)}, u32[]{:S(2)}) %collective-permute-start.4) | collective-permute-done | bytes 393248 | tf_op jit(solution)/shard_map/ppermute | solution.py:124
  58.6 1.4 pad_maximum_fusion
  60.0 1.3 broadcast_in_dim.45
  61.4 4.7 %scatter_fusion = bf16[4,384,512]{2,1,0:T(8,128)(2,1)} fusion(bf16[4,384,512]{2,1,0:T(8,128)(2,1)} %broadcast_in_dim.45, s32[4]{0:T(128)S(1)} %fusion.10, bf16[4,384,512]{2,1,0:T(8,128)(2,1)S(1)} %pad_maximum_fusion), kind=kCustom, calls=%fused_computation.4 | custom fusion | bytes 4718608 | tf_op jit(solution)/shard_map/scatter | solution.py:127
  66.1 2.2 %fusion.8 = bf16[128,1024]{1,0:T(8,128)(2,1)S(1)} fusion(bf16[512,1024]{1,0:T(8,128)(2,1)S(1)} %copy-done, bf16[128,1536]{0,1:T(8,128)(2,1)S(1)} %bitcast.67, bf16[1536,512]{1,0:T(8,128)(2,1)} %bitcast.52), kind=kOutput, calls=%fused_computation.17 | convolution fusion | flops 336789504 | bytes 3276800 | tf_op jit(solution)/shard_map/dot_general | solution.py:162
  68.3 0.3 fusion.13
  68.6 0.8 concatenate.7.q_ref
  69.4 51.7 %all-gather.2.cloned.1.call-done.kv_ref = bf16[32768,128]{1,0:T(8,128)(2,1)} async-done(((bf16[1024,128]{1,0:T(8,128)(2,1)}), bf16[32768,128]{1,0:T(8,128)(2,1)}) %all-gather.2.cloned.1.call-update) | async-done | bytes 8388624 | tf_op jit(solution)/shard_map/all_gather | solution.py:149
  121.1 38.9 %shard_map.136 = bf16[1024,64]{1,0:T(8,128)(2,1)} custom-call(bf16[1024,128]{1,0:T(8,128)(2,1)} %concatenate.7.q_ref, bf16[32768,128]{1,0:T(8,128)(2,1)} %all-gather.2.cloned.1.call-done.kv_ref), custom_call_target="tpu_custom_call" | custom-call | flops 17179869184 | bytes 9175040 | tf_op jit(solution)/shard_map/pallas_call | solution.py:84
  160.0 1.7 copy.48
  161.7 4.3 %all-to-all-start.2 = ((bf16[8,128,64]{1,2,0:T(8,128)(2,1)}), bf16[8,128,64]{1,2,0:T(8,128)(2,1)S(1)}, u32[]{:S(2)}, u32[]{:S(2)}) async-start(bf16[8,128,64]{1,2,0:T(8,128)(2,1)} %copy.48), calls=%async_computation.2 | async-start | bytes 262144 | tf_op jit(solution)/shard_map/all_to_all | solution.py:169
  166.0 6.1 %all-to-all-done.2 = bf16[8,128,64]{1,2,0:T(8,128)(2,1)S(1)} async-done(((bf16[8,128,64]{1,2,0:T(8,128)(2,1)}), bf16[8,128,64]{1,2,0:T(8,128)(2,1)S(1)}, u32[]{:S(2)}, u32[]{:S(2)}) %all-to-all-start.2) | async-done | bytes 131104 | tf_op jit(solution)/shard_map/all_to_all | solution.py:169
  172.2 0.6 gather_fusion.3
  172.7 0.3 multiply_reduce_fusion
  173.1 0.8 add_convert_fusion
  (56 shorter events, 0.9 us)
Async XLA Ops:
  6.5 59.5 %copy-start = (bf16[512,1024]{1,0:T(8,128)(2,1)S(1)}, bf16[512,1024]{1,0:T(8,128)(2,1)}, u32[]{:S(2)}) copy-start(bf16[512,1024]{1,0:T(8,128)(2,1)} %param.21) | copy-start | bytes 3145732
  6.5 114.6 %all-gather.2.cloned.1.call-start = ((), (), s32[]{:S(2)}) async-start(), calls=%async_computation.3 | async-start | bytes 8650752 | tf_op jit(solution)/shard_map/all_gather | solution.py:149
  7.6 1.9 %copy-start.1 = (bf16[128,512]{1,0:T(8,128)(2,1)S(1)}, bf16[128,512]{1,0:T(8,128)(2,1)}, u32[]{:S(2)}) copy-start(bf16[128,512]{1,0:T(8,128)(2,1)} %param.14) | copy-start | bytes 393220
  7.6 1.9 %copy-start.3 = (bf16[512,512]{1,0:T(8,128)(2,1)S(1)}, bf16[512,512]{1,0:T(8,128)(2,1)}, u32[]{:S(2)}) copy-start(bf16[512,512]{1,0:T(8,128)(2,1)} %param.19) | copy-start | bytes 1572868
  9.1 0.8 copy-start.11
  9.8 23.9 %copy-start.4 = (bf16[512,512]{1,0:T(8,128)(2,1)S(1)}, bf16[512,512]{1,0:T(8,128)(2,1)}, u32[]{:S(2)}) copy-start(bf16[512,512]{1,0:T(8,128)(2,1)} %param.17) | copy-start | bytes 1572868
  23.2 11.0 %copy-start.12 = (f32[8]{0:T(128)S(1)}, f32[8]{0:T(128)}, u32[]{:S(2)}) copy-start(f32[8]{0:T(128)} %param.23) | copy-start | bytes 100
  23.2 15.9 %collective-permute-start = (bf16[128,512]{1,0:T(8,128)(2,1)S(1)}, bf16[128,512]{1,0:T(8,128)(2,1)S(1)}, u32[]{:S(2)}, u32[]{:S(2)}) collective-permute-start(bf16[128,512]{1,0:T(8,128)(2,1)S(1)} %copy-done.1), channel_id=1, source_target_pairs={{0,4},{4,8},{8,12},{12,16},{16,20},{20,24},{24,28},{28,32},{32,36}... | collective-permute-start | bytes 393224 | tf_op jit(solution)/shard_map/ppermute | solution.py:33
  25.5 13.7 %collective-permute-start.1 = (bf16[128,512]{1,0:T(8,128)(2,1)S(1)}, bf16[128,512]{1,0:T(8,128)(2,1)S(1)}, u32[]{:S(2)}, u32[]{:S(2)}) collective-permute-start(bf16[128,512]{1,0:T(8,128)(2,1)S(1)} %copy-done.1), channel_id=1, source_target_pairs={{4,0},{8,4},{12,8},{16,12},{20,16},{24,20},{28,24},{32,28},{36,32}... | collective-permute-start | bytes 393224 | tf_op jit(solution)/shard_map/ppermute | solution.py:34
  34.1 8.6 %copy-start.13 = (s32[1,1,12]{2,1,0:T(1,128)S(1)}, s32[1,1,12]{2,1,0:T(1,128)}, u32[]{:S(2)}) copy-start(s32[1,1,12]{2,1,0:T(1,128)} %param.15) | copy-start | bytes 148
  34.1 9.2 %copy-start.8 = (bf16[16,128,128]{2,1,0:T(8,128)(2,1)S(1)}, bf16[16,128,128]{2,1,0:T(8,128)(2,1)}, u32[]{:S(2)}) copy-start(bf16[16,128,128]{2,1,0:T(8,128)(2,1)} %param.16) | copy-start | bytes 1572868
  35.8 9.8 %all-to-all-start = ((bf16[128,8,64]{0,2,1:T(8,128)(2,1)}), bf16[128,8,64]{0,2,1:T(8,128)(2,1)S(1)}, u32[]{:S(2)}, u32[]{:S(2)}) async-start(bf16[128,8,64]{0,2,1:T(8,128)(2,1)} %bitcast.14), calls=%async_computation | async-start | bytes 262144 | tf_op jit(solution)/shard_map/all_to_all | solution.py:144
  39.3 12.4 %collective-permute-start.2 = (bf16[384,512]{1,0:T(8,128)(2,1)S(1)}, bf16[384,512]{1,0:T(8,128)(2,1)S(1)}, u32[]{:S(2)}, u32[]{:S(2)}) collective-permute-start(bf16[384,512]{1,0:T(8,128)(2,1)S(1)} %constant_dynamic-update-slice_fusion), channel_id=1, source_target_pairs={{0,1},{1,2},{2,3},{3,0},{4,5},{5,6},{6,7},{7,4},{8,9},{9,10},{10,1... | collective-permute-start | bytes 1179656 | tf_op jit(solution)/shard_map/ppermute | solution.py:124
  39.7 13.0 %collective-permute-start.3 = (bf16[384,512]{1,0:T(8,128)(2,1)S(1)}, bf16[384,512]{1,0:T(8,128)(2,1)}, u32[]{:S(2)}, u32[]{:S(2)}) collective-permute-start(bf16[384,512]{1,0:T(8,128)(2,1)S(1)} %constant_dynamic-update-slice_fusion), channel_id=1, source_target_pairs={{0,2},{1,3},{2,0},{3,1},{4,6},{5,7},{6,4},{7,5},{8,10},{9,11},{10,... | collective-permute-start | bytes 1179656 | tf_op jit(solution)/shard_map/ppermute | solution.py:124
  41.4 17.2 %collective-permute-start.4 = (bf16[384,512]{1,0:T(8,128)(2,1)S(1)}, bf16[384,512]{1,0:T(8,128)(2,1)}, u32[]{:S(2)}, u32[]{:S(2)}) collective-permute-start(bf16[384,512]{1,0:T(8,128)(2,1)S(1)} %constant_dynamic-update-slice_fusion), channel_id=1, source_target_pairs={{0,3},{1,0},{2,1},{3,2},{4,7},{5,4},{6,5},{7,6},{8,11},{9,8},{10,9... | collective-permute-start | bytes 1179656 | tf_op jit(solution)/shard_map/ppermute | solution.py:124
  51.7 6.9 %copy-start.6 = (bf16[384,512]{1,0:T(8,128)(2,1)}, bf16[384,512]{1,0:T(8,128)(2,1)S(1)}, u32[]{:S(2)}) copy-start(bf16[384,512]{1,0:T(8,128)(2,1)S(1)} %collective-permute-done.2) | copy-start | bytes 1179652
  61.4 4.7 %copy-start.7 = (bf16[128,12,128]{0,2,1:T(8,128)(2,1)S(1)}, bf16[128,12,128]{0,2,1:T(8,128)(2,1)}, u32[]{:S(2)}) copy-start(bf16[128,12,128]{0,2,1:T(8,128)(2,1)} %copy.36) | copy-start | bytes 1179652
  66.1 2.2 %copy-start.2 = (bf16[1024,512]{1,0:T(8,128)(2,1)S(1)}, bf16[1024,512]{1,0:T(8,128)(2,1)}, u32[]{:S(2)}) copy-start(bf16[1024,512]{1,0:T(8,128)(2,1)} %param.22) | copy-start | bytes 3145732
  69.4 96.6 %copy-start.10 = (s32[8]{0:T(128)S(1)}, s32[8]{0:T(128)}, u32[]{:S(2)}) copy-start(s32[8]{0:T(128)} %constant.88) | copy-start | bytes 100
  69.4 103.3 %copy-start.5 = (bf16[512,512]{1,0:T(8,128)(2,1)S(1)}, bf16[512,512]{1,0:T(8,128)(2,1)}, u32[]{:S(2)}) copy-start(bf16[512,512]{1,0:T(8,128)(2,1)} %param.20) | copy-start | bytes 1572868
  160.0 13.1 %copy-start.9 = (f32[512]{0:T(512)S(1)}, f32[512]{0:T(512)}, u32[]{:S(2)}) copy-start(f32[512]{0:T(512)} %param.24) | copy-start | bytes 6148
  161.7 10.4 %all-to-all-start.2 = ((bf16[8,128,64]{1,2,0:T(8,128)(2,1)}), bf16[8,128,64]{1,2,0:T(8,128)(2,1)S(1)}, u32[]{:S(2)}, u32[]{:S(2)}) async-start(bf16[8,128,64]{1,2,0:T(8,128)(2,1)} %copy.48), calls=%async_computation.2 | async-start | bytes 262144 | tf_op jit(solution)/shard_map/all_to_all | solution.py:169
Sparse Core Ops, SparseCore 0:
  23.4 97.6 all-gather.1

commit v14 on v13

--- a/solution.py
+++ b/solution.py
@@ -96,6 +96,75 @@
             flops=flops, transcendentals=rows * keys, bytes_accessed=2 * keys * width + 6 * rows * width
         ),
     )(padded_queries, key_values)
+
+
+def return_kernel(m_ref, o_ref, landing, send_sem, recv_sem):
+    group_size = lax.axis_size("head")
+    members = lax.axis_size(PAIR) * group_size
+    me = lax.axis_index(PAIR) * group_size + lax.axis_index("head")
+    row = lax.axis_index(ROW)
+    column = lax.axis_index(COLUMN)
+    rows = o_ref.shape[1]
+
+    def device(t):
+        return (row, column, t // group_size, lax.rem(t, group_size))
+
+    barrier = pltpu.get_barrier_semaphore()
+    for shift in range(1, members):
+        pl.semaphore_signal(
+            barrier, inc=1, device_id=device(lax.rem(me + shift, members)),
+            device_id_type=pl.DeviceIdType.MESH,
+        )
+    pl.semaphore_wait(barrier, members - 1)
+
+    def copy_to(shift):
+        target = lax.rem(me + shift, members)
+        return pltpu.make_async_remote_copy(
+            src_ref=m_ref.at[pl.ds(pl.multiple_of(target * rows, rows), rows)],
+            dst_ref=landing.at[me],
+            send_sem=send_sem.at[shift],
+            recv_sem=recv_sem.at[me],
+            device_id=device(target),
+            device_id_type=pl.DeviceIdType.MESH,
+        )
+
+    def arrival(shift):
+        source = lax.rem(me - shift + members, members)
+        return source, pltpu.make_async_remote_copy(
+            src_ref=m_ref.at[pl.ds(0, rows)],
+            dst_ref=landing.at[source],
+            send_sem=send_sem.at[shift],
+            recv_sem=recv_sem.at[source],
+            device_id=device(source),
+            device_id_type=pl.DeviceIdType.MESH,
+        )
+
+    for shift in range(1, members):
+        copy_to(shift).start()
+    o_ref[me] = m_ref[pl.ds(pl.multiple_of(me * rows, rows), rows), :]
+    for shift in range(1, members):
+        source, landed = arrival(shift)
+        landed.wait_recv()
+        o_ref[source] = landing[source]
+    for shift in range(1, members):
+        copy_to(shift).wait_send()
+
+
+def return_pieces(merged, members):
+    rows = merged.shape[0] // members
+    piece = (members, rows, merged.shape[1])
+    return pl.pallas_call(
+        return_kernel,
+        in_specs=[pl.BlockSpec(memory_space=pltpu.VMEM)],
+        out_specs=pl.BlockSpec(memory_space=pltpu.VMEM),
+        out_shape=jax.ShapeDtypeStruct(piece, merged.dtype),
+        scratch_shapes=[
+            pltpu.VMEM(piece, merged.dtype),
+            pltpu.SemaphoreType.DMA((members,)),
+            pltpu.SemaphoreType.DMA((members,)),
+        ],
+        compiler_params=pltpu.CompilerParams(collective_id=0, has_side_effects=True),
+    )(merged)
 
 
 def shards(
@@ -166,8 +235,8 @@
     local_term, head_queries = lax.optimization_barrier((local_term, head_queries))
     padded_queries = jnp.concatenate([head_queries, jnp.zeros_like(head_queries)], axis=1)
     merged = attend(padded_queries, kv_in)
-    back = lax.all_to_all(merged, GROUP, split_axis=0, concat_axis=1, tiled=True)
-    node_heads = back.reshape(block_len, members, SUBSPACE_WIDTH)[:, jnp.array(member_of)]
+    back = return_pieces(merged, members)
+    node_heads = jnp.transpose(back, (1, 0, 2))[:, jnp.array(member_of)]
     node_heads = node_heads.reshape(block_len, -1)
     attended = jnp.dot(node_heads, final_projector, preferred_element_type=jnp.float32)
     normed = (

time: 183 us -> 181 us (0.989)
  Pallas kernels: 38.9 us -> 48.4 us
  waiting for transfers between devices: 71.2 us -> 64.8 us
  starting transfers between devices: 21.5 us -> 17.2 us
    pallas_call x0 -> x1, Pallas kernels: none -> 9.55 us  [return_pieces(): pl.pallas_call(return_kernel, in_specs=[pl.BlockSpec(memory_space=pltpu.V...]
    all_to_all x1 -> x0, waiting for transfers between devices: 6.12 us -> none  [shards(): lax.all_to_all(merged, GROUP, split_axis=0, concat_axis=1, tiled=True)]
    all_to_all x1 -> x0, starting transfers between devices: 4.29 us -> none  [shards(): lax.all_to_all(merged, GROUP, split_axis=0, concat_axis=1, tiled=True)]
  transfers between devices with their start and end apart: 8 -> 7, of which waited for: 6 -> 4; matrix products, arithmetic and copies ran while one was open for 8% -> 9% of each run, Pallas kernels for 0% -> 0%
where the time goes in v14:
time: 181 us; the launch traced here: 178 us
  waiting for transfers between devices  64.8 us (36%)
  Pallas kernels  48.4 us (27%)
  starting transfers between devices  17.2 us (10%)
  local copies, waits for them, and re-layouts  14.9 us (8%)
  between operations  13.8 us (8%)
  blocking collectives  11.8 us (7%)
  matrix products  4.78 us (3%)
  other arithmetic  2.57 us (1%)
    all_gather x1, waiting for transfers between devices, shards(): kv_in = lax.all_gather(key_values, (COLUMN, ROW), axis=0, tiled=True)  51.4 us
    pallas_call x1, Pallas kernels, attend(): pl.pallas_call(attention_kernel, grid=(keys // block,), in_specs=[pl.Bloc...  38.9 us
    ppermute x3, waiting for transfers between devices, shards(): gathered.append(lax.ppermute(halo_rows, 'head', pairs))  13.4 us
    all_to_all x1, blocking collectives, to_members(): lax.all_to_all(packed.reshape(block_len, -1), GROUP, split_axis=1, concat...  11.8 us
    pallas_call x1, Pallas kernels, return_pieces(): pl.pallas_call(return_kernel, in_specs=[pl.BlockSpec(memory_space=pltpu.V...  9.55 us
    ppermute x1, starting transfers between devices, extended(): after = lax.ppermute(first, DOM, down)  8.08 us
    scatter x1, local copies, waits for them, and re-layouts, shards(): jnp.zeros_like(stacked).at[order].set(stacked)  4.74 us
  transfers between devices with their start and end apart: 7, of which 4 were waited for; matrix products, arithmetic and copies ran while one was open for 9% of the time, Pallas kernels for 0%

profile of v14, /device:TPU:4, one launch (start us, length us, event | category | flops | bytes accessed | tf_op | source)
XLA Modules:
  0.0 178.3 jit_solution(5797403603667061953)
XLA Ops:
  6.5 1.5 fusion.12
  8.0 0.1 copy.42
  8.2 0.1 copy.43
  8.4 0.1 copy.44
  8.6 0.2 convolution_convert_fusion
  8.8 0.1 copy.45
  9.0 0.6 gather_fusion.2
  9.6 11.8 %all_to_all.38 = bf16[128,8,128]{0,2,1:T(8,128)(2,1)S(1)} all-to-all(bf16[128,8,128]{0,2,1:T(8,128)(2,1)S(1)} %bitcast.51), channel_id=1, replica_groups=mesh['x'=4,'z'=8,'yhi'=2,'head'=4] {'yhi','head'}, dimensions={1} | all-to-all | bytes 524288 | tf_op jit(solution)/shard_map/all_to_all | solution.py:213
  21.4 0.9 copy.48
  22.3 2.3 %collective-permute-start = (bf16[128,512]{1,0:T(8,128)(2,1)S(1)}, bf16[128,512]{1,0:T(8,128)(2,1)S(1)}, u32[]{:S(2)}, u32[]{:S(2)}) collective-permute-start(bf16[128,512]{1,0:T(8,128)(2,1)S(1)} %copy-done.1), channel_id=1, source_target_pairs={{0,4},{4,8},{8,12},{12,16},{16,20},{20,24},{24,28},{28,32},{32,36}... | collective-permute-start | bytes 393224 | tf_op jit(solution)/shard_map/ppermute | solution.py:33
  24.6 8.1 %collective-permute-start.1 = (bf16[128,512]{1,0:T(8,128)(2,1)S(1)}, bf16[128,512]{1,0:T(8,128)(2,1)S(1)}, u32[]{:S(2)}, u32[]{:S(2)}) collective-permute-start(bf16[128,512]{1,0:T(8,128)(2,1)S(1)} %copy-done.1), channel_id=1, source_target_pairs={{4,0},{8,4},{12,8},{16,12},{20,16},{24,20},{28,24},{32,28},{36,32}... | collective-permute-start | bytes 393224 | tf_op jit(solution)/shard_map/ppermute | solution.py:34
  32.7 0.2 fusion.11
  33.0 0.1 copy.38
  33.2 0.1 copy.39
  33.5 0.1 copy.40
  33.6 1.2 gather_fusion.1
  34.9 3.4 %all-to-all-start = ((bf16[128,8,64]{0,2,1:T(8,128)(2,1)}), bf16[128,8,64]{0,2,1:T(8,128)(2,1)S(1)}, u32[]{:S(2)}, u32[]{:S(2)}) async-start(bf16[128,8,64]{0,2,1:T(8,128)(2,1)} %bitcast.14), calls=%async_computation | async-start | bytes 262144 | tf_op jit(solution)/shard_map/all_to_all | solution.py:213
  38.3 0.1 max.25
  38.4 0.1 copy.36
  38.5 0.1 reshape.146
  38.6 0.5 collective-permute-start.2
  39.1 1.7 collective-permute-start.3
  40.8 1.3 collective-permute-start.4
  42.2 0.1 copy.34
  42.3 0.1 ge.24
  42.4 0.1 le.17
  42.5 0.1 copy.35
  42.6 0.1 le.19
  42.7 0.6 gather_fusion
  43.3 0.1 select_bitcast_fusion
  43.5 0.9 copy.37
  44.4 0.2 copy.41
  44.6 6.1 %collective-permute-done.2 = bf16[384,512]{1,0:T(8,128)(2,1)S(1)} collective-permute-done((bf16[384,512]{1,0:T(8,128)(2,1)S(1)}, bf16[384,512]{1,0:T(8,128)(2,1)S(1)}, u32[]{:S(2)}, u32[]{:S(2)}) %collective-permute-start.2) | collective-permute-done | bytes 393248 | tf_op jit(solution)/shard_map/ppermute | solution.py:193
  50.7 1.1 collective-permute-done.3
  51.8 6.2 %collective-permute-done.4 = bf16[384,512]{1,0:T(8,128)(2,1)} collective-permute-done((bf16[384,512]{1,0:T(8,128)(2,1)S(1)}, bf16[384,512]{1,0:T(8,128)(2,1)}, u32[]{:S(2)}, u32[]{:S(2)}) %collective-permute-start.4) | collective-permute-done | bytes 393248 | tf_op jit(solution)/shard_map/ppermute | solution.py:193
  58.0 1.4 pad_maximum_fusion
  59.4 1.3 broadcast_in_dim.45
  60.8 4.7 %scatter_fusion = bf16[4,384,512]{2,1,0:T(8,128)(2,1)} fusion(bf16[4,384,512]{2,1,0:T(8,128)(2,1)} %broadcast_in_dim.45, s32[4]{0:T(128)S(1)} %fusion.10, bf16[4,384,512]{2,1,0:T(8,128)(2,1)S(1)} %pad_maximum_fusion), kind=kCustom, calls=%fused_computation.4 | custom fusion | bytes 4718608 | tf_op jit(solution)/shard_map/scatter | solution.py:196
  65.5 2.2 %fusion.8 = bf16[128,1024]{1,0:T(8,128)(2,1)S(1)} fusion(bf16[512,1024]{1,0:T(8,128)(2,1)S(1)} %copy-done, bf16[128,1536]{0,1:T(8,128)(2,1)S(1)} %bitcast.66, bf16[1536,512]{1,0:T(8,128)(2,1)} %bitcast.50), kind=kOutput, calls=%fused_computation.17 | convolution fusion | flops 336789504 | bytes 3276800 | tf_op jit(solution)/shard_map/dot_general | solution.py:231
  67.8 0.3 fusion.13
  68.1 0.8 concatenate.7.q_ref
  68.9 51.4 %all-gather.2.cloned.1.call-done.kv_ref = bf16[32768,128]{1,0:T(8,128)(2,1)} async-done(((bf16[1024,128]{1,0:T(8,128)(2,1)}), bf16[32768,128]{1,0:T(8,128)(2,1)}) %all-gather.2.cloned.1.call-update) | async-done | bytes 8388624 | tf_op jit(solution)/shard_map/all_gather | solution.py:218
  120.2 38.9 %shard_map.136.m_ref = bf16[1024,64]{1,0:T(8,128)(2,1)} custom-call(bf16[1024,128]{1,0:T(8,128)(2,1)} %concatenate.7.q_ref, bf16[32768,128]{1,0:T(8,128)(2,1)} %all-gather.2.cloned.1.call-done.kv_ref), custom_call_target="tpu_custom_call" | custom-call | flops 17179869184 | bytes 9175040 | tf_op jit(solution)/shard_map/pallas_call | solution.py:84
  159.1 9.5 %shard_map.137 = bf16[8,128,64]{2,1,0:T(8,128)(2,1)} custom-call(bf16[1024,64]{1,0:T(8,128)(2,1)} %shard_map.136.m_ref), custom_call_target="tpu_custom_call" | custom-call | tf_op jit(solution)/shard_map/pallas_call | solution.py:156
  168.7 1.5 gather_fusion.3
  170.2 0.1 copy.49
  170.4 0.3 multiply_reduce_fusion
  170.7 0.8 add_convert_fusion
  (55 shorter events, 0.6 us)
Async XLA Ops:
  6.5 59.0 %copy-start = (bf16[512,1024]{1,0:T(8,128)(2,1)S(1)}, bf16[512,1024]{1,0:T(8,128)(2,1)}, u32[]{:S(2)}) copy-start(bf16[512,1024]{1,0:T(8,128)(2,1)} %param.21) | copy-start | bytes 3145732
  6.5 2.0 %copy-start.1 = (bf16[128,512]{1,0:T(8,128)(2,1)S(1)}, bf16[128,512]{1,0:T(8,128)(2,1)}, u32[]{:S(2)}) copy-start(bf16[128,512]{1,0:T(8,128)(2,1)} %param.14) | copy-start | bytes 393220
  6.5 2.0 %copy-start.3 = (bf16[512,512]{1,0:T(8,128)(2,1)S(1)}, bf16[512,512]{1,0:T(8,128)(2,1)}, u32[]{:S(2)}) copy-start(bf16[512,512]{1,0:T(8,128)(2,1)} %param.19) | copy-start | bytes 1572868
  6.5 113.7 %all-gather.2.cloned.1.call-start = ((), (), s32[]{:S(2)}) async-start(), calls=%async_computation.2 | async-start | bytes 8650752 | tf_op jit(solution)/shard_map/all_gather | solution.py:218
  8.1 0.8 copy-start.10
  8.2 0.8 copy-start.11
  8.8 23.9 %copy-start.4 = (bf16[512,512]{1,0:T(8,128)(2,1)S(1)}, bf16[512,512]{1,0:T(8,128)(2,1)}, u32[]{:S(2)}) copy-start(bf16[512,512]{1,0:T(8,128)(2,1)} %param.17) | copy-start | bytes 1572868
  22.3 11.0 %copy-start.12 = (f32[8]{0:T(128)S(1)}, f32[8]{0:T(128)}, u32[]{:S(2)}) copy-start(f32[8]{0:T(128)} %param.23) | copy-start | bytes 100
  22.3 16.3 %collective-permute-start = (bf16[128,512]{1,0:T(8,128)(2,1)S(1)}, bf16[128,512]{1,0:T(8,128)(2,1)S(1)}, u32[]{:S(2)}, u32[]{:S(2)}) collective-permute-start(bf16[128,512]{1,0:T(8,128)(2,1)S(1)} %copy-done.1), channel_id=1, source_target_pairs={{0,4},{4,8},{8,12},{12,16},{16,20},{20,24},{24,28},{28,32},{32,36}... | collective-permute-start | bytes 393224 | tf_op jit(solution)/shard_map/ppermute | solution.py:33
  24.6 14.0 %collective-permute-start.1 = (bf16[128,512]{1,0:T(8,128)(2,1)S(1)}, bf16[128,512]{1,0:T(8,128)(2,1)S(1)}, u32[]{:S(2)}, u32[]{:S(2)}) collective-permute-start(bf16[128,512]{1,0:T(8,128)(2,1)S(1)} %copy-done.1), channel_id=1, source_target_pairs={{4,0},{8,4},{12,8},{16,12},{20,16},{24,20},{28,24},{32,28},{36,32}... | collective-permute-start | bytes 393224 | tf_op jit(solution)/shard_map/ppermute | solution.py:34
  32.9 5.3 %copy-start.13 = (s32[1,1,12]{2,1,0:T(1,128)S(1)}, s32[1,1,12]{2,1,0:T(1,128)}, u32[]{:S(2)}) copy-start(s32[1,1,12]{2,1,0:T(1,128)} %param.15) | copy-start | bytes 148
  33.2 9.5 %copy-start.8 = (bf16[16,128,128]{2,1,0:T(8,128)(2,1)S(1)}, bf16[16,128,128]{2,1,0:T(8,128)(2,1)}, u32[]{:S(2)}) copy-start(bf16[16,128,128]{2,1,0:T(8,128)(2,1)} %param.16) | copy-start | bytes 1572868
  34.9 9.5 %all-to-all-start = ((bf16[128,8,64]{0,2,1:T(8,128)(2,1)}), bf16[128,8,64]{0,2,1:T(8,128)(2,1)S(1)}, u32[]{:S(2)}, u32[]{:S(2)}) async-start(bf16[128,8,64]{0,2,1:T(8,128)(2,1)} %bitcast.14), calls=%async_computation | async-start | bytes 262144 | tf_op jit(solution)/shard_map/all_to_all | solution.py:213
  38.6 12.1 %collective-permute-start.2 = (bf16[384,512]{1,0:T(8,128)(2,1)S(1)}, bf16[384,512]{1,0:T(8,128)(2,1)S(1)}, u32[]{:S(2)}, u32[]{:S(2)}) collective-permute-start(bf16[384,512]{1,0:T(8,128)(2,1)S(1)} %constant_dynamic-update-slice_fusion), channel_id=1, source_target_pairs={{0,1},{1,2},{2,3},{3,0},{4,5},{5,6},{6,7},{7,4},{8,9},{9,10},{10,1... | collective-permute-start | bytes 1179656 | tf_op jit(solution)/shard_map/ppermute | solution.py:193
  39.1 12.7 %collective-permute-start.3 = (bf16[384,512]{1,0:T(8,128)(2,1)S(1)}, bf16[384,512]{1,0:T(8,128)(2,1)}, u32[]{:S(2)}, u32[]{:S(2)}) collective-permute-start(bf16[384,512]{1,0:T(8,128)(2,1)S(1)} %constant_dynamic-update-slice_fusion), channel_id=1, source_target_pairs={{0,2},{1,3},{2,0},{3,1},{4,6},{5,7},{6,4},{7,5},{8,10},{9,11},{10,... | collective-permute-start | bytes 1179656 | tf_op jit(solution)/shard_map/ppermute | solution.py:193
  40.8 17.2 %collective-permute-start.4 = (bf16[384,512]{1,0:T(8,128)(2,1)S(1)}, bf16[384,512]{1,0:T(8,128)(2,1)}, u32[]{:S(2)}, u32[]{:S(2)}) collective-permute-start(bf16[384,512]{1,0:T(8,128)(2,1)S(1)} %constant_dynamic-update-slice_fusion), channel_id=1, source_target_pairs={{0,3},{1,0},{2,1},{3,2},{4,7},{5,4},{6,5},{7,6},{8,11},{9,8},{10,9... | collective-permute-start | bytes 1179656 | tf_op jit(solution)/shard_map/ppermute | solution.py:193
  50.7 7.3 %copy-start.6 = (bf16[384,512]{1,0:T(8,128)(2,1)}, bf16[384,512]{1,0:T(8,128)(2,1)S(1)}, u32[]{:S(2)}) copy-start(bf16[384,512]{1,0:T(8,128)(2,1)S(1)} %collective-permute-done.2) | copy-start | bytes 1179652
  60.8 4.7 %copy-start.7 = (bf16[128,12,128]{0,2,1:T(8,128)(2,1)S(1)}, bf16[128,12,128]{0,2,1:T(8,128)(2,1)}, u32[]{:S(2)}) copy-start(bf16[128,12,128]{0,2,1:T(8,128)(2,1)} %copy.37) | copy-start | bytes 1179652
  65.5 2.2 %copy-start.2 = (bf16[1024,512]{1,0:T(8,128)(2,1)S(1)}, bf16[1024,512]{1,0:T(8,128)(2,1)}, u32[]{:S(2)}) copy-start(bf16[1024,512]{1,0:T(8,128)(2,1)} %param.22) | copy-start | bytes 3145732
  159.1 11.3 %copy-start.5 = (bf16[512,512]{1,0:T(8,128)(2,1)S(1)}, bf16[512,512]{1,0:T(8,128)(2,1)}, u32[]{:S(2)}) copy-start(bf16[512,512]{1,0:T(8,128)(2,1)} %param.20) | copy-start | bytes 1572868
  159.1 11.6 %copy-start.9 = (f32[512]{0:T(512)S(1)}, f32[512]{0:T(512)}, u32[]{:S(2)}) copy-start(f32[512]{0:T(512)} %param.24) | copy-start | bytes 6148
Sparse Core Ops, SparseCore 0:
  22.4 97.7 all-gather.1

commit v15 on v14

--- a/solution.py
+++ b/solution.py
@@ -150,7 +150,7 @@
         copy_to(shift).wait_send()
 
 
-def return_pieces(merged, members):
+def return_pieces(merged, members, collective_id=0):
     rows = merged.shape[0] // members
     piece = (members, rows, merged.shape[1])
     return pl.pallas_call(
@@ -163,7 +163,7 @@
             pltpu.SemaphoreType.DMA((members,)),
             pltpu.SemaphoreType.DMA((members,)),
         ],
-        compiler_params=pltpu.CompilerParams(collective_id=0, has_side_effects=True),
+        compiler_params=pltpu.CompilerParams(collective_id=collective_id, has_side_effects=True),
     )(merged)
 
 
@@ -214,7 +214,12 @@
             packed.reshape(block_len, -1), GROUP, split_axis=1, concat_axis=0, tiled=True
         )
 
-    key_values = to_members((keys_all, values_all))
+    kv_packed = jnp.stack(
+        [t.reshape(block_len, NUM_SUBSPACES, SUBSPACE_WIDTH) for t in (keys_all, values_all)],
+        axis=2,
+    )[:, jnp.array(head_of)]
+    kv_pieces = jnp.transpose(kv_packed, (1, 0, 2, 3)).reshape(members * block_len, -1)
+    key_values = return_pieces(kv_pieces, members, collective_id=1).reshape(members * block_len, -1)
     kv_in = lax.all_gather(key_values, (COLUMN, ROW), axis=0, tiled=True)
     queries = head_norm(
         jnp.dot(vertex_embeddings, asking_projector, preferred_element_type=jnp.float32),

time: 181 us -> 181 us (level)
  blocking collectives: 11.8 us -> 0 us
  Pallas kernels: 48.4 us -> 58.2 us
    all_to_all x1 -> x0, blocking collectives: 11.8 us -> none  [to_members(): lax.all_to_all(packed.reshape(block_len, -1), GROUP, split_axis=1, concat...]
    pallas_call x1 -> x2, Pallas kernels: 9.55 us -> 19.3 us  [return_pieces(): pl.pallas_call(return_kernel, in_specs=[pl.BlockSpec(memory_space=pltpu.V...]
    ppermute x1, starting transfers between devices: 2.28 us -> 4.15 us  [extended(): before = lax.ppermute(last, DOM, up)]
where the time goes in v15:
time: 181 us; the launch traced here: 178 us
  waiting for transfers between devices  64.8 us (36%)
  Pallas kernels  58.2 us (32%)
  starting transfers between devices  18.2 us (10%)
  local copies, waits for them, and re-layouts  15.4 us (9%)
  between operations  13.9 us (8%)
  matrix products  4.78 us (3%)
  other arithmetic  2.56 us (1%)
    all_gather x1, waiting for transfers between devices, shards(): kv_in = lax.all_gather(key_values, (COLUMN, ROW), axis=0, tiled=True)  51.4 us
    pallas_call x1, Pallas kernels, attend(): pl.pallas_call(attention_kernel, grid=(keys // block,), in_specs=[pl.Bloc...  38.9 us
    pallas_call x2, Pallas kernels, return_pieces(): pl.pallas_call(return_kernel, in_specs=[pl.BlockSpec(memory_space=pltpu.V...  19.3 us
    ppermute x3, waiting for transfers between devices, shards(): gathered.append(lax.ppermute(halo_rows, 'head', pairs))  13.4 us
    ppermute x1, starting transfers between devices, extended(): after = lax.ppermute(first, DOM, down)  7.18 us
    scatter x1, local copies, waits for them, and re-layouts, shards(): jnp.zeros_like(stacked).at[order].set(stacked)  4.74 us
    ppermute x1, starting transfers between devices, extended(): before = lax.ppermute(last, DOM, up)  4.15 us
  transfers between devices with their start and end apart: 7, of which 4 were waited for; matrix products, arithmetic and copies ran while one was open for 9% of the time, Pallas kernels for 0%

profile of v15, /device:TPU:4, one launch (start us, length us, event | category | flops | bytes accessed | tf_op | source)
XLA Modules:
  0.0 177.8 jit_solution(10535097162225484190)
XLA Ops:
  6.5 1.5 fusion.12
  8.0 0.1 copy.42
  8.2 0.1 copy.43
  8.4 0.1 copy.44
  8.6 0.2 convolution_convert_fusion
  8.8 0.1 copy.45
  9.0 0.6 gather_fusion.2
  9.6 0.4 copy.51
  10.0 0.9 reshape.192.m_ref
  11.0 9.8 %shard_map.136 = bf16[8,128,128]{2,1,0:T(8,128)(2,1)} custom-call(bf16[1024,128]{1,0:T(8,128)(2,1)} %reshape.192.m_ref), custom_call_target="tpu_custom_call" | custom-call | tf_op jit(solution)/shard_map/pallas_call | solution.py:156
  20.8 4.2 %collective-permute-start = (bf16[128,512]{1,0:T(8,128)(2,1)S(1)}, bf16[128,512]{1,0:T(8,128)(2,1)S(1)}, u32[]{:S(2)}, u32[]{:S(2)}) collective-permute-start(bf16[128,512]{1,0:T(8,128)(2,1)S(1)} %copy-done.1), channel_id=1, source_target_pairs={{0,4},{4,8},{8,12},{12,16},{16,20},{20,24},{24,28},{28,32},{32,36}... | collective-permute-start | bytes 393224 | tf_op jit(solution)/shard_map/ppermute | solution.py:33
  25.0 7.2 %collective-permute-start.1 = (bf16[128,512]{1,0:T(8,128)(2,1)S(1)}, bf16[128,512]{1,0:T(8,128)(2,1)S(1)}, u32[]{:S(2)}, u32[]{:S(2)}) collective-permute-start(bf16[128,512]{1,0:T(8,128)(2,1)S(1)} %copy-done.1), channel_id=1, source_target_pairs={{4,0},{8,4},{12,8},{16,12},{20,16},{24,20},{28,24},{32,28},{36,32}... | collective-permute-start | bytes 393224 | tf_op jit(solution)/shard_map/ppermute | solution.py:34
  32.2 0.2 fusion.11
  32.4 0.1 copy.38
  32.6 0.1 copy.39
  33.0 0.1 copy.40
  33.1 1.2 gather_fusion.1
  34.3 3.4 %all-to-all-start = ((bf16[128,8,64]{0,2,1:T(8,128)(2,1)}), bf16[128,8,64]{0,2,1:T(8,128)(2,1)S(1)}, u32[]{:S(2)}, u32[]{:S(2)}) async-start(bf16[128,8,64]{0,2,1:T(8,128)(2,1)} %bitcast.14), calls=%async_computation | async-start | bytes 262144 | tf_op jit(solution)/shard_map/all_to_all | solution.py:213
  37.8 0.1 copy.36
  37.9 0.1 reshape.149
  38.1 0.5 collective-permute-start.2
  38.6 1.7 collective-permute-start.3
  40.2 1.3 collective-permute-start.4
  41.6 0.1 ge.22
  41.7 0.1 copy.34
  41.8 0.1 ge.24
  41.9 0.1 copy.35
  42.1 0.1 le.19
  42.1 0.6 gather_fusion
  42.8 0.1 select_bitcast_fusion
  42.9 0.9 copy.37
  43.9 0.2 copy.41
  44.0 6.1 %collective-permute-done.2 = bf16[384,512]{1,0:T(8,128)(2,1)S(1)} collective-permute-done((bf16[384,512]{1,0:T(8,128)(2,1)S(1)}, bf16[384,512]{1,0:T(8,128)(2,1)S(1)}, u32[]{:S(2)}, u32[]{:S(2)}) %collective-permute-start.2) | collective-permute-done | bytes 393248 | tf_op jit(solution)/shard_map/ppermute | solution.py:193
  50.2 1.1 collective-permute-done.3
  51.2 6.2 %collective-permute-done.4 = bf16[384,512]{1,0:T(8,128)(2,1)} collective-permute-done((bf16[384,512]{1,0:T(8,128)(2,1)S(1)}, bf16[384,512]{1,0:T(8,128)(2,1)}, u32[]{:S(2)}, u32[]{:S(2)}) %collective-permute-start.4) | collective-permute-done | bytes 393248 | tf_op jit(solution)/shard_map/ppermute | solution.py:193
  57.5 1.4 pad_maximum_fusion
  58.9 1.3 broadcast_in_dim.45
  60.2 4.7 %scatter_fusion = bf16[4,384,512]{2,1,0:T(8,128)(2,1)} fusion(bf16[4,384,512]{2,1,0:T(8,128)(2,1)} %broadcast_in_dim.45, s32[4]{0:T(128)S(1)} %fusion.10, bf16[4,384,512]{2,1,0:T(8,128)(2,1)S(1)} %pad_maximum_fusion), kind=kCustom, calls=%fused_computation.4 | custom fusion | bytes 4718608 | tf_op jit(solution)/shard_map/scatter | solution.py:196
  65.0 2.2 %fusion.8 = bf16[128,1024]{1,0:T(8,128)(2,1)S(1)} fusion(bf16[512,1024]{1,0:T(8,128)(2,1)S(1)} %copy-done, bf16[128,1536]{0,1:T(8,128)(2,1)S(1)} %bitcast.60, bf16[1536,512]{1,0:T(8,128)(2,1)} %bitcast.46), kind=kOutput, calls=%fused_computation.17 | convolution fusion | flops 336789504 | bytes 3276800 | tf_op jit(solution)/shard_map/dot_general | solution.py:236
  67.2 0.3 fusion.13
  67.5 0.8 concatenate.7.q_ref
  68.3 51.4 %all-gather.2.cloned.1.call-done.kv_ref = bf16[32768,128]{1,0:T(8,128)(2,1)} async-done(((bf16[1024,128]{1,0:T(8,128)(2,1)}), bf16[32768,128]{1,0:T(8,128)(2,1)}) %all-gather.2.cloned.1.call-update) | async-done | bytes 8388624 | tf_op jit(solution)/shard_map/all_gather | solution.py:223
  119.7 38.9 %shard_map.137.m_ref = bf16[1024,64]{1,0:T(8,128)(2,1)} custom-call(bf16[1024,128]{1,0:T(8,128)(2,1)} %concatenate.7.q_ref, bf16[32768,128]{1,0:T(8,128)(2,1)} %all-gather.2.cloned.1.call-done.kv_ref), custom_call_target="tpu_custom_call" | custom-call | flops 17179869184 | bytes 9175040 | tf_op jit(solution)/shard_map/pallas_call | solution.py:84
  158.6 9.5 %shard_map.138 = bf16[8,128,64]{2,1,0:T(8,128)(2,1)} custom-call(bf16[1024,64]{1,0:T(8,128)(2,1)} %shard_map.137.m_ref), custom_call_target="tpu_custom_call" | custom-call | tf_op jit(solution)/shard_map/pallas_call | solution.py:156
  168.2 1.5 gather_fusion.3
  169.7 0.1 copy.50
  169.9 0.3 multiply_reduce_fusion
  170.2 0.8 add_convert_fusion
  (56 shorter events, 0.7 us)
Async XLA Ops:
  6.5 58.4 %copy-start = (bf16[512,1024]{1,0:T(8,128)(2,1)S(1)}, bf16[512,1024]{1,0:T(8,128)(2,1)}, u32[]{:S(2)}) copy-start(bf16[512,1024]{1,0:T(8,128)(2,1)} %param.21) | copy-start | bytes 3145732
  6.5 2.0 %copy-start.1 = (bf16[128,512]{1,0:T(8,128)(2,1)S(1)}, bf16[128,512]{1,0:T(8,128)(2,1)}, u32[]{:S(2)}) copy-start(bf16[128,512]{1,0:T(8,128)(2,1)} %param.14) | copy-start | bytes 393220
  6.5 2.0 %copy-start.3 = (bf16[512,512]{1,0:T(8,128)(2,1)S(1)}, bf16[512,512]{1,0:T(8,128)(2,1)}, u32[]{:S(2)}) copy-start(bf16[512,512]{1,0:T(8,128)(2,1)} %param.19) | copy-start | bytes 1572868
  6.5 113.2 %all-gather.2.cloned.1.call-start = ((), (), s32[]{:S(2)}) async-start(), calls=%async_computation.1 | async-start | bytes 8650752 | tf_op jit(solution)/shard_map/all_gather | solution.py:223
  8.1 0.8 copy-start.10
  8.2 0.8 copy-start.11
  9.0 23.2 %copy-start.4 = (bf16[512,512]{1,0:T(8,128)(2,1)S(1)}, bf16[512,512]{1,0:T(8,128)(2,1)}, u32[]{:S(2)}) copy-start(bf16[512,512]{1,0:T(8,128)(2,1)} %param.17) | copy-start | bytes 1572868
  20.8 12.0 %copy-start.12 = (f32[8]{0:T(128)S(1)}, f32[8]{0:T(128)}, u32[]{:S(2)}) copy-start(f32[8]{0:T(128)} %param.23) | copy-start | bytes 100
  20.8 17.2 %collective-permute-start = (bf16[128,512]{1,0:T(8,128)(2,1)S(1)}, bf16[128,512]{1,0:T(8,128)(2,1)S(1)}, u32[]{:S(2)}, u32[]{:S(2)}) collective-permute-start(bf16[128,512]{1,0:T(8,128)(2,1)S(1)} %copy-done.1), channel_id=1, source_target_pairs={{0,4},{4,8},{8,12},{12,16},{16,20},{20,24},{24,28},{28,32},{32,36}... | collective-permute-start | bytes 393224 | tf_op jit(solution)/shard_map/ppermute | solution.py:33
  25.0 13.1 %collective-permute-start.1 = (bf16[128,512]{1,0:T(8,128)(2,1)S(1)}, bf16[128,512]{1,0:T(8,128)(2,1)S(1)}, u32[]{:S(2)}, u32[]{:S(2)}) collective-permute-start(bf16[128,512]{1,0:T(8,128)(2,1)S(1)} %copy-done.1), channel_id=1, source_target_pairs={{4,0},{8,4},{12,8},{16,12},{20,16},{24,20},{28,24},{32,28},{36,32}... | collective-permute-start | bytes 393224 | tf_op jit(solution)/shard_map/ppermute | solution.py:34
  32.4 5.3 %copy-start.13 = (s32[1,1,12]{2,1,0:T(1,128)S(1)}, s32[1,1,12]{2,1,0:T(1,128)}, u32[]{:S(2)}) copy-start(s32[1,1,12]{2,1,0:T(1,128)} %param.15) | copy-start | bytes 148
  32.6 9.5 %copy-start.8 = (bf16[16,128,128]{2,1,0:T(8,128)(2,1)S(1)}, bf16[16,128,128]{2,1,0:T(8,128)(2,1)}, u32[]{:S(2)}) copy-start(bf16[16,128,128]{2,1,0:T(8,128)(2,1)} %param.16) | copy-start | bytes 1572868
  34.3 9.5 %all-to-all-start = ((bf16[128,8,64]{0,2,1:T(8,128)(2,1)}), bf16[128,8,64]{0,2,1:T(8,128)(2,1)S(1)}, u32[]{:S(2)}, u32[]{:S(2)}) async-start(bf16[128,8,64]{0,2,1:T(8,128)(2,1)} %bitcast.14), calls=%async_computation | async-start | bytes 262144 | tf_op jit(solution)/shard_map/all_to_all | solution.py:213
  38.1 12.1 %collective-permute-start.2 = (bf16[384,512]{1,0:T(8,128)(2,1)S(1)}, bf16[384,512]{1,0:T(8,128)(2,1)S(1)}, u32[]{:S(2)}, u32[]{:S(2)}) collective-permute-start(bf16[384,512]{1,0:T(8,128)(2,1)S(1)} %constant_dynamic-update-slice_fusion), channel_id=1, source_target_pairs={{0,1},{1,2},{2,3},{3,0},{4,5},{5,6},{6,7},{7,4},{8,9},{9,10},{10,1... | collective-permute-start | bytes 1179656 | tf_op jit(solution)/shard_map/ppermute | solution.py:193
  38.6 12.7 %collective-permute-start.3 = (bf16[384,512]{1,0:T(8,128)(2,1)S(1)}, bf16[384,512]{1,0:T(8,128)(2,1)}, u32[]{:S(2)}, u32[]{:S(2)}) collective-permute-start(bf16[384,512]{1,0:T(8,128)(2,1)S(1)} %constant_dynamic-update-slice_fusion), channel_id=1, source_target_pairs={{0,2},{1,3},{2,0},{3,1},{4,6},{5,7},{6,4},{7,5},{8,10},{9,11},{10,... | collective-permute-start | bytes 1179656 | tf_op jit(solution)/shard_map/ppermute | solution.py:193
  40.2 17.2 %collective-permute-start.4 = (bf16[384,512]{1,0:T(8,128)(2,1)S(1)}, bf16[384,512]{1,0:T(8,128)(2,1)}, u32[]{:S(2)}, u32[]{:S(2)}) collective-permute-start(bf16[384,512]{1,0:T(8,128)(2,1)S(1)} %constant_dynamic-update-slice_fusion), channel_id=1, source_target_pairs={{0,3},{1,0},{2,1},{3,2},{4,7},{5,4},{6,5},{7,6},{8,11},{9,8},{10,9... | collective-permute-start | bytes 1179656 | tf_op jit(solution)/shard_map/ppermute | solution.py:193
  50.2 7.3 %copy-start.6 = (bf16[384,512]{1,0:T(8,128)(2,1)}, bf16[384,512]{1,0:T(8,128)(2,1)S(1)}, u32[]{:S(2)}) copy-start(bf16[384,512]{1,0:T(8,128)(2,1)S(1)} %collective-permute-done.2) | copy-start | bytes 1179652
  60.2 4.7 %copy-start.7 = (bf16[128,12,128]{0,2,1:T(8,128)(2,1)S(1)}, bf16[128,12,128]{0,2,1:T(8,128)(2,1)}, u32[]{:S(2)}) copy-start(bf16[128,12,128]{0,2,1:T(8,128)(2,1)} %copy.37) | copy-start | bytes 1179652
  65.0 2.2 %copy-start.2 = (bf16[1024,512]{1,0:T(8,128)(2,1)S(1)}, bf16[1024,512]{1,0:T(8,128)(2,1)}, u32[]{:S(2)}) copy-start(bf16[1024,512]{1,0:T(8,128)(2,1)} %param.22) | copy-start | bytes 3145732
  158.6 11.3 %copy-start.5 = (bf16[512,512]{1,0:T(8,128)(2,1)S(1)}, bf16[512,512]{1,0:T(8,128)(2,1)}, u32[]{:S(2)}) copy-start(bf16[512,512]{1,0:T(8,128)(2,1)} %param.20) | copy-start | bytes 1572868
  158.6 11.6 %copy-start.9 = (f32[512]{0:T(512)S(1)}, f32[512]{0:T(512)}, u32[]{:S(2)}) copy-start(f32[512]{0:T(512)} %param.24) | copy-start | bytes 6148
Sparse Core Ops, SparseCore 0:
  20.9 98.7 all-gather.1

commit v16 on v14

--- a/solution.py
+++ b/solution.py
@@ -104,7 +104,7 @@
     me = lax.axis_index(PAIR) * group_size + lax.axis_index("head")
     row = lax.axis_index(ROW)
     column = lax.axis_index(COLUMN)
-    rows = o_ref.shape[1]
+    rows = o_ref.shape[0]
 
     def device(t):
         return (row, column, t // group_size, lax.rem(t, group_size))
@@ -141,11 +141,14 @@
 
     for shift in range(1, members):
         copy_to(shift).start()
-    o_ref[me] = m_ref[pl.ds(pl.multiple_of(me * rows, rows), rows), :]
-    for shift in range(1, members):
-        source, landed = arrival(shift)
+    landing[me] = m_ref[pl.ds(pl.multiple_of(me * rows, rows), rows), :]
+    for shift in range(1, members):
+        landed = arrival(shift)[1]
         landed.wait_recv()
-        o_ref[source] = landing[source]
+    width = m_ref.shape[1]
+    for j in range(members):
+        head = (j % group_size) * (members // group_size) + j // group_size
+        o_ref[:, head * width : (head + 1) * width] = landing[j]
     for shift in range(1, members):
         copy_to(shift).wait_send()
 
@@ -157,7 +160,7 @@
         return_kernel,
         in_specs=[pl.BlockSpec(memory_space=pltpu.VMEM)],
         out_specs=pl.BlockSpec(memory_space=pltpu.VMEM),
-        out_shape=jax.ShapeDtypeStruct(piece, merged.dtype),
+        out_shape=jax.ShapeDtypeStruct((rows, members * merged.shape[1]), merged.dtype),
         scratch_shapes=[
             pltpu.VMEM(piece, merged.dtype),
             pltpu.SemaphoreType.DMA((members,)),
@@ -235,8 +238,7 @@
     local_term, head_queries = lax.optimization_barrier((local_term, head_queries))
     padded_queries = jnp.concatenate([head_queries, jnp.zeros_like(head_queries)], axis=1)
     merged = attend(padded_queries, kv_in)
-    back = return_pieces(merged, members)
-    node_heads = jnp.transpose(back, (1, 0, 2))[:, jnp.array(member_of)]
+    node_heads = return_pieces(merged, members)
     node_heads = node_heads.reshape(block_len, -1)
     attended = jnp.dot(node_heads, final_projector, preferred_element_type=jnp.float32)
     normed = (

time: 181 us -> 182 us (level)
  no operation moved by 1% of the time
where the time goes in v16:
time: 182 us; the launch traced here: 178 us
  waiting for transfers between devices  63.2 us (35%)
  Pallas kernels  48.4 us (27%)
  starting transfers between devices  17.2 us (9%)
  local copies, waits for them, and re-layouts  15.1 us (8%)
  between operations  13.8 us (8%)
  blocking collectives  11.8 us (6%)
  matrix products  5.61 us (3%)
  other arithmetic  3.3 us (2%)
    all_gather x1, waiting for transfers between devices, shards(): kv_in = lax.all_gather(key_values, (COLUMN, ROW), axis=0, tiled=True)  50.8 us
    pallas_call x1, Pallas kernels, attend(): pl.pallas_call(attention_kernel, grid=(keys // block,), in_specs=[pl.Bloc...  38.9 us
    ppermute x3, waiting for transfers between devices, shards(): gathered.append(lax.ppermute(halo_rows, 'head', pairs))  12.3 us
    all_to_all x1, blocking collectives, to_members(): lax.all_to_all(packed.reshape(block_len, -1), GROUP, split_axis=1, concat...  11.8 us
    pallas_call x1, Pallas kernels, return_pieces(): pl.pallas_call(return_kernel, in_specs=[pl.BlockSpec(memory_space=pltpu.V...  9.55 us
    ppermute x1, starting transfers between devices, extended(): after = lax.ppermute(first, DOM, down)  8.08 us
    scatter x1, local copies, waits for them, and re-layouts, shards(): jnp.zeros_like(stacked).at[order].set(stacked)  4.75 us
  transfers between devices with their start and end apart: 7, of which 4 were waited for; matrix products, arithmetic and copies ran while one was open for 9% of the time, Pallas kernels for 0%

profile of v16, /device:TPU:4, one launch (start us, length us, event | category | flops | bytes accessed | tf_op | source)
XLA Modules:
  0.0 178.4 jit_solution(8971183250895742288)
XLA Ops:
  6.5 0.8 maximum_reduce_fusion
  7.3 0.1 max.25
  7.4 0.1 copy.34
  7.5 0.1 reshape.142
  7.6 1.4 fusion.12
  9.0 0.1 copy.40
  9.2 0.1 copy.41
  9.4 0.1 copy.42
  9.5 0.2 convolution_convert_fusion
  9.8 0.1 copy.43
  10.0 0.6 gather_fusion.2
  10.6 11.8 %all_to_all.38 = bf16[128,8,128]{0,2,1:T(8,128)(2,1)S(1)} all-to-all(bf16[128,8,128]{0,2,1:T(8,128)(2,1)S(1)} %bitcast.48), channel_id=1, replica_groups=mesh['x'=4,'z'=8,'yhi'=2,'head'=4] {'yhi','head'}, dimensions={1} | all-to-all | bytes 524288 | tf_op jit(solution)/shard_map/all_to_all | solution.py:216
  22.4 0.9 copy.46
  23.3 2.3 %collective-permute-start = (bf16[128,512]{1,0:T(8,128)(2,1)S(1)}, bf16[128,512]{1,0:T(8,128)(2,1)S(1)}, u32[]{:S(2)}, u32[]{:S(2)}) collective-permute-start(bf16[128,512]{1,0:T(8,128)(2,1)S(1)} %copy-done.1), channel_id=1, source_target_pairs={{0,4},{4,8},{8,12},{12,16},{16,20},{20,24},{24,28},{28,32},{32,36}... | collective-permute-start | bytes 393224 | tf_op jit(solution)/shard_map/ppermute | solution.py:33
  25.6 8.1 %collective-permute-start.1 = (bf16[128,512]{1,0:T(8,128)(2,1)S(1)}, bf16[128,512]{1,0:T(8,128)(2,1)S(1)}, u32[]{:S(2)}, u32[]{:S(2)}) collective-permute-start(bf16[128,512]{1,0:T(8,128)(2,1)S(1)} %copy-done.1), channel_id=1, source_target_pairs={{4,0},{8,4},{12,8},{16,12},{20,16},{24,20},{28,24},{32,28},{36,32}... | collective-permute-start | bytes 393224 | tf_op jit(solution)/shard_map/ppermute | solution.py:34
  33.7 0.2 fusion.11
  33.9 0.1 copy.36
  34.1 0.1 copy.37
  34.5 0.1 copy.38
  34.6 1.2 gather_fusion.1
  35.8 3.4 %all-to-all-start = ((bf16[128,8,64]{0,2,1:T(8,128)(2,1)}), bf16[128,8,64]{0,2,1:T(8,128)(2,1)S(1)}, u32[]{:S(2)}, u32[]{:S(2)}) async-start(bf16[128,8,64]{0,2,1:T(8,128)(2,1)} %bitcast.14), calls=%async_computation | async-start | bytes 262144 | tf_op jit(solution)/shard_map/all_to_all | solution.py:216
  39.3 0.5 collective-permute-start.2
  39.7 1.7 collective-permute-start.3
  41.4 1.3 collective-permute-start.4
  42.7 0.1 ge.22
  42.8 0.1 copy.32
  42.9 0.1 ge.24
  43.1 0.1 copy.33
  43.2 0.1 le.19
  43.3 1.7 gather_fusion
  45.0 0.1 select_bitcast_fusion
  45.1 0.9 copy.35
  46.1 0.2 copy.39
  46.3 5.4 %collective-permute-done.2 = bf16[384,512]{1,0:T(8,128)(2,1)S(1)} collective-permute-done((bf16[384,512]{1,0:T(8,128)(2,1)S(1)}, bf16[384,512]{1,0:T(8,128)(2,1)S(1)}, u32[]{:S(2)}, u32[]{:S(2)}) %collective-permute-start.2) | collective-permute-done | bytes 393248 | tf_op jit(solution)/shard_map/ppermute | solution.py:196
  51.7 1.1 collective-permute-done.3
  52.7 5.9 %collective-permute-done.4 = bf16[384,512]{1,0:T(8,128)(2,1)S(1)} collective-permute-done((bf16[384,512]{1,0:T(8,128)(2,1)S(1)}, bf16[384,512]{1,0:T(8,128)(2,1)S(1)}, u32[]{:S(2)}, u32[]{:S(2)}) %collective-permute-start.4) | collective-permute-done | bytes 393248 | tf_op jit(solution)/shard_map/ppermute | solution.py:196
  58.6 0.8 copy-done.7
  59.4 1.4 pad_maximum_fusion
  60.9 1.3 broadcast_in_dim.42
  62.2 4.7 %scatter_fusion = bf16[4,384,512]{2,1,0:T(8,128)(2,1)} fusion(bf16[4,384,512]{2,1,0:T(8,128)(2,1)} %broadcast_in_dim.42, s32[4]{0:T(128)S(1)} %fusion.10, bf16[4,384,512]{2,1,0:T(8,128)(2,1)S(1)} %pad_maximum_fusion), kind=kCustom, calls=%fused_computation.3 | custom fusion | bytes 4718608 | tf_op jit(solution)/shard_map/scatter | solution.py:199
  66.9 2.2 %fusion.8 = bf16[128,1024]{1,0:T(8,128)(2,1)S(1)} fusion(bf16[512,1024]{1,0:T(8,128)(2,1)S(1)} %copy-done, bf16[128,1536]{0,1:T(8,128)(2,1)S(1)} %bitcast.61, bf16[1536,512]{1,0:T(8,128)(2,1)} %bitcast.47), kind=kOutput, calls=%fused_computation.16 | convolution fusion | flops 336789504 | bytes 3276800 | tf_op jit(solution)/shard_map/dot_general | solution.py:234
  69.2 0.3 fusion.13
  69.5 0.8 concatenate.7.q_ref
  70.3 50.8 %all-gather.2.cloned.1.call-done.kv_ref = bf16[32768,128]{1,0:T(8,128)(2,1)} async-done(((bf16[1024,128]{1,0:T(8,128)(2,1)}), bf16[32768,128]{1,0:T(8,128)(2,1)}) %all-gather.2.cloned.1.call-update) | async-done | bytes 8388624 | tf_op jit(solution)/shard_map/all_gather | solution.py:221
  121.1 38.9 %shard_map.127.m_ref = bf16[1024,64]{1,0:T(8,128)(2,1)} custom-call(bf16[1024,128]{1,0:T(8,128)(2,1)} %concatenate.7.q_ref, bf16[32768,128]{1,0:T(8,128)(2,1)} %all-gather.2.cloned.1.call-done.kv_ref), custom_call_target="tpu_custom_call" | custom-call | flops 17179869184 | bytes 9175040 | tf_op jit(solution)/shard_map/pallas_call | solution.py:84
  160.0 9.6 %shard_map.128 = bf16[128,512]{1,0:T(8,128)(2,1)} custom-call(bf16[1024,64]{1,0:T(8,128)(2,1)} %shard_map.127.m_ref), custom_call_target="tpu_custom_call" | custom-call | tf_op jit(solution)/shard_map/pallas_call | solution.py:159
  169.6 1.2 multiply_reduce_fusion
  170.8 0.8 add_convert_fusion
  (50 shorter events, 0.6 us)
Async XLA Ops:
  6.5 60.4 %copy-start = (bf16[512,1024]{1,0:T(8,128)(2,1)S(1)}, bf16[512,1024]{1,0:T(8,128)(2,1)}, u32[]{:S(2)}) copy-start(bf16[512,1024]{1,0:T(8,128)(2,1)} %param.20) | copy-start | bytes 3145732
  6.5 114.6 %all-gather.2.cloned.1.call-start = ((), (), s32[]{:S(2)}) async-start(), calls=%async_computation.2 | async-start | bytes 8650752 | tf_op jit(solution)/shard_map/all_gather | solution.py:221
  7.6 1.9 %copy-start.1 = (bf16[128,512]{1,0:T(8,128)(2,1)S(1)}, bf16[128,512]{1,0:T(8,128)(2,1)}, u32[]{:S(2)}) copy-start(bf16[128,512]{1,0:T(8,128)(2,1)} %param.13) | copy-start | bytes 393220
  7.6 1.9 %copy-start.3 = (bf16[512,512]{1,0:T(8,128)(2,1)S(1)}, bf16[512,512]{1,0:T(8,128)(2,1)}, u32[]{:S(2)}) copy-start(bf16[512,512]{1,0:T(8,128)(2,1)} %param.18) | copy-start | bytes 1572868
  9.1 0.8 copy-start.10
  9.8 23.9 %copy-start.4 = (bf16[512,512]{1,0:T(8,128)(2,1)S(1)}, bf16[512,512]{1,0:T(8,128)(2,1)}, u32[]{:S(2)}) copy-start(bf16[512,512]{1,0:T(8,128)(2,1)} %param.16) | copy-start | bytes 1572868
  23.2 11.0 %copy-start.11 = (f32[8]{0:T(128)S(1)}, f32[8]{0:T(128)}, u32[]{:S(2)}) copy-start(f32[8]{0:T(128)} %param.22) | copy-start | bytes 100
  23.3 15.9 %collective-permute-start = (bf16[128,512]{1,0:T(8,128)(2,1)S(1)}, bf16[128,512]{1,0:T(8,128)(2,1)S(1)}, u32[]{:S(2)}, u32[]{:S(2)}) collective-permute-start(bf16[128,512]{1,0:T(8,128)(2,1)S(1)} %copy-done.1), channel_id=1, source_target_pairs={{0,4},{4,8},{8,12},{12,16},{16,20},{20,24},{24,28},{28,32},{32,36}... | collective-permute-start | bytes 393224 | tf_op jit(solution)/shard_map/ppermute | solution.py:33
  25.6 13.7 %collective-permute-start.1 = (bf16[128,512]{1,0:T(8,128)(2,1)S(1)}, bf16[128,512]{1,0:T(8,128)(2,1)S(1)}, u32[]{:S(2)}, u32[]{:S(2)}) collective-permute-start(bf16[128,512]{1,0:T(8,128)(2,1)S(1)} %copy-done.1), channel_id=1, source_target_pairs={{4,0},{8,4},{12,8},{16,12},{20,16},{24,20},{28,24},{32,28},{36,32}... | collective-permute-start | bytes 393224 | tf_op jit(solution)/shard_map/ppermute | solution.py:34
  34.1 8.6 %copy-start.12 = (s32[1,1,12]{2,1,0:T(1,128)S(1)}, s32[1,1,12]{2,1,0:T(1,128)}, u32[]{:S(2)}) copy-start(s32[1,1,12]{2,1,0:T(1,128)} %param.14) | copy-start | bytes 148
  35.8 10.3 %all-to-all-start = ((bf16[128,8,64]{0,2,1:T(8,128)(2,1)}), bf16[128,8,64]{0,2,1:T(8,128)(2,1)S(1)}, u32[]{:S(2)}, u32[]{:S(2)}) async-start(bf16[128,8,64]{0,2,1:T(8,128)(2,1)} %bitcast.14), calls=%async_computation | async-start | bytes 262144 | tf_op jit(solution)/shard_map/all_to_all | solution.py:216
  39.3 12.4 %collective-permute-start.2 = (bf16[384,512]{1,0:T(8,128)(2,1)S(1)}, bf16[384,512]{1,0:T(8,128)(2,1)S(1)}, u32[]{:S(2)}, u32[]{:S(2)}) collective-permute-start(bf16[384,512]{1,0:T(8,128)(2,1)S(1)} %constant_dynamic-update-slice_fusion), channel_id=1, source_target_pairs={{0,1},{1,2},{2,3},{3,0},{4,5},{5,6},{6,7},{7,4},{8,9},{9,10},{10,1... | collective-permute-start | bytes 1179656 | tf_op jit(solution)/shard_map/ppermute | solution.py:196
  39.7 13.0 %collective-permute-start.3 = (bf16[384,512]{1,0:T(8,128)(2,1)S(1)}, bf16[384,512]{1,0:T(8,128)(2,1)}, u32[]{:S(2)}, u32[]{:S(2)}) collective-permute-start(bf16[384,512]{1,0:T(8,128)(2,1)S(1)} %constant_dynamic-update-slice_fusion), channel_id=1, source_target_pairs={{0,2},{1,3},{2,0},{3,1},{4,6},{5,7},{6,4},{7,5},{8,10},{9,11},{10,... | collective-permute-start | bytes 1179656 | tf_op jit(solution)/shard_map/ppermute | solution.py:196
  41.4 17.2 %collective-permute-start.4 = (bf16[384,512]{1,0:T(8,128)(2,1)S(1)}, bf16[384,512]{1,0:T(8,128)(2,1)S(1)}, u32[]{:S(2)}, u32[]{:S(2)}) collective-permute-start(bf16[384,512]{1,0:T(8,128)(2,1)S(1)} %constant_dynamic-update-slice_fusion), channel_id=1, source_target_pairs={{0,3},{1,0},{2,1},{3,2},{4,7},{5,4},{6,5},{7,6},{8,11},{9,8},{10,9... | collective-permute-start | bytes 1179656 | tf_op jit(solution)/shard_map/ppermute | solution.py:196
  51.7 7.0 %copy-start.6 = (bf16[384,512]{1,0:T(8,128)(2,1)}, bf16[384,512]{1,0:T(8,128)(2,1)S(1)}, u32[]{:S(2)}) copy-start(bf16[384,512]{1,0:T(8,128)(2,1)S(1)} %collective-permute-done.2) | copy-start | bytes 1179652
  58.6 0.8 copy-start.7
  62.2 4.8 %copy-start.8 = (bf16[128,12,128]{0,2,1:T(8,128)(2,1)S(1)}, bf16[128,12,128]{0,2,1:T(8,128)(2,1)}, u32[]{:S(2)}) copy-start(bf16[128,12,128]{0,2,1:T(8,128)(2,1)} %copy.35) | copy-start | bytes 1179652
  66.9 2.2 %copy-start.2 = (bf16[1024,512]{1,0:T(8,128)(2,1)S(1)}, bf16[1024,512]{1,0:T(8,128)(2,1)}, u32[]{:S(2)}) copy-start(bf16[1024,512]{1,0:T(8,128)(2,1)} %param.21) | copy-start | bytes 3145732
  70.3 99.3 %copy-start.5 = (bf16[512,512]{1,0:T(8,128)(2,1)S(1)}, bf16[512,512]{1,0:T(8,128)(2,1)}, u32[]{:S(2)}) copy-start(bf16[512,512]{1,0:T(8,128)(2,1)} %param.19) | copy-start | bytes 1572868
  70.3 100.5 %copy-start.9 = (f32[512]{0:T(512)S(1)}, f32[512]{0:T(512)}, u32[]{:S(2)}) copy-start(f32[512]{0:T(512)} %param.23) | copy-start | bytes 6148
Sparse Core Ops, SparseCore 0:
  23.4 97.6 all-gather.1

commit v17 on v16

--- a/solution.py
+++ b/solution.py
@@ -153,7 +153,7 @@
         copy_to(shift).wait_send()
 
 
-def return_pieces(merged, members):
+def return_pieces(merged, members, collective_id=0):
     rows = merged.shape[0] // members
     piece = (members, rows, merged.shape[1])
     return pl.pallas_call(
@@ -166,7 +166,7 @@
             pltpu.SemaphoreType.DMA((members,)),
             pltpu.SemaphoreType.DMA((members,)),
         ],
-        compiler_params=pltpu.CompilerParams(collective_id=0, has_side_effects=True),
+        compiler_params=pltpu.CompilerParams(collective_id=collective_id, has_side_effects=True),
     )(merged)
 
 
@@ -217,7 +217,12 @@
             packed.reshape(block_len, -1), GROUP, split_axis=1, concat_axis=0, tiled=True
         )
 
-    key_values = to_members((keys_all, values_all))
+    kv_packed = jnp.stack(
+        [t.reshape(block_len, NUM_SUBSPACES, SUBSPACE_WIDTH) for t in (keys_all, values_all)],
+        axis=2,
+    )[:, jnp.array(head_of)]
+    kv_pieces = jnp.transpose(kv_packed, (1, 0, 2, 3)).reshape(members * block_len, -1)
+    key_values = return_pieces(kv_pieces, members, collective_id=1).reshape(members * block_len, -1)
     kv_in = lax.all_gather(key_values, (COLUMN, ROW), axis=0, tiled=True)
     queries = head_norm(
         jnp.dot(vertex_embeddings, asking_projector, preferred_element_type=jnp.float32),

time: 182 us -> 183 us (level)
  blocking collectives: 11.8 us -> 0 us
  Pallas kernels: 48.4 us -> 58.2 us
    all_to_all x1 -> x0, blocking collectives: 11.8 us -> none  [to_members(): lax.all_to_all(packed.reshape(block_len, -1), GROUP, split_axis=1, concat...]
    pallas_call x1 -> x2, Pallas kernels: 9.55 us -> 19.4 us  [return_pieces(): pl.pallas_call(return_kernel, in_specs=[pl.BlockSpec(memory_space=pltpu.V...]
    reshape x0 -> x3, local copies, waits for them, and re-layouts: none -> 3.17 us  [the longest x1 1.8 us: shards(): return_pieces(kv_pieces, members, collective_id=1)]
    ppermute x1, starting transfers between devices: 2.28 us -> 4.15 us  [extended(): before = lax.ppermute(last, DOM, up)]
where the time goes in v17:
time: 183 us; the launch traced here: 180 us
  waiting for transfers between devices  64.1 us (35%)
  Pallas kernels  58.2 us (32%)
  starting transfers between devices  18.2 us (10%)
  local copies, waits for them, and re-layouts  16.6 us (9%)
  between operations  13.8 us (8%)
  matrix products  5.6 us (3%)
  other arithmetic  3.3 us (2%)
    all_gather x1, waiting for transfers between devices, shards(): kv_in = lax.all_gather(key_values, (COLUMN, ROW), axis=0, tiled=True)  51.7 us
    pallas_call x1, Pallas kernels, attend(): pl.pallas_call(attention_kernel, grid=(keys // block,), in_specs=[pl.Bloc...  38.9 us
    pallas_call x2, Pallas kernels, return_pieces(): pl.pallas_call(return_kernel, in_specs=[pl.BlockSpec(memory_space=pltpu.V...  19.4 us
    ppermute x3, waiting for transfers between devices, shards(): gathered.append(lax.ppermute(halo_rows, 'head', pairs))  12.3 us
    ppermute x1, starting transfers between devices, extended(): after = lax.ppermute(first, DOM, down)  7.18 us
    scatter x1, local copies, waits for them, and re-layouts, shards(): jnp.zeros_like(stacked).at[order].set(stacked)  4.75 us
    ppermute x1, starting transfers between devices, extended(): before = lax.ppermute(last, DOM, up)  4.15 us
  transfers between devices with their start and end apart: 7, of which 4 were waited for; matrix products, arithmetic and copies ran while one was open for 9% of the time, Pallas kernels for 0%

profile of v17, /device:TPU:4, one launch (start us, length us, event | category | flops | bytes accessed | tf_op | source)
XLA Modules:
  0.0 179.8 jit_solution(3223713008802524322)
XLA Ops:
  6.5 0.8 maximum_reduce_fusion
  7.4 0.1 copy.34
  7.5 0.1 reshape.145
  7.6 1.4 fusion.12
  9.0 0.1 copy.40
  9.2 0.1 copy.41
  9.4 0.1 copy.42
  9.5 0.2 convolution_convert_fusion
  9.8 0.1 copy.43
  9.9 0.6 gather_fusion.2
  10.6 0.4 copy.48
  11.0 1.0 reshape.180.m_ref
  11.9 9.8 %shard_map.127 = bf16[128,1024]{1,0:T(8,128)(2,1)} custom-call(bf16[1024,128]{1,0:T(8,128)(2,1)} %reshape.180.m_ref), custom_call_target="tpu_custom_call" | custom-call | tf_op jit(solution)/shard_map/pallas_call | solution.py:159
  21.7 1.8 %reshape.142 = bf16[1024,128]{1,0:T(8,128)(2,1)} reshape(bf16[128,1024]{1,0:T(8,128)(2,1)} %shard_map.127) | data formatting | bytes 524288 | tf_op jit(solution)/shard_map/reshape | solution.py:225
  23.6 4.2 %collective-permute-start = (bf16[128,512]{1,0:T(8,128)(2,1)S(1)}, bf16[128,512]{1,0:T(8,128)(2,1)S(1)}, u32[]{:S(2)}, u32[]{:S(2)}) collective-permute-start(bf16[128,512]{1,0:T(8,128)(2,1)S(1)} %copy-done.1), channel_id=1, source_target_pairs={{0,4},{4,8},{8,12},{12,16},{16,20},{20,24},{24,28},{28,32},{32,36}... | collective-permute-start | bytes 393224 | tf_op jit(solution)/shard_map/ppermute | solution.py:33
  27.7 7.2 %collective-permute-start.1 = (bf16[128,512]{1,0:T(8,128)(2,1)S(1)}, bf16[128,512]{1,0:T(8,128)(2,1)S(1)}, u32[]{:S(2)}, u32[]{:S(2)}) collective-permute-start(bf16[128,512]{1,0:T(8,128)(2,1)S(1)} %copy-done.1), channel_id=1, source_target_pairs={{4,0},{8,4},{12,8},{16,12},{20,16},{24,20},{28,24},{32,28},{36,32}... | collective-permute-start | bytes 393224 | tf_op jit(solution)/shard_map/ppermute | solution.py:34
  34.9 0.2 fusion.11
  35.2 0.1 copy.36
  35.4 0.1 copy.37
  35.7 0.1 copy.38
  35.9 1.2 gather_fusion.1
  37.1 3.4 %all-to-all-start = ((bf16[128,8,64]{0,2,1:T(8,128)(2,1)}), bf16[128,8,64]{0,2,1:T(8,128)(2,1)S(1)}, u32[]{:S(2)}, u32[]{:S(2)}) async-start(bf16[128,8,64]{0,2,1:T(8,128)(2,1)} %bitcast.14), calls=%async_computation | async-start | bytes 262144 | tf_op jit(solution)/shard_map/all_to_all | solution.py:216
  40.5 0.5 collective-permute-start.2
  41.0 1.7 collective-permute-start.3
  42.7 1.3 collective-permute-start.4
  44.0 0.1 ge.22
  44.1 0.1 copy.32
  44.2 0.1 ge.24
  44.4 0.1 copy.33
  44.5 0.1 le.19
  44.6 1.7 gather_fusion
  46.3 0.1 select_bitcast_fusion
  46.4 0.9 copy.35
  47.4 0.2 copy.39
  47.6 5.4 %collective-permute-done.2 = bf16[384,512]{1,0:T(8,128)(2,1)S(1)} collective-permute-done((bf16[384,512]{1,0:T(8,128)(2,1)S(1)}, bf16[384,512]{1,0:T(8,128)(2,1)S(1)}, u32[]{:S(2)}, u32[]{:S(2)}) %collective-permute-start.2) | collective-permute-done | bytes 393248 | tf_op jit(solution)/shard_map/ppermute | solution.py:196
  53.0 0.9 collective-permute-done.3
  53.9 6.0 %collective-permute-done.4 = bf16[384,512]{1,0:T(8,128)(2,1)} collective-permute-done((bf16[384,512]{1,0:T(8,128)(2,1)S(1)}, bf16[384,512]{1,0:T(8,128)(2,1)}, u32[]{:S(2)}, u32[]{:S(2)}) %collective-permute-start.4) | collective-permute-done | bytes 393248 | tf_op jit(solution)/shard_map/ppermute | solution.py:196
  59.9 1.4 pad_maximum_fusion
  61.3 1.3 broadcast_in_dim.42
  62.7 4.7 %scatter_fusion = bf16[4,384,512]{2,1,0:T(8,128)(2,1)} fusion(bf16[4,384,512]{2,1,0:T(8,128)(2,1)} %broadcast_in_dim.42, s32[4]{0:T(128)S(1)} %fusion.10, bf16[4,384,512]{2,1,0:T(8,128)(2,1)S(1)} %pad_maximum_fusion), kind=kCustom, calls=%fused_computation.3 | custom fusion | bytes 4718608 | tf_op jit(solution)/shard_map/scatter | solution.py:199
  67.4 2.2 %fusion.8 = bf16[128,1024]{1,0:T(8,128)(2,1)S(1)} fusion(bf16[512,1024]{1,0:T(8,128)(2,1)S(1)} %copy-done, bf16[128,1536]{0,1:T(8,128)(2,1)S(1)} %bitcast.53, bf16[1536,512]{1,0:T(8,128)(2,1)} %bitcast.42), kind=kOutput, calls=%fused_computation.16 | convolution fusion | flops 336789504 | bytes 3276800 | tf_op jit(solution)/shard_map/dot_general | solution.py:239
  69.7 0.3 fusion.13
  70.0 0.8 concatenate.7.q_ref
  70.8 51.7 %all-gather.2.cloned.1.call-done.kv_ref = bf16[32768,128]{1,0:T(8,128)(2,1)} async-done(((bf16[1024,128]{1,0:T(8,128)(2,1)}), bf16[32768,128]{1,0:T(8,128)(2,1)}) %all-gather.2.cloned.1.call-update) | async-done | bytes 8388624 | tf_op jit(solution)/shard_map/all_gather | solution.py:226
  122.5 38.9 %shard_map.128.m_ref = bf16[1024,64]{1,0:T(8,128)(2,1)} custom-call(bf16[1024,128]{1,0:T(8,128)(2,1)} %concatenate.7.q_ref, bf16[32768,128]{1,0:T(8,128)(2,1)} %all-gather.2.cloned.1.call-done.kv_ref), custom_call_target="tpu_custom_call" | custom-call | flops 17179869184 | bytes 9175040 | tf_op jit(solution)/shard_map/pallas_call | solution.py:84
  161.4 9.6 %shard_map.129 = bf16[128,512]{1,0:T(8,128)(2,1)} custom-call(bf16[1024,64]{1,0:T(8,128)(2,1)} %shard_map.128.m_ref), custom_call_target="tpu_custom_call" | custom-call | tf_op jit(solution)/shard_map/pallas_call | solution.py:159
  170.9 1.2 multiply_reduce_fusion
  172.2 0.8 add_convert_fusion
  (52 shorter events, 0.7 us)
Async XLA Ops:
  6.5 60.9 %copy-start = (bf16[512,1024]{1,0:T(8,128)(2,1)S(1)}, bf16[512,1024]{1,0:T(8,128)(2,1)}, u32[]{:S(2)}) copy-start(bf16[512,1024]{1,0:T(8,128)(2,1)} %param.20) | copy-start | bytes 3145732
  6.5 116.0 %all-gather.2.cloned.1.call-start = ((), (), s32[]{:S(2)}) async-start(), calls=%async_computation.1 | async-start | bytes 8650752 | tf_op jit(solution)/shard_map/all_gather | solution.py:226
  7.6 1.9 %copy-start.1 = (bf16[128,512]{1,0:T(8,128)(2,1)S(1)}, bf16[128,512]{1,0:T(8,128)(2,1)}, u32[]{:S(2)}) copy-start(bf16[128,512]{1,0:T(8,128)(2,1)} %param.13) | copy-start | bytes 393220
  7.6 1.9 %copy-start.3 = (bf16[512,512]{1,0:T(8,128)(2,1)S(1)}, bf16[512,512]{1,0:T(8,128)(2,1)}, u32[]{:S(2)}) copy-start(bf16[512,512]{1,0:T(8,128)(2,1)} %param.18) | copy-start | bytes 1572868
  9.1 0.8 copy-start.10
  10.5 24.4 %copy-start.4 = (bf16[512,512]{1,0:T(8,128)(2,1)S(1)}, bf16[512,512]{1,0:T(8,128)(2,1)}, u32[]{:S(2)}) copy-start(bf16[512,512]{1,0:T(8,128)(2,1)} %param.16) | copy-start | bytes 1572868
  23.5 12.0 %copy-start.11 = (f32[8]{0:T(128)S(1)}, f32[8]{0:T(128)}, u32[]{:S(2)}) copy-start(f32[8]{0:T(128)} %param.22) | copy-start | bytes 100
  23.6 16.9 %collective-permute-start = (bf16[128,512]{1,0:T(8,128)(2,1)S(1)}, bf16[128,512]{1,0:T(8,128)(2,1)S(1)}, u32[]{:S(2)}, u32[]{:S(2)}) collective-permute-start(bf16[128,512]{1,0:T(8,128)(2,1)S(1)} %copy-done.1), channel_id=1, source_target_pairs={{0,4},{4,8},{8,12},{12,16},{16,20},{20,24},{24,28},{28,32},{32,36}... | collective-permute-start | bytes 393224 | tf_op jit(solution)/shard_map/ppermute | solution.py:33
  27.7 12.8 %collective-permute-start.1 = (bf16[128,512]{1,0:T(8,128)(2,1)S(1)}, bf16[128,512]{1,0:T(8,128)(2,1)S(1)}, u32[]{:S(2)}, u32[]{:S(2)}) collective-permute-start(bf16[128,512]{1,0:T(8,128)(2,1)S(1)} %copy-done.1), channel_id=1, source_target_pairs={{4,0},{8,4},{12,8},{16,12},{20,16},{24,20},{28,24},{32,28},{36,32}... | collective-permute-start | bytes 393224 | tf_op jit(solution)/shard_map/ppermute | solution.py:34
  35.4 8.6 %copy-start.12 = (s32[1,1,12]{2,1,0:T(1,128)S(1)}, s32[1,1,12]{2,1,0:T(1,128)}, u32[]{:S(2)}) copy-start(s32[1,1,12]{2,1,0:T(1,128)} %param.14) | copy-start | bytes 148
  37.1 10.3 %all-to-all-start = ((bf16[128,8,64]{0,2,1:T(8,128)(2,1)}), bf16[128,8,64]{0,2,1:T(8,128)(2,1)S(1)}, u32[]{:S(2)}, u32[]{:S(2)}) async-start(bf16[128,8,64]{0,2,1:T(8,128)(2,1)} %bitcast.14), calls=%async_computation | async-start | bytes 262144 | tf_op jit(solution)/shard_map/all_to_all | solution.py:216
  40.5 12.4 %collective-permute-start.2 = (bf16[384,512]{1,0:T(8,128)(2,1)S(1)}, bf16[384,512]{1,0:T(8,128)(2,1)S(1)}, u32[]{:S(2)}, u32[]{:S(2)}) collective-permute-start(bf16[384,512]{1,0:T(8,128)(2,1)S(1)} %constant_dynamic-update-slice_fusion), channel_id=1, source_target_pairs={{0,1},{1,2},{2,3},{3,0},{4,5},{5,6},{6,7},{7,4},{8,9},{9,10},{10,1... | collective-permute-start | bytes 1179656 | tf_op jit(solution)/shard_map/ppermute | solution.py:196
  41.0 12.9 %collective-permute-start.3 = (bf16[384,512]{1,0:T(8,128)(2,1)S(1)}, bf16[384,512]{1,0:T(8,128)(2,1)S(1)}, u32[]{:S(2)}, u32[]{:S(2)}) collective-permute-start(bf16[384,512]{1,0:T(8,128)(2,1)S(1)} %constant_dynamic-update-slice_fusion), channel_id=1, source_target_pairs={{0,2},{1,3},{2,0},{3,1},{4,6},{5,7},{6,4},{7,5},{8,10},{9,11},{10,... | collective-permute-start | bytes 1179656 | tf_op jit(solution)/shard_map/ppermute | solution.py:196
  42.7 17.2 %collective-permute-start.4 = (bf16[384,512]{1,0:T(8,128)(2,1)S(1)}, bf16[384,512]{1,0:T(8,128)(2,1)}, u32[]{:S(2)}, u32[]{:S(2)}) collective-permute-start(bf16[384,512]{1,0:T(8,128)(2,1)S(1)} %constant_dynamic-update-slice_fusion), channel_id=1, source_target_pairs={{0,3},{1,0},{2,1},{3,2},{4,7},{5,4},{6,5},{7,6},{8,11},{9,8},{10,9... | collective-permute-start | bytes 1179656 | tf_op jit(solution)/shard_map/ppermute | solution.py:196
  53.0 6.9 %copy-start.6 = (bf16[384,512]{1,0:T(8,128)(2,1)}, bf16[384,512]{1,0:T(8,128)(2,1)S(1)}, u32[]{:S(2)}) copy-start(bf16[384,512]{1,0:T(8,128)(2,1)S(1)} %collective-permute-done.2) | copy-start | bytes 1179652
  53.9 6.0 %copy-start.7 = (bf16[384,512]{1,0:T(8,128)(2,1)}, bf16[384,512]{1,0:T(8,128)(2,1)S(1)}, u32[]{:S(2)}) copy-start(bf16[384,512]{1,0:T(8,128)(2,1)S(1)} %collective-permute-done.3) | copy-start | bytes 1179652
  62.7 4.8 %copy-start.8 = (bf16[128,12,128]{0,2,1:T(8,128)(2,1)S(1)}, bf16[128,12,128]{0,2,1:T(8,128)(2,1)}, u32[]{:S(2)}) copy-start(bf16[128,12,128]{0,2,1:T(8,128)(2,1)} %copy.35) | copy-start | bytes 1179652
  67.4 2.2 %copy-start.2 = (bf16[1024,512]{1,0:T(8,128)(2,1)S(1)}, bf16[1024,512]{1,0:T(8,128)(2,1)}, u32[]{:S(2)}) copy-start(bf16[1024,512]{1,0:T(8,128)(2,1)} %param.21) | copy-start | bytes 3145732
  70.8 100.2 %copy-start.5 = (bf16[512,512]{1,0:T(8,128)(2,1)S(1)}, bf16[512,512]{1,0:T(8,128)(2,1)}, u32[]{:S(2)}) copy-start(bf16[512,512]{1,0:T(8,128)(2,1)} %param.19) | copy-start | bytes 1572868
  70.8 101.4 %copy-start.9 = (f32[512]{0:T(512)S(1)}, f32[512]{0:T(512)}, u32[]{:S(2)}) copy-start(f32[512]{0:T(512)} %param.23) | copy-start | bytes 6148
Sparse Core Ops, SparseCore 0:
  23.7 98.7 all-gather.1
